TPU v7x, 256 devices: a whole 4x4x8 slice. The times are simulated.
256 devices in a mesh: kv: 2 (over y_hi), blk: 128 (over x, y_lo, z, core).
Axes of the slice: x: 4, y: 4 (y_hi: 2, y_lo: 2; y = y_hi * 2 + y_lo), z: 8, core: 2. Of those that a mesh axis runs over, the one named last changes fastest.
Arguments:
- hidden_in: bfloat16 [65536, 1280], P('blk'), may hold values from -6 to 6
- w_query: bfloat16 [1280, 1280], P(None, 'kv'), may hold values from -0.15625 to 0.15625
- w_key: bfloat16 [1280, 1280], P(None, 'kv'), may hold values from -0.15625 to 0.15625
- w_value: bfloat16 [1280, 1280], P(None, 'kv'), may hold values from -0.15625 to 0.15625
- w_out: bfloat16 [1280, 1280], P('kv'), may hold values from -0.15625 to 0.15625
- head_gain: float32 [1280], P('kv'), may hold values from 1 to 2.5
- eigen_rate: float32 [1280], replicated, may hold values from 0.15 to 0.6
- pool_keys: bfloat16 [512, 256, 1280], P('blk', None, 'kv'), may hold values from -2 to 2
- pool_values: bfloat16 [512, 256, 1280], P('blk', None, 'kv'), may hold values from -6 to 6
- req_len: int32 [128], P('blk'), may hold values from 1 to 512, as said below
- prefix_len: int32 [128], P('blk'), may hold values from 0 to 4, as said below
- prefix_pages: int32 [128, 4], replicated, may hold values from 0 to 511, as said below
- placement: int32 [256], replicated, may hold values from 0 to 255, as said below
Outputs:
- layer_out: bfloat16 [65536, 1280], P('blk')
- new_keys: bfloat16 [256, 256, 1280], P('blk', None, 'kv')
- new_values: bfloat16 [256, 256, 1280], P('blk', None, 'kv')
Inputs may be any that keep to these rules, and one draw needn't show every extreme that they name: `req_len`: some request has all 512 tokens live. `prefix_len`: some request has 4 cached pages. Page prefix_pages[r, s] lies among pages h * 4 to (h + 1) * 4 - 1 with h = (r + 1 + s * 32) mod 128, for every slot s. Each page once; placement[b] lies among pages e * 2 to (e + 1) * 2 - 1 with e = (b // 2 + (2 * (b mod 2) + 1) * 32) mod 128.
All inputs are finite; a program needn't handle non-finite values.
Results may differ from a plain program's by a relative error of at most 0.0067.
Values may be sent and summed in bfloat16 or wider, within the bound.
A program may use at most 128 MiB of HBM per device.

v0:
```python
import math

import jax
import jax.numpy as jnp
from jax import lax
from jax.sharding import PartitionSpec as P

HD = 64
PAGE = 256
PMAX = 4


epsilon = 1e-06


def from_behind(block, axis, distance):
    devices = range(lax.axis_size(axis))
    route = [((i - distance) % len(devices), i) for i in devices]
    return lax.ppermute(block, axis, route)


def rms_scale(values):
    return values * lax.rsqrt(jnp.mean(values * values, axis=-1, keepdims=True) + epsilon)


def head_normed(projected, head_gain):
    count = projected.shape[0]
    split_heads = projected.reshape(count, -1, HD)
    return (rms_scale(split_heads).reshape(count, -1) * head_gain).astype(jnp.bfloat16)


def attend(query_heads, key_rows, value_rows, visible):
    key_heads = key_rows.reshape(key_rows.shape[0], -1, HD)
    value_heads = value_rows.reshape(value_rows.shape[0], -1, HD)
    scores = jnp.einsum(
        "qhd,khd->hqk", query_heads, key_heads, preferred_element_type=jnp.float32
    ) / math.sqrt(HD)
    weights = jnp.where(visible, jnp.exp(scores), 0.0)
    totals = jnp.sum(weights, axis=-1)
    mixed = jnp.einsum(
        "hqk,khd->qhd",
        weights.astype(jnp.bfloat16),
        value_heads,
        preferred_element_type=jnp.float32,
    )
    return (totals, mixed)


def fetch_page(pool_keys, pool_values, prefix_pages, slot_index):
    devices = lax.axis_size("blk")
    here = lax.axis_index("blk")
    offset = slot_index * devices // PMAX + 1
    asker = (here - offset) % devices
    local = prefix_pages[asker, slot_index] % pool_keys.shape[0]
    send_keys = lax.dynamic_index_in_dim(pool_keys, local, 0, keepdims=False)
    send_values = lax.dynamic_index_in_dim(pool_values, local, 0, keepdims=False)
    return from_behind((send_keys, send_values), "blk", devices - offset)


def relay(key_rows, value_rows, placement):
    devices = lax.axis_size("blk")
    here = lax.axis_index("blk")
    blocks = key_rows.shape[0] // PAGE
    width = key_rows.shape[1]
    key_pages = key_rows.reshape(blocks, PAGE, width)
    value_pages = value_rows.reshape(blocks, PAGE, width)
    key_out = jnp.zeros_like(key_pages)
    value_out = jnp.zeros_like(value_pages)
    for block_index in range(blocks):
        offset = (2 * block_index + 1) * devices // (2 * blocks)
        key_recv, value_recv = from_behind(
            (key_pages[block_index], value_pages[block_index]), "blk", offset
        )
        source = (here - offset) % devices
        target = placement[source * blocks + block_index] % blocks
        key_out = lax.dynamic_update_index_in_dim(key_out, key_recv, target, 0)
        value_out = lax.dynamic_update_index_in_dim(value_out, value_recv, target, 0)
    return (key_out, value_out)


def body(
    hidden_in,
    w_query,
    w_key,
    w_value,
    w_out,
    head_gain,
    eigen_rate,
    pool_keys,
    pool_values,
    req_len,
    prefix_len,
    prefix_pages,
    placement,
):
    tokens_here = hidden_in.shape[0]
    width_half = w_query.shape[1]
    heads_here = width_half // HD
    hidden_f = hidden_in.astype(jnp.float32)
    row_scale = lax.rsqrt(jnp.mean(hidden_f * hidden_f, axis=-1, keepdims=True) + epsilon)
    anchor = hidden_f * row_scale
    queries = head_normed(
        jnp.dot(hidden_in, w_query, preferred_element_type=jnp.float32), head_gain
    )
    key_rows = head_normed(jnp.dot(hidden_in, w_key, preferred_element_type=jnp.float32), head_gain)
    value_rows = (
        jnp.dot(hidden_in, w_value, preferred_element_type=jnp.float32) * row_scale
    ).astype(jnp.bfloat16)
    live_count = req_len[0]
    depth = prefix_len[0]
    query_heads = queries.reshape(tokens_here, heads_here, HD)
    row_index = jnp.arange(tokens_here, dtype=jnp.int32)[:, None]
    col_index = jnp.arange(tokens_here, dtype=jnp.int32)[None, :]
    own_visible = ((col_index <= row_index) & (col_index < live_count))[None]
    totals, mixed = attend(query_heads, key_rows, value_rows, own_visible)
    fetched_keys = []
    fetched_values = []
    for slot_index in range(PMAX):
        page_keys, page_values = fetch_page(pool_keys, pool_values, prefix_pages, slot_index)
        fetched_keys.append(page_keys)
        fetched_values.append(page_values)
    cached_keys = jnp.concatenate(fetched_keys, axis=0)
    cached_values = jnp.concatenate(fetched_values, axis=0)
    page_number = jnp.arange(cached_keys.shape[0], dtype=jnp.int32) // PAGE
    cached_visible = (page_number < depth)[None, None, :]
    more_totals, more_mixed = attend(query_heads, cached_keys, cached_values, cached_visible)
    totals = totals + more_totals
    mixed = mixed + more_mixed
    attended = (mixed / totals.T[:, :, None]).astype(jnp.bfloat16).reshape(tokens_here, width_half)
    partial_branch = jnp.dot(attended, w_out, preferred_element_type=jnp.float32)
    branch = lax.psum(partial_branch, "kv")
    updated = anchor + eigen_rate * (rms_scale(branch) - anchor)
    layer_out = rms_scale(updated).astype(jnp.bfloat16)
    new_keys, new_values = relay(key_rows, value_rows, placement)
    return (layer_out, new_keys, new_values)


def solution(mesh):
    in_specs = (
        P("blk", None),
        P(None, "kv"),
        P(None, "kv"),
        P(None, "kv"),
        P("kv", None),
        P("kv"),
        P(),
        P("blk", None, "kv"),
        P("blk", None, "kv"),
        P("blk"),
        P("blk"),
        P(),
        P(),
    )
    out_specs = (P("blk", None), P("blk", None, "kv"), P("blk", None, "kv"))
    return jax.shard_map(body, mesh=mesh, in_specs=in_specs, out_specs=out_specs, check_vma=False)
```

profile of v0, /device:TPU:6, one launch (start us, length us, event | category | flops | bytes accessed | tf_op | source)
XLA Modules:
  0.0 204.2 jit_solution(14092505884325169063)
XLA Ops:
  7.2 0.0 copy-start
  7.2 0.0 all-reduce.2.cloned.1.call-start
  7.3 1.4 constant_dynamic-slice_fusion
  16.5 0.0 copy-start.8
  16.5 2.5 %dynamic-slice_bitcast_fusion.3 = (bf16[256,640]{1,0:T(8,128)(2,1)}, bf16[256,640]{1,0:T(8,128)(2,1)}, bf16[256,640]{1,0:T(8,128)(2,1)}, bf16[256,640]{1,0:T(8,128)(2,1)}) fusion(bf16[4,256,640]{2,1,0:T(8,128)(2,1)} %param.20, s32[]{:T(128)S(6)} %select_n.116, s32[]{:T(128)S(6)} %select_n.120, s32[]{:T(128)S(6)} %select_n.128, s32[]{:T(128)S(6)} %select_n.124), kind=kLoop, calls=%fused_computation.39 | loop fusion | bytes 2621456 | tf_op jit(solution)/shard_map/jit(dynamic_index_in_dim)/squeeze | solution.py:55
  19.0 6.6 %collective-permute-start.4 = (bf16[256,640]{1,0:T(8,128)(2,1)}, bf16[256,640]{1,0:T(8,128)(2,1)S(1)}, u32[]{:S(2)}, u32[]{:S(2)}) collective-permute-start(bf16[256,640]{1,0:T(8,128)(2,1)} %get-tuple-element.3), channel_id=1, source_target_pairs={{1,0},{2,1},{3,2},{4,3},{5,4},{6,5},{7,6},{8,7},{9,8},{10,9},{11,1... | collective-permute-start | bytes 983048 | tf_op jit(solution)/shard_map/ppermute | solution.py:19
  25.6 1.3 collective-permute-start.5
  26.8 0.0 collective-permute-start.7
  26.9 1.9 collective-permute-start.6
  28.7 1.1 dynamic-slice_bitcast_fusion.7
  29.9 1.0 collective-permute-start
  31.5 0.3 fusion.15
  31.8 0.1 fusion.23
  32.0 2.0 fusion.22
  34.0 2.2 %copy.21 = bf16[512,640]{0,1:T(8,128)(2,1)} copy(bf16[512,640]{1,0:T(8,128)(2,1)} %fusion.22) | data formatting | bytes 1310720 | tf_op jit(solution)/shard_map/convert_element_type | solution.py:108
  36.2 2.7 %fusion.38 = (f32[512,640]{1,0:T(8,128)}, f32[512,640]{1,0:T(8,128)}) fusion(bf16[512,1280]{1,0:T(8,128)(2,1)S(1)} %copy-done.3, bf16[1280,640]{1,0:T(8,128)(2,1)S(1)} %copy-done), kind=kOutput, calls=%fused_computation.71 | convolution fusion | flops 839188480 | bytes 5570560 | tf_op jit(solution)/shard_map/dot_general | solution.py:103
  38.8 1.7 copy.22
  40.6 0.2 reduce_sum.64
  40.8 0.1 mul.111
  40.9 1.5 copy.23
  42.4 4.1 %fusion.37 = (f32[512,640]{1,0:T(8,128)}, f32[512,640]{1,0:T(8,128)}) fusion(bf16[512,1280]{1,0:T(8,128)(2,1)S(1)} %copy-done.3, bf16[1280,640]{1,0:T(8,128)(2,1)} %param.15), kind=kOutput, calls=%fused_computation.70 | convolution fusion | flops 839188480 | bytes 5570560 | tf_op jit(solution)/shard_map/dot_general | solution.py:105
  46.5 1.7 copy.25
  48.2 0.2 reduce_sum.65
  48.4 0.1 mul.118
  48.5 0.0 copy-start.15
  48.6 1.5 copy.26
  50.0 2.8 %multiply_convert_fusion.1 = (bf16[512,640]{1,0:T(8,128)(2,1)S(1)}, bf16[512,640]{1,0:T(8,128)(2,1)S(1)}) fusion(f32[512,640]{1,0:T(8,128)} %get-tuple-element.24, f32[512,640]{1,0:T(8,128)} %copy.26, f32[640]{0:T(1024)S(1)} %copy-done.15, f32[512,640]{1,0:T(8,128)} %get-tuple-element.26, f32[512,640]{1,0:T(8,128)} %copy.23), kind=kLoop, calls=%fused_computation.28 | loop fusion | flops 1966080 | bytes 6556160 | tf_op jit(solution)/shard_map/convert_element_type | solution.py:29
  52.8 1.1 copy.24
  53.9 1.1 copy.27
  55.0 4.7 %fusion.5 = (f32[10,512]{1,0:T(8,128)}, f32[10,512,512]{1,2,0:T(8,128)S(1)}) fusion(pred[512,512]{0,1:T(8,128)(4,1)S(1)} %fusion.23, bf16[512,10,64]{0,2,1:T(8,128)(2,1)} %bitcast.71, bf16[512,10,64]{0,2,1:T(8,128)(2,1)} %bitcast.73), kind=kOutput, calls=%fused_computation.6 | convolution fusion | flops 343403520 | bytes 12079104 | tf_op jit(solution)/shard_map/qhd,khd->hqk/dot_general | solution.py:35
  59.7 3.2 %collective-permute-start.1 = (bf16[256,640]{1,0:T(8,128)(2,1)}, bf16[256,640]{1,0:T(8,128)(2,1)}, u32[]{:S(2)}, u32[]{:S(2)}) collective-permute-start(bf16[256,640]{1,0:T(8,128)(2,1)} %get-tuple-element.8), channel_id=1, source_target_pairs={{33,0},{34,1},{35,2},{36,3},{37,4},{38,5},{39,6},{40,7},{41,8},{42... | collective-permute-start | bytes 983048 | tf_op jit(solution)/shard_map/ppermute | solution.py:19
  63.0 1.0 collective-permute-start.2
  63.9 2.9 %fusion.7 = f32[10,64,512]{2,1,0:T(8,128)} fusion(bf16[512,10,64]{0,2,1:T(8,128)(2,1)S(1)} %bitcast.68, f32[10,512,512]{1,2,0:T(8,128)S(1)} %get-tuple-element.28, pred[512,512]{0,1:T(8,128)(4,1)S(1)} %fusion.23), kind=kOutput, calls=%fused_computation.8 | convolution fusion | flops 343408640 | bytes 12713984 | tf_op jit(solution)/shard_map/hqk,khd->qhd/dot_general | solution.py:40
  67.5 2.4 %pad_maximum_fusion.1 = bf16[1024,640]{1,0:T(8,128)(2,1)} fusion(bf16[256,640]{1,0:T(8,128)(2,1)} %collective-permute-done.7, bf16[256,640]{1,0:T(8,128)(2,1)} %collective-permute-done.6, bf16[256,640]{1,0:T(8,128)(2,1)} %collective-permute-done.5, bf16[256,640]{1,0:T(8,128)(2,1)S(1)} %collective-permute-done.4), kind=kLoop, calls=%fused_computation.26 | loop fusion | flops 5242880 | bytes 2621440 | tf_op jit(solution)/shard_map/concatenate | solution.py:122
  69.9 2.5 %copy.30 = bf16[1024,640]{0,1:T(8,128)(2,1)} copy(bf16[1024,640]{1,0:T(8,128)(2,1)} %pad_maximum_fusion.1) | data formatting | bytes 2621440 | tf_op jit(solution)/shard_map/concatenate | solution.py:122
  72.4 4.4 %collective-permute-done.3 = bf16[256,640]{1,0:T(8,128)(2,1)} collective-permute-done((bf16[256,640]{1,0:T(8,128)(2,1)}, bf16[256,640]{1,0:T(8,128)(2,1)}, u32[]{:S(2)}, u32[]{:S(2)}) %collective-permute-start.3) | collective-permute-done | bytes 327712 | tf_op jit(solution)/shard_map/ppermute | solution.py:19
  76.8 2.2 %collective-permute-done.2 = bf16[256,640]{1,0:T(8,128)(2,1)} collective-permute-done((bf16[256,640]{1,0:T(8,128)(2,1)S(1)}, bf16[256,640]{1,0:T(8,128)(2,1)}, u32[]{:S(2)}, u32[]{:S(2)}) %collective-permute-start.2) | collective-permute-done | bytes 327712 | tf_op jit(solution)/shard_map/ppermute | solution.py:19
  79.0 2.5 %pad_maximum_fusion = bf16[1024,640]{1,0:T(8,128)(2,1)} fusion(bf16[256,640]{1,0:T(8,128)(2,1)} %collective-permute-done.3, bf16[256,640]{1,0:T(8,128)(2,1)} %collective-permute-done.2, bf16[256,640]{1,0:T(8,128)(2,1)} %collective-permute-done.1, bf16[256,640]{1,0:T(8,128)(2,1)} %collective-permute-done), kind=kLoop, calls=%fused_computation.25 | loop fusion | flops 5242880 | bytes 2621440 | tf_op jit(solution)/shard_map/concatenate | solution.py:123
  81.5 2.6 %copy.29 = bf16[1024,640]{0,1:T(8,128)(2,1)} copy(bf16[1024,640]{1,0:T(8,128)(2,1)} %pad_maximum_fusion) | data formatting | bytes 2621440 | tf_op jit(solution)/shard_map/concatenate | solution.py:123
  84.1 10.9 %fusion = (f32[10,512]{1,0:T(8,128)S(1)}, f32[10,512,1024]{2,1,0:T(8,128)}) fusion(pred[1024]{0:T(1024)(128)(4,1)S(1)} %fusion.26, bf16[512,10,64]{0,2,1:T(8,128)(2,1)S(1)} %bitcast.72, bf16[1024,10,64]{0,2,1:T(8,128)(2,1)} %bitcast.69), kind=kOutput, calls=%fused_computation.1 | convolution fusion | flops 686812160 | bytes 22959104 | tf_op jit(solution)/shard_map/qhd,khd->hqk/dot_general | solution.py:35
  95.1 9.0 %divide_convert_fusion = bf16[512,10,64]{0,2,1:T(8,128)(2,1)S(1)} fusion(f32[10,64,512]{2,1,0:T(8,128)S(1)} %copy-done.6, bf16[1024,10,64]{0,2,1:T(8,128)(2,1)S(1)} %bitcast.70, f32[10,512,1024]{2,1,0:T(8,128)} %get-tuple-element.30, pred[1024]{0:T(1024)(128)(4,1)S(1)} %fusion.26, f32[512,10]{0,1:T(8,128)S(1)} %add_bitcast_fusion), kind=kOutput, calls=%fused_computation.27 | convolution fusion | flops 687800320 | bytes 24269824 | tf_op jit(solution)/shard_map/hqk,khd->qhd/dot_general | solution.py:40
  104.1 2.7 %fusion.39 = f32[512,1280]{1,0:T(8,128)} fusion(bf16[512,640]{0,1:T(8,128)(2,1)S(1)} %bitcast.74, bf16[640,1280]{1,0:T(8,128)(2,1)S(1)} %copy-done.18), kind=kOutput, calls=%fused_computation.72 | convolution fusion | flops 838860800 | bytes 4915200 | tf_op jit(solution)/shard_map/dot_general | solution.py:130
  106.8 0.0 all-reduce.2.cloned.1.call-update
  106.8 1.1 copy-done.5
  107.9 0.8 fusion.34
  108.7 4.0 %collective-permute-start.10 = (bf16[256,640]{1,0:T(8,128)(2,1)}, bf16[256,640]{1,0:T(8,128)(2,1)}, u32[]{:S(2)}, u32[]{:S(2)}) collective-permute-start(bf16[256,640]{1,0:T(8,128)(2,1)} %get-tuple-element.12), channel_id=1, source_target_pairs={{96,0},{97,1},{98,2},{99,3},{100,4},{101,5},{102,6},{103,7},{104,8... | collective-permute-start | bytes 983048 | tf_op jit(solution)/shard_map/ppermute | solution.py:19
  112.6 0.8 fusion.35
  113.4 2.0 collective-permute-start.11
  115.5 0.0 collective-permute-start.9
  115.5 0.7 fusion.36
  120.1 0.1 broadcast.150.clone.1
  120.2 1.0 bitcast_dynamic-update-slice_fusion.1
  121.2 3.5 %collective-permute-done.8 = bf16[256,640]{1,0:T(8,128)(2,1)} collective-permute-done((bf16[256,640]{1,0:T(8,128)(2,1)}, bf16[256,640]{1,0:T(8,128)(2,1)}, u32[]{:S(2)}, u32[]{:S(2)}) %collective-permute-start.8) | collective-permute-done | bytes 327712 | tf_op jit(solution)/shard_map/ppermute | solution.py:19
  124.7 0.1 broadcast.150.clone
  124.8 1.0 bitcast_dynamic-update-slice_fusion.3
  125.8 1.0 bitcast_dynamic-update-slice_fusion
  126.9 0.5 collective-permute-done.9
  127.4 1.0 bitcast_dynamic-update-slice_fusion.2
  128.4 0.8 copy-done.10
  129.3 62.9 %all-reduce.2.cloned.1.call-done = f32[512,1280]{1,0:T(8,128)} async-done(((f32[512,1280]{1,0:T(8,128)}), f32[512,1280]{1,0:T(8,128)}) %all-reduce.2.cloned.1.call-update) | async-done | bytes 2621456 | tf_op jit(solution)/shard_map/psum | solution.py:131
  192.2 2.1 %multiply_reduce_fusion.1 = f32[512]{0:T(512)S(1)} fusion(f32[512,1280]{1,0:T(8,128)} %all-reduce.2.cloned.1.call-done), kind=kLoop, calls=%fused_computation.20 | loop fusion | flops 1310208 | bytes 2623488 | tf_op jit(solution)/shard_map/reduce_sum | solution.py:23
  194.3 0.4 copy-done.2
  194.7 0.8 multiply_reduce_fusion
  195.5 1.8 multiply_convert_fusion
  (50 shorter events, 0.2 us)
Async XLA Ops:
  7.2 29.0 %copy-start = (bf16[1280,640]{1,0:T(8,128)(2,1)S(1)}, bf16[1280,640]{1,0:T(8,128)(2,1)}, u32[]{:S(2)}) copy-start(bf16[1280,640]{1,0:T(8,128)(2,1)} %param.14) | copy-start | bytes 4915204
  7.2 185.0 %all-reduce.2.cloned.1.call-start = ((), (), s32[]{:S(2)}) async-start(), calls=%async_computation | async-start | bytes 5242880 | tf_op jit(solution)/shard_map/psum | solution.py:131
  16.5 12.2 %copy-start.8 = (bf16[4,256,640]{2,1,0:T(8,128)(2,1)S(1)}, bf16[4,256,640]{2,1,0:T(8,128)(2,1)}, u32[]{:S(2)}) copy-start(bf16[4,256,640]{2,1,0:T(8,128)(2,1)} %param.21) | copy-start | bytes 3932164
  19.0 12.5 %copy-start.3 = (bf16[512,1280]{1,0:T(8,128)(2,1)S(1)}, bf16[512,1280]{1,0:T(8,128)(2,1)}, u32[]{:S(2)}) copy-start(bf16[512,1280]{1,0:T(8,128)(2,1)} %param.13) | copy-start | bytes 3932164
  19.0 40.7 %collective-permute-start.4 = (bf16[256,640]{1,0:T(8,128)(2,1)}, bf16[256,640]{1,0:T(8,128)(2,1)S(1)}, u32[]{:S(2)}, u32[]{:S(2)}) collective-permute-start(bf16[256,640]{1,0:T(8,128)(2,1)} %get-tuple-element.3), channel_id=1, source_target_pairs={{1,0},{2,1},{3,2},{4,3},{5,4},{6,5},{7,6},{8,7},{9,8},{10,9},{11,1... | collective-permute-start | bytes 983048 | tf_op jit(solution)/shard_map/ppermute | solution.py:19
  25.6 37.4 %collective-permute-start.5 = (bf16[256,640]{1,0:T(8,128)(2,1)}, bf16[256,640]{1,0:T(8,128)(2,1)}, u32[]{:S(2)}, u32[]{:S(2)}) collective-permute-start(bf16[256,640]{1,0:T(8,128)(2,1)} %get-tuple-element.4), channel_id=1, source_target_pairs={{33,0},{34,1},{35,2},{36,3},{37,4},{38,5},{39,6},{40,7},{41,8},{42... | collective-permute-start | bytes 983048 | tf_op jit(solution)/shard_map/ppermute | solution.py:19
  26.8 36.1 %collective-permute-start.7 = (bf16[256,640]{1,0:T(8,128)(2,1)}, bf16[256,640]{1,0:T(8,128)(2,1)}, u32[]{:S(2)}, u32[]{:S(2)}) collective-permute-start(bf16[256,640]{1,0:T(8,128)(2,1)} %get-tuple-element.5), channel_id=1, source_target_pairs={{97,0},{98,1},{99,2},{100,3},{101,4},{102,5},{103,6},{104,7},{105,... | collective-permute-start | bytes 983048 | tf_op jit(solution)/shard_map/ppermute | solution.py:19
  26.9 5.1 %copy-start.17 = (bf16[1280,640]{1,0:T(8,128)(2,1)S(1)}, bf16[1280,640]{1,0:T(8,128)(2,1)}, u32[]{:S(2)}) copy-start(bf16[1280,640]{1,0:T(8,128)(2,1)} %param.16) | copy-start | bytes 4915204
  26.9 40.7 %collective-permute-start.6 = (bf16[256,640]{1,0:T(8,128)(2,1)}, bf16[256,640]{1,0:T(8,128)(2,1)}, u32[]{:S(2)}, u32[]{:S(2)}) collective-permute-start(bf16[256,640]{1,0:T(8,128)(2,1)} %get-tuple-element.6), channel_id=1, source_target_pairs={{65,0},{66,1},{67,2},{68,3},{69,4},{70,5},{71,6},{72,7},{73,8},{74... | collective-permute-start | bytes 983048 | tf_op jit(solution)/shard_map/ppermute | solution.py:19
  29.9 42.6 %collective-permute-start = (bf16[256,640]{1,0:T(8,128)(2,1)}, bf16[256,640]{1,0:T(8,128)(2,1)}, u32[]{:S(2)}, u32[]{:S(2)}) collective-permute-start(bf16[256,640]{1,0:T(8,128)(2,1)} %get-tuple-element.7), channel_id=1, source_target_pairs={{1,0},{2,1},{3,2},{4,3},{5,4},{6,5},{7,6},{8,7},{9,8},{10,9},{11,1... | collective-permute-start | bytes 983048 | tf_op jit(solution)/shard_map/ppermute | solution.py:19
  48.5 1.5 copy-start.15
  55.0 8.0 %copy-start.12 = (bf16[256,640]{1,0:T(8,128)(2,1)S(1)}, bf16[256,640]{1,0:T(8,128)(2,1)}, u32[]{:S(2)}) copy-start(bf16[256,640]{1,0:T(8,128)(2,1)} %get-tuple-element.10) | copy-start | bytes 983044
  55.0 8.9 %copy-start.4 = (bf16[512,640]{0,1:T(8,128)(2,1)S(1)}, bf16[512,640]{0,1:T(8,128)(2,1)}, u32[]{:S(2)}) copy-start(bf16[512,640]{0,1:T(8,128)(2,1)} %copy.21) | copy-start | bytes 1966084
  59.7 12.7 %collective-permute-start.1 = (bf16[256,640]{1,0:T(8,128)(2,1)}, bf16[256,640]{1,0:T(8,128)(2,1)}, u32[]{:S(2)}, u32[]{:S(2)}) collective-permute-start(bf16[256,640]{1,0:T(8,128)(2,1)} %get-tuple-element.8), channel_id=1, source_target_pairs={{33,0},{34,1},{35,2},{36,3},{37,4},{38,5},{39,6},{40,7},{41,8},{42... | collective-permute-start | bytes 983048 | tf_op jit(solution)/shard_map/ppermute | solution.py:19
  63.0 13.8 %collective-permute-start.3 = (bf16[256,640]{1,0:T(8,128)(2,1)}, bf16[256,640]{1,0:T(8,128)(2,1)}, u32[]{:S(2)}, u32[]{:S(2)}) collective-permute-start(bf16[256,640]{1,0:T(8,128)(2,1)} %get-tuple-element.9), channel_id=1, source_target_pairs={{97,0},{98,1},{99,2},{100,3},{101,4},{102,5},{103,6},{104,7},{105,... | collective-permute-start | bytes 983048 | tf_op jit(solution)/shard_map/ppermute | solution.py:19
  63.0 16.0 %collective-permute-start.2 = (bf16[256,640]{1,0:T(8,128)(2,1)S(1)}, bf16[256,640]{1,0:T(8,128)(2,1)}, u32[]{:S(2)}, u32[]{:S(2)}) collective-permute-start(bf16[256,640]{1,0:T(8,128)(2,1)S(1)} %copy-done.12), channel_id=1, source_target_pairs={{65,0},{66,1},{67,2},{68,3},{69,4},{70,5},{71,6},{72,7},{73,8},{74... | collective-permute-start | bytes 983048 | tf_op jit(solution)/shard_map/ppermute | solution.py:19
  81.5 2.6 %copy-start.9 = (bf16[512,640]{0,1:T(8,128)(2,1)S(1)}, bf16[512,640]{0,1:T(8,128)(2,1)}, u32[]{:S(2)}) copy-start(bf16[512,640]{0,1:T(8,128)(2,1)} %copy.24) | copy-start | bytes 1966084
  84.1 11.0 %copy-start.14 = (f32[10,512]{1,0:T(8,128)S(1)}, f32[10,512]{1,0:T(8,128)}, u32[]{:S(2)}) copy-start(f32[10,512]{1,0:T(8,128)} %get-tuple-element.27) | copy-start | bytes 61444
  84.1 11.0 %copy-start.6 = (f32[10,64,512]{2,1,0:T(8,128)S(1)}, f32[10,64,512]{2,1,0:T(8,128)}, u32[]{:S(2)}) copy-start(f32[10,64,512]{2,1,0:T(8,128)} %fusion.7) | copy-start | bytes 3932164
  84.1 11.0 %copy-start.7 = (bf16[1024,640]{0,1:T(8,128)(2,1)S(1)}, bf16[1024,640]{0,1:T(8,128)(2,1)}, u32[]{:S(2)}) copy-start(bf16[1024,640]{0,1:T(8,128)(2,1)} %copy.29) | copy-start | bytes 3932164
  95.0 9.0 %copy-start.18 = (bf16[640,1280]{1,0:T(8,128)(2,1)S(1)}, bf16[640,1280]{1,0:T(8,128)(2,1)}, u32[]{:S(2)}) copy-start(bf16[640,1280]{1,0:T(8,128)(2,1)} %param.17) | copy-start | bytes 4915204
  106.8 1.1 copy-start.5
  107.9 7.6 %copy-start.16 = (s32[256]{0:T(256)S(1)}, s32[256]{0:T(256)}, u32[]{:S(2)}) copy-start(s32[256]{0:T(256)} %param.25) | copy-start | bytes 3076
  108.7 11.4 %collective-permute-start.10 = (bf16[256,640]{1,0:T(8,128)(2,1)}, bf16[256,640]{1,0:T(8,128)(2,1)}, u32[]{:S(2)}, u32[]{:S(2)}) collective-permute-start(bf16[256,640]{1,0:T(8,128)(2,1)} %get-tuple-element.12), channel_id=1, source_target_pairs={{96,0},{97,1},{98,2},{99,3},{100,4},{101,5},{102,6},{103,7},{104,8... | collective-permute-start | bytes 983048 | tf_op jit(solution)/shard_map/ppermute | solution.py:19
  113.4 11.3 %collective-permute-start.8 = (bf16[256,640]{1,0:T(8,128)(2,1)}, bf16[256,640]{1,0:T(8,128)(2,1)}, u32[]{:S(2)}, u32[]{:S(2)}) collective-permute-start(bf16[256,640]{1,0:T(8,128)(2,1)} %get-tuple-element.14), channel_id=1, source_target_pairs={{96,0},{97,1},{98,2},{99,3},{100,4},{101,5},{102,6},{103,7},{104,8... | collective-permute-start | bytes 983048 | tf_op jit(solution)/shard_map/ppermute | solution.py:19
  113.4 12.4 %collective-permute-start.11 = (bf16[256,640]{1,0:T(8,128)(2,1)S(1)}, bf16[256,640]{1,0:T(8,128)(2,1)}, u32[]{:S(2)}, u32[]{:S(2)}) collective-permute-start(bf16[256,640]{1,0:T(8,128)(2,1)S(1)} %get-tuple-element.11), channel_id=1, source_target_pairs={{32,0},{33,1},{34,2},{35,3},{36,4},{37,5},{38,6},{39,7},{40,8},{41... | collective-permute-start | bytes 983048 | tf_op jit(solution)/shard_map/ppermute | solution.py:19
  115.5 11.9 %collective-permute-start.9 = (bf16[256,640]{1,0:T(8,128)(2,1)S(1)}, bf16[256,640]{1,0:T(8,128)(2,1)}, u32[]{:S(2)}, u32[]{:S(2)}) collective-permute-start(bf16[256,640]{1,0:T(8,128)(2,1)S(1)} %get-tuple-element.13), channel_id=1, source_target_pairs={{32,0},{33,1},{34,2},{35,3},{36,4},{37,5},{38,6},{39,7},{40,8},{41... | collective-permute-start | bytes 983048 | tf_op jit(solution)/shard_map/ppermute | solution.py:19
  126.9 67.4 %copy-start.11 = (bf16[2,256,640]{2,1,0:T(8,128)(2,1)}, bf16[2,256,640]{2,1,0:T(8,128)(2,1)S(1)}, u32[]{:S(2)}) copy-start(bf16[2,256,640]{2,1,0:T(8,128)(2,1)S(1)} %bitcast_dynamic-update-slice_fusion) | copy-start | bytes 1966084
  126.9 67.4 %copy-start.13 = (f32[1280]{0:T(1024)S(1)}, f32[1280]{0:T(1024)}, u32[]{:S(2)}) copy-start(f32[1280]{0:T(1024)} %param.19) | copy-start | bytes 15364
  128.4 0.8 copy-start.10
  192.1 2.5 %copy-start.2 = (f32[512,1280]{1,0:T(8,128)S(1)}, f32[512,1280]{1,0:T(8,128)}, u32[]{:S(2)}) copy-start(f32[512,1280]{1,0:T(8,128)} %all-reduce.2.cloned.1.call-done) | copy-start | bytes 7864324
  195.5 1.8 copy-start.1
Sparse Core Ops, SparseCore 0:
  107.0 85.1 all-reduce.1
where the time goes:
time: 206 us; the launch traced here: 204 us
  waiting for transfers between devices  73.5 us (36%)
  matrix products  39.1 us (19%)
  local copies, waits for them, and re-layouts  29.9 us (15%)
  between operations  27.5 us (13%)
  starting transfers between devices  20.9 us (10%)
  other arithmetic  13.2 us (6%)
    psum x1, waiting for transfers between devices, body(): branch = lax.psum(partial_branch, 'kv')  62.9 us
    ppermute x12, starting transfers between devices, from_behind(): return lax.ppermute(block, axis, route)  20.9 us
    dot_general x2, matrix products, attend(): jnp.einsum('qhd,khd->hqk', query_heads, key_heads, preferred_element_type...  15.6 us
    dot_general x2, matrix products, attend(): jnp.einsum('hqk,khd->qhd', weights.astype(jnp.bfloat16), value_heads, pre...  11.9 us
    ppermute x12, waiting for transfers between devices, from_behind(): return lax.ppermute(block, axis, route)  10.6 us
  transfers between devices with their start and end apart: 13, of which 5 were waited for; matrix products, arithmetic and copies ran while one was open for 21% of the time, Pallas kernels for 0%

commit v1 on v0

--- a/solution.py
+++ b/solution.py
@@ -44,6 +44,13 @@
         preferred_element_type=jnp.float32,
     )
     return (totals, mixed)
+
+
+def in_kv_order(mine, other, axis):
+    first = lax.axis_index("kv") == 0
+    low = jnp.where(first, mine, other)
+    high = jnp.where(first, other, mine)
+    return jnp.concatenate([low, high], axis=axis)
 
 
 def fetch_page(pool_keys, pool_values, prefix_pages, slot_index):
@@ -94,6 +101,7 @@
     placement,
 ):
     tokens_here = hidden_in.shape[0]
+    other_w_out = from_behind(w_out, "kv", 1)
     width_half = w_query.shape[1]
     heads_here = width_half // HD
     hidden_f = hidden_in.astype(jnp.float32)
@@ -127,8 +135,12 @@
     totals = totals + more_totals
     mixed = mixed + more_mixed
     attended = (mixed / totals.T[:, :, None]).astype(jnp.bfloat16).reshape(tokens_here, width_half)
-    partial_branch = jnp.dot(attended, w_out, preferred_element_type=jnp.float32)
-    branch = lax.psum(partial_branch, "kv")
+    other_attended = from_behind(attended, "kv", 1)
+    branch = jnp.dot(
+        in_kv_order(attended, other_attended, 1),
+        in_kv_order(w_out, other_w_out, 0),
+        preferred_element_type=jnp.float32,
+    )
     updated = anchor + eigen_rate * (rms_scale(branch) - anchor)
     layer_out = rms_scale(updated).astype(jnp.bfloat16)
     new_keys, new_values = relay(key_rows, value_rows, placement)

time: 206 us -> 142 us (0.69)
  waiting for transfers between devices: 73.5 us -> 20 us
  between operations: 27.5 us -> 14 us
  starting transfers between devices: 20.9 us -> 31.3 us
  local copies, waits for them, and re-layouts: 29.9 us -> 25.3 us
  other arithmetic: 13.2 us -> 10.7 us
    psum x1 -> x0, waiting for transfers between devices: 62.9 us -> none  [body(): branch = lax.psum(partial_branch, 'kv')]
    ppermute x12 -> x14, starting transfers between devices: 20.9 us -> 31.3 us  [from_behind(): return lax.ppermute(block, axis, route)]
    ppermute x12 -> x14, waiting for transfers between devices: 10.6 us -> 20 us  [from_behind(): return lax.ppermute(block, axis, route)]
    unnamed x38 -> x32, local copies, waits for them, and re-layouts: 2.33 us -> 0.08 us
    reduce_sum x4 -> x3, other arithmetic: 3.3 us -> 1.16 us  [rms_scale(): jnp.mean(values * values, axis=-1, keepdims=True) + epsilon]
  transfers between devices with their start and end apart: 13 -> 14, of which waited for: 5 -> 3; matrix products, arithmetic and copies ran while one was open for 21% -> 46% of each run, Pallas kernels for 0% -> 0%
where the time goes in v1:
time: 142 us; the launch traced here: 141 us
  matrix products  39.5 us (28%)
  starting transfers between devices  31.3 us (22%)
  local copies, waits for them, and re-layouts  25.3 us (18%)
  waiting for transfers between devices  20 us (14%)
  between operations  14 us (10%)
  other arithmetic  10.7 us (8%)
    ppermute x14, starting transfers between devices, from_behind(): return lax.ppermute(block, axis, route)  31.3 us
    ppermute x14, waiting for transfers between devices, from_behind(): return lax.ppermute(block, axis, route)  20 us
    dot_general x2, matrix products, attend(): jnp.einsum('qhd,khd->hqk', query_heads, key_heads, preferred_element_type...  15.4 us
    dot_general x2, matrix products, attend(): jnp.einsum('hqk,khd->qhd', weights.astype(jnp.bfloat16), value_heads, pre...  11.8 us
    dot_general x1, matrix products, body(): jnp.dot(hidden_in, w_key, preferred_element_type=jnp.float32)  4.1 us
    dot_general x1, matrix products, body(): jnp.dot(hidden_in, w_value, preferred_element_type=jnp.float32) * row_scale  3.45 us
    mul x2, local copies, waits for them, and re-layouts, rms_scale(): values * values  3.43 us
    mul x4, local copies, waits for them, and re-layouts, rms_scale(): values * lax.rsqrt(jnp.mean(values * values, axis=-1, keepdims=True) + ep...  3.23 us
  transfers between devices with their start and end apart: 14, of which 3 were waited for; matrix products, arithmetic and copies ran while one was open for 46% of the time, Pallas kernels for 0%

profile of v1, /device:TPU:6, one launch (start us, length us, event | category | flops | bytes accessed | tf_op | source)
XLA Modules:
  0.0 140.8 jit_solution(11771703965426239457)
XLA Ops:
  0.6 0.0 copy-start
  0.7 1.5 %constant_dynamic-slice_fusion = (s32[1,1]{0,1:T(1,128)}, s32[1,1]{0,1:T(1,128)}, s32[1,1]{0,1:T(1,128)}, s32[1,1]{0,1:T(1,128)}) fusion(s32[128,4]{0,1:T(4,128)} %param.24, s32[]{:T(128)S(6)} %select_n.139, s32[]{:T(128)S(6)} %select_n.143, s32[]{:T(128)S(6)} %select_n.151, s32[]{:T(128)S(6)} %select_n.147), kind=kLoop, calls=%fused_computation.66 | loop fusion | bytes 48 | tf_op jit(solution)/shard_map/dynamic_slice | solution.py:61
  10.0 0.0 copy-start.8
  10.0 2.5 %dynamic-slice_bitcast_fusion.3 = (bf16[256,640]{1,0:T(8,128)(2,1)}, bf16[256,640]{1,0:T(8,128)(2,1)}, bf16[256,640]{1,0:T(8,128)(2,1)}, bf16[256,640]{1,0:T(8,128)(2,1)}) fusion(bf16[4,256,640]{2,1,0:T(8,128)(2,1)} %param.20, s32[]{:T(128)S(6)} %select_n.141, s32[]{:T(128)S(6)} %select_n.145, s32[]{:T(128)S(6)} %select_n.153, s32[]{:T(128)S(6)} %select_n.149), kind=kLoop, calls=%fused_computation.50 | loop fusion | bytes 2621456 | tf_op jit(solution)/shard_map/jit(dynamic_index_in_dim)/squeeze | solution.py:62
  12.5 6.6 %collective-permute-start.4 = (bf16[256,640]{1,0:T(8,128)(2,1)}, bf16[256,640]{1,0:T(8,128)(2,1)}, u32[]{:S(2)}, u32[]{:S(2)}) collective-permute-start(bf16[256,640]{1,0:T(8,128)(2,1)} %get-tuple-element.7), channel_id=1, source_target_pairs={{1,0},{2,1},{3,2},{4,3},{5,4},{6,5},{7,6},{8,7},{9,8},{10,9},{11,1... | collective-permute-start | bytes 983048 | tf_op jit(solution)/shard_map/ppermute | solution.py:19
  19.1 1.3 collective-permute-start.5
  20.4 0.0 collective-permute-start.7
  20.4 1.8 %collective-permute-start.6 = (bf16[256,640]{1,0:T(8,128)(2,1)}, bf16[256,640]{1,0:T(8,128)(2,1)}, u32[]{:S(2)}, u32[]{:S(2)}) collective-permute-start(bf16[256,640]{1,0:T(8,128)(2,1)} %get-tuple-element.10), channel_id=1, source_target_pairs={{65,0},{66,1},{67,2},{68,3},{69,4},{70,5},{71,6},{72,7},{73,8},{74... | collective-permute-start | bytes 983048 | tf_op jit(solution)/shard_map/ppermute | solution.py:19
  22.3 1.1 dynamic-slice_bitcast_fusion.7
  23.4 1.0 collective-permute-start
  24.4 0.6 fusion.44
  30.2 0.3 fusion.19
  30.5 0.1 fusion.30
  30.7 3.5 %fusion.26 = bf16[512,640]{1,0:T(8,128)(2,1)} fusion(bf16[512,1280]{1,0:T(8,128)(2,1)S(1)} %copy-done.2, bf16[1280,640]{1,0:T(8,128)(2,1)} %param.16, f32[512]{0:T(512)S(1)} %add_rsqrt_fusion.4), kind=kOutput, calls=%fused_computation.30 | convolution fusion | flops 839516160 | bytes 3606528 | tf_op jit(solution)/shard_map/dot_general | solution.py:115
  34.1 2.2 %copy.21 = bf16[512,640]{0,1:T(8,128)(2,1)} copy(bf16[512,640]{1,0:T(8,128)(2,1)} %fusion.26) | data formatting | bytes 1310720 | tf_op jit(solution)/shard_map/convert_element_type | solution.py:116
  36.3 2.7 %fusion.46 = (f32[512,640]{1,0:T(8,128)}, f32[512,640]{1,0:T(8,128)}) fusion(bf16[512,1280]{1,0:T(8,128)(2,1)S(1)} %copy-done.2, bf16[1280,640]{1,0:T(8,128)(2,1)S(1)} %copy-done), kind=kOutput, calls=%fused_computation.83 | convolution fusion | flops 839188480 | bytes 5570560 | tf_op jit(solution)/shard_map/dot_general | solution.py:111
  39.0 1.7 %copy.22 = f32[512,640]{0,1:T(8,128)S(1)} copy(f32[512,640]{1,0:T(8,128)} %get-tuple-element.29) | data formatting | bytes 2621440 | tf_op jit(solution)/shard_map/mul | solution.py:23
  40.7 0.2 reduce_sum.64
  40.9 0.1 mul.111
  41.0 1.5 %copy.23 = f32[512,640]{1,0:T(8,128)} copy(f32[512,640]{0,1:T(8,128)S(1)} %bitcast.66) | data formatting | bytes 2621440 | tf_op jit(solution)/shard_map/mul | solution.py:23
  42.5 4.1 %fusion.45 = (f32[512,640]{1,0:T(8,128)}, f32[512,640]{1,0:T(8,128)}) fusion(bf16[512,1280]{1,0:T(8,128)(2,1)S(1)} %copy-done.2, bf16[1280,640]{1,0:T(8,128)(2,1)} %param.15), kind=kOutput, calls=%fused_computation.82 | convolution fusion | flops 839188480 | bytes 5570560 | tf_op jit(solution)/shard_map/dot_general | solution.py:113
  46.6 1.7 %copy.25 = f32[512,640]{0,1:T(8,128)S(1)} copy(f32[512,640]{1,0:T(8,128)} %get-tuple-element.27) | data formatting | bytes 2621440 | tf_op jit(solution)/shard_map/mul | solution.py:23
  48.3 0.2 reduce_sum.65
  48.5 0.1 mul.118
  48.7 0.0 copy-start.14
  48.7 1.5 %copy.26 = f32[512,640]{1,0:T(8,128)} copy(f32[512,640]{0,1:T(8,128)S(1)} %bitcast.67) | data formatting | bytes 2621440 | tf_op jit(solution)/shard_map/mul | solution.py:23
  50.1 2.8 %multiply_convert_fusion.1 = (bf16[512,640]{1,0:T(8,128)(2,1)S(1)}, bf16[512,640]{1,0:T(8,128)(2,1)S(1)}) fusion(f32[512,640]{1,0:T(8,128)} %get-tuple-element.28, f32[512,640]{1,0:T(8,128)} %copy.26, f32[640]{0:T(1024)S(1)} %copy-done.14, f32[512,640]{1,0:T(8,128)} %get-tuple-element.30, f32[512,640]{1,0:T(8,128)} %copy.23), kind=kLoop, calls=%fused_computation.37 | loop fusion | flops 1966080 | bytes 6556160 | tf_op jit(solution)/shard_map/convert_element_type | solution.py:29
  52.9 1.2 copy.24
  54.1 1.1 copy.27
  55.2 4.7 %fusion.5 = (f32[10,512]{1,0:T(8,128)}, f32[10,512,512]{1,2,0:T(8,128)S(1)}) fusion(pred[512,512]{0,1:T(8,128)(4,1)S(1)} %fusion.30, bf16[512,10,64]{0,2,1:T(8,128)(2,1)} %bitcast.71, bf16[512,10,64]{0,2,1:T(8,128)(2,1)} %bitcast.73), kind=kOutput, calls=%fused_computation.6 | convolution fusion | flops 343403520 | bytes 12079104 | tf_op jit(solution)/shard_map/qhd,khd->hqk/dot_general | solution.py:35
  59.9 2.9 %fusion.7 = f32[10,64,512]{2,1,0:T(8,128)} fusion(bf16[512,10,64]{0,2,1:T(8,128)(2,1)S(1)} %bitcast.68, f32[10,512,512]{1,2,0:T(8,128)S(1)} %get-tuple-element.32, pred[512,512]{0,1:T(8,128)(4,1)S(1)} %fusion.30), kind=kOutput, calls=%fused_computation.8 | convolution fusion | flops 343408640 | bytes 12713984 | tf_op jit(solution)/shard_map/hqk,khd->qhd/dot_general | solution.py:40
  62.8 0.9 fusion.42
  63.8 3.3 %collective-permute-start.1 = (bf16[256,640]{1,0:T(8,128)(2,1)}, bf16[256,640]{1,0:T(8,128)(2,1)}, u32[]{:S(2)}, u32[]{:S(2)}) collective-permute-start(bf16[256,640]{1,0:T(8,128)(2,1)} %get-tuple-element.12), channel_id=1, source_target_pairs={{33,0},{34,1},{35,2},{36,3},{37,4},{38,5},{39,6},{40,7},{41,8},{42... | collective-permute-start | bytes 983048 | tf_op jit(solution)/shard_map/ppermute | solution.py:19
  67.1 0.9 collective-permute-start.2
  68.0 0.9 fusion.43
  68.9 1.1 collective-permute-start.13
  70.1 1.4 pad_maximum_fusion.1
  71.4 1.5 %copy.30 = bf16[1024,640]{0,1:T(8,128)(2,1)} copy(bf16[1024,640]{1,0:T(8,128)(2,1)S(1)} %pad_maximum_fusion.1) | data formatting | bytes 2621440 | tf_op jit(solution)/shard_map/concatenate | solution.py:130
  73.0 2.1 %collective-permute-start.12 = (bf16[256,640]{1,0:T(8,128)(2,1)}, bf16[256,640]{1,0:T(8,128)(2,1)}, u32[]{:S(2)}, u32[]{:S(2)}) collective-permute-start(bf16[256,640]{1,0:T(8,128)(2,1)} %get-tuple-element.16), channel_id=1, source_target_pairs={{96,0},{97,1},{98,2},{99,3},{100,4},{101,5},{102,6},{103,7},{104,8... | collective-permute-start | bytes 983048 | tf_op jit(solution)/shard_map/ppermute | solution.py:19
  75.1 5.1 %collective-permute-done.1 = bf16[256,640]{1,0:T(8,128)(2,1)} collective-permute-done((bf16[256,640]{1,0:T(8,128)(2,1)}, bf16[256,640]{1,0:T(8,128)(2,1)}, u32[]{:S(2)}, u32[]{:S(2)}) %collective-permute-start.1) | collective-permute-done | bytes 327712 | tf_op jit(solution)/shard_map/ppermute | solution.py:19
  80.2 2.9 %collective-permute-start.9 = (bf16[640,1280]{1,0:T(8,128)(2,1)}, bf16[640,1280]{1,0:T(8,128)(2,1)}, u32[]{:S(2)}, u32[]{:S(2)}) collective-permute-start(bf16[640,1280]{1,0:T(8,128)(2,1)} %param.17), channel_id=1, source_target_pairs={{128,0},{0,128},{129,1},{1,129},{130,2},{2,130},{131,3},{3,131},{1... | collective-permute-start | bytes 4915208 | tf_op jit(solution)/shard_map/ppermute | solution.py:19
  83.1 3.0 %collective-permute-start.11 = (bf16[256,640]{1,0:T(8,128)(2,1)}, bf16[256,640]{1,0:T(8,128)(2,1)}, u32[]{:S(2)}, u32[]{:S(2)}) collective-permute-start(bf16[256,640]{1,0:T(8,128)(2,1)} %get-tuple-element.17), channel_id=1, source_target_pairs={{32,0},{33,1},{34,2},{35,3},{36,4},{37,5},{38,6},{39,7},{40,8},{41... | collective-permute-start | bytes 983048 | tf_op jit(solution)/shard_map/ppermute | solution.py:19
  86.1 0.7 collective-permute-done.2
  86.7 4.0 %collective-permute-start.10 = (bf16[256,640]{1,0:T(8,128)(2,1)}, bf16[256,640]{1,0:T(8,128)(2,1)S(1)}, u32[]{:S(2)}, u32[]{:S(2)}) collective-permute-start(bf16[256,640]{1,0:T(8,128)(2,1)} %get-tuple-element.18), channel_id=1, source_target_pairs={{96,0},{97,1},{98,2},{99,3},{100,4},{101,5},{102,6},{103,7},{104,8... | collective-permute-start | bytes 983048 | tf_op jit(solution)/shard_map/ppermute | solution.py:19
  90.7 1.3 pad_maximum_fusion
  92.0 1.5 %copy.29 = bf16[1024,640]{0,1:T(8,128)(2,1)} copy(bf16[1024,640]{1,0:T(8,128)(2,1)S(1)} %pad_maximum_fusion) | data formatting | bytes 2621440 | tf_op jit(solution)/shard_map/concatenate | solution.py:131
  93.5 10.8 %fusion = (f32[10,512]{1,0:T(8,128)S(1)}, f32[10,512,1024]{2,1,0:T(8,128)}) fusion(pred[1024]{0:T(1024)(128)(4,1)S(1)} %fusion.33, bf16[512,10,64]{0,2,1:T(8,128)(2,1)} %bitcast.72, bf16[1024,10,64]{0,2,1:T(8,128)(2,1)} %bitcast.69), kind=kOutput, calls=%fused_computation.1 | convolution fusion | flops 686812160 | bytes 22959104 | tf_op jit(solution)/shard_map/qhd,khd->hqk/dot_general | solution.py:35
  104.3 8.9 %divide_convert_fusion = bf16[512,10,64]{0,2,1:T(8,128)(2,1)S(1)} fusion(f32[10,64,512]{2,1,0:T(8,128)S(1)} %copy-done.6, bf16[1024,10,64]{0,2,1:T(8,128)(2,1)S(1)} %bitcast.70, f32[10,512,1024]{2,1,0:T(8,128)} %get-tuple-element.34, pred[1024]{0:T(1024)(128)(4,1)S(1)} %fusion.33, f32[512,10]{0,1:T(8,128)S(1)} %add_bitcast_fusion), kind=kOutput, calls=%fused_computation.36 | convolution fusion | flops 687800320 | bytes 24269824 | tf_op jit(solution)/shard_map/hqk,khd->qhd/dot_general | solution.py:40
  113.2 3.3 %collective-permute-start.8 = (bf16[512,640]{0,1:T(8,128)(2,1)S(1)}, bf16[512,640]{0,1:T(8,128)(2,1)S(1)}, u32[]{:S(2)}, u32[]{:S(2)}) collective-permute-start(bf16[512,640]{0,1:T(8,128)(2,1)S(1)} %bitcast.74), channel_id=1, source_target_pairs={{128,0},{0,128},{129,1},{1,129},{130,2},{2,130},{131,3},{3,131},{1... | collective-permute-start | bytes 1966088 | tf_op jit(solution)/shard_map/ppermute | solution.py:19
  116.4 0.1 broadcast.150.clone.1
  116.5 1.0 bitcast_dynamic-update-slice_fusion.1
  117.5 0.1 broadcast.150.clone
  117.7 1.0 bitcast_dynamic-update-slice_fusion
  118.7 0.0 copy-start.10
  118.7 0.0 copy-start.5
  118.7 1.3 bitcast_dynamic-update-slice_fusion.2
  120.0 0.0 copy-start.9
  120.0 14.3 %collective-permute-done.8 = bf16[512,640]{0,1:T(8,128)(2,1)S(1)} collective-permute-done((bf16[512,640]{0,1:T(8,128)(2,1)S(1)}, bf16[512,640]{0,1:T(8,128)(2,1)S(1)}, u32[]{:S(2)}, u32[]{:S(2)}) %collective-permute-start.8) | collective-permute-done | bytes 655392 | tf_op jit(solution)/shard_map/ppermute | solution.py:19
  134.3 0.1 broadcast_select_fusion.3
  134.4 1.6 %broadcast_select_fusion.1 = (bf16[640,1280]{1,0:T(8,128)(2,1)S(1)}, bf16[640,1280]{1,0:T(8,128)(2,1)S(1)}) fusion(bf16[640,1280]{1,0:T(8,128)(2,1)S(1)} %copy-done.5, bf16[640,1280]{1,0:T(8,128)(2,1)} %collective-permute-done.9, pred[]{:T(512)S(6)} %eq.17), kind=kLoop, calls=%fused_computation.26 | loop fusion | flops 1638400 | bytes 6553601 | tf_op jit(solution)/shard_map/jit(_where)/select_n | solution.py:51
  136.1 0.0 copy-start.12
  136.1 2.0 %multiply_reduce_fusion.1 = (f32[512]{0:T(512)S(1)}, f32[512,1280]{1,0:T(8,128)S(1)}) fusion(bf16[640,1280]{1,0:T(8,128)(2,1)S(1)} %get-tuple-element.4, bf16[640,1280]{1,0:T(8,128)(2,1)S(1)} %get-tuple-element.3, bf16[512,640]{0,1:T(8,128)(2,1)S(1)} %get-tuple-element.6, bf16[512,640]{0,1:T(8,128)(2,1)S(1)} %get-tuple-element.5), kind=kOutput, calls=%fused_computation.24 | convolution fusion | flops 1688206848 | bytes 7211008 | tf_op jit(solution)/shard_map/dot_general | solution.py:139
  138.2 0.8 multiply_reduce_fusion
  139.0 1.8 %multiply_convert_fusion = bf16[512,1280]{1,0:T(8,128)(2,1)} fusion(f32[512]{0:T(512)S(1)} %add_rsqrt_fusion.2, f32[512,1280]{1,0:T(8,128)S(1)} %get-tuple-element.36, f32[512]{0:T(512)S(1)} %add_rsqrt_fusion.3, f32[1280]{0:T(1024)S(1)} %copy-done.12, f32[512]{0:T(512)S(1)} %add_rsqrt_fusion.4, bf16[512,1280]{1,0:T(8,128)(2,1)S(1)} %copy-done.2), kind=kLoop, calls=%fused_computation.22 | loop fusion | flops 5242880 | bytes 5254144 | tf_op jit(solution)/shard_map/convert_element_type | solution.py:145
  (46 shorter events, 0.2 us)
Async XLA Ops:
  0.6 35.7 %copy-start = (bf16[1280,640]{1,0:T(8,128)(2,1)S(1)}, bf16[1280,640]{1,0:T(8,128)(2,1)}, u32[]{:S(2)}) copy-start(bf16[1280,640]{1,0:T(8,128)(2,1)} %param.14) | copy-start | bytes 4915204
  10.0 12.3 %copy-start.8 = (bf16[4,256,640]{2,1,0:T(8,128)(2,1)S(1)}, bf16[4,256,640]{2,1,0:T(8,128)(2,1)}, u32[]{:S(2)}) copy-start(bf16[4,256,640]{2,1,0:T(8,128)(2,1)} %param.21) | copy-start | bytes 3932164
  12.5 11.8 %copy-start.15 = (s32[256]{0:T(256)S(1)}, s32[256]{0:T(256)}, u32[]{:S(2)}) copy-start(s32[256]{0:T(256)} %param.25) | copy-start | bytes 3076
  12.5 17.6 %copy-start.2 = (bf16[512,1280]{1,0:T(8,128)(2,1)S(1)}, bf16[512,1280]{1,0:T(8,128)(2,1)}, u32[]{:S(2)}) copy-start(bf16[512,1280]{1,0:T(8,128)(2,1)} %param.13) | copy-start | bytes 3932164
  12.5 51.2 %collective-permute-start.4 = (bf16[256,640]{1,0:T(8,128)(2,1)}, bf16[256,640]{1,0:T(8,128)(2,1)}, u32[]{:S(2)}, u32[]{:S(2)}) collective-permute-start(bf16[256,640]{1,0:T(8,128)(2,1)} %get-tuple-element.7), channel_id=1, source_target_pairs={{1,0},{2,1},{3,2},{4,3},{5,4},{6,5},{7,6},{8,7},{9,8},{10,9},{11,1... | collective-permute-start | bytes 983048 | tf_op jit(solution)/shard_map/ppermute | solution.py:19
  19.1 47.9 %collective-permute-start.5 = (bf16[256,640]{1,0:T(8,128)(2,1)}, bf16[256,640]{1,0:T(8,128)(2,1)}, u32[]{:S(2)}, u32[]{:S(2)}) collective-permute-start(bf16[256,640]{1,0:T(8,128)(2,1)} %get-tuple-element.8), channel_id=1, source_target_pairs={{33,0},{34,1},{35,2},{36,3},{37,4},{38,5},{39,6},{40,7},{41,8},{42... | collective-permute-start | bytes 983048 | tf_op jit(solution)/shard_map/ppermute | solution.py:19
  20.4 46.7 %collective-permute-start.7 = (bf16[256,640]{1,0:T(8,128)(2,1)}, bf16[256,640]{1,0:T(8,128)(2,1)}, u32[]{:S(2)}, u32[]{:S(2)}) collective-permute-start(bf16[256,640]{1,0:T(8,128)(2,1)} %get-tuple-element.9), channel_id=1, source_target_pairs={{97,0},{98,1},{99,2},{100,3},{101,4},{102,5},{103,6},{104,7},{105,... | collective-permute-start | bytes 983048 | tf_op jit(solution)/shard_map/ppermute | solution.py:19
  20.4 48.5 %collective-permute-start.6 = (bf16[256,640]{1,0:T(8,128)(2,1)}, bf16[256,640]{1,0:T(8,128)(2,1)}, u32[]{:S(2)}, u32[]{:S(2)}) collective-permute-start(bf16[256,640]{1,0:T(8,128)(2,1)} %get-tuple-element.10), channel_id=1, source_target_pairs={{65,0},{66,1},{67,2},{68,3},{69,4},{70,5},{71,6},{72,7},{73,8},{74... | collective-permute-start | bytes 983048 | tf_op jit(solution)/shard_map/ppermute | solution.py:19
  23.4 49.6 %collective-permute-start = (bf16[256,640]{1,0:T(8,128)(2,1)}, bf16[256,640]{1,0:T(8,128)(2,1)S(1)}, u32[]{:S(2)}, u32[]{:S(2)}) collective-permute-start(bf16[256,640]{1,0:T(8,128)(2,1)} %get-tuple-element.11), channel_id=1, source_target_pairs={{1,0},{2,1},{3,2},{4,3},{5,4},{6,5},{7,6},{8,7},{9,8},{10,9},{11,1... | collective-permute-start | bytes 983048 | tf_op jit(solution)/shard_map/ppermute | solution.py:19
  48.7 1.5 %copy-start.14 = (f32[640]{0:T(1024)S(1)}, f32[640]{0:T(1024)}, u32[]{:S(2)}) copy-start(f32[640]{0:T(1024)} %param.18) | copy-start | bytes 7684
  55.2 4.7 %copy-start.3 = (bf16[512,640]{0,1:T(8,128)(2,1)S(1)}, bf16[512,640]{0,1:T(8,128)(2,1)}, u32[]{:S(2)}) copy-start(bf16[512,640]{0,1:T(8,128)(2,1)} %copy.21) | copy-start | bytes 1966084
  59.9 2.9 %copy-start.4 = (bf16[512,640]{1,0:T(8,128)(2,1)S(1)}, bf16[512,640]{1,0:T(8,128)(2,1)}, u32[]{:S(2)}) copy-start(bf16[512,640]{1,0:T(8,128)(2,1)} %fusion.26) | copy-start | bytes 1966084
  59.9 7.2 %copy-start.11 = (bf16[256,640]{1,0:T(8,128)(2,1)S(1)}, bf16[256,640]{1,0:T(8,128)(2,1)}, u32[]{:S(2)}) copy-start(bf16[256,640]{1,0:T(8,128)(2,1)} %get-tuple-element.14) | copy-start | bytes 983044
  63.8 16.4 %collective-permute-start.1 = (bf16[256,640]{1,0:T(8,128)(2,1)}, bf16[256,640]{1,0:T(8,128)(2,1)}, u32[]{:S(2)}, u32[]{:S(2)}) collective-permute-start(bf16[256,640]{1,0:T(8,128)(2,1)} %get-tuple-element.12), channel_id=1, source_target_pairs={{33,0},{34,1},{35,2},{36,3},{37,4},{38,5},{39,6},{40,7},{41,8},{42... | collective-permute-start | bytes 983048 | tf_op jit(solution)/shard_map/ppermute | solution.py:19
  67.1 16.0 %collective-permute-start.3 = (bf16[256,640]{1,0:T(8,128)(2,1)}, bf16[256,640]{1,0:T(8,128)(2,1)}, u32[]{:S(2)}, u32[]{:S(2)}) collective-permute-start(bf16[256,640]{1,0:T(8,128)(2,1)} %get-tuple-element.13), channel_id=1, source_target_pairs={{97,0},{98,1},{99,2},{100,3},{101,4},{102,5},{103,6},{104,7},{105,... | collective-permute-start | bytes 983048 | tf_op jit(solution)/shard_map/ppermute | solution.py:19
  67.1 19.7 %collective-permute-start.2 = (bf16[256,640]{1,0:T(8,128)(2,1)S(1)}, bf16[256,640]{1,0:T(8,128)(2,1)}, u32[]{:S(2)}, u32[]{:S(2)}) collective-permute-start(bf16[256,640]{1,0:T(8,128)(2,1)S(1)} %copy-done.11), channel_id=1, source_target_pairs={{65,0},{66,1},{67,2},{68,3},{69,4},{70,5},{71,6},{72,7},{73,8},{74... | collective-permute-start | bytes 983048 | tf_op jit(solution)/shard_map/ppermute | solution.py:19
  68.9 48.7 %collective-permute-start.13 = (bf16[256,640]{1,0:T(8,128)(2,1)}, bf16[256,640]{1,0:T(8,128)(2,1)}, u32[]{:S(2)}, u32[]{:S(2)}) collective-permute-start(bf16[256,640]{1,0:T(8,128)(2,1)} %get-tuple-element.15), channel_id=1, source_target_pairs={{32,0},{33,1},{34,2},{35,3},{36,4},{37,5},{38,6},{39,7},{40,8},{41... | collective-permute-start | bytes 983048 | tf_op jit(solution)/shard_map/ppermute | solution.py:19
  73.0 40.2 %collective-permute-start.12 = (bf16[256,640]{1,0:T(8,128)(2,1)}, bf16[256,640]{1,0:T(8,128)(2,1)}, u32[]{:S(2)}, u32[]{:S(2)}) collective-permute-start(bf16[256,640]{1,0:T(8,128)(2,1)} %get-tuple-element.16), channel_id=1, source_target_pairs={{96,0},{97,1},{98,2},{99,3},{100,4},{101,5},{102,6},{103,7},{104,8... | collective-permute-start | bytes 983048 | tf_op jit(solution)/shard_map/ppermute | solution.py:19
  80.2 54.3 %collective-permute-start.9 = (bf16[640,1280]{1,0:T(8,128)(2,1)}, bf16[640,1280]{1,0:T(8,128)(2,1)}, u32[]{:S(2)}, u32[]{:S(2)}) collective-permute-start(bf16[640,1280]{1,0:T(8,128)(2,1)} %param.17), channel_id=1, source_target_pairs={{128,0},{0,128},{129,1},{1,129},{130,2},{2,130},{131,3},{3,131},{1... | collective-permute-start | bytes 4915208 | tf_op jit(solution)/shard_map/ppermute | solution.py:19
  83.1 35.6 %collective-permute-start.11 = (bf16[256,640]{1,0:T(8,128)(2,1)}, bf16[256,640]{1,0:T(8,128)(2,1)}, u32[]{:S(2)}, u32[]{:S(2)}) collective-permute-start(bf16[256,640]{1,0:T(8,128)(2,1)} %get-tuple-element.17), channel_id=1, source_target_pairs={{32,0},{33,1},{34,2},{35,3},{36,4},{37,5},{38,6},{39,7},{40,8},{41... | collective-permute-start | bytes 983048 | tf_op jit(solution)/shard_map/ppermute | solution.py:19
  86.7 30.8 %collective-permute-start.10 = (bf16[256,640]{1,0:T(8,128)(2,1)}, bf16[256,640]{1,0:T(8,128)(2,1)S(1)}, u32[]{:S(2)}, u32[]{:S(2)}) collective-permute-start(bf16[256,640]{1,0:T(8,128)(2,1)} %get-tuple-element.18), channel_id=1, source_target_pairs={{96,0},{97,1},{98,2},{99,3},{100,4},{101,5},{102,6},{103,7},{104,8... | collective-permute-start | bytes 983048 | tf_op jit(solution)/shard_map/ppermute | solution.py:19
  93.5 10.8 %copy-start.13 = (f32[10,512]{1,0:T(8,128)S(1)}, f32[10,512]{1,0:T(8,128)}, u32[]{:S(2)}) copy-start(f32[10,512]{1,0:T(8,128)} %get-tuple-element.31) | copy-start | bytes 61444
  93.5 10.8 %copy-start.6 = (f32[10,64,512]{2,1,0:T(8,128)S(1)}, f32[10,64,512]{2,1,0:T(8,128)}, u32[]{:S(2)}) copy-start(f32[10,64,512]{2,1,0:T(8,128)} %fusion.7) | copy-start | bytes 3932164
  93.5 10.8 %copy-start.7 = (bf16[1024,640]{0,1:T(8,128)(2,1)S(1)}, bf16[1024,640]{0,1:T(8,128)(2,1)}, u32[]{:S(2)}) copy-start(bf16[1024,640]{0,1:T(8,128)(2,1)} %copy.29) | copy-start | bytes 3932164
  113.2 21.1 %collective-permute-start.8 = (bf16[512,640]{0,1:T(8,128)(2,1)S(1)}, bf16[512,640]{0,1:T(8,128)(2,1)S(1)}, u32[]{:S(2)}, u32[]{:S(2)}) collective-permute-start(bf16[512,640]{0,1:T(8,128)(2,1)S(1)} %bitcast.74), channel_id=1, source_target_pairs={{128,0},{0,128},{129,1},{1,129},{130,2},{2,130},{131,3},{3,131},{1... | collective-permute-start | bytes 1966088 | tf_op jit(solution)/shard_map/ppermute | solution.py:19
  118.7 15.7 %copy-start.10 = (bf16[2,256,640]{2,1,0:T(8,128)(2,1)}, bf16[2,256,640]{2,1,0:T(8,128)(2,1)S(1)}, u32[]{:S(2)}) copy-start(bf16[2,256,640]{2,1,0:T(8,128)(2,1)S(1)} %bitcast_dynamic-update-slice_fusion) | copy-start | bytes 1966084
  118.7 15.7 %copy-start.5 = (bf16[640,1280]{1,0:T(8,128)(2,1)S(1)}, bf16[640,1280]{1,0:T(8,128)(2,1)}, u32[]{:S(2)}) copy-start(bf16[640,1280]{1,0:T(8,128)(2,1)} %param.17) | copy-start | bytes 4915204
  120.0 16.1 %copy-start.9 = (bf16[2,256,640]{2,1,0:T(8,128)(2,1)}, bf16[2,256,640]{2,1,0:T(8,128)(2,1)S(1)}, u32[]{:S(2)}) copy-start(bf16[2,256,640]{2,1,0:T(8,128)(2,1)S(1)} %bitcast_dynamic-update-slice_fusion.2) | copy-start | bytes 1966084
  136.1 2.0 %copy-start.12 = (f32[1280]{0:T(1024)S(1)}, f32[1280]{0:T(1024)}, u32[]{:S(2)}) copy-start(f32[1280]{0:T(1024)} %param.19) | copy-start | bytes 15364
  139.0 1.8 %copy-start.1 = (bf16[1280,640]{1,0:T(8,128)(2,1)S(1)}, bf16[1280,640]{1,0:T(8,128)(2,1)}, u32[]{:S(2)}) copy-start(bf16[1280,640]{1,0:T(8,128)(2,1)} %param.14) | copy-start | bytes 4915204

commit v2 on v1

--- a/solution.py
+++ b/solution.py
@@ -3,6 +3,8 @@
 import jax
 import jax.numpy as jnp
 from jax import lax
+from jax.experimental import pallas as pl
+from jax.experimental.pallas import tpu as pltpu
 from jax.sharding import PartitionSpec as P
 
 HD = 64
@@ -51,6 +53,66 @@
     low = jnp.where(first, mine, other)
     high = jnp.where(first, other, mine)
     return jnp.concatenate([low, high], axis=axis)
+
+
+def attention_kernel(live_ref, depth_ref, q_ref, k_ref, v_ref, *refs):
+    page_refs, out_ref = refs[:-1], refs[-1]
+    tile = q_ref.shape[0]
+    own = k_ref.shape[0]
+    live = live_ref[0]
+    depth = depth_ref[0]
+    query = q_ref[...]
+    lane = lax.broadcasted_iota(jnp.int32, query.shape, 1)
+    first = lane < HD
+    row = pl.program_id(1) * tile + lax.broadcasted_iota(jnp.int32, (tile, own), 0)
+    col = lax.broadcasted_iota(jnp.int32, (tile, own), 1)
+    own_visible = (col <= row) & (col < live)
+    contract = (((1,), (1,)), ((), ()))
+    results = []
+    for in_head in (first, jnp.logical_not(first)):
+        query_head = jnp.where(in_head, query, jnp.zeros_like(query))
+        scores = lax.dot_general(
+            query_head, k_ref[...], contract, preferred_element_type=jnp.float32
+        ) * (1.0 / math.sqrt(HD))
+        weights = jnp.where(own_visible, jnp.exp(scores), 0.0)
+        total = jnp.sum(weights, axis=1, keepdims=True)
+        mixed = jnp.dot(
+            weights.astype(jnp.bfloat16), v_ref[...], preferred_element_type=jnp.float32
+        )
+        for page in range(PMAX):
+            key_page = page_refs[page]
+            value_page = page_refs[PMAX + page]
+            scores = lax.dot_general(
+                query_head, key_page[...], contract, preferred_element_type=jnp.float32
+            ) * (1.0 / math.sqrt(HD))
+            weights = jnp.where(page < depth, jnp.exp(scores), 0.0)
+            total = total + jnp.sum(weights, axis=1, keepdims=True)
+            mixed = mixed + jnp.dot(
+                weights.astype(jnp.bfloat16), value_page[...], preferred_element_type=jnp.float32
+            )
+        results.append(mixed / total)
+    out_ref[...] = jnp.where(first, results[0], results[1]).astype(out_ref.dtype)
+
+
+def attention(queries, key_rows, value_rows, page_keys, page_values, req_len, prefix_len):
+    tokens, width = queries.shape
+    tile = 128
+    lanes = 2 * HD
+    grid = (width // lanes, tokens // tile)
+    own_spec = pl.BlockSpec((tokens, lanes), lambda h, t, *_: (0, h))
+    page_spec = pl.BlockSpec((PAGE, lanes), lambda h, t, *_: (0, h))
+    tile_spec = pl.BlockSpec((tile, lanes), lambda h, t, *_: (t, h))
+    grid_spec = pltpu.PrefetchScalarGridSpec(
+        num_scalar_prefetch=2,
+        grid=grid,
+        in_specs=[tile_spec, own_spec, own_spec] + [page_spec] * (2 * PMAX),
+        out_specs=tile_spec,
+    )
+    return pl.pallas_call(
+        attention_kernel,
+        out_shape=jax.ShapeDtypeStruct((tokens, width), jnp.bfloat16),
+        grid_spec=grid_spec,
+    )(req_len, prefix_len, queries, key_rows, value_rows, *page_keys, *page_values)
 
 
 def fetch_page(pool_keys, pool_values, prefix_pages, slot_index):
@@ -114,27 +176,15 @@
     value_rows = (
         jnp.dot(hidden_in, w_value, preferred_element_type=jnp.float32) * row_scale
     ).astype(jnp.bfloat16)
-    live_count = req_len[0]
-    depth = prefix_len[0]
-    query_heads = queries.reshape(tokens_here, heads_here, HD)
-    row_index = jnp.arange(tokens_here, dtype=jnp.int32)[:, None]
-    col_index = jnp.arange(tokens_here, dtype=jnp.int32)[None, :]
-    own_visible = ((col_index <= row_index) & (col_index < live_count))[None]
-    totals, mixed = attend(query_heads, key_rows, value_rows, own_visible)
     fetched_keys = []
     fetched_values = []
     for slot_index in range(PMAX):
         page_keys, page_values = fetch_page(pool_keys, pool_values, prefix_pages, slot_index)
         fetched_keys.append(page_keys)
         fetched_values.append(page_values)
-    cached_keys = jnp.concatenate(fetched_keys, axis=0)
-    cached_values = jnp.concatenate(fetched_values, axis=0)
-    page_number = jnp.arange(cached_keys.shape[0], dtype=jnp.int32) // PAGE
-    cached_visible = (page_number < depth)[None, None, :]
-    more_totals, more_mixed = attend(query_heads, cached_keys, cached_values, cached_visible)
-    totals = totals + more_totals
-    mixed = mixed + more_mixed
-    attended = (mixed / totals.T[:, :, None]).astype(jnp.bfloat16).reshape(tokens_here, width_half)
+    attended = attention(
+        queries, key_rows, value_rows, fetched_keys, fetched_values, req_len, prefix_len
+    )
     other_attended = from_behind(attended, "kv", 1)
     branch = jnp.dot(
         in_kv_order(attended, other_attended, 1),

time: 142 us -> 134 us (0.944)
  matrix products: 39.5 us -> 9.94 us
  Pallas kernels: 0 us -> 21.2 us
  waiting for transfers between devices: 20 us -> 16.1 us
  starting transfers between devices: 31.3 us -> 32.9 us
    dot_general x4 -> x0, matrix products: 27.2 us -> none  [the longest x2 15.4 us: attend(): jnp.einsum('qhd,khd->hqk', query_heads, key_heads, preferred_element_type...]
    pallas_call x0 -> x1, Pallas kernels: none -> 21.2 us  [attention(): pl.pallas_call(attention_kernel, out_shape=jax.ShapeDtypeStruct((tokens,...]
    mul x4, local copies, waits for them, and re-layouts: 3.23 us -> 8.06 us  [rms_scale(): values * lax.rsqrt(jnp.mean(values * values, axis=-1, keepdims=True) + ep...]
    convert_element_type x3 -> x0, local copies, waits for them, and re-layouts: 4.45 us -> none  [the longest x2 2.28 us: head_normed(): (rms_scale(split_heads).reshape(count, -1) * head_gain).astype(jnp.bfloat16)]
    ppermute x14, waiting for transfers between devices: 20 us -> 16.1 us  [from_behind(): return lax.ppermute(block, axis, route)]
    concatenate x2 -> x0, local copies, waits for them, and re-layouts: 3.07 us -> none  [the longest x1 1.54 us: body(): cached_keys = jnp.concatenate(fetched_keys, axis=0)]
    concatenate x2 -> x0, other arithmetic: 2.67 us -> none  [the longest x1 1.38 us: body(): cached_keys = jnp.concatenate(fetched_keys, axis=0)]
    reduce_sum x3, other arithmetic: 1.16 us -> 3.8 us  [rms_scale(): jnp.mean(values * values, axis=-1, keepdims=True) + epsilon]
  transfers between devices with their start and end apart: 14 -> 14, of which waited for: 3 -> 4; matrix products, arithmetic and copies ran while one was open for 46% -> 28% of each run, Pallas kernels for 0% -> 16%
where the time goes in v2:
time: 134 us; the launch traced here: 132 us
  starting transfers between devices  32.9 us (25%)
  local copies, waits for them, and re-layouts  26.4 us (20%)
  Pallas kernels  21.2 us (16%)
  waiting for transfers between devices  16.1 us (12%)
  between operations  13.7 us (10%)
  other arithmetic  12 us (9%)
  matrix products  9.94 us (7%)
    ppermute x14, starting transfers between devices, from_behind(): return lax.ppermute(block, axis, route)  32.9 us
    pallas_call x1, Pallas kernels, attention(): pl.pallas_call(attention_kernel, out_shape=jax.ShapeDtypeStruct((tokens,...  21.2 us
    ppermute x14, waiting for transfers between devices, from_behind(): return lax.ppermute(block, axis, route)  16.1 us
    mul x4, local copies, waits for them, and re-layouts, rms_scale(): values * lax.rsqrt(jnp.mean(values * values, axis=-1, keepdims=True) + ep...  8.06 us
    mul x2, local copies, waits for them, and re-layouts, rms_scale(): values * values  5.57 us
    dot_general x1, matrix products, body(): jnp.dot(hidden_in, w_key, preferred_element_type=jnp.float32)  4.1 us
    reduce_sum x3, other arithmetic, rms_scale(): jnp.mean(values * values, axis=-1, keepdims=True) + epsilon  3.8 us
    convert_element_type x1, other arithmetic, head_normed(): (rms_scale(split_heads).reshape(count, -1) * head_gain).astype(jnp.bfloat16)  3.74 us
  transfers between devices with their start and end apart: 14, of which 4 were waited for; matrix products, arithmetic and copies ran while one was open for 28% of the time, Pallas kernels for 16%

profile of v2, /device:TPU:6, one launch (start us, length us, event | category | flops | bytes accessed | tf_op | source)
XLA Modules:
  0.0 132.2 jit_solution(8369865162647907272)
XLA Ops:
  0.6 0.0 copy-start
  0.7 1.4 %constant_dynamic-slice_fusion.3 = (s32[1,1]{0,1:T(1,128)}, s32[1,1]{0,1:T(1,128)}, s32[1,1]{0,1:T(1,128)}, s32[1,1]{0,1:T(1,128)}) fusion(s32[128,4]{0,1:T(4,128)} %param.24, s32[]{:T(128)S(6)} %select_n.133, s32[]{:T(128)S(6)} %select_n.125, s32[]{:T(128)S(6)} %select_n.121, s32[]{:T(128)S(6)} %select_n.129), kind=kLoop, calls=%fused_computation.44 | loop fusion | bytes 48 | tf_op jit(solution)/shard_map/dynamic_slice | solution.py:123
  9.8 0.0 copy-start.5
  9.8 2.5 %dynamic-slice_bitcast_fusion = (bf16[256,640]{1,0:T(8,128)(2,1)}, bf16[256,640]{1,0:T(8,128)(2,1)}, bf16[256,640]{1,0:T(8,128)(2,1)}, bf16[256,640]{1,0:T(8,128)(2,1)}) fusion(bf16[4,256,640]{2,1,0:T(8,128)(2,1)} %param.21, s32[]{:T(128)S(6)} %select_n.135, s32[]{:T(128)S(6)} %select_n.127, s32[]{:T(128)S(6)} %select_n.123, s32[]{:T(128)S(6)} %select_n.131), kind=kLoop, calls=%fused_computation.28 | loop fusion | bytes 2621456 | tf_op jit(solution)/shard_map/jit(dynamic_index_in_dim)/squeeze | solution.py:125
  12.3 6.6 %collective-permute-start.4 = (bf16[256,640]{1,0:T(8,128)(2,1)}, bf16[256,640]{1,0:T(8,128)(2,1)S(1)}, u32[]{:S(2)}, u32[]{:S(2)}) collective-permute-start(bf16[256,640]{1,0:T(8,128)(2,1)} %get-tuple-element.9), channel_id=1, source_target_pairs={{1,0},{2,1},{3,2},{4,3},{5,4},{6,5},{7,6},{8,7},{9,8},{10,9},{11,1... | collective-permute-start | bytes 983048 | tf_op jit(solution)/shard_map/ppermute | solution.py:21
  18.9 1.3 collective-permute-start.5
  20.1 1.9 %collective-permute-start.6 = (bf16[256,640]{1,0:T(8,128)(2,1)}, bf16[256,640]{1,0:T(8,128)(2,1)}, u32[]{:S(2)}, u32[]{:S(2)}) collective-permute-start(bf16[256,640]{1,0:T(8,128)(2,1)} %get-tuple-element.10), channel_id=1, source_target_pairs={{65,0},{66,1},{67,2},{68,3},{69,4},{70,5},{71,6},{72,7},{73,8},{74... | collective-permute-start | bytes 983048 | tf_op jit(solution)/shard_map/ppermute | solution.py:21
  22.0 0.0 collective-permute-start.7
  22.0 1.1 dynamic-slice_bitcast_fusion.4
  23.1 1.0 collective-permute-start
  24.1 0.3 fusion.7
  24.4 2.7 %fusion.17 = (f32[512,640]{1,0:T(8,128)}, f32[512,640]{1,0:T(8,128)}) fusion(bf16[512,1280]{1,0:T(8,128)(2,1)S(1)} %copy-done.1, bf16[1280,640]{1,0:T(8,128)(2,1)S(1)} %copy-done), kind=kOutput, calls=%fused_computation.50 | convolution fusion | flops 839188480 | bytes 5570560 | tf_op jit(solution)/shard_map/dot_general | solution.py:173
  27.1 2.8 %copy.16 = f32[512,640]{0,1:T(8,128)} copy(f32[512,640]{1,0:T(8,128)} %get-tuple-element.29) | data formatting | bytes 2621440 | tf_op jit(solution)/shard_map/mul | solution.py:25
  29.9 1.5 %reduce_sum.46 = f32[512,10]{0,1:T(8,128)S(1)} reduce(f32[512,10,64]{0,2,1:T(8,128)} %bitcast.41, f32[]{:T(128)} %constant.123.clone.1), dimensions={2}, to_apply=%region_1.0 | reduce | flops 322560 | bytes 1331204 | tf_op jit(solution)/shard_map/reduce_sum | solution.py:25
  31.4 1.2 mul.109
  32.6 2.8 %copy.17 = f32[512,640]{1,0:T(8,128)} copy(f32[512,640]{0,1:T(8,128)} %bitcast.42) | data formatting | bytes 2621440 | tf_op jit(solution)/shard_map/mul | solution.py:25
  35.4 4.1 %fusion.16 = (f32[512,640]{1,0:T(8,128)}, f32[512,640]{1,0:T(8,128)}) fusion(bf16[512,1280]{1,0:T(8,128)(2,1)S(1)} %copy-done.1, bf16[1280,640]{1,0:T(8,128)(2,1)} %param.15), kind=kOutput, calls=%fused_computation.49 | convolution fusion | flops 839188480 | bytes 5570560 | tf_op jit(solution)/shard_map/dot_general | solution.py:175
  39.5 2.8 %copy.18 = f32[512,640]{0,1:T(8,128)} copy(f32[512,640]{1,0:T(8,128)} %get-tuple-element.27) | data formatting | bytes 2621440 | tf_op jit(solution)/shard_map/mul | solution.py:25
  42.3 1.5 %reduce_sum.47 = f32[512,10]{0,1:T(8,128)S(1)} reduce(f32[512,10,64]{0,2,1:T(8,128)} %bitcast.40, f32[]{:T(128)} %constant.123.clone.1), dimensions={2}, to_apply=%region_2.0 | reduce | flops 322560 | bytes 1331204 | tf_op jit(solution)/shard_map/reduce_sum | solution.py:25
  43.8 1.2 mul.116
  45.0 2.8 %copy.19 = f32[512,640]{1,0:T(8,128)} copy(f32[512,640]{0,1:T(8,128)} %bitcast.43) | data formatting | bytes 2621440 | tf_op jit(solution)/shard_map/mul | solution.py:25
  47.9 3.7 %multiply_convert_fusion.1 = (bf16[512,640]{1,0:T(8,128)(2,1)S(1)}, bf16[512,640]{1,0:T(8,128)(2,1)}) fusion(f32[512,640]{1,0:T(8,128)} %get-tuple-element.28, f32[512,640]{1,0:T(8,128)} %copy.19, f32[640]{0:T(1024)S(1)} %copy-done.12, f32[512,640]{1,0:T(8,128)} %get-tuple-element.30, f32[512,640]{1,0:T(8,128)} %copy.17), kind=kLoop, calls=%fused_computation.20 | loop fusion | flops 1966080 | bytes 6556160 | tf_op jit(solution)/shard_map/convert_element_type | solution.py:31
  51.6 1.2 fusion.8.v_ref
  52.8 0.0 copy-start.3
  52.8 0.0 copy-start.13
  52.8 0.0 collective-permute-done.4.refs_4_
  52.9 2.7 %collective-permute-start.1 = (bf16[256,640]{1,0:T(8,128)(2,1)S(1)}, bf16[256,640]{1,0:T(8,128)(2,1)S(1)}, u32[]{:S(2)}, u32[]{:S(2)}) collective-permute-start(bf16[256,640]{1,0:T(8,128)(2,1)S(1)} %copy-done.10), channel_id=1, source_target_pairs={{33,0},{34,1},{35,2},{36,3},{37,4},{38,5},{39,6},{40,7},{41,8},{42... | collective-permute-start | bytes 983048 | tf_op jit(solution)/shard_map/ppermute | solution.py:21
  55.6 0.0 collective-permute-done.5.refs_5_
  55.6 2.9 %collective-permute-start.9 = (bf16[640,1280]{1,0:T(8,128)(2,1)}, bf16[640,1280]{1,0:T(8,128)(2,1)}, u32[]{:S(2)}, u32[]{:S(2)}) collective-permute-start(bf16[640,1280]{1,0:T(8,128)(2,1)} %param.17), channel_id=1, source_target_pairs={{128,0},{0,128},{129,1},{1,129},{130,2},{2,130},{131,3},{3,131},{1... | collective-permute-start | bytes 4915208 | tf_op jit(solution)/shard_map/ppermute | solution.py:21
  58.5 0.9 fusion.13
  59.4 0.0 collective-permute-done.6.refs_6_
  59.4 0.7 collective-permute-start.12
  60.1 0.0 collective-permute-done.7.refs_7_
  60.1 0.0 collective-permute-start.2
  60.1 0.0 collective-permute-done.refs_0_
  60.1 1.5 %collective-permute-start.3 = (bf16[256,640]{1,0:T(8,128)(2,1)}, bf16[256,640]{1,0:T(8,128)(2,1)}, u32[]{:S(2)}, u32[]{:S(2)}) collective-permute-start(bf16[256,640]{1,0:T(8,128)(2,1)} %get-tuple-element.11), channel_id=1, source_target_pairs={{97,0},{98,1},{99,2},{100,3},{101,4},{102,5},{103,6},{104,7},{105,... | collective-permute-start | bytes 983048 | tf_op jit(solution)/shard_map/ppermute | solution.py:21
  61.6 0.9 fusion.14
  62.5 1.7 %collective-permute-done.1.refs_1_ = bf16[256,640]{1,0:T(8,128)(2,1)S(1)} collective-permute-done((bf16[256,640]{1,0:T(8,128)(2,1)S(1)}, bf16[256,640]{1,0:T(8,128)(2,1)S(1)}, u32[]{:S(2)}, u32[]{:S(2)}) %collective-permute-start.1) | collective-permute-done | bytes 327712 | tf_op jit(solution)/shard_map/ppermute | solution.py:21
  64.2 0.7 copy-done.9
  64.9 0.9 collective-permute-start.10
  65.8 0.7 fusion.15
  71.6 0.4 collective-permute-done.2.refs_2_
  71.9 12.3 %collective-permute-start.13 = (bf16[256,640]{1,0:T(8,128)(2,1)}, bf16[256,640]{1,0:T(8,128)(2,1)}, u32[]{:S(2)}, u32[]{:S(2)}) collective-permute-start(bf16[256,640]{1,0:T(8,128)(2,1)} %get-tuple-element.15), channel_id=1, source_target_pairs={{32,0},{33,1},{34,2},{35,3},{36,4},{37,5},{38,6},{39,7},{40,8},{41... | collective-permute-start | bytes 983048 | tf_op jit(solution)/shard_map/ppermute | solution.py:21
  84.2 1.9 %collective-permute-done.3.refs_3_ = bf16[256,640]{1,0:T(8,128)(2,1)} collective-permute-done((bf16[256,640]{1,0:T(8,128)(2,1)}, bf16[256,640]{1,0:T(8,128)(2,1)}, u32[]{:S(2)}, u32[]{:S(2)}) %collective-permute-start.3) | collective-permute-done | bytes 327712 | tf_op jit(solution)/shard_map/ppermute | solution.py:21
  86.1 0.4 collective-permute-start.11
  86.6 21.2 %shard_map.148 = bf16[512,640]{1,0:T(8,128)(2,1)} custom-call(s32[1]{0:T(128)S(6)} %copy.24.live_ref, s32[1]{0:T(128)S(6)} %copy.25.depth_ref, bf16[512,640]{1,0:T(8,128)(2,1)} %get-tuple-element.20.q_ref, bf16[512,640]{1,0:T(8,128)(2,1)} %copy-done.2, bf16[512,640]{1,0:T(8,128)(2,1)} %copy-done.3, bf16[256,640]{1,0:T(8,128)(2,1)} %collective-permute-done.refs_0_, ...), custom_call_target="tpu_custom_call" | custom-call | tf_op jit(solution)/shard_map/pallas_call | solution.py:111
  107.8 0.0 collective-permute-done.12
  107.8 0.7 collective-permute-start.8
  108.5 0.1 broadcast.90.clone.1
  108.6 1.1 bitcast_dynamic-update-slice_fusion.1
  109.7 0.0 collective-permute-done.10
  109.7 0.1 broadcast.90.clone
  109.8 1.0 bitcast_dynamic-update-slice_fusion.3
  110.8 1.0 bitcast_dynamic-update-slice_fusion
  111.8 0.0 copy-start.7
  111.8 1.2 bitcast_dynamic-update-slice_fusion.2
  113.1 0.0 copy-start.6
  113.1 12.1 %collective-permute-done.8 = bf16[512,640]{1,0:T(8,128)(2,1)S(1)} collective-permute-done((bf16[512,640]{1,0:T(8,128)(2,1)}, bf16[512,640]{1,0:T(8,128)(2,1)S(1)}, u32[]{:S(2)}, u32[]{:S(2)}) %collective-permute-start.8) | collective-permute-done | bytes 655392 | tf_op jit(solution)/shard_map/ppermute | solution.py:21
  125.2 0.1 broadcast_select_fusion.3
  125.3 2.1 %broadcast_select_fusion.1 = (bf16[640,1280]{1,0:T(8,128)(2,1)S(1)}, bf16[640,1280]{1,0:T(8,128)(2,1)S(1)}) fusion(bf16[640,1280]{1,0:T(8,128)(2,1)} %param.17, bf16[640,1280]{1,0:T(8,128)(2,1)} %collective-permute-done.9, pred[]{:T(512)S(6)} %eq.17), kind=kLoop, calls=%fused_computation.14 | loop fusion | flops 1638400 | bytes 6553601 | tf_op jit(solution)/shard_map/jit(_where)/select_n | solution.py:53
  127.5 0.0 copy-start.11
  127.5 2.0 %multiply_reduce_fusion.1 = (f32[512]{0:T(512)S(1)}, f32[512,1280]{1,0:T(8,128)S(1)}) fusion(bf16[640,1280]{1,0:T(8,128)(2,1)S(1)} %get-tuple-element.4, bf16[640,1280]{1,0:T(8,128)(2,1)S(1)} %get-tuple-element.3, bf16[512,640]{1,0:T(8,128)(2,1)S(1)} %get-tuple-element.6, bf16[512,640]{1,0:T(8,128)(2,1)S(1)} %get-tuple-element.5), kind=kOutput, calls=%fused_computation.12 | convolution fusion | flops 1688206848 | bytes 7211008 | tf_op jit(solution)/shard_map/dot_general | solution.py:189
  129.5 0.8 multiply_reduce_fusion
  130.4 1.8 %multiply_convert_fusion = bf16[512,1280]{1,0:T(8,128)(2,1)} fusion(f32[512]{0:T(512)S(1)} %add_rsqrt_fusion.2, f32[512,1280]{1,0:T(8,128)S(1)} %get-tuple-element.32, f32[512]{0:T(512)S(1)} %add_rsqrt_fusion.3, f32[1280]{0:T(1024)S(1)} %copy-done.11, f32[512]{0:T(512)S(1)} %add_rsqrt_fusion.4, bf16[512,1280]{1,0:T(8,128)(2,1)S(1)} %copy-done.1), kind=kLoop, calls=%fused_computation.10 | loop fusion | flops 5242880 | bytes 5254144 | tf_op jit(solution)/shard_map/convert_element_type | solution.py:195
  (30 shorter events, 0.1 us)
Async XLA Ops:
  0.6 23.8 %copy-start = (bf16[1280,640]{1,0:T(8,128)(2,1)S(1)}, bf16[1280,640]{1,0:T(8,128)(2,1)}, u32[]{:S(2)}) copy-start(bf16[1280,640]{1,0:T(8,128)(2,1)} %param.14) | copy-start | bytes 4915204
  9.8 12.2 %copy-start.5 = (bf16[4,256,640]{2,1,0:T(8,128)(2,1)S(1)}, bf16[4,256,640]{2,1,0:T(8,128)(2,1)}, u32[]{:S(2)}) copy-start(bf16[4,256,640]{2,1,0:T(8,128)(2,1)} %param.20) | copy-start | bytes 3932164
  12.3 11.8 %copy-start.1 = (bf16[512,1280]{1,0:T(8,128)(2,1)S(1)}, bf16[512,1280]{1,0:T(8,128)(2,1)}, u32[]{:S(2)}) copy-start(bf16[512,1280]{1,0:T(8,128)(2,1)} %param.13) | copy-start | bytes 3932164
  12.3 40.5 %collective-permute-start.4 = (bf16[256,640]{1,0:T(8,128)(2,1)}, bf16[256,640]{1,0:T(8,128)(2,1)S(1)}, u32[]{:S(2)}, u32[]{:S(2)}) collective-permute-start(bf16[256,640]{1,0:T(8,128)(2,1)} %get-tuple-element.9), channel_id=1, source_target_pairs={{1,0},{2,1},{3,2},{4,3},{5,4},{6,5},{7,6},{8,7},{9,8},{10,9},{11,1... | collective-permute-start | bytes 983048 | tf_op jit(solution)/shard_map/ppermute | solution.py:21
  18.9 36.7 %collective-permute-start.5 = (bf16[256,640]{1,0:T(8,128)(2,1)}, bf16[256,640]{1,0:T(8,128)(2,1)}, u32[]{:S(2)}, u32[]{:S(2)}) collective-permute-start(bf16[256,640]{1,0:T(8,128)(2,1)} %get-tuple-element.8), channel_id=1, source_target_pairs={{33,0},{34,1},{35,2},{36,3},{37,4},{38,5},{39,6},{40,7},{41,8},{42... | collective-permute-start | bytes 983048 | tf_op jit(solution)/shard_map/ppermute | solution.py:21
  20.1 39.2 %collective-permute-start.6 = (bf16[256,640]{1,0:T(8,128)(2,1)}, bf16[256,640]{1,0:T(8,128)(2,1)}, u32[]{:S(2)}, u32[]{:S(2)}) collective-permute-start(bf16[256,640]{1,0:T(8,128)(2,1)} %get-tuple-element.10), channel_id=1, source_target_pairs={{65,0},{66,1},{67,2},{68,3},{69,4},{70,5},{71,6},{72,7},{73,8},{74... | collective-permute-start | bytes 983048 | tf_op jit(solution)/shard_map/ppermute | solution.py:21
  22.0 38.1 %collective-permute-start.7 = (bf16[256,640]{1,0:T(8,128)(2,1)}, bf16[256,640]{1,0:T(8,128)(2,1)}, u32[]{:S(2)}, u32[]{:S(2)}) collective-permute-start(bf16[256,640]{1,0:T(8,128)(2,1)} %get-tuple-element.7), channel_id=1, source_target_pairs={{97,0},{98,1},{99,2},{100,3},{101,4},{102,5},{103,6},{104,7},{105,... | collective-permute-start | bytes 983048 | tf_op jit(solution)/shard_map/ppermute | solution.py:21
  23.1 37.0 %collective-permute-start = (bf16[256,640]{1,0:T(8,128)(2,1)}, bf16[256,640]{1,0:T(8,128)(2,1)}, u32[]{:S(2)}, u32[]{:S(2)}) collective-permute-start(bf16[256,640]{1,0:T(8,128)(2,1)} %get-tuple-element.13), channel_id=1, source_target_pairs={{1,0},{2,1},{3,2},{4,3},{5,4},{6,5},{7,6},{8,7},{9,8},{10,9},{11,1... | collective-permute-start | bytes 983048 | tf_op jit(solution)/shard_map/ppermute | solution.py:21
  45.0 2.8 %copy-start.12 = (f32[640]{0:T(1024)S(1)}, f32[640]{0:T(1024)}, u32[]{:S(2)}) copy-start(f32[640]{0:T(1024)} %param.18) | copy-start | bytes 7684
  47.8 3.7 %copy-start.14 = (bf16[1280,640]{1,0:T(8,128)(2,1)S(1)}, bf16[1280,640]{1,0:T(8,128)(2,1)}, u32[]{:S(2)}) copy-start(bf16[1280,640]{1,0:T(8,128)(2,1)} %param.16) | copy-start | bytes 4915204
  51.6 10.0 %copy-start.2 = (bf16[512,640]{1,0:T(8,128)(2,1)}, bf16[512,640]{1,0:T(8,128)(2,1)S(1)}, u32[]{:S(2)}) copy-start(bf16[512,640]{1,0:T(8,128)(2,1)S(1)} %get-tuple-element.19.k_ref) | copy-start | bytes 1966084
  51.6 1.3 copy-start.10
  52.8 9.7 %copy-start.3 = (bf16[512,640]{1,0:T(8,128)(2,1)}, bf16[512,640]{1,0:T(8,128)(2,1)S(1)}, u32[]{:S(2)}) copy-start(bf16[512,640]{1,0:T(8,128)(2,1)S(1)} %fusion.8.v_ref) | copy-start | bytes 1966084
  52.8 13.0 %copy-start.13 = (s32[256]{0:T(256)S(1)}, s32[256]{0:T(256)}, u32[]{:S(2)}) copy-start(s32[256]{0:T(256)} %param.25) | copy-start | bytes 3076
  52.8 33.7 %copy-start.8 = (bf16[256,640]{1,0:T(8,128)(2,1)}, bf16[256,640]{1,0:T(8,128)(2,1)S(1)}, u32[]{:S(2)}) copy-start(bf16[256,640]{1,0:T(8,128)(2,1)S(1)} %collective-permute-done.4.refs_4_) | copy-start | bytes 983044
  52.9 11.3 %collective-permute-start.1 = (bf16[256,640]{1,0:T(8,128)(2,1)S(1)}, bf16[256,640]{1,0:T(8,128)(2,1)S(1)}, u32[]{:S(2)}, u32[]{:S(2)}) collective-permute-start(bf16[256,640]{1,0:T(8,128)(2,1)S(1)} %copy-done.10), channel_id=1, source_target_pairs={{33,0},{34,1},{35,2},{36,3},{37,4},{38,5},{39,6},{40,7},{41,8},{42... | collective-permute-start | bytes 983048 | tf_op jit(solution)/shard_map/ppermute | solution.py:21
  55.6 69.8 %collective-permute-start.9 = (bf16[640,1280]{1,0:T(8,128)(2,1)}, bf16[640,1280]{1,0:T(8,128)(2,1)}, u32[]{:S(2)}, u32[]{:S(2)}) collective-permute-start(bf16[640,1280]{1,0:T(8,128)(2,1)} %param.17), channel_id=1, source_target_pairs={{128,0},{0,128},{129,1},{1,129},{130,2},{2,130},{131,3},{3,131},{1... | collective-permute-start | bytes 4915208 | tf_op jit(solution)/shard_map/ppermute | solution.py:21
  59.4 48.4 %collective-permute-start.12 = (bf16[256,640]{1,0:T(8,128)(2,1)}, bf16[256,640]{1,0:T(8,128)(2,1)}, u32[]{:S(2)}, u32[]{:S(2)}) collective-permute-start(bf16[256,640]{1,0:T(8,128)(2,1)} %get-tuple-element.16), channel_id=1, source_target_pairs={{96,0},{97,1},{98,2},{99,3},{100,4},{101,5},{102,6},{103,7},{104,8... | collective-permute-start | bytes 983048 | tf_op jit(solution)/shard_map/ppermute | solution.py:21
  60.1 11.8 %collective-permute-start.2 = (bf16[256,640]{1,0:T(8,128)(2,1)}, bf16[256,640]{1,0:T(8,128)(2,1)}, u32[]{:S(2)}, u32[]{:S(2)}) collective-permute-start(bf16[256,640]{1,0:T(8,128)(2,1)} %get-tuple-element.14), channel_id=1, source_target_pairs={{65,0},{66,1},{67,2},{68,3},{69,4},{70,5},{71,6},{72,7},{73,8},{74... | collective-permute-start | bytes 983048 | tf_op jit(solution)/shard_map/ppermute | solution.py:21
  60.1 26.0 %collective-permute-start.3 = (bf16[256,640]{1,0:T(8,128)(2,1)}, bf16[256,640]{1,0:T(8,128)(2,1)}, u32[]{:S(2)}, u32[]{:S(2)}) collective-permute-start(bf16[256,640]{1,0:T(8,128)(2,1)} %get-tuple-element.11), channel_id=1, source_target_pairs={{97,0},{98,1},{99,2},{100,3},{101,4},{102,5},{103,6},{104,7},{105,... | collective-permute-start | bytes 983048 | tf_op jit(solution)/shard_map/ppermute | solution.py:21
  64.2 0.7 copy-start.9
  64.9 44.8 %collective-permute-start.10 = (bf16[256,640]{1,0:T(8,128)(2,1)}, bf16[256,640]{1,0:T(8,128)(2,1)}, u32[]{:S(2)}, u32[]{:S(2)}) collective-permute-start(bf16[256,640]{1,0:T(8,128)(2,1)} %get-tuple-element.18), channel_id=1, source_target_pairs={{96,0},{97,1},{98,2},{99,3},{100,4},{101,5},{102,6},{103,7},{104,8... | collective-permute-start | bytes 983048 | tf_op jit(solution)/shard_map/ppermute | solution.py:21
  71.9 38.9 %collective-permute-start.13 = (bf16[256,640]{1,0:T(8,128)(2,1)}, bf16[256,640]{1,0:T(8,128)(2,1)}, u32[]{:S(2)}, u32[]{:S(2)}) collective-permute-start(bf16[256,640]{1,0:T(8,128)(2,1)} %get-tuple-element.15), channel_id=1, source_target_pairs={{32,0},{33,1},{34,2},{35,3},{36,4},{37,5},{38,6},{39,7},{40,8},{41... | collective-permute-start | bytes 983048 | tf_op jit(solution)/shard_map/ppermute | solution.py:21
  86.1 25.7 %collective-permute-start.11 = (bf16[256,640]{1,0:T(8,128)(2,1)}, bf16[256,640]{1,0:T(8,128)(2,1)}, u32[]{:S(2)}, u32[]{:S(2)}) collective-permute-start(bf16[256,640]{1,0:T(8,128)(2,1)} %get-tuple-element.17), channel_id=1, source_target_pairs={{32,0},{33,1},{34,2},{35,3},{36,4},{37,5},{38,6},{39,7},{40,8},{41... | collective-permute-start | bytes 983048 | tf_op jit(solution)/shard_map/ppermute | solution.py:21
  107.8 17.4 %collective-permute-start.8 = (bf16[512,640]{1,0:T(8,128)(2,1)}, bf16[512,640]{1,0:T(8,128)(2,1)S(1)}, u32[]{:S(2)}, u32[]{:S(2)}) collective-permute-start(bf16[512,640]{1,0:T(8,128)(2,1)} %shard_map.148), channel_id=1, source_target_pairs={{128,0},{0,128},{129,1},{1,129},{130,2},{2,130},{131,3},{3,131},{1... | collective-permute-start | bytes 1966088 | tf_op jit(solution)/shard_map/ppermute | solution.py:21
  108.6 16.6 %copy-start.4 = (bf16[512,640]{1,0:T(8,128)(2,1)S(1)}, bf16[512,640]{1,0:T(8,128)(2,1)}, u32[]{:S(2)}) copy-start(bf16[512,640]{1,0:T(8,128)(2,1)} %shard_map.148) | copy-start | bytes 1966084
  111.8 13.5 %copy-start.7 = (bf16[2,256,640]{2,1,0:T(8,128)(2,1)}, bf16[2,256,640]{2,1,0:T(8,128)(2,1)S(1)}, u32[]{:S(2)}) copy-start(bf16[2,256,640]{2,1,0:T(8,128)(2,1)S(1)} %bitcast_dynamic-update-slice_fusion) | copy-start | bytes 1966084
  113.1 14.4 %copy-start.6 = (bf16[2,256,640]{2,1,0:T(8,128)(2,1)}, bf16[2,256,640]{2,1,0:T(8,128)(2,1)S(1)}, u32[]{:S(2)}) copy-start(bf16[2,256,640]{2,1,0:T(8,128)(2,1)S(1)} %bitcast_dynamic-update-slice_fusion.2) | copy-start | bytes 1966084
  127.5 2.0 %copy-start.11 = (f32[1280]{0:T(1024)S(1)}, f32[1280]{0:T(1024)}, u32[]{:S(2)}) copy-start(f32[1280]{0:T(1024)} %param.19) | copy-start | bytes 15364

commit v3 on v2

--- a/solution.py
+++ b/solution.py
@@ -56,15 +56,40 @@
 
 
 def attention_kernel(live_ref, depth_ref, q_ref, k_ref, v_ref, *refs):
-    page_refs, out_ref = refs[:-1], refs[-1]
-    tile = q_ref.shape[0]
+    page_refs = refs[: 2 * PMAX]
+    out_ref, other_ref, held, send_sems, recv_sems = refs[2 * PMAX :]
+    tile, lanes = q_ref.shape
     own = k_ref.shape[0]
+    h, t = pl.program_id(0), pl.program_id(1)
+    tiles_down = pl.num_programs(1)
+    steps = pl.num_programs(0) * tiles_down
+    step = h * tiles_down + t
+    partner = (1 - lax.axis_index("kv"), lax.axis_index("blk"))
+
+    @pl.when(step == 0)
+    def _():
+        barrier = pltpu.get_barrier_semaphore()
+        pl.semaphore_signal(barrier, inc=1, device_id=partner, device_id_type=pl.DeviceIdType.MESH)
+        pl.semaphore_wait(barrier, 1)
+
+    def tile_copy(index):
+        rows = pl.ds(pl.multiple_of((index % tiles_down) * tile, tile), tile)
+        cols = pl.ds(pl.multiple_of((index // tiles_down) * lanes, lanes), lanes)
+        return pltpu.make_async_remote_copy(
+            src_ref=held.at[index % 2],
+            dst_ref=other_ref.at[rows, cols],
+            send_sem=send_sems.at[index],
+            recv_sem=recv_sems.at[index],
+            device_id=partner,
+            device_id_type=pl.DeviceIdType.MESH,
+        )
+
     live = live_ref[0]
     depth = depth_ref[0]
     query = q_ref[...]
     lane = lax.broadcasted_iota(jnp.int32, query.shape, 1)
     first = lane < HD
-    row = pl.program_id(1) * tile + lax.broadcasted_iota(jnp.int32, (tile, own), 0)
+    row = t * tile + lax.broadcasted_iota(jnp.int32, (tile, own), 0)
     col = lax.broadcasted_iota(jnp.int32, (tile, own), 1)
     own_visible = (col <= row) & (col < live)
     contract = (((1,), (1,)), ((), ()))
@@ -91,7 +116,26 @@
                 weights.astype(jnp.bfloat16), value_page[...], preferred_element_type=jnp.float32
             )
         results.append(mixed / total)
-    out_ref[...] = jnp.where(first, results[0], results[1]).astype(out_ref.dtype)
+    result = jnp.where(first, results[0], results[1]).astype(out_ref.dtype)
+    out_ref[...] = result
+
+    @pl.when(step >= 2)
+    def _():
+        tile_copy(step - 2).wait_send()
+
+    held[step % 2] = result
+    tile_copy(step).start()
+
+    @pl.when(step == steps - 1)
+    def _():
+        tile_copy(step - 1).wait_send()
+        tile_copy(step).wait_send()
+
+        def drain(index, carry):
+            tile_copy(index).wait_recv()
+            return carry
+
+        lax.fori_loop(0, steps, drain, 0)
 
 
 def attention(queries, key_rows, value_rows, page_keys, page_values, req_len, prefix_len):
@@ -99,6 +143,7 @@
     tile = 128
     lanes = 2 * HD
     grid = (width // lanes, tokens // tile)
+    steps = grid[0] * grid[1]
     own_spec = pl.BlockSpec((tokens, lanes), lambda h, t, *_: (0, h))
     page_spec = pl.BlockSpec((PAGE, lanes), lambda h, t, *_: (0, h))
     tile_spec = pl.BlockSpec((tile, lanes), lambda h, t, *_: (t, h))
@@ -106,12 +151,23 @@
         num_scalar_prefetch=2,
         grid=grid,
         in_specs=[tile_spec, own_spec, own_spec] + [page_spec] * (2 * PMAX),
-        out_specs=tile_spec,
-    )
+        out_specs=[tile_spec, pl.BlockSpec(memory_space=pl.ANY)],
+        scratch_shapes=[
+            pltpu.VMEM((2, tile, lanes), jnp.bfloat16),
+            pltpu.SemaphoreType.DMA((steps,)),
+            pltpu.SemaphoreType.DMA((steps,)),
+        ],
+    )
+    shape = jax.ShapeDtypeStruct((tokens, width), jnp.bfloat16)
     return pl.pallas_call(
         attention_kernel,
-        out_shape=jax.ShapeDtypeStruct((tokens, width), jnp.bfloat16),
+        out_shape=(shape, shape),
         grid_spec=grid_spec,
+        compiler_params=pltpu.CompilerParams(
+            collective_id=0,
+            has_side_effects=True,
+            dimension_semantics=("arbitrary", "arbitrary"),
+        ),
     )(req_len, prefix_len, queries, key_rows, value_rows, *page_keys, *page_values)
 
 
@@ -182,10 +238,9 @@
         page_keys, page_values = fetch_page(pool_keys, pool_values, prefix_pages, slot_index)
         fetched_keys.append(page_keys)
         fetched_values.append(page_values)
-    attended = attention(
+    attended, other_attended = attention(
         queries, key_rows, value_rows, fetched_keys, fetched_values, req_len, prefix_len
     )
-    other_attended = from_behind(attended, "kv", 1)
     branch = jnp.dot(
         in_kv_order(attended, other_attended, 1),
         in_kv_order(w_out, other_w_out, 0),

time: 134 us -> 151 us (1.13)
  the two profiles are of different devices: /device:TPU:6 before, /device:TPU:224 now
where the time goes in v3:
time: 151 us; the launch traced here: 150 us
  Pallas kernels  49.5 us (33%)
  local copies, waits for them, and re-layouts  29.8 us (20%)
  starting transfers between devices  24.8 us (16%)
  between operations  13.7 us (9%)
  other arithmetic  13.3 us (9%)
  matrix products  11.9 us (8%)
  waiting for transfers between devices  7.19 us (5%)
    pallas_call x1, Pallas kernels, attention(): pl.pallas_call(attention_kernel, out_shape=(shape, shape), grid_spec=grid...  49.5 us
    ppermute x13, starting transfers between devices, from_behind(): return lax.ppermute(block, axis, route)  24.8 us
    mul x4, local copies, waits for them, and re-layouts, rms_scale(): values * lax.rsqrt(jnp.mean(values * values, axis=-1, keepdims=True) + ep...  8.02 us
    ppermute x13, waiting for transfers between devices, from_behind(): return lax.ppermute(block, axis, route)  7.19 us
    mul x2, local copies, waits for them, and re-layouts, rms_scale(): values * values  5.55 us
    dot_general x1, matrix products, body(): jnp.dot(hidden_in, w_key, preferred_element_type=jnp.float32)  4.1 us
    reduce_sum x3, other arithmetic, rms_scale(): jnp.mean(values * values, axis=-1, keepdims=True) + epsilon  3.8 us
    convert_element_type x1, other arithmetic, head_normed(): (rms_scale(split_heads).reshape(count, -1) * head_gain).astype(jnp.bfloat16)  3.63 us
  transfers between devices with their start and end apart: 13, of which 3 were waited for; matrix products, arithmetic and copies ran while one was open for 28% of the time, Pallas kernels for 33%

profile of v3, /device:TPU:224, one launch (start us, length us, event | category | flops | bytes accessed | tf_op | source)
XLA Modules:
  0.0 150.2 jit_solution(9260673584717252644)
XLA Ops:
  0.6 0.0 copy-start
  0.6 1.8 %fusion.7 = f32[512]{0:T(512)S(1)} fusion(bf16[512,1280]{1,0:T(8,128)(2,1)} %param.13), kind=kLoop, calls=%fused_computation.9 | loop fusion | flops 1965568 | bytes 1312768 | tf_op jit(solution)/shard_map/reduce_sum | solution.py:226
  2.4 0.0 copy-start.1
  2.4 3.1 %fusion.8.v_ref = bf16[512,640]{1,0:T(8,128)(2,1)S(1)} fusion(bf16[512,1280]{1,0:T(8,128)(2,1)} %param.13, bf16[1280,640]{1,0:T(8,128)(2,1)} %param.16, f32[512]{0:T(512)S(1)} %add_rsqrt_fusion.4), kind=kOutput, calls=%fused_computation.16 | convolution fusion | flops 839516160 | bytes 3606528 | tf_op jit(solution)/shard_map/dot_general | solution.py:233
  5.6 1.0 fusion.13
  6.5 1.5 collective-permute-start.11
  8.0 2.7 %fusion.17 = (f32[512,640]{1,0:T(8,128)}, f32[512,640]{1,0:T(8,128)}) fusion(bf16[512,1280]{1,0:T(8,128)(2,1)S(1)} %copy-done.1, bf16[1280,640]{1,0:T(8,128)(2,1)S(1)} %copy-done), kind=kOutput, calls=%fused_computation.50 | convolution fusion | flops 839188480 | bytes 5570560 | tf_op jit(solution)/shard_map/dot_general | solution.py:229
  10.7 2.8 %copy.16 = f32[512,640]{0,1:T(8,128)} copy(f32[512,640]{1,0:T(8,128)} %get-tuple-element.33) | data formatting | bytes 2621440 | tf_op jit(solution)/shard_map/mul | solution.py:25
  13.5 1.5 reduce_sum.46
  15.0 1.2 mul.109
  16.2 2.8 %copy.17 = f32[512,640]{1,0:T(8,128)} copy(f32[512,640]{0,1:T(8,128)} %bitcast.42) | data formatting | bytes 2621440 | tf_op jit(solution)/shard_map/mul | solution.py:25
  19.0 4.1 %fusion.16 = (f32[512,640]{1,0:T(8,128)}, f32[512,640]{1,0:T(8,128)}) fusion(bf16[512,1280]{1,0:T(8,128)(2,1)S(1)} %copy-done.1, bf16[1280,640]{1,0:T(8,128)(2,1)} %param.15), kind=kOutput, calls=%fused_computation.49 | convolution fusion | flops 839188480 | bytes 5570560 | tf_op jit(solution)/shard_map/dot_general | solution.py:231
  23.1 2.8 %copy.18 = f32[512,640]{0,1:T(8,128)} copy(f32[512,640]{1,0:T(8,128)} %get-tuple-element.31) | data formatting | bytes 2621440 | tf_op jit(solution)/shard_map/mul | solution.py:25
  25.9 1.5 reduce_sum.47
  27.4 1.2 mul.116
  28.6 2.8 %copy.19 = f32[512,640]{1,0:T(8,128)} copy(f32[512,640]{0,1:T(8,128)} %bitcast.43) | data formatting | bytes 2621440 | tf_op jit(solution)/shard_map/mul | solution.py:25
  31.4 3.6 %multiply_convert_fusion.1 = (bf16[512,640]{1,0:T(8,128)(2,1)S(1)}, bf16[512,640]{1,0:T(8,128)(2,1)}) fusion(f32[512,640]{1,0:T(8,128)} %get-tuple-element.32, f32[512,640]{1,0:T(8,128)} %copy.19, f32[640]{0:T(1024)S(1)} %copy-done.9, f32[512,640]{1,0:T(8,128)} %get-tuple-element.34, f32[512,640]{1,0:T(8,128)} %copy.17), kind=kLoop, calls=%fused_computation.20 | loop fusion | flops 1966080 | bytes 6556160 | tf_op jit(solution)/shard_map/convert_element_type | solution.py:31
  35.0 0.8 copy-done.2
  35.9 0.9 fusion.14
  36.8 1.5 collective-permute-start.9
  38.3 0.6 constant_dynamic-slice_fusion.3
  46.5 0.0 copy-start.4
  46.5 2.3 %dynamic-slice_bitcast_fusion = (bf16[256,640]{1,0:T(8,128)(2,1)}, bf16[256,640]{1,0:T(8,128)(2,1)S(1)}, bf16[256,640]{1,0:T(8,128)(2,1)S(1)}, bf16[256,640]{1,0:T(8,128)(2,1)}) fusion(bf16[4,256,640]{2,1,0:T(8,128)(2,1)} %param.21, s32[]{:T(128)S(6)} %select_n.135, s32[]{:T(128)S(6)} %select_n.127, s32[]{:T(128)S(6)} %select_n.123, s32[]{:T(128)S(6)} %select_n.131), kind=kLoop, calls=%fused_computation.28 | loop fusion | bytes 2621456 | tf_op jit(solution)/shard_map/jit(dynamic_index_in_dim)/squeeze | solution.py:181
  48.9 0.0 collective-permute-start.4
  48.9 2.3 %collective-permute-start.5 = (bf16[256,640]{1,0:T(8,128)(2,1)S(1)}, bf16[256,640]{1,0:T(8,128)(2,1)}, u32[]{:S(2)}, u32[]{:S(2)}) collective-permute-start(bf16[256,640]{1,0:T(8,128)(2,1)S(1)} %get-tuple-element.12), channel_id=1, source_target_pairs={{33,0},{34,1},{35,2},{36,3},{37,4},{38,5},{39,6},{40,7},{41,8},{42... | collective-permute-start | bytes 983048 | tf_op jit(solution)/shard_map/ppermute | solution.py:21
  51.2 3.2 %collective-permute-start.8 = (bf16[640,1280]{1,0:T(8,128)(2,1)}, bf16[640,1280]{1,0:T(8,128)(2,1)}, u32[]{:S(2)}, u32[]{:S(2)}) collective-permute-start(bf16[640,1280]{1,0:T(8,128)(2,1)} %param.17), channel_id=1, source_target_pairs={{128,0},{0,128},{129,1},{1,129},{130,2},{2,130},{131,3},{3,131},{1... | collective-permute-start | bytes 4915208 | tf_op jit(solution)/shard_map/ppermute | solution.py:21
  54.4 1.1 dynamic-slice_bitcast_fusion.4
  55.5 0.0 collective-permute-done.11
  55.5 0.9 collective-permute-start.6
  56.3 0.0 collective-permute-done.9
  56.4 0.7 collective-permute-start.7
  57.0 0.0 collective-permute-done.4.refs_4_
  57.0 0.8 collective-permute-start
  57.8 4.7 %collective-permute-done.5.refs_5_ = bf16[256,640]{1,0:T(8,128)(2,1)} collective-permute-done((bf16[256,640]{1,0:T(8,128)(2,1)S(1)}, bf16[256,640]{1,0:T(8,128)(2,1)}, u32[]{:S(2)}, u32[]{:S(2)}) %collective-permute-start.5) | collective-permute-done | bytes 327712 | tf_op jit(solution)/shard_map/ppermute | solution.py:21
  62.5 0.0 collective-permute-start.1
  62.5 0.0 copy-done.11
  62.5 0.7 fusion.15
  68.5 1.6 %collective-permute-done.6.refs_6_ = bf16[256,640]{1,0:T(8,128)(2,1)} collective-permute-done((bf16[256,640]{1,0:T(8,128)(2,1)}, bf16[256,640]{1,0:T(8,128)(2,1)}, u32[]{:S(2)}, u32[]{:S(2)}) %collective-permute-start.6) | collective-permute-done | bytes 327712 | tf_op jit(solution)/shard_map/ppermute | solution.py:21
  70.0 5.0 %collective-permute-start.12 = (bf16[256,640]{1,0:T(8,128)(2,1)}, bf16[256,640]{1,0:T(8,128)(2,1)}, u32[]{:S(2)}, u32[]{:S(2)}) collective-permute-start(bf16[256,640]{1,0:T(8,128)(2,1)} %get-tuple-element.19), channel_id=1, source_target_pairs={{32,0},{33,1},{34,2},{35,3},{36,4},{37,5},{38,6},{39,7},{40,8},{41... | collective-permute-start | bytes 983048 | tf_op jit(solution)/shard_map/ppermute | solution.py:21
  75.0 0.0 collective-permute-done.7.refs_7_
  75.0 0.0 collective-permute-start.2
  75.0 0.0 collective-permute-done.refs_0_
  75.0 2.0 %collective-permute-start.3 = (bf16[256,640]{1,0:T(8,128)(2,1)}, bf16[256,640]{1,0:T(8,128)(2,1)}, u32[]{:S(2)}, u32[]{:S(2)}) collective-permute-start(bf16[256,640]{1,0:T(8,128)(2,1)} %get-tuple-element.15), channel_id=1, source_target_pairs={{97,0},{98,1},{99,2},{100,3},{101,4},{102,5},{103,6},{104,7},{105,... | collective-permute-start | bytes 983048 | tf_op jit(solution)/shard_map/ppermute | solution.py:21
  77.0 0.9 broadcast.90.clone.1
  77.9 1.7 %bitcast_dynamic-update-slice_fusion.1 = bf16[2,256,640]{2,1,0:T(8,128)(2,1)} fusion(bf16[2,256,640]{2,1,0:T(8,128)(2,1)} %broadcast.90.clone.1, s32[]{:T(128)S(6)} %select_n.144, bf16[256,640]{1,0:T(8,128)(2,1)} %collective-permute-done.11), kind=kLoop, calls=%fused_computation.25 | loop fusion | bytes 655364 | tf_op jit(solution)/shard_map/jit(dynamic_update_index_in_dim)/dynamic_update_slice | solution.py:202
  79.6 0.0 collective-permute-done.1.refs_1_
  79.6 7.0 %collective-permute-start.10 = (bf16[256,640]{1,0:T(8,128)(2,1)}, bf16[256,640]{1,0:T(8,128)(2,1)}, u32[]{:S(2)}, u32[]{:S(2)}) collective-permute-start(bf16[256,640]{1,0:T(8,128)(2,1)} %get-tuple-element.21), channel_id=1, source_target_pairs={{32,0},{33,1},{34,2},{35,3},{36,4},{37,5},{38,6},{39,7},{40,8},{41... | collective-permute-start | bytes 983048 | tf_op jit(solution)/shard_map/ppermute | solution.py:21
  86.7 0.9 broadcast.90.clone
  87.6 1.7 %bitcast_dynamic-update-slice_fusion.3 = bf16[2,256,640]{2,1,0:T(8,128)(2,1)} fusion(bf16[2,256,640]{2,1,0:T(8,128)(2,1)} %broadcast.90.clone, s32[]{:T(128)S(6)} %select_n.144, bf16[256,640]{1,0:T(8,128)(2,1)} %collective-permute-done.9), kind=kLoop, calls=%fused_computation.27 | loop fusion | bytes 655364 | tf_op jit(solution)/shard_map/jit(dynamic_update_index_in_dim)/dynamic_update_slice | solution.py:201
  89.3 0.0 collective-permute-done.2.refs_2_
  89.3 0.9 collective-permute-done.3.refs_3_
  90.2 49.5 %shard_map.148 = (bf16[512,640]{1,0:T(8,128)(2,1)}, bf16[512,640]{1,0:T(8,128)(2,1)}) custom-call(s32[1]{0:T(128)S(6)} %copy.24.live_ref, s32[1]{0:T(128)S(6)} %copy.25.depth_ref, bf16[512,640]{1,0:T(8,128)(2,1)} %get-tuple-element.24.q_ref, bf16[512,640]{1,0:T(8,128)(2,1)} %copy-done.2, bf16[512,640]{1,0:T(8,128)(2,1)} %copy-done.3, ...), custom_call_target="tpu_custom_call" | custom-call | tf_op jit(solution)/shard_map/pallas_call | solution.py:162
  139.7 0.0 copy-start.5
  139.7 0.0 collective-permute-done.12
  139.7 1.8 %bitcast_dynamic-update-slice_fusion = bf16[2,256,640]{2,1,0:T(8,128)(2,1)} fusion(bf16[2,256,640]{2,1,0:T(8,128)(2,1)} %bitcast_dynamic-update-slice_fusion.1, s32[]{:T(128)S(6)} %select_n.148, bf16[256,640]{1,0:T(8,128)(2,1)} %collective-permute-done.12), kind=kLoop, calls=%fused_computation.24 | loop fusion | bytes 655364 | tf_op jit(solution)/shard_map/jit(dynamic_update_index_in_dim)/dynamic_update_slice | solution.py:202
  141.6 0.0 collective-permute-done.10
  141.6 1.7 %bitcast_dynamic-update-slice_fusion.2 = bf16[2,256,640]{2,1,0:T(8,128)(2,1)} fusion(bf16[2,256,640]{2,1,0:T(8,128)(2,1)} %bitcast_dynamic-update-slice_fusion.3, s32[]{:T(128)S(6)} %select_n.148, bf16[256,640]{1,0:T(8,128)(2,1)} %collective-permute-done.10), kind=kLoop, calls=%fused_computation.26 | loop fusion | bytes 655364 | tf_op jit(solution)/shard_map/jit(dynamic_update_index_in_dim)/dynamic_update_slice | solution.py:201
  143.3 0.1 broadcast_select_fusion.3
  143.4 0.0 collective-permute-done.8
  143.4 2.1 %broadcast_select_fusion.1 = (bf16[640,1280]{1,0:T(8,128)(2,1)S(1)}, bf16[640,1280]{1,0:T(8,128)(2,1)S(1)}) fusion(bf16[640,1280]{1,0:T(8,128)(2,1)} %param.17, bf16[640,1280]{1,0:T(8,128)(2,1)} %collective-permute-done.8, pred[]{:T(512)S(6)} %eq.17), kind=kLoop, calls=%fused_computation.14 | loop fusion | flops 1638400 | bytes 6553601 | tf_op jit(solution)/shard_map/jit(_where)/select_n | solution.py:53
  145.6 0.0 copy-start.8
  145.6 2.0 %multiply_reduce_fusion.1 = (f32[512]{0:T(512)S(1)}, f32[512,1280]{1,0:T(8,128)S(1)}) fusion(bf16[640,1280]{1,0:T(8,128)(2,1)S(1)} %get-tuple-element.8, bf16[640,1280]{1,0:T(8,128)(2,1)S(1)} %get-tuple-element.7, bf16[512,640]{1,0:T(8,128)(2,1)S(1)} %get-tuple-element.10, bf16[512,640]{1,0:T(8,128)(2,1)S(1)} %get-tuple-element.9), kind=kOutput, calls=%fused_computation.12 | convolution fusion | flops 1688206848 | bytes 7211008 | tf_op jit(solution)/shard_map/dot_general | solution.py:244
  147.6 0.8 multiply_reduce_fusion
  148.4 1.8 %multiply_convert_fusion = bf16[512,1280]{1,0:T(8,128)(2,1)} fusion(f32[512]{0:T(512)S(1)} %add_rsqrt_fusion.2, f32[512,1280]{1,0:T(8,128)S(1)} %get-tuple-element.36, f32[512]{0:T(512)S(1)} %add_rsqrt_fusion.3, f32[1280]{0:T(1024)S(1)} %copy-done.8, f32[512]{0:T(512)S(1)} %add_rsqrt_fusion.4, bf16[512,1280]{1,0:T(8,128)(2,1)S(1)} %copy-done.1), kind=kLoop, calls=%fused_computation.10 | loop fusion | flops 5242880 | bytes 5254144 | tf_op jit(solution)/shard_map/convert_element_type | solution.py:250
  (22 shorter events, 0.1 us)
Async XLA Ops:
  0.6 7.4 %copy-start = (bf16[1280,640]{1,0:T(8,128)(2,1)S(1)}, bf16[1280,640]{1,0:T(8,128)(2,1)}, u32[]{:S(2)}) copy-start(bf16[1280,640]{1,0:T(8,128)(2,1)} %param.14) | copy-start | bytes 4915204
  2.4 5.6 %copy-start.1 = (bf16[512,1280]{1,0:T(8,128)(2,1)S(1)}, bf16[512,1280]{1,0:T(8,128)(2,1)}, u32[]{:S(2)}) copy-start(bf16[512,1280]{1,0:T(8,128)(2,1)} %param.13) | copy-start | bytes 3932164
  5.6 5.2 %copy-start.3 = (bf16[512,640]{1,0:T(8,128)(2,1)}, bf16[512,640]{1,0:T(8,128)(2,1)S(1)}, u32[]{:S(2)}) copy-start(bf16[512,640]{1,0:T(8,128)(2,1)S(1)} %fusion.8.v_ref) | copy-start | bytes 1966084
  6.5 48.9 %collective-permute-start.11 = (bf16[256,640]{1,0:T(8,128)(2,1)}, bf16[256,640]{1,0:T(8,128)(2,1)}, u32[]{:S(2)}, u32[]{:S(2)}) collective-permute-start(bf16[256,640]{1,0:T(8,128)(2,1)} %get-tuple-element.20), channel_id=1, source_target_pairs={{96,0},{97,1},{98,2},{99,3},{100,4},{101,5},{102,6},{103,7},{104,8... | collective-permute-start | bytes 983048 | tf_op jit(solution)/shard_map/ppermute | solution.py:21
  28.6 2.8 %copy-start.9 = (f32[640]{0:T(1024)S(1)}, f32[640]{0:T(1024)}, u32[]{:S(2)}) copy-start(f32[640]{0:T(1024)} %param.18) | copy-start | bytes 7684
  31.4 6.9 %copy-start.10 = (s32[128,4]{0,1:T(4,128)S(1)}, s32[128,4]{0,1:T(4,128)}, u32[]{:S(2)}) copy-start(s32[128,4]{0,1:T(4,128)} %param.24) | copy-start | bytes 6148
  35.0 0.8 copy-start.2
  36.8 19.6 %collective-permute-start.9 = (bf16[256,640]{1,0:T(8,128)(2,1)}, bf16[256,640]{1,0:T(8,128)(2,1)}, u32[]{:S(2)}, u32[]{:S(2)}) collective-permute-start(bf16[256,640]{1,0:T(8,128)(2,1)} %get-tuple-element.22), channel_id=1, source_target_pairs={{96,0},{97,1},{98,2},{99,3},{100,4},{101,5},{102,6},{103,7},{104,8... | collective-permute-start | bytes 983048 | tf_op jit(solution)/shard_map/ppermute | solution.py:21
  46.5 7.8 %copy-start.4 = (bf16[4,256,640]{2,1,0:T(8,128)(2,1)S(1)}, bf16[4,256,640]{2,1,0:T(8,128)(2,1)}, u32[]{:S(2)}) copy-start(bf16[4,256,640]{2,1,0:T(8,128)(2,1)} %param.20) | copy-start | bytes 3932164
  48.9 13.7 %copy-start.11 = (s32[256]{0:T(256)S(1)}, s32[256]{0:T(256)}, u32[]{:S(2)}) copy-start(s32[256]{0:T(256)} %param.25) | copy-start | bytes 3076
  48.9 8.2 %collective-permute-start.4 = (bf16[256,640]{1,0:T(8,128)(2,1)S(1)}, bf16[256,640]{1,0:T(8,128)(2,1)S(1)}, u32[]{:S(2)}, u32[]{:S(2)}) collective-permute-start(bf16[256,640]{1,0:T(8,128)(2,1)S(1)} %get-tuple-element.13), channel_id=1, source_target_pairs={{1,0},{2,1},{3,2},{4,3},{5,4},{6,5},{7,6},{8,7},{9,8},{10,9},{11,1... | collective-permute-start | bytes 983048 | tf_op jit(solution)/shard_map/ppermute | solution.py:21
  48.9 13.7 %collective-permute-start.5 = (bf16[256,640]{1,0:T(8,128)(2,1)S(1)}, bf16[256,640]{1,0:T(8,128)(2,1)}, u32[]{:S(2)}, u32[]{:S(2)}) collective-permute-start(bf16[256,640]{1,0:T(8,128)(2,1)S(1)} %get-tuple-element.12), channel_id=1, source_target_pairs={{33,0},{34,1},{35,2},{36,3},{37,4},{38,5},{39,6},{40,7},{41,8},{42... | collective-permute-start | bytes 983048 | tf_op jit(solution)/shard_map/ppermute | solution.py:21
  51.2 92.3 %collective-permute-start.8 = (bf16[640,1280]{1,0:T(8,128)(2,1)}, bf16[640,1280]{1,0:T(8,128)(2,1)}, u32[]{:S(2)}, u32[]{:S(2)}) collective-permute-start(bf16[640,1280]{1,0:T(8,128)(2,1)} %param.17), channel_id=1, source_target_pairs={{128,0},{0,128},{129,1},{1,129},{130,2},{2,130},{131,3},{3,131},{1... | collective-permute-start | bytes 4915208 | tf_op jit(solution)/shard_map/ppermute | solution.py:21
  55.5 14.6 %collective-permute-start.6 = (bf16[256,640]{1,0:T(8,128)(2,1)}, bf16[256,640]{1,0:T(8,128)(2,1)}, u32[]{:S(2)}, u32[]{:S(2)}) collective-permute-start(bf16[256,640]{1,0:T(8,128)(2,1)} %get-tuple-element.14), channel_id=1, source_target_pairs={{65,0},{66,1},{67,2},{68,3},{69,4},{70,5},{71,6},{72,7},{73,8},{74... | collective-permute-start | bytes 983048 | tf_op jit(solution)/shard_map/ppermute | solution.py:21
  56.4 18.7 %collective-permute-start.7 = (bf16[256,640]{1,0:T(8,128)(2,1)}, bf16[256,640]{1,0:T(8,128)(2,1)}, u32[]{:S(2)}, u32[]{:S(2)}) collective-permute-start(bf16[256,640]{1,0:T(8,128)(2,1)} %get-tuple-element.11), channel_id=1, source_target_pairs={{97,0},{98,1},{99,2},{100,3},{101,4},{102,5},{103,6},{104,7},{105,... | collective-permute-start | bytes 983048 | tf_op jit(solution)/shard_map/ppermute | solution.py:21
  57.0 33.1 %copy-start.7 = (bf16[256,640]{1,0:T(8,128)(2,1)}, bf16[256,640]{1,0:T(8,128)(2,1)S(1)}, u32[]{:S(2)}) copy-start(bf16[256,640]{1,0:T(8,128)(2,1)S(1)} %collective-permute-done.4.refs_4_) | copy-start | bytes 983044
  57.0 18.0 %collective-permute-start = (bf16[256,640]{1,0:T(8,128)(2,1)}, bf16[256,640]{1,0:T(8,128)(2,1)}, u32[]{:S(2)}, u32[]{:S(2)}) collective-permute-start(bf16[256,640]{1,0:T(8,128)(2,1)} %get-tuple-element.17), channel_id=1, source_target_pairs={{1,0},{2,1},{3,2},{4,3},{5,4},{6,5},{7,6},{8,7},{9,8},{10,9},{11,1... | collective-permute-start | bytes 983048 | tf_op jit(solution)/shard_map/ppermute | solution.py:21
  62.5 17.1 %collective-permute-start.1 = (bf16[256,640]{1,0:T(8,128)(2,1)}, bf16[256,640]{1,0:T(8,128)(2,1)}, u32[]{:S(2)}, u32[]{:S(2)}) collective-permute-start(bf16[256,640]{1,0:T(8,128)(2,1)} %get-tuple-element.16), channel_id=1, source_target_pairs={{33,0},{34,1},{35,2},{36,3},{37,4},{38,5},{39,6},{40,7},{41,8},{42... | collective-permute-start | bytes 983048 | tf_op jit(solution)/shard_map/ppermute | solution.py:21
  70.0 69.7 %collective-permute-start.12 = (bf16[256,640]{1,0:T(8,128)(2,1)}, bf16[256,640]{1,0:T(8,128)(2,1)}, u32[]{:S(2)}, u32[]{:S(2)}) collective-permute-start(bf16[256,640]{1,0:T(8,128)(2,1)} %get-tuple-element.19), channel_id=1, source_target_pairs={{32,0},{33,1},{34,2},{35,3},{36,4},{37,5},{38,6},{39,7},{40,8},{41... | collective-permute-start | bytes 983048 | tf_op jit(solution)/shard_map/ppermute | solution.py:21
  75.0 14.3 %collective-permute-start.2 = (bf16[256,640]{1,0:T(8,128)(2,1)}, bf16[256,640]{1,0:T(8,128)(2,1)}, u32[]{:S(2)}, u32[]{:S(2)}) collective-permute-start(bf16[256,640]{1,0:T(8,128)(2,1)} %get-tuple-element.18), channel_id=1, source_target_pairs={{65,0},{66,1},{67,2},{68,3},{69,4},{70,5},{71,6},{72,7},{73,8},{74... | collective-permute-start | bytes 983048 | tf_op jit(solution)/shard_map/ppermute | solution.py:21
  75.0 15.1 %collective-permute-start.3 = (bf16[256,640]{1,0:T(8,128)(2,1)}, bf16[256,640]{1,0:T(8,128)(2,1)}, u32[]{:S(2)}, u32[]{:S(2)}) collective-permute-start(bf16[256,640]{1,0:T(8,128)(2,1)} %get-tuple-element.15), channel_id=1, source_target_pairs={{97,0},{98,1},{99,2},{100,3},{101,4},{102,5},{103,6},{104,7},{105,... | collective-permute-start | bytes 983048 | tf_op jit(solution)/shard_map/ppermute | solution.py:21
  79.6 61.9 %collective-permute-start.10 = (bf16[256,640]{1,0:T(8,128)(2,1)}, bf16[256,640]{1,0:T(8,128)(2,1)}, u32[]{:S(2)}, u32[]{:S(2)}) collective-permute-start(bf16[256,640]{1,0:T(8,128)(2,1)} %get-tuple-element.21), channel_id=1, source_target_pairs={{32,0},{33,1},{34,2},{35,3},{36,4},{37,5},{38,6},{39,7},{40,8},{41... | collective-permute-start | bytes 983048 | tf_op jit(solution)/shard_map/ppermute | solution.py:21
  139.7 3.6 %copy-start.5 = (bf16[512,640]{1,0:T(8,128)(2,1)S(1)}, bf16[512,640]{1,0:T(8,128)(2,1)}, u32[]{:S(2)}) copy-start(bf16[512,640]{1,0:T(8,128)(2,1)} %get-tuple-element.5) | copy-start | bytes 1966084
  139.7 3.6 %copy-start.6 = (bf16[512,640]{1,0:T(8,128)(2,1)S(1)}, bf16[512,640]{1,0:T(8,128)(2,1)}, u32[]{:S(2)}) copy-start(bf16[512,640]{1,0:T(8,128)(2,1)} %get-tuple-element.6) | copy-start | bytes 1966084
  145.6 2.0 %copy-start.8 = (f32[1280]{0:T(1024)S(1)}, f32[1280]{0:T(1024)}, u32[]{:S(2)}) copy-start(f32[1280]{0:T(1024)} %param.19) | copy-start | bytes 15364

commit v4 on v2

--- a/solution.py
+++ b/solution.py
@@ -94,25 +94,26 @@
     out_ref[...] = jnp.where(first, results[0], results[1]).astype(out_ref.dtype)
 
 
-def attention(queries, key_rows, value_rows, page_keys, page_values, req_len, prefix_len):
+def attention(queries, key_rows, value_rows, pages, req_len, prefix_len):
     tokens, width = queries.shape
     tile = 128
     lanes = 2 * HD
     grid = (width // lanes, tokens // tile)
     own_spec = pl.BlockSpec((tokens, lanes), lambda h, t, *_: (0, h))
-    page_spec = pl.BlockSpec((PAGE, lanes), lambda h, t, *_: (0, h))
+    key_spec = pl.BlockSpec((None, PAGE, lanes), lambda h, t, *_: (0, 0, h))
+    value_spec = pl.BlockSpec((None, PAGE, lanes), lambda h, t, *_: (1, 0, h))
     tile_spec = pl.BlockSpec((tile, lanes), lambda h, t, *_: (t, h))
     grid_spec = pltpu.PrefetchScalarGridSpec(
         num_scalar_prefetch=2,
         grid=grid,
-        in_specs=[tile_spec, own_spec, own_spec] + [page_spec] * (2 * PMAX),
+        in_specs=[tile_spec, own_spec, own_spec] + [key_spec] * PMAX + [value_spec] * PMAX,
         out_specs=tile_spec,
     )
     return pl.pallas_call(
         attention_kernel,
         out_shape=jax.ShapeDtypeStruct((tokens, width), jnp.bfloat16),
         grid_spec=grid_spec,
-    )(req_len, prefix_len, queries, key_rows, value_rows, *page_keys, *page_values)
+    )(req_len, prefix_len, queries, key_rows, value_rows, *pages, *pages)
 
 
 def fetch_page(pool_keys, pool_values, prefix_pages, slot_index):
@@ -123,7 +124,7 @@
     local = prefix_pages[asker, slot_index] % pool_keys.shape[0]
     send_keys = lax.dynamic_index_in_dim(pool_keys, local, 0, keepdims=False)
     send_values = lax.dynamic_index_in_dim(pool_values, local, 0, keepdims=False)
-    return from_behind((send_keys, send_values), "blk", devices - offset)
+    return from_behind(jnp.stack([send_keys, send_values]), "blk", devices - offset)
 
 
 def relay(key_rows, value_rows, placement):
@@ -137,13 +138,13 @@
     value_out = jnp.zeros_like(value_pages)
     for block_index in range(blocks):
         offset = (2 * block_index + 1) * devices // (2 * blocks)
-        key_recv, value_recv = from_behind(
-            (key_pages[block_index], value_pages[block_index]), "blk", offset
+        received = from_behind(
+            jnp.stack([key_pages[block_index], value_pages[block_index]]), "blk", offset
         )
         source = (here - offset) % devices
         target = placement[source * blocks + block_index] % blocks
-        key_out = lax.dynamic_update_index_in_dim(key_out, key_recv, target, 0)
-        value_out = lax.dynamic_update_index_in_dim(value_out, value_recv, target, 0)
+        key_out = lax.dynamic_update_index_in_dim(key_out, received[0], target, 0)
+        value_out = lax.dynamic_update_index_in_dim(value_out, received[1], target, 0)
     return (key_out, value_out)
 
 
@@ -176,15 +177,11 @@
     value_rows = (
         jnp.dot(hidden_in, w_value, preferred_element_type=jnp.float32) * row_scale
     ).astype(jnp.bfloat16)
-    fetched_keys = []
-    fetched_values = []
-    for slot_index in range(PMAX):
-        page_keys, page_values = fetch_page(pool_keys, pool_values, prefix_pages, slot_index)
-        fetched_keys.append(page_keys)
-        fetched_values.append(page_values)
-    attended = attention(
-        queries, key_rows, value_rows, fetched_keys, fetched_values, req_len, prefix_len
-    )
+    fetched = [
+        fetch_page(pool_keys, pool_values, prefix_pages, slot_index) for slot_index in range(PMAX)
+    ]
+    key_rows, value_rows, fetched = lax.optimization_barrier((key_rows, value_rows, fetched))
+    attended = attention(queries, key_rows, value_rows, fetched, req_len, prefix_len)
     other_attended = from_behind(attended, "kv", 1)
     branch = jnp.dot(
         in_kv_order(attended, other_attended, 1),

time: 134 us -> 119 us (0.89)
  starting transfers between devices: 32.9 us -> 15.7 us
  local copies, waits for them, and re-layouts: 26.4 us -> 21.5 us
  other arithmetic: 12 us -> 15 us
  waiting for transfers between devices: 16.1 us -> 17.9 us
  matrix products: 9.94 us -> 11.5 us
    ppermute x14 -> x8, starting transfers between devices: 32.9 us -> 15.7 us  [from_behind(): return lax.ppermute(block, axis, route)]
    another operation x0 -> x6, other arithmetic: none -> 5.64 us  [the longest x4 3.81 us: fetch_page(): jnp.stack([send_keys, send_values])]
    squeeze x2 -> x0, local copies, waits for them, and re-layouts: 3.62 us -> none  [the longest x1 2.51 us: fetch_page(): lax.dynamic_index_in_dim(pool_values, local, 0, keepdims=False)]
    convert_element_type x1, other arithmetic: 3.74 us -> 1.14 us  [head_normed(): (rms_scale(split_heads).reshape(count, -1) * head_gain).astype(jnp.bfloat16)]
    dynamic_slice x0 -> x1, local copies, waits for them, and re-layouts: none -> 2.08 us  [fetch_page(): lax.dynamic_index_in_dim(pool_values, local, 0, keepdims=False)]
    ppermute x14 -> x8, waiting for transfers between devices: 16.1 us -> 17.9 us  [from_behind(): return lax.ppermute(block, axis, route)]
    dot_general x1, matrix products: 1.19 us -> 2.76 us  [body(): jnp.dot(hidden_in, w_value, preferred_element_type=jnp.float32) * row_scale]
    dynamic_update_slice x4 -> x3, local copies, waits for them, and re-layouts: 4.37 us -> 3.28 us  [the longest x2 2.19 us: relay(): lax.dynamic_update_index_in_dim(value_out, received[1], target, 0)]
  transfers between devices with their start and end apart: 14 -> 8, of which waited for: 4 -> 1; matrix products, arithmetic and copies ran while one was open for 28% -> 30% of each run, Pallas kernels for 16% -> 18%
where the time goes in v4:
time: 119 us; the launch traced here: 117 us
  local copies, waits for them, and re-layouts  21.5 us (18%)
  Pallas kernels  21.3 us (18%)
  waiting for transfers between devices  17.9 us (15%)
  starting transfers between devices  15.7 us (13%)
  other arithmetic  15 us (13%)
  between operations  14 us (12%)
  matrix products  11.5 us (10%)
    pallas_call x1, Pallas kernels, attention(): pl.pallas_call(attention_kernel, out_shape=jax.ShapeDtypeStruct((tokens,...  21.3 us
    ppermute x8, waiting for transfers between devices, from_behind(): return lax.ppermute(block, axis, route)  17.9 us
    ppermute x8, starting transfers between devices, from_behind(): return lax.ppermute(block, axis, route)  15.7 us
    mul x4, local copies, waits for them, and re-layouts, rms_scale(): values * lax.rsqrt(jnp.mean(values * values, axis=-1, keepdims=True) + ep...  8 us
    mul x2, local copies, waits for them, and re-layouts, rms_scale(): values * values  5.56 us
    dot_general x1, matrix products, body(): jnp.dot(hidden_in, w_key, preferred_element_type=jnp.float32)  4.1 us
    another operation x4, other arithmetic, fetch_page(): jnp.stack([send_keys, send_values])  3.81 us
    reduce_sum x3, other arithmetic, rms_scale(): jnp.mean(values * values, axis=-1, keepdims=True) + epsilon  3.8 us
  transfers between devices with their start and end apart: 8, of which 1 were waited for; matrix products, arithmetic and copies ran while one was open for 30% of the time, Pallas kernels for 18%

profile of v4, /device:TPU:6, one launch (start us, length us, event | category | flops | bytes accessed | tf_op | source)
XLA Modules:
  0.0 116.9 jit_solution(11203604837428332726)
XLA Ops:
  0.6 0.0 copy-start
  0.7 1.5 %constant_dynamic-slice_fusion.11 = (s32[1,1]{0,1:T(1,128)}, s32[1,1]{0,1:T(1,128)}, s32[1,1]{0,1:T(1,128)}, s32[1,1]{0,1:T(1,128)}) fusion(s32[128,4]{0,1:T(4,128)} %param.24, s32[]{:T(128)S(6)} %select_n.133, s32[]{:T(128)S(6)} %select_n.125, s32[]{:T(128)S(6)} %select_n.121, s32[]{:T(128)S(6)} %select_n.129), kind=kLoop, calls=%fused_computation.54 | loop fusion | bytes 48 | tf_op jit(solution)/shard_map/dynamic_slice | solution.py:124
  10.2 2.1 %constant_dynamic-slice_fusion = (bf16[1,256,640]{2,1,0:T(8,128)(2,1)S(1)}, bf16[1,256,640]{2,1,0:T(8,128)(2,1)S(1)}, bf16[1,256,640]{2,1,0:T(8,128)(2,1)S(1)}, ...) fusion(bf16[4,256,640]{2,1,0:T(8,128)(2,1)} %param.21, ...), kind=kLoop, calls=%fused_computation.40 | loop fusion | bytes 5242896 | tf_op jit(solution)/shard_map/jit(dynamic_index_in_dim)/dynamic_slice | solution.py:126
  12.3 1.0 pad_maximum_fusion.3
  13.3 6.3 %collective-permute-start.3 = (bf16[2,256,640]{2,1,0:T(8,128)(2,1)}, bf16[2,256,640]{2,1,0:T(8,128)(2,1)}, u32[]{:S(2)}, u32[]{:S(2)}) collective-permute-start(bf16[2,256,640]{2,1,0:T(8,128)(2,1)} %pad_maximum_fusion.3), channel_id=1, source_target_pairs={{97,0},{98,1},{99,2},{100,3},{101,4},{102,5},{103,6},{104,7},{105,... | collective-permute-start | bytes 1966088 | tf_op jit(solution)/shard_map/ppermute | solution.py:21
  19.5 1.0 pad_maximum_fusion.2
  20.5 1.7 %collective-permute-start.2 = (bf16[2,256,640]{2,1,0:T(8,128)(2,1)}, bf16[2,256,640]{2,1,0:T(8,128)(2,1)}, u32[]{:S(2)}, u32[]{:S(2)}) collective-permute-start(bf16[2,256,640]{2,1,0:T(8,128)(2,1)} %pad_maximum_fusion.2), channel_id=1, source_target_pairs={{65,0},{66,1},{67,2},{68,3},{69,4},{70,5},{71,6},{72,7},{73,8},{74... | collective-permute-start | bytes 1966088 | tf_op jit(solution)/shard_map/ppermute | solution.py:21
  22.2 0.9 pad_maximum_fusion.1
  23.1 1.8 %collective-permute-start.1 = (bf16[2,256,640]{2,1,0:T(8,128)(2,1)}, bf16[2,256,640]{2,1,0:T(8,128)(2,1)}, u32[]{:S(2)}, u32[]{:S(2)}) collective-permute-start(bf16[2,256,640]{2,1,0:T(8,128)(2,1)} %pad_maximum_fusion.1), channel_id=1, source_target_pairs={{33,0},{34,1},{35,2},{36,3},{37,4},{38,5},{39,6},{40,7},{41,8},{42... | collective-permute-start | bytes 1966088 | tf_op jit(solution)/shard_map/ppermute | solution.py:21
  24.9 0.9 pad_maximum_fusion
  25.8 0.4 collective-permute-start
  26.3 0.0 copy-done.1
  26.3 0.3 fusion.7
  26.6 0.0 copy-done
  26.6 2.7 %fusion.15 = (f32[512,640]{1,0:T(8,128)}, f32[512,640]{1,0:T(8,128)}) fusion(bf16[512,1280]{1,0:T(8,128)(2,1)S(1)} %copy-done.1, bf16[1280,640]{1,0:T(8,128)(2,1)S(1)} %copy-done), kind=kOutput, calls=%fused_computation.58 | convolution fusion | flops 839188480 | bytes 5570560 | tf_op jit(solution)/shard_map/dot_general | solution.py:174
  29.3 2.8 %copy.16 = f32[512,640]{0,1:T(8,128)} copy(f32[512,640]{1,0:T(8,128)} %get-tuple-element.43) | data formatting | bytes 2621440 | tf_op jit(solution)/shard_map/mul | solution.py:25
  32.1 1.5 %reduce_sum.46 = f32[512,10]{0,1:T(8,128)S(1)} reduce(f32[512,10,64]{0,2,1:T(8,128)} %bitcast.25, f32[]{:T(128)} %constant.123.clone.1), dimensions={2}, to_apply=%region_1.0 | reduce | flops 322560 | bytes 1331204 | tf_op jit(solution)/shard_map/reduce_sum | solution.py:25
  33.6 1.2 %mul.109 = f32[512,10,64]{0,2,1:T(8,128)} broadcast(f32[512,10]{0,1:T(8,128)S(1)} %add_rsqrt_fusion.1), dimensions={0,1} | broadcast | bytes 1331200 | tf_op jit(solution)/shard_map/mul | solution.py:25
  34.8 2.8 %copy.17 = f32[512,640]{1,0:T(8,128)} copy(f32[512,640]{0,1:T(8,128)} %bitcast.26) | data formatting | bytes 2621440 | tf_op jit(solution)/shard_map/mul | solution.py:25
  37.6 4.1 %fusion.14 = (f32[512,640]{1,0:T(8,128)}, f32[512,640]{1,0:T(8,128)}) fusion(bf16[512,1280]{1,0:T(8,128)(2,1)S(1)} %copy-done.1, bf16[1280,640]{1,0:T(8,128)(2,1)} %param.15), kind=kOutput, calls=%fused_computation.57 | convolution fusion | flops 839188480 | bytes 5570560 | tf_op jit(solution)/shard_map/dot_general | solution.py:176
  41.7 2.8 %copy.18 = f32[512,640]{0,1:T(8,128)} copy(f32[512,640]{1,0:T(8,128)} %get-tuple-element.41) | data formatting | bytes 2621440 | tf_op jit(solution)/shard_map/mul | solution.py:25
  44.5 1.5 %reduce_sum.47 = f32[512,10]{0,1:T(8,128)S(1)} reduce(f32[512,10,64]{0,2,1:T(8,128)} %bitcast.24, f32[]{:T(128)} %constant.123.clone.1), dimensions={2}, to_apply=%region_2.0 | reduce | flops 322560 | bytes 1331204 | tf_op jit(solution)/shard_map/reduce_sum | solution.py:25
  46.0 1.2 %mul.116 = f32[512,10,64]{0,2,1:T(8,128)} broadcast(f32[512,10]{0,1:T(8,128)S(1)} %add_rsqrt_fusion), dimensions={0,1} | broadcast | bytes 1331200 | tf_op jit(solution)/shard_map/mul | solution.py:25
  47.2 2.8 %copy.19 = f32[512,640]{1,0:T(8,128)} copy(f32[512,640]{0,1:T(8,128)} %bitcast.27) | data formatting | bytes 2621440 | tf_op jit(solution)/shard_map/mul | solution.py:25
  50.0 0.0 copy-start.12
  50.0 2.8 %fusion.8.v_ref = bf16[512,640]{1,0:T(8,128)(2,1)S(1)} fusion(bf16[512,1280]{1,0:T(8,128)(2,1)S(1)} %copy-done.1, bf16[1280,640]{1,0:T(8,128)(2,1)} %param.16, f32[512]{0:T(512)S(1)} %add_rsqrt_fusion.4), kind=kOutput, calls=%fused_computation.16 | convolution fusion | flops 839516160 | bytes 3606528 | tf_op jit(solution)/shard_map/dot_general | solution.py:178
  52.8 0.0 copy-start.5
  52.8 0.1 copy-done.8
  53.0 1.1 multiply_convert_fusion.1
  54.1 0.0 collective-permute-done.3.refs_3_.refs_7_
  54.1 0.0 collective-permute-done.2.refs_2_.refs_6_
  54.1 0.0 collective-permute-done.1.refs_1_.refs_5_
  54.1 0.0 collective-permute-done.refs_0_.refs_4_
  54.1 0.1 slice_bitcast_fusion.1
  54.2 0.1 slice_bitcast_fusion
  54.3 0.0 copy-start.13
  54.3 0.9 pad_maximum_fusion.4
  55.2 2.0 %collective-permute-start.6 = (bf16[2,256,640]{2,1,0:T(8,128)(2,1)}, bf16[2,256,640]{2,1,0:T(8,128)(2,1)}, u32[]{:S(2)}, u32[]{:S(2)}) collective-permute-start(bf16[2,256,640]{2,1,0:T(8,128)(2,1)} %pad_maximum_fusion.4), channel_id=1, source_target_pairs={{96,0},{97,1},{98,2},{99,3},{100,4},{101,5},{102,6},{103,7},{104,8... | collective-permute-start | bytes 1966088 | tf_op jit(solution)/shard_map/ppermute | solution.py:21
  57.2 2.9 %collective-permute-start.5 = (bf16[640,1280]{1,0:T(8,128)(2,1)}, bf16[640,1280]{1,0:T(8,128)(2,1)}, u32[]{:S(2)}, u32[]{:S(2)}) collective-permute-start(bf16[640,1280]{1,0:T(8,128)(2,1)} %param.17), channel_id=1, source_target_pairs={{128,0},{0,128},{129,1},{1,129},{130,2},{2,130},{131,3},{3,131},{1... | collective-permute-start | bytes 4915208 | tf_op jit(solution)/shard_map/ppermute | solution.py:21
  60.1 0.9 pad_maximum_fusion.5
  61.0 0.0 collective-permute-start.7
  61.1 0.0 copy-done.13
  61.1 0.7 fusion.13
  66.7 21.3 %shard_map.148 = bf16[512,640]{1,0:T(8,128)(2,1)} custom-call(s32[1]{0:T(128)S(6)} %copy.24.live_ref, s32[1]{0:T(128)S(6)} %copy.25.depth_ref, bf16[512,640]{1,0:T(8,128)(2,1)} %get-tuple-element.34.q_ref, bf16[512,640]{1,0:T(8,128)(2,1)} %copy-done.2, bf16[512,640]{1,0:T(8,128)(2,1)} %copy-done.5, ...), custom_call_target="tpu_custom_call" | custom-call | tf_op jit(solution)/shard_map/pallas_call | solution.py:112
  88.0 0.6 collective-permute-start.4
  88.6 0.0 collective-permute-done.6
  88.6 0.1 broadcast.90.clone.1
  88.7 1.1 slice_dynamic-update-slice_fusion.3
  89.8 0.1 broadcast.90.clone
  89.9 1.0 slice_dynamic-update-slice_fusion.1
  90.9 0.0 collective-permute-done.7
  90.9 1.2 %slice_dynamic-update-slice_fusion = (bf16[2,256,640]{2,1,0:T(8,128)(2,1)S(1)}, bf16[2,256,640]{2,1,0:T(8,128)(2,1)S(1)}) fusion(bf16[2,256,640]{2,1,0:T(8,128)(2,1)S(1)} %slice_dynamic-update-slice_fusion.1, s32[]{:T(128)S(6)} %select_n.148, bf16[2,256,640]{2,1,0:T(8,128)(2,1)} %collective-permute-done.7, ...), kind=kLoop, calls=%fused_computation.30 | loop fusion | bytes 1310724 | tf_op jit(solution)/shard_map/jit(dynamic_update_index_in_dim)/dynamic_update_slice | solution.py:147
  92.1 0.0 copy-start.9
  92.1 0.0 copy-start.10
  92.1 17.9 %collective-permute-done.4 = bf16[512,640]{1,0:T(8,128)(2,1)S(1)} collective-permute-done((bf16[512,640]{1,0:T(8,128)(2,1)}, bf16[512,640]{1,0:T(8,128)(2,1)S(1)}, u32[]{:S(2)}, u32[]{:S(2)}) %collective-permute-start.4) | collective-permute-done | bytes 655392 | tf_op jit(solution)/shard_map/ppermute | solution.py:21
  110.0 0.1 broadcast_select_fusion.3
  110.1 0.0 collective-permute-done.5
  110.1 2.1 %broadcast_select_fusion.1 = (bf16[640,1280]{1,0:T(8,128)(2,1)S(1)}, bf16[640,1280]{1,0:T(8,128)(2,1)S(1)}) fusion(bf16[640,1280]{1,0:T(8,128)(2,1)} %param.17, bf16[640,1280]{1,0:T(8,128)(2,1)} %collective-permute-done.5, pred[]{:T(512)S(6)} %eq.17), kind=kLoop, calls=%fused_computation.14 | loop fusion | flops 1638400 | bytes 6553601 | tf_op jit(solution)/shard_map/jit(_where)/select_n | solution.py:53
  112.2 0.0 copy-done.9
  112.3 0.0 copy-done.10
  112.3 0.0 copy-start.11
  112.3 2.0 %multiply_reduce_fusion.1 = (f32[512]{0:T(512)S(1)}, f32[512,1280]{1,0:T(8,128)S(1)}) fusion(bf16[640,1280]{1,0:T(8,128)(2,1)S(1)} %get-tuple-element.16, bf16[640,1280]{1,0:T(8,128)(2,1)S(1)} %get-tuple-element.15, bf16[512,640]{1,0:T(8,128)(2,1)S(1)} %get-tuple-element.18, bf16[512,640]{1,0:T(8,128)(2,1)S(1)} %get-tuple-element.17), kind=kOutput, calls=%fused_computation.12 | convolution fusion | flops 1688206848 | bytes 7211008 | tf_op jit(solution)/shard_map/dot_general | solution.py:186
  114.3 0.8 multiply_reduce_fusion
  115.1 1.8 %multiply_convert_fusion = bf16[512,1280]{1,0:T(8,128)(2,1)} fusion(f32[512]{0:T(512)S(1)} %add_rsqrt_fusion.2, f32[512,1280]{1,0:T(8,128)S(1)} %get-tuple-element.46, f32[512]{0:T(512)S(1)} %add_rsqrt_fusion.3, f32[1280]{0:T(1024)S(1)} %copy-done.11, f32[512]{0:T(512)S(1)} %add_rsqrt_fusion.4, bf16[512,1280]{1,0:T(8,128)(2,1)S(1)} %copy-done.1), kind=kLoop, calls=%fused_computation.10 | loop fusion | flops 5242880 | bytes 5254144 | tf_op jit(solution)/shard_map/convert_element_type | solution.py:192
  (20 shorter events, 0.1 us)
Async XLA Ops:
  0.6 26.0 %copy-start = (bf16[1280,640]{1,0:T(8,128)(2,1)S(1)}, bf16[1280,640]{1,0:T(8,128)(2,1)}, u32[]{:S(2)}) copy-start(bf16[1280,640]{1,0:T(8,128)(2,1)} %param.14) | copy-start | bytes 4915204
  13.3 40.9 %collective-permute-start.3 = (bf16[2,256,640]{2,1,0:T(8,128)(2,1)}, bf16[2,256,640]{2,1,0:T(8,128)(2,1)}, u32[]{:S(2)}, u32[]{:S(2)}) collective-permute-start(bf16[2,256,640]{2,1,0:T(8,128)(2,1)} %pad_maximum_fusion.3), channel_id=1, source_target_pairs={{97,0},{98,1},{99,2},{100,3},{101,4},{102,5},{103,6},{104,7},{105,... | collective-permute-start | bytes 1966088 | tf_op jit(solution)/shard_map/ppermute | solution.py:21
  20.5 5.8 %copy-start.1 = (bf16[512,1280]{1,0:T(8,128)(2,1)S(1)}, bf16[512,1280]{1,0:T(8,128)(2,1)}, u32[]{:S(2)}) copy-start(bf16[512,1280]{1,0:T(8,128)(2,1)} %param.13) | copy-start | bytes 3932164
  20.5 33.6 %collective-permute-start.2 = (bf16[2,256,640]{2,1,0:T(8,128)(2,1)}, bf16[2,256,640]{2,1,0:T(8,128)(2,1)}, u32[]{:S(2)}, u32[]{:S(2)}) collective-permute-start(bf16[2,256,640]{2,1,0:T(8,128)(2,1)} %pad_maximum_fusion.2), channel_id=1, source_target_pairs={{65,0},{66,1},{67,2},{68,3},{69,4},{70,5},{71,6},{72,7},{73,8},{74... | collective-permute-start | bytes 1966088 | tf_op jit(solution)/shard_map/ppermute | solution.py:21
  23.1 31.0 %collective-permute-start.1 = (bf16[2,256,640]{2,1,0:T(8,128)(2,1)}, bf16[2,256,640]{2,1,0:T(8,128)(2,1)}, u32[]{:S(2)}, u32[]{:S(2)}) collective-permute-start(bf16[2,256,640]{2,1,0:T(8,128)(2,1)} %pad_maximum_fusion.1), channel_id=1, source_target_pairs={{33,0},{34,1},{35,2},{36,3},{37,4},{38,5},{39,6},{40,7},{41,8},{42... | collective-permute-start | bytes 1966088 | tf_op jit(solution)/shard_map/ppermute | solution.py:21
  25.8 28.3 %collective-permute-start = (bf16[2,256,640]{2,1,0:T(8,128)(2,1)}, bf16[2,256,640]{2,1,0:T(8,128)(2,1)}, u32[]{:S(2)}, u32[]{:S(2)}) collective-permute-start(bf16[2,256,640]{2,1,0:T(8,128)(2,1)} %pad_maximum_fusion), channel_id=1, source_target_pairs={{1,0},{2,1},{3,2},{4,3},{5,4},{6,5},{7,6},{8,7},{9,8},{10,9},{11,1... | collective-permute-start | bytes 1966088 | tf_op jit(solution)/shard_map/ppermute | solution.py:21
  50.0 2.8 %copy-start.3 = (f32[512,640]{1,0:T(8,128)S(1)}, f32[512,640]{1,0:T(8,128)}, u32[]{:S(2)}) copy-start(f32[512,640]{1,0:T(8,128)} %copy.17) | copy-start | bytes 3932164
  50.0 2.8 %copy-start.4 = (f32[512,640]{1,0:T(8,128)S(1)}, f32[512,640]{1,0:T(8,128)}, u32[]{:S(2)}) copy-start(f32[512,640]{1,0:T(8,128)} %copy.19) | copy-start | bytes 3932164
  50.0 2.8 %copy-start.7 = (f32[512,640]{1,0:T(8,128)S(1)}, f32[512,640]{1,0:T(8,128)}, u32[]{:S(2)}) copy-start(f32[512,640]{1,0:T(8,128)} %get-tuple-element.44) | copy-start | bytes 3932164
  50.0 3.0 %copy-start.8 = (f32[512,640]{1,0:T(8,128)S(1)}, f32[512,640]{1,0:T(8,128)}, u32[]{:S(2)}) copy-start(f32[512,640]{1,0:T(8,128)} %get-tuple-element.42) | copy-start | bytes 3932164
  50.0 3.0 %copy-start.12 = (f32[640]{0:T(1024)S(1)}, f32[640]{0:T(1024)}, u32[]{:S(2)}) copy-start(f32[640]{0:T(1024)} %param.18) | copy-start | bytes 7684
  52.8 1.4 %copy-start.5 = (bf16[512,640]{1,0:T(8,128)(2,1)}, bf16[512,640]{1,0:T(8,128)(2,1)S(1)}, u32[]{:S(2)}) copy-start(bf16[512,640]{1,0:T(8,128)(2,1)S(1)} %fusion.8.v_ref) | copy-start | bytes 1966084
  54.1 1.1 copy-start.2
  54.3 6.8 %copy-start.13 = (s32[256]{0:T(256)S(1)}, s32[256]{0:T(256)}, u32[]{:S(2)}) copy-start(s32[256]{0:T(256)} %param.25) | copy-start | bytes 3076
  55.2 33.4 %collective-permute-start.6 = (bf16[2,256,640]{2,1,0:T(8,128)(2,1)}, bf16[2,256,640]{2,1,0:T(8,128)(2,1)}, u32[]{:S(2)}, u32[]{:S(2)}) collective-permute-start(bf16[2,256,640]{2,1,0:T(8,128)(2,1)} %pad_maximum_fusion.4), channel_id=1, source_target_pairs={{96,0},{97,1},{98,2},{99,3},{100,4},{101,5},{102,6},{103,7},{104,8... | collective-permute-start | bytes 1966088 | tf_op jit(solution)/shard_map/ppermute | solution.py:21
  57.2 52.9 %collective-permute-start.5 = (bf16[640,1280]{1,0:T(8,128)(2,1)}, bf16[640,1280]{1,0:T(8,128)(2,1)}, u32[]{:S(2)}, u32[]{:S(2)}) collective-permute-start(bf16[640,1280]{1,0:T(8,128)(2,1)} %param.17), channel_id=1, source_target_pairs={{128,0},{0,128},{129,1},{1,129},{130,2},{2,130},{131,3},{3,131},{1... | collective-permute-start | bytes 4915208 | tf_op jit(solution)/shard_map/ppermute | solution.py:21
  61.0 29.8 %collective-permute-start.7 = (bf16[2,256,640]{2,1,0:T(8,128)(2,1)}, bf16[2,256,640]{2,1,0:T(8,128)(2,1)}, u32[]{:S(2)}, u32[]{:S(2)}) collective-permute-start(bf16[2,256,640]{2,1,0:T(8,128)(2,1)} %pad_maximum_fusion.5), channel_id=1, source_target_pairs={{32,0},{33,1},{34,2},{35,3},{36,4},{37,5},{38,6},{39,7},{40,8},{41... | collective-permute-start | bytes 1966088 | tf_op jit(solution)/shard_map/ppermute | solution.py:21
  88.0 22.0 %collective-permute-start.4 = (bf16[512,640]{1,0:T(8,128)(2,1)}, bf16[512,640]{1,0:T(8,128)(2,1)S(1)}, u32[]{:S(2)}, u32[]{:S(2)}) collective-permute-start(bf16[512,640]{1,0:T(8,128)(2,1)} %shard_map.148), channel_id=1, source_target_pairs={{128,0},{0,128},{129,1},{1,129},{130,2},{2,130},{131,3},{3,131},{1... | collective-permute-start | bytes 1966088 | tf_op jit(solution)/shard_map/ppermute | solution.py:21
  88.7 21.3 %copy-start.6 = (bf16[512,640]{1,0:T(8,128)(2,1)S(1)}, bf16[512,640]{1,0:T(8,128)(2,1)}, u32[]{:S(2)}) copy-start(bf16[512,640]{1,0:T(8,128)(2,1)} %shard_map.148) | copy-start | bytes 1966084
  92.1 20.2 %copy-start.9 = (bf16[2,256,640]{2,1,0:T(8,128)(2,1)}, bf16[2,256,640]{2,1,0:T(8,128)(2,1)S(1)}, u32[]{:S(2)}) copy-start(bf16[2,256,640]{2,1,0:T(8,128)(2,1)S(1)} %get-tuple-element.27) | copy-start | bytes 1966084
  92.1 20.2 %copy-start.10 = (bf16[2,256,640]{2,1,0:T(8,128)(2,1)}, bf16[2,256,640]{2,1,0:T(8,128)(2,1)S(1)}, u32[]{:S(2)}) copy-start(bf16[2,256,640]{2,1,0:T(8,128)(2,1)S(1)} %get-tuple-element.28) | copy-start | bytes 1966084
  112.3 2.0 %copy-start.11 = (f32[1280]{0:T(1024)S(1)}, f32[1280]{0:T(1024)}, u32[]{:S(2)}) copy-start(f32[1280]{0:T(1024)} %param.19) | copy-start | bytes 15364

commit v5 on v4

--- a/solution.py
+++ b/solution.py
@@ -180,7 +180,9 @@
     fetched = [
         fetch_page(pool_keys, pool_values, prefix_pages, slot_index) for slot_index in range(PMAX)
     ]
-    key_rows, value_rows, fetched = lax.optimization_barrier((key_rows, value_rows, fetched))
+    key_rows, value_rows, fetched, other_w_out = lax.optimization_barrier(
+        (key_rows, value_rows, fetched, other_w_out)
+    )
     attended = attention(queries, key_rows, value_rows, fetched, req_len, prefix_len)
     other_attended = from_behind(attended, "kv", 1)
     branch = jnp.dot(

time: 119 us -> 135 us (1.13)
  the two profiles are of different devices: /device:TPU:6 before, /device:TPU:230 now
where the time goes in v5:
time: 135 us; the launch traced here: 134 us
  waiting for transfers between devices  40.1 us (30%)
  Pallas kernels  21.2 us (16%)
  local copies, waits for them, and re-layouts  20.8 us (15%)
  other arithmetic  15.2 us (11%)
  between operations  14.2 us (11%)
  matrix products  11.5 us (9%)
  starting transfers between devices  10.9 us (8%)
    ppermute x8, waiting for transfers between devices, from_behind(): return lax.ppermute(block, axis, route)  40.1 us
    pallas_call x1, Pallas kernels, attention(): pl.pallas_call(attention_kernel, out_shape=jax.ShapeDtypeStruct((tokens,...  21.2 us
    ppermute x8, starting transfers between devices, from_behind(): return lax.ppermute(block, axis, route)  10.9 us
    mul x4, local copies, waits for them, and re-layouts, rms_scale(): values * lax.rsqrt(jnp.mean(values * values, axis=-1, keepdims=True) + ep...  8.05 us
    mul x2, local copies, waits for them, and re-layouts, rms_scale(): values * values  5.58 us
    dot_general x1, matrix products, body(): jnp.dot(hidden_in, w_key, preferred_element_type=jnp.float32)  4.1 us
    reduce_sum x3, other arithmetic, rms_scale(): jnp.mean(values * values, axis=-1, keepdims=True) + epsilon  3.8 us
    another operation x4, other arithmetic, fetch_page(): jnp.stack([send_keys, send_values])  3.66 us
  transfers between devices with their start and end apart: 8, of which 2 were waited for; matrix products, arithmetic and copies ran while one was open for 30% of the time, Pallas kernels for 0%

profile of v5, /device:TPU:230, one launch (start us, length us, event | category | flops | bytes accessed | tf_op | source)
XLA Modules:
  0.0 134.0 jit_solution(4928014325272098010)
XLA Ops:
  0.6 0.0 copy-start
  0.7 1.5 %constant_dynamic-slice_fusion.11 = (s32[1,1]{0,1:T(1,128)}, s32[1,1]{0,1:T(1,128)}, s32[1,1]{0,1:T(1,128)}, s32[1,1]{0,1:T(1,128)}) fusion(s32[128,4]{0,1:T(4,128)} %param.24, s32[]{:T(128)S(6)} %select_n.133, s32[]{:T(128)S(6)} %select_n.125, s32[]{:T(128)S(6)} %select_n.121, s32[]{:T(128)S(6)} %select_n.129), kind=kLoop, calls=%fused_computation.54 | loop fusion | bytes 48 | tf_op jit(solution)/shard_map/dynamic_slice | solution.py:124
  10.2 1.9 %constant_dynamic-slice_fusion = (bf16[1,256,640]{2,1,0:T(8,128)(2,1)S(1)}, bf16[1,256,640]{2,1,0:T(8,128)(2,1)S(1)}, bf16[1,256,640]{2,1,0:T(8,128)(2,1)S(1)}, ...) fusion(bf16[4,256,640]{2,1,0:T(8,128)(2,1)} %param.21, ...), kind=kLoop, calls=%fused_computation.40 | loop fusion | bytes 5242896 | tf_op jit(solution)/shard_map/jit(dynamic_index_in_dim)/dynamic_slice | solution.py:126
  12.1 0.9 pad_maximum_fusion
  13.0 0.7 collective-permute-start
  13.7 0.9 pad_maximum_fusion.1
  14.6 0.8 collective-permute-start.1
  15.4 0.9 pad_maximum_fusion.2
  16.3 1.2 collective-permute-start.2
  17.5 0.9 pad_maximum_fusion.3
  18.4 2.1 %collective-permute-start.3 = (bf16[2,256,640]{2,1,0:T(8,128)(2,1)}, bf16[2,256,640]{2,1,0:T(8,128)(2,1)}, u32[]{:S(2)}, u32[]{:S(2)}) collective-permute-start(bf16[2,256,640]{2,1,0:T(8,128)(2,1)} %pad_maximum_fusion.3), channel_id=1, source_target_pairs={{97,0},{98,1},{99,2},{100,3},{101,4},{102,5},{103,6},{104,7},{105,... | collective-permute-start | bytes 1966088 | tf_op jit(solution)/shard_map/ppermute | solution.py:21
  20.5 3.2 %collective-permute-start.4 = (bf16[640,1280]{1,0:T(8,128)(2,1)}, bf16[640,1280]{1,0:T(8,128)(2,1)}, u32[]{:S(2)}, u32[]{:S(2)}) collective-permute-start(bf16[640,1280]{1,0:T(8,128)(2,1)} %param.17), channel_id=1, source_target_pairs={{128,0},{0,128},{129,1},{1,129},{130,2},{2,130},{131,3},{3,131},{1... | collective-permute-start | bytes 4915208 | tf_op jit(solution)/shard_map/ppermute | solution.py:21
  23.7 0.0 copy-done.13
  23.7 0.6 fusion.13
  28.2 0.0 copy-done
  28.2 0.0 copy-done.1
  28.3 2.7 %fusion.14 = (f32[512,640]{1,0:T(8,128)}, f32[512,640]{1,0:T(8,128)}) fusion(bf16[512,1280]{1,0:T(8,128)(2,1)S(1)} %copy-done.1, bf16[1280,640]{1,0:T(8,128)(2,1)S(1)} %copy-done), kind=kOutput, calls=%fused_computation.57 | convolution fusion | flops 839188480 | bytes 5570560 | tf_op jit(solution)/shard_map/dot_general | solution.py:174
  30.9 2.8 %copy.16 = f32[512,640]{0,1:T(8,128)} copy(f32[512,640]{1,0:T(8,128)} %get-tuple-element.43) | data formatting | bytes 2621440 | tf_op jit(solution)/shard_map/mul | solution.py:25
  33.7 1.5 %reduce_sum.46 = f32[512,10]{0,1:T(8,128)S(1)} reduce(f32[512,10,64]{0,2,1:T(8,128)} %bitcast.25, f32[]{:T(128)} %constant.123.clone.1), dimensions={2}, to_apply=%region_1.0 | reduce | flops 322560 | bytes 1331204 | tf_op jit(solution)/shard_map/reduce_sum | solution.py:25
  35.2 1.2 mul.109
  36.4 2.8 %copy.17 = f32[512,640]{1,0:T(8,128)} copy(f32[512,640]{0,1:T(8,128)} %bitcast.26) | data formatting | bytes 2621440 | tf_op jit(solution)/shard_map/mul | solution.py:25
  39.2 4.1 %fusion.15 = (f32[512,640]{1,0:T(8,128)}, f32[512,640]{1,0:T(8,128)}) fusion(bf16[512,1280]{1,0:T(8,128)(2,1)S(1)} %copy-done.1, bf16[1280,640]{1,0:T(8,128)(2,1)} %param.15), kind=kOutput, calls=%fused_computation.58 | convolution fusion | flops 839188480 | bytes 5570560 | tf_op jit(solution)/shard_map/dot_general | solution.py:176
  43.3 2.8 %copy.18 = f32[512,640]{0,1:T(8,128)} copy(f32[512,640]{1,0:T(8,128)} %get-tuple-element.45) | data formatting | bytes 2621440 | tf_op jit(solution)/shard_map/mul | solution.py:25
  46.1 1.5 %reduce_sum.47 = f32[512,10]{0,1:T(8,128)S(1)} reduce(f32[512,10,64]{0,2,1:T(8,128)} %bitcast.24, f32[]{:T(128)} %constant.123.clone.1), dimensions={2}, to_apply=%region_2.0 | reduce | flops 322560 | bytes 1331204 | tf_op jit(solution)/shard_map/reduce_sum | solution.py:25
  47.6 1.2 mul.116
  48.9 2.8 %copy.19 = f32[512,640]{1,0:T(8,128)} copy(f32[512,640]{0,1:T(8,128)} %bitcast.27) | data formatting | bytes 2621440 | tf_op jit(solution)/shard_map/mul | solution.py:25
  53.0 0.3 fusion.7
  53.3 0.0 copy-start.3
  53.3 0.0 copy-start.4
  53.3 0.0 copy-start.12
  53.4 2.8 %fusion.8.v_ref = bf16[512,640]{1,0:T(8,128)(2,1)S(1)} fusion(bf16[512,1280]{1,0:T(8,128)(2,1)S(1)} %copy-done.1, bf16[1280,640]{1,0:T(8,128)(2,1)} %param.16, f32[512]{0:T(512)S(1)} %add_rsqrt_fusion.4), kind=kOutput, calls=%fused_computation.16 | convolution fusion | flops 839516160 | bytes 3606528 | tf_op jit(solution)/shard_map/dot_general | solution.py:178
  56.1 0.0 copy-start.5
  56.2 0.1 copy-done.8
  56.3 0.0 copy-done.12
  56.3 1.1 multiply_convert_fusion.2
  57.5 0.0 collective-permute-done.refs_0_.refs_4_
  57.5 0.0 collective-permute-done.1.refs_1_.refs_5_
  57.5 0.0 collective-permute-done.2.refs_2_.refs_6_
  57.5 0.0 collective-permute-done.3.refs_3_.refs_7_
  57.5 29.1 %collective-permute-done.4 = bf16[640,1280]{1,0:T(8,128)(2,1)} collective-permute-done((bf16[640,1280]{1,0:T(8,128)(2,1)}, bf16[640,1280]{1,0:T(8,128)(2,1)}, u32[]{:S(2)}, u32[]{:S(2)}) %collective-permute-start.4) | collective-permute-done | bytes 1638432 | tf_op jit(solution)/shard_map/ppermute | solution.py:21
  86.6 0.8 slice_bitcast_fusion
  87.3 0.9 slice_bitcast_fusion.1
  88.2 21.2 %shard_map.148 = bf16[512,640]{1,0:T(8,128)(2,1)} custom-call(s32[1]{0:T(128)S(6)} %copy.24.live_ref, s32[1]{0:T(128)S(6)} %copy.25.depth_ref, bf16[512,640]{1,0:T(8,128)(2,1)} %get-tuple-element.35.q_ref, bf16[512,640]{1,0:T(8,128)(2,1)} %copy-done.2, bf16[512,640]{1,0:T(8,128)(2,1)} %copy-done.5, ...), custom_call_target="tpu_custom_call" | custom-call | tf_op jit(solution)/shard_map/pallas_call | solution.py:112
  109.5 0.6 collective-permute-start.5
  110.1 1.1 pad_maximum_fusion.4
  111.2 0.3 collective-permute-start.6
  111.5 1.0 pad_maximum_fusion.5
  112.6 2.1 %collective-permute-start.7 = (bf16[2,256,640]{2,1,0:T(8,128)(2,1)S(1)}, bf16[2,256,640]{2,1,0:T(8,128)(2,1)S(1)}, u32[]{:S(2)}, u32[]{:S(2)}) collective-permute-start(bf16[2,256,640]{2,1,0:T(8,128)(2,1)S(1)} %pad_maximum_fusion.5), channel_id=1, source_target_pairs={{32,0},{33,1},{34,2},{35,3},{36,4},{37,5},{38,6},{39,7},{40,8},{41... | collective-permute-start | bytes 1966088 | tf_op jit(solution)/shard_map/ppermute | solution.py:21
  114.6 2.1 %broadcast_select_fusion.1 = (bf16[640,1280]{1,0:T(8,128)(2,1)S(1)}, bf16[640,1280]{1,0:T(8,128)(2,1)S(1)}) fusion(bf16[640,1280]{1,0:T(8,128)(2,1)} %param.17, bf16[640,1280]{1,0:T(8,128)(2,1)} %collective-permute-done.4, pred[]{:T(512)S(6)} %eq.17), kind=kLoop, calls=%fused_computation.14 | loop fusion | flops 1638400 | bytes 6553601 | tf_op jit(solution)/shard_map/jit(_where)/select_n | solution.py:53
  116.8 11.0 %collective-permute-done.5 = bf16[512,640]{1,0:T(8,128)(2,1)S(1)} collective-permute-done((bf16[512,640]{1,0:T(8,128)(2,1)}, bf16[512,640]{1,0:T(8,128)(2,1)S(1)}, u32[]{:S(2)}, u32[]{:S(2)}) %collective-permute-start.5) | collective-permute-done | bytes 655392 | tf_op jit(solution)/shard_map/ppermute | solution.py:21
  127.8 0.1 broadcast_select_fusion.3
  128.0 0.0 copy-start.11
  128.0 2.0 %multiply_reduce_fusion.1 = (f32[512]{0:T(512)S(1)}, f32[512,1280]{1,0:T(8,128)S(1)}) fusion(bf16[640,1280]{1,0:T(8,128)(2,1)S(1)} %get-tuple-element.18, bf16[640,1280]{1,0:T(8,128)(2,1)S(1)} %get-tuple-element.17, bf16[512,640]{1,0:T(8,128)(2,1)S(1)} %get-tuple-element.20, bf16[512,640]{1,0:T(8,128)(2,1)S(1)} %get-tuple-element.19), kind=kOutput, calls=%fused_computation.12 | convolution fusion | flops 1688206848 | bytes 7211008 | tf_op jit(solution)/shard_map/dot_general | solution.py:188
  130.0 0.8 multiply_reduce_fusion
  130.8 0.0 collective-permute-done.6
  130.8 0.1 broadcast.90.clone
  130.9 0.1 broadcast.90.clone.1
  131.1 1.8 %multiply_convert_fusion = bf16[512,1280]{1,0:T(8,128)(2,1)} fusion(f32[512]{0:T(512)S(1)} %add_rsqrt_fusion.2, f32[512,1280]{1,0:T(8,128)S(1)} %get-tuple-element.48, f32[512]{0:T(512)S(1)} %add_rsqrt_fusion.3, f32[1280]{0:T(1024)S(1)} %copy-done.11, f32[512]{0:T(512)S(1)} %add_rsqrt_fusion.4, bf16[512,1280]{1,0:T(8,128)(2,1)S(1)} %copy-done.1), kind=kLoop, calls=%fused_computation.10 | loop fusion | flops 5242880 | bytes 5254144 | tf_op jit(solution)/shard_map/convert_element_type | solution.py:194
  132.8 0.0 collective-permute-done.7
  132.9 0.1 slice_dynamic-update-slice_fusion
  133.0 0.0 copy-start.9
  133.0 0.0 copy-start.10
  133.0 0.8 copy-done.9
  133.8 0.2 copy-done.10
  (20 shorter events, 0.2 us)
Async XLA Ops:
  0.6 27.6 %copy-start = (bf16[1280,640]{1,0:T(8,128)(2,1)S(1)}, bf16[1280,640]{1,0:T(8,128)(2,1)}, u32[]{:S(2)}) copy-start(bf16[1280,640]{1,0:T(8,128)(2,1)} %param.14) | copy-start | bytes 4915204
  13.0 44.4 %collective-permute-start = (bf16[2,256,640]{2,1,0:T(8,128)(2,1)}, bf16[2,256,640]{2,1,0:T(8,128)(2,1)}, u32[]{:S(2)}, u32[]{:S(2)}) collective-permute-start(bf16[2,256,640]{2,1,0:T(8,128)(2,1)} %pad_maximum_fusion), channel_id=1, source_target_pairs={{1,0},{2,1},{3,2},{4,3},{5,4},{6,5},{7,6},{8,7},{9,8},{10,9},{11,1... | collective-permute-start | bytes 1966088 | tf_op jit(solution)/shard_map/ppermute | solution.py:21
  14.6 9.1 %copy-start.13 = (s32[256]{0:T(256)S(1)}, s32[256]{0:T(256)}, u32[]{:S(2)}) copy-start(s32[256]{0:T(256)} %param.25) | copy-start | bytes 3076
  14.6 13.6 %copy-start.1 = (bf16[512,1280]{1,0:T(8,128)(2,1)S(1)}, bf16[512,1280]{1,0:T(8,128)(2,1)}, u32[]{:S(2)}) copy-start(bf16[512,1280]{1,0:T(8,128)(2,1)} %param.13) | copy-start | bytes 3932164
  14.6 42.9 %collective-permute-start.1 = (bf16[2,256,640]{2,1,0:T(8,128)(2,1)}, bf16[2,256,640]{2,1,0:T(8,128)(2,1)}, u32[]{:S(2)}, u32[]{:S(2)}) collective-permute-start(bf16[2,256,640]{2,1,0:T(8,128)(2,1)} %pad_maximum_fusion.1), channel_id=1, source_target_pairs={{33,0},{34,1},{35,2},{36,3},{37,4},{38,5},{39,6},{40,7},{41,8},{42... | collective-permute-start | bytes 1966088 | tf_op jit(solution)/shard_map/ppermute | solution.py:21
  16.3 41.2 %collective-permute-start.2 = (bf16[2,256,640]{2,1,0:T(8,128)(2,1)}, bf16[2,256,640]{2,1,0:T(8,128)(2,1)}, u32[]{:S(2)}, u32[]{:S(2)}) collective-permute-start(bf16[2,256,640]{2,1,0:T(8,128)(2,1)} %pad_maximum_fusion.2), channel_id=1, source_target_pairs={{65,0},{66,1},{67,2},{68,3},{69,4},{70,5},{71,6},{72,7},{73,8},{74... | collective-permute-start | bytes 1966088 | tf_op jit(solution)/shard_map/ppermute | solution.py:21
  18.4 39.1 %collective-permute-start.3 = (bf16[2,256,640]{2,1,0:T(8,128)(2,1)}, bf16[2,256,640]{2,1,0:T(8,128)(2,1)}, u32[]{:S(2)}, u32[]{:S(2)}) collective-permute-start(bf16[2,256,640]{2,1,0:T(8,128)(2,1)} %pad_maximum_fusion.3), channel_id=1, source_target_pairs={{97,0},{98,1},{99,2},{100,3},{101,4},{102,5},{103,6},{104,7},{105,... | collective-permute-start | bytes 1966088 | tf_op jit(solution)/shard_map/ppermute | solution.py:21
  20.5 66.0 %collective-permute-start.4 = (bf16[640,1280]{1,0:T(8,128)(2,1)}, bf16[640,1280]{1,0:T(8,128)(2,1)}, u32[]{:S(2)}, u32[]{:S(2)}) collective-permute-start(bf16[640,1280]{1,0:T(8,128)(2,1)} %param.17), channel_id=1, source_target_pairs={{128,0},{0,128},{129,1},{1,129},{130,2},{2,130},{131,3},{3,131},{1... | collective-permute-start | bytes 4915208 | tf_op jit(solution)/shard_map/ppermute | solution.py:21
  53.3 2.8 %copy-start.3 = (f32[512,640]{1,0:T(8,128)S(1)}, f32[512,640]{1,0:T(8,128)}, u32[]{:S(2)}) copy-start(f32[512,640]{1,0:T(8,128)} %copy.17) | copy-start | bytes 3932164
  53.3 2.8 %copy-start.4 = (f32[512,640]{1,0:T(8,128)S(1)}, f32[512,640]{1,0:T(8,128)}, u32[]{:S(2)}) copy-start(f32[512,640]{1,0:T(8,128)} %copy.19) | copy-start | bytes 3932164
  53.3 2.8 %copy-start.7 = (f32[512,640]{1,0:T(8,128)S(1)}, f32[512,640]{1,0:T(8,128)}, u32[]{:S(2)}) copy-start(f32[512,640]{1,0:T(8,128)} %get-tuple-element.44) | copy-start | bytes 3932164
  53.3 3.0 %copy-start.8 = (f32[512,640]{1,0:T(8,128)S(1)}, f32[512,640]{1,0:T(8,128)}, u32[]{:S(2)}) copy-start(f32[512,640]{1,0:T(8,128)} %get-tuple-element.46) | copy-start | bytes 3932164
  53.3 3.0 %copy-start.12 = (f32[640]{0:T(1024)S(1)}, f32[640]{0:T(1024)}, u32[]{:S(2)}) copy-start(f32[640]{0:T(1024)} %param.18) | copy-start | bytes 7684
  56.1 30.4 %copy-start.5 = (bf16[512,640]{1,0:T(8,128)(2,1)}, bf16[512,640]{1,0:T(8,128)(2,1)S(1)}, u32[]{:S(2)}) copy-start(bf16[512,640]{1,0:T(8,128)(2,1)S(1)} %fusion.8.v_ref) | copy-start | bytes 1966084
  57.5 29.9 %copy-start.2 = (bf16[512,640]{1,0:T(8,128)(2,1)}, bf16[512,640]{1,0:T(8,128)(2,1)S(1)}, u32[]{:S(2)}) copy-start(bf16[512,640]{1,0:T(8,128)(2,1)S(1)} %get-tuple-element.10.k_ref) | copy-start | bytes 1966084
  109.5 18.4 %collective-permute-start.5 = (bf16[512,640]{1,0:T(8,128)(2,1)}, bf16[512,640]{1,0:T(8,128)(2,1)S(1)}, u32[]{:S(2)}, u32[]{:S(2)}) collective-permute-start(bf16[512,640]{1,0:T(8,128)(2,1)} %shard_map.148), channel_id=1, source_target_pairs={{128,0},{0,128},{129,1},{1,129},{130,2},{2,130},{131,3},{3,131},{1... | collective-permute-start | bytes 1966088 | tf_op jit(solution)/shard_map/ppermute | solution.py:21
  111.2 19.6 %collective-permute-start.6 = (bf16[2,256,640]{2,1,0:T(8,128)(2,1)S(1)}, bf16[2,256,640]{2,1,0:T(8,128)(2,1)S(1)}, u32[]{:S(2)}, u32[]{:S(2)}) collective-permute-start(bf16[2,256,640]{2,1,0:T(8,128)(2,1)S(1)} %pad_maximum_fusion.4), channel_id=1, source_target_pairs={{96,0},{97,1},{98,2},{99,3},{100,4},{101,5},{102,6},{103,7},{104,8... | collective-permute-start | bytes 1966088 | tf_op jit(solution)/shard_map/ppermute | solution.py:21
  112.6 15.3 %copy-start.6 = (bf16[512,640]{1,0:T(8,128)(2,1)S(1)}, bf16[512,640]{1,0:T(8,128)(2,1)}, u32[]{:S(2)}) copy-start(bf16[512,640]{1,0:T(8,128)(2,1)} %shard_map.148) | copy-start | bytes 1966084
  112.6 20.3 %collective-permute-start.7 = (bf16[2,256,640]{2,1,0:T(8,128)(2,1)S(1)}, bf16[2,256,640]{2,1,0:T(8,128)(2,1)S(1)}, u32[]{:S(2)}, u32[]{:S(2)}) collective-permute-start(bf16[2,256,640]{2,1,0:T(8,128)(2,1)S(1)} %pad_maximum_fusion.5), channel_id=1, source_target_pairs={{32,0},{33,1},{34,2},{35,3},{36,4},{37,5},{38,6},{39,7},{40,8},{41... | collective-permute-start | bytes 1966088 | tf_op jit(solution)/shard_map/ppermute | solution.py:21
  128.0 2.0 %copy-start.11 = (f32[1280]{0:T(1024)S(1)}, f32[1280]{0:T(1024)}, u32[]{:S(2)}) copy-start(f32[1280]{0:T(1024)} %param.19) | copy-start | bytes 15364
  133.0 0.8 copy-start.9
  133.0 1.0 copy-start.10

commit v6 on v4

--- a/solution.py
+++ b/solution.py
@@ -53,6 +53,48 @@
     low = jnp.where(first, mine, other)
     high = jnp.where(first, other, mine)
     return jnp.concatenate([low, high], axis=axis)
+
+
+def projection_kernel(x_ref, scale_ref, wq_ref, wk_ref, wv_ref, gain_ref, q_ref, k_ref, v_ref):
+    hidden = x_ref[...]
+    lane = lax.broadcasted_iota(jnp.int32, q_ref.shape, 1)
+    first = lane < HD
+
+    def normed(w_ref):
+        projected = jnp.dot(hidden, w_ref[...], preferred_element_type=jnp.float32)
+        squares = projected * projected
+        low = jnp.sum(jnp.where(first, squares, 0.0), axis=1, keepdims=True)
+        high = jnp.sum(jnp.where(first, 0.0, squares), axis=1, keepdims=True)
+        mean = jnp.where(first, low, high) / HD
+        return projected * lax.rsqrt(mean + epsilon) * gain_ref[...]
+
+    q_ref[...] = normed(wq_ref).astype(q_ref.dtype)
+    k_ref[...] = normed(wk_ref).astype(k_ref.dtype)
+    projected = jnp.dot(hidden, wv_ref[...], preferred_element_type=jnp.float32)
+    v_ref[...] = (projected * scale_ref[...]).astype(v_ref.dtype)
+
+
+def projections(hidden_in, row_scale, w_query, w_key, w_value, head_gain):
+    tokens, width = hidden_in.shape
+    lanes = 2 * HD
+    columns = w_query.shape[1]
+    weight_spec = pl.BlockSpec((width, lanes), lambda j: (0, j))
+    out_spec = pl.BlockSpec((tokens, lanes), lambda j: (0, j))
+    shape = jax.ShapeDtypeStruct((tokens, columns), jnp.bfloat16)
+    return pl.pallas_call(
+        projection_kernel,
+        out_shape=(shape, shape, shape),
+        grid=(columns // lanes,),
+        in_specs=[
+            pl.BlockSpec((tokens, width), lambda j: (0, 0)),
+            pl.BlockSpec((tokens, 1), lambda j: (0, 0)),
+            weight_spec,
+            weight_spec,
+            weight_spec,
+            pl.BlockSpec((1, lanes), lambda j: (0, j)),
+        ],
+        out_specs=[out_spec, out_spec, out_spec],
+    )(hidden_in, row_scale, w_query, w_key, w_value, head_gain.reshape(1, columns))
 
 
 def attention_kernel(live_ref, depth_ref, q_ref, k_ref, v_ref, *refs):
@@ -170,13 +212,9 @@
     hidden_f = hidden_in.astype(jnp.float32)
     row_scale = lax.rsqrt(jnp.mean(hidden_f * hidden_f, axis=-1, keepdims=True) + epsilon)
     anchor = hidden_f * row_scale
-    queries = head_normed(
-        jnp.dot(hidden_in, w_query, preferred_element_type=jnp.float32), head_gain
-    )
-    key_rows = head_normed(jnp.dot(hidden_in, w_key, preferred_element_type=jnp.float32), head_gain)
-    value_rows = (
-        jnp.dot(hidden_in, w_value, preferred_element_type=jnp.float32) * row_scale
-    ).astype(jnp.bfloat16)
+    queries, key_rows, value_rows = projections(
+        hidden_in, row_scale, w_query, w_key, w_value, head_gain
+    )
     fetched = [
         fetch_page(pool_keys, pool_values, prefix_pages, slot_index) for slot_index in range(PMAX)
     ]

time: 119 us -> 114 us (0.958); the launches traced: 117 us -> 113 us
  waiting for transfers between devices: 17.9 us -> 33.1 us
  local copies, waits for them, and re-layouts: 21.5 us -> 10.3 us
  matrix products: 11.5 us -> 1.97 us
  Pallas kernels: 21.3 us -> 30.3 us
  other arithmetic: 15 us -> 8.24 us
    ppermute x8, waiting for transfers between devices: 17.9 us -> 33.1 us  [from_behind(): return lax.ppermute(block, axis, route)]
    mul x6 -> x0, local copies, waits for them, and re-layouts: 13.6 us -> none  [the longest x4 8 us: rms_scale(): values * lax.rsqrt(jnp.mean(values * values, axis=-1, keepdims=True) + ep...]
    dot_general x3 -> x0, matrix products: 9.54 us -> none  [the longest x1 4.1 us: body(): jnp.dot(hidden_in, w_key, preferred_element_type=jnp.float32)]
    pallas_call x0 -> x1, Pallas kernels: none -> 9.09 us  [projections(): pl.pallas_call(projection_kernel, out_shape=(shape, shape, shape), grid=(...]
    reduce_sum x3 -> x1, other arithmetic: 3.8 us -> 0.83 us  [rms_scale(): jnp.mean(values * values, axis=-1, keepdims=True) + epsilon]
    another operation x4, other arithmetic: 3.81 us -> 1.99 us  [fetch_page(): jnp.stack([send_keys, send_values])]
    slice x1, local copies, waits for them, and re-layouts: 0.06 us -> 1.38 us  [relay(): key_pages[block_index]]
  transfers between devices with their start and end apart: 8 -> 8, of which waited for: 1 -> 4; matrix products, arithmetic and copies ran while one was open for 30% -> 7% of each run, Pallas kernels for 18% -> 27%
where the time goes in v6:
time: 114 us; the launch traced here: 113 us
  waiting for transfers between devices  33.1 us (29%)
  Pallas kernels  30.3 us (27%)
  starting transfers between devices  16.3 us (14%)
  between operations  13.2 us (12%)
  local copies, waits for them, and re-layouts  10.3 us (9%)
  other arithmetic  8.24 us (7%)
  matrix products  1.97 us (2%)
    ppermute x8, waiting for transfers between devices, from_behind(): return lax.ppermute(block, axis, route)  33.1 us
    pallas_call x1, Pallas kernels, attention(): pl.pallas_call(attention_kernel, out_shape=jax.ShapeDtypeStruct((tokens,...  21.2 us
    ppermute x8, starting transfers between devices, from_behind(): return lax.ppermute(block, axis, route)  16.3 us
    pallas_call x1, Pallas kernels, projections(): pl.pallas_call(projection_kernel, out_shape=(shape, shape, shape), grid=(...  9.09 us
  transfers between devices with their start and end apart: 8, of which 4 were waited for; matrix products, arithmetic and copies ran while one was open for 7% of the time, Pallas kernels for 27%

profile of v6, /device:TPU:6, one launch (start us, length us, event | category | flops | bytes accessed | tf_op | source)
XLA Modules:
  0.0 113.4 jit_solution(1729994352877273308)
XLA Ops:
  0.7 1.4 %constant_dynamic-slice_fusion.11 = (s32[1,1]{0,1:T(1,128)}, s32[1,1]{0,1:T(1,128)}, s32[1,1]{0,1:T(1,128)}, s32[1,1]{0,1:T(1,128)}) fusion(s32[128,4]{0,1:T(4,128)} %param.24, s32[]{:T(128)S(6)} %select_n.133, s32[]{:T(128)S(6)} %select_n.125, s32[]{:T(128)S(6)} %select_n.121, s32[]{:T(128)S(6)} %select_n.129), kind=kLoop, calls=%fused_computation.48 | loop fusion | bytes 48 | tf_op jit(solution)/shard_map/dynamic_slice | solution.py:166
  9.7 2.0 %constant_dynamic-slice_fusion = (bf16[1,256,640]{2,1,0:T(8,128)(2,1)S(1)}, bf16[1,256,640]{2,1,0:T(8,128)(2,1)S(1)}, bf16[1,256,640]{2,1,0:T(8,128)(2,1)S(1)}, ...) fusion(bf16[4,256,640]{2,1,0:T(8,128)(2,1)} %param.21, ...), kind=kLoop, calls=%fused_computation.34 | loop fusion | bytes 5242896 | tf_op jit(solution)/shard_map/jit(dynamic_index_in_dim)/dynamic_slice | solution.py:168
  11.7 0.0 copy-start
  11.7 0.1 pad_maximum_fusion.3
  11.8 6.3 %collective-permute-start.3 = (bf16[2,256,640]{2,1,0:T(8,128)(2,1)S(1)}, bf16[2,256,640]{2,1,0:T(8,128)(2,1)S(1)}, u32[]{:S(2)}, u32[]{:S(2)}) collective-permute-start(bf16[2,256,640]{2,1,0:T(8,128)(2,1)S(1)} %pad_maximum_fusion.3), channel_id=1, source_target_pairs={{97,0},{98,1},{99,2},{100,3},{101,4},{102,5},{103,6},{104,7},{105,... | collective-permute-start | bytes 1966088 | tf_op jit(solution)/shard_map/ppermute | solution.py:21
  18.1 0.0 copy-start.9
  18.1 0.1 pad_maximum_fusion.2
  18.2 1.9 %collective-permute-start.2 = (bf16[2,256,640]{2,1,0:T(8,128)(2,1)S(1)}, bf16[2,256,640]{2,1,0:T(8,128)(2,1)S(1)}, u32[]{:S(2)}, u32[]{:S(2)}) collective-permute-start(bf16[2,256,640]{2,1,0:T(8,128)(2,1)S(1)} %pad_maximum_fusion.2), channel_id=1, source_target_pairs={{65,0},{66,1},{67,2},{68,3},{69,4},{70,5},{71,6},{72,7},{73,8},{74... | collective-permute-start | bytes 1966088 | tf_op jit(solution)/shard_map/ppermute | solution.py:21
  20.1 0.9 pad_maximum_fusion.1
  21.1 1.7 %collective-permute-start.1 = (bf16[2,256,640]{2,1,0:T(8,128)(2,1)}, bf16[2,256,640]{2,1,0:T(8,128)(2,1)S(1)}, u32[]{:S(2)}, u32[]{:S(2)}) collective-permute-start(bf16[2,256,640]{2,1,0:T(8,128)(2,1)} %pad_maximum_fusion.1), channel_id=1, source_target_pairs={{33,0},{34,1},{35,2},{36,3},{37,4},{38,5},{39,6},{40,7},{41,8},{42... | collective-permute-start | bytes 1966088 | tf_op jit(solution)/shard_map/ppermute | solution.py:21
  22.8 0.9 pad_maximum_fusion
  23.7 0.3 collective-permute-start
  24.0 0.0 copy-done
  24.0 0.3 fusion.7
  24.4 0.9 copy.16.scale_ref
  25.2 0.0 copy-done.9
  25.2 0.6 reshape.53.gain_ref
  25.8 9.1 %shard_map.148 = (bf16[512,640]{1,0:T(8,128)(2,1)}, bf16[512,640]{1,0:T(8,128)(2,1)}, bf16[512,640]{1,0:T(8,128)(2,1)}) custom-call(bf16[512,1280]{1,0:T(8,128)(2,1)} %x_ref.1, f32[512,1]{1,0:T(8,128)} %copy.16.scale_ref, bf16[1280,640]{1,0:T(8,128)(2,1)} %wq_ref.1, bf16[1280,640]{1,0:T(8,128)(2,1)} %wk_ref.1, bf16[1280,640]{1,0:T(8,128)(2,1)} %wv_ref.1, ...), custom_call_target="tpu_custom_call" | custom-call | tf_op jit(solution)/shard_map/pallas_call | solution.py:84
  34.9 1.0 collective-permute-done.3.refs_3_.refs_7_
  35.9 0.0 copy-start.2
  35.9 8.0 %collective-permute-done.2.refs_2_.refs_6_ = bf16[2,256,640]{2,1,0:T(8,128)(2,1)S(1)} collective-permute-done((bf16[2,256,640]{2,1,0:T(8,128)(2,1)S(1)}, bf16[2,256,640]{2,1,0:T(8,128)(2,1)S(1)}, u32[]{:S(2)}, u32[]{:S(2)}) %collective-permute-start.2) | collective-permute-done | bytes 655392 | tf_op jit(solution)/shard_map/ppermute | solution.py:21
  43.9 0.0 copy-start.3
  43.9 6.9 %collective-permute-done.1.refs_1_.refs_5_ = bf16[2,256,640]{2,1,0:T(8,128)(2,1)S(1)} collective-permute-done((bf16[2,256,640]{2,1,0:T(8,128)(2,1)}, bf16[2,256,640]{2,1,0:T(8,128)(2,1)S(1)}, u32[]{:S(2)}, u32[]{:S(2)}) %collective-permute-start.1) | collective-permute-done | bytes 655392 | tf_op jit(solution)/shard_map/ppermute | solution.py:21
  50.8 0.0 copy-start.4
  50.8 0.0 collective-permute-done.refs_0_.refs_4_
  50.9 0.0 copy-start.10
  50.9 1.4 %slice_bitcast_fusion.1 = (bf16[1,256,640]{2,1,0:T(8,128)(2,1)S(1)}, bf16[1,256,640]{2,1,0:T(8,128)(2,1)S(1)}) fusion(bf16[512,640]{1,0:T(8,128)(2,1)} %get-tuple-element.15.k_ref), kind=kLoop, calls=%fused_computation.31 | loop fusion | bytes 1310720 | tf_op jit(solution)/shard_map/slice | solution.py:184
  52.2 1.1 slice_bitcast_fusion
  53.4 0.1 pad_maximum_fusion.4
  53.5 0.7 collective-permute-start.6
  54.1 2.9 %collective-permute-start.5 = (bf16[640,1280]{1,0:T(8,128)(2,1)}, bf16[640,1280]{1,0:T(8,128)(2,1)}, u32[]{:S(2)}, u32[]{:S(2)}) collective-permute-start(bf16[640,1280]{1,0:T(8,128)(2,1)} %param.17), channel_id=1, source_target_pairs={{128,0},{0,128},{129,1},{1,129},{130,2},{2,130},{131,3},{3,131},{1... | collective-permute-start | bytes 4915208 | tf_op jit(solution)/shard_map/ppermute | solution.py:21
  57.0 0.9 pad_maximum_fusion.5
  58.0 0.0 copy-done.2
  58.0 0.0 copy-done.3
  58.0 0.0 copy-done.4
  58.0 1.5 %collective-permute-start.7 = (bf16[2,256,640]{2,1,0:T(8,128)(2,1)}, bf16[2,256,640]{2,1,0:T(8,128)(2,1)S(1)}, u32[]{:S(2)}, u32[]{:S(2)}) collective-permute-start(bf16[2,256,640]{2,1,0:T(8,128)(2,1)} %pad_maximum_fusion.5), channel_id=1, source_target_pairs={{32,0},{33,1},{34,2},{35,3},{36,4},{37,5},{38,6},{39,7},{40,8},{41... | collective-permute-start | bytes 1966088 | tf_op jit(solution)/shard_map/ppermute | solution.py:21
  59.5 0.0 copy-done.10
  59.5 0.6 fusion.12
  64.9 21.2 %shard_map.149 = bf16[512,640]{1,0:T(8,128)(2,1)} custom-call(s32[1]{0:T(128)S(6)} %copy.21.live_ref, s32[1]{0:T(128)S(6)} %copy.22.depth_ref, bf16[512,640]{1,0:T(8,128)(2,1)} %get-tuple-element.12.q_ref, bf16[512,640]{1,0:T(8,128)(2,1)} %get-tuple-element.15.k_ref, bf16[512,640]{1,0:T(8,128)(2,1)} %get-tuple-element.16.v_ref, ...), custom_call_target="tpu_custom_call" | custom-call | tf_op jit(solution)/shard_map/pallas_call | solution.py:154
  86.1 0.0 copy-start.5
  86.1 0.9 collective-permute-start.4
  87.0 0.0 collective-permute-done.6
  87.0 0.1 broadcast.69.clone.1
  87.1 1.0 slice_dynamic-update-slice_fusion.3
  88.1 0.1 broadcast.69.clone
  88.2 1.0 slice_dynamic-update-slice_fusion.1
  89.2 0.0 collective-permute-done.7
  89.2 0.1 slice_dynamic-update-slice_fusion
  89.3 0.0 copy-start.6
  89.3 0.0 copy-start.7
  89.3 17.1 %collective-permute-done.4 = bf16[512,640]{1,0:T(8,128)(2,1)S(1)} collective-permute-done((bf16[512,640]{1,0:T(8,128)(2,1)}, bf16[512,640]{1,0:T(8,128)(2,1)S(1)}, u32[]{:S(2)}, u32[]{:S(2)}) %collective-permute-start.4) | collective-permute-done | bytes 655392 | tf_op jit(solution)/shard_map/ppermute | solution.py:21
  106.5 0.0 copy-done.5
  106.5 0.1 broadcast_select_fusion.3
  106.6 0.0 collective-permute-done.5
  106.6 2.1 %broadcast_select_fusion.1 = (bf16[640,1280]{1,0:T(8,128)(2,1)S(1)}, bf16[640,1280]{1,0:T(8,128)(2,1)S(1)}) fusion(bf16[640,1280]{1,0:T(8,128)(2,1)} %param.17, bf16[640,1280]{1,0:T(8,128)(2,1)} %collective-permute-done.5, pred[]{:T(512)S(6)} %eq.17), kind=kLoop, calls=%fused_computation.14 | loop fusion | flops 1638400 | bytes 6553601 | tf_op jit(solution)/shard_map/jit(_where)/select_n | solution.py:53
  108.8 0.0 copy-done.6
  108.8 0.0 copy-done.7
  108.8 0.0 copy-start.1
  108.8 0.0 copy-start.8
  108.8 2.0 %multiply_reduce_fusion.1 = (f32[512]{0:T(512)S(1)}, f32[512,1280]{1,0:T(8,128)S(1)}) fusion(bf16[640,1280]{1,0:T(8,128)(2,1)S(1)} %get-tuple-element.22, bf16[640,1280]{1,0:T(8,128)(2,1)S(1)} %get-tuple-element.21, bf16[512,640]{1,0:T(8,128)(2,1)S(1)} %get-tuple-element.24, bf16[512,640]{1,0:T(8,128)(2,1)S(1)} %get-tuple-element.23), kind=kOutput, calls=%fused_computation.12 | convolution fusion | flops 1688206848 | bytes 7211008 | tf_op jit(solution)/shard_map/dot_general | solution.py:224
  110.8 0.0 copy-done.1
  110.8 0.0 copy-done.8
  110.8 0.8 multiply_reduce_fusion
  111.6 1.8 %multiply_convert_fusion = bf16[512,1280]{1,0:T(8,128)(2,1)} fusion(f32[512]{0:T(512)S(1)} %add_rsqrt_fusion, f32[512,1280]{1,0:T(8,128)S(1)} %get-tuple-element.46, f32[512]{0:T(512)S(1)} %add_rsqrt_fusion.1, f32[1280]{0:T(1024)S(1)} %copy-done.8, f32[512]{0:T(512)S(1)} %add_rsqrt_fusion.2, bf16[512,1280]{1,0:T(8,128)(2,1)S(1)} %copy-done.1), kind=kLoop, calls=%fused_computation.10 | loop fusion | flops 5242880 | bytes 5254144 | tf_op jit(solution)/shard_map/convert_element_type | solution.py:230
  (3 shorter events, 0.0 us)
Async XLA Ops:
  11.7 12.4 %copy-start = (bf16[512,1280]{1,0:T(8,128)(2,1)S(1)}, bf16[512,1280]{1,0:T(8,128)(2,1)}, u32[]{:S(2)}) copy-start(bf16[512,1280]{1,0:T(8,128)(2,1)} %x_ref.1) | copy-start | bytes 3932164
  11.8 24.1 %collective-permute-start.3 = (bf16[2,256,640]{2,1,0:T(8,128)(2,1)S(1)}, bf16[2,256,640]{2,1,0:T(8,128)(2,1)S(1)}, u32[]{:S(2)}, u32[]{:S(2)}) collective-permute-start(bf16[2,256,640]{2,1,0:T(8,128)(2,1)S(1)} %pad_maximum_fusion.3), channel_id=1, source_target_pairs={{97,0},{98,1},{99,2},{100,3},{101,4},{102,5},{103,6},{104,7},{105,... | collective-permute-start | bytes 1966088 | tf_op jit(solution)/shard_map/ppermute | solution.py:21
  18.1 7.1 %copy-start.9 = (f32[640]{0:T(1024)S(1)}, f32[640]{0:T(1024)}, u32[]{:S(2)}) copy-start(f32[640]{0:T(1024)} %param.18) | copy-start | bytes 7684
  18.2 25.7 %collective-permute-start.2 = (bf16[2,256,640]{2,1,0:T(8,128)(2,1)S(1)}, bf16[2,256,640]{2,1,0:T(8,128)(2,1)S(1)}, u32[]{:S(2)}, u32[]{:S(2)}) collective-permute-start(bf16[2,256,640]{2,1,0:T(8,128)(2,1)S(1)} %pad_maximum_fusion.2), channel_id=1, source_target_pairs={{65,0},{66,1},{67,2},{68,3},{69,4},{70,5},{71,6},{72,7},{73,8},{74... | collective-permute-start | bytes 1966088 | tf_op jit(solution)/shard_map/ppermute | solution.py:21
  21.1 29.8 %collective-permute-start.1 = (bf16[2,256,640]{2,1,0:T(8,128)(2,1)}, bf16[2,256,640]{2,1,0:T(8,128)(2,1)S(1)}, u32[]{:S(2)}, u32[]{:S(2)}) collective-permute-start(bf16[2,256,640]{2,1,0:T(8,128)(2,1)} %pad_maximum_fusion.1), channel_id=1, source_target_pairs={{33,0},{34,1},{35,2},{36,3},{37,4},{38,5},{39,6},{40,7},{41,8},{42... | collective-permute-start | bytes 1966088 | tf_op jit(solution)/shard_map/ppermute | solution.py:21
  23.7 27.1 %collective-permute-start = (bf16[2,256,640]{2,1,0:T(8,128)(2,1)}, bf16[2,256,640]{2,1,0:T(8,128)(2,1)}, u32[]{:S(2)}, u32[]{:S(2)}) collective-permute-start(bf16[2,256,640]{2,1,0:T(8,128)(2,1)} %pad_maximum_fusion), channel_id=1, source_target_pairs={{1,0},{2,1},{3,2},{4,3},{5,4},{6,5},{7,6},{8,7},{9,8},{10,9},{11,1... | collective-permute-start | bytes 1966088 | tf_op jit(solution)/shard_map/ppermute | solution.py:21
  35.9 22.1 %copy-start.2 = (bf16[2,256,640]{2,1,0:T(8,128)(2,1)}, bf16[2,256,640]{2,1,0:T(8,128)(2,1)S(1)}, u32[]{:S(2)}) copy-start(bf16[2,256,640]{2,1,0:T(8,128)(2,1)S(1)} %collective-permute-done.3.refs_3_.refs_7_) | copy-start | bytes 1966084
  43.9 14.1 %copy-start.3 = (bf16[2,256,640]{2,1,0:T(8,128)(2,1)}, bf16[2,256,640]{2,1,0:T(8,128)(2,1)S(1)}, u32[]{:S(2)}) copy-start(bf16[2,256,640]{2,1,0:T(8,128)(2,1)S(1)} %collective-permute-done.2.refs_2_.refs_6_) | copy-start | bytes 1966084
  50.8 7.1 %copy-start.4 = (bf16[2,256,640]{2,1,0:T(8,128)(2,1)}, bf16[2,256,640]{2,1,0:T(8,128)(2,1)S(1)}, u32[]{:S(2)}) copy-start(bf16[2,256,640]{2,1,0:T(8,128)(2,1)S(1)} %collective-permute-done.1.refs_1_.refs_5_) | copy-start | bytes 1966084
  50.9 8.6 %copy-start.10 = (s32[256]{0:T(256)S(1)}, s32[256]{0:T(256)}, u32[]{:S(2)}) copy-start(s32[256]{0:T(256)} %param.25) | copy-start | bytes 3076
  53.5 33.6 %collective-permute-start.6 = (bf16[2,256,640]{2,1,0:T(8,128)(2,1)S(1)}, bf16[2,256,640]{2,1,0:T(8,128)(2,1)}, u32[]{:S(2)}, u32[]{:S(2)}) collective-permute-start(bf16[2,256,640]{2,1,0:T(8,128)(2,1)S(1)} %pad_maximum_fusion.4), channel_id=1, source_target_pairs={{96,0},{97,1},{98,2},{99,3},{100,4},{101,5},{102,6},{103,7},{104,8... | collective-permute-start | bytes 1966088 | tf_op jit(solution)/shard_map/ppermute | solution.py:21
  54.1 52.5 %collective-permute-start.5 = (bf16[640,1280]{1,0:T(8,128)(2,1)}, bf16[640,1280]{1,0:T(8,128)(2,1)}, u32[]{:S(2)}, u32[]{:S(2)}) collective-permute-start(bf16[640,1280]{1,0:T(8,128)(2,1)} %param.17), channel_id=1, source_target_pairs={{128,0},{0,128},{129,1},{1,129},{130,2},{2,130},{131,3},{3,131},{1... | collective-permute-start | bytes 4915208 | tf_op jit(solution)/shard_map/ppermute | solution.py:21
  58.0 31.2 %collective-permute-start.7 = (bf16[2,256,640]{2,1,0:T(8,128)(2,1)}, bf16[2,256,640]{2,1,0:T(8,128)(2,1)S(1)}, u32[]{:S(2)}, u32[]{:S(2)}) collective-permute-start(bf16[2,256,640]{2,1,0:T(8,128)(2,1)} %pad_maximum_fusion.5), channel_id=1, source_target_pairs={{32,0},{33,1},{34,2},{35,3},{36,4},{37,5},{38,6},{39,7},{40,8},{41... | collective-permute-start | bytes 1966088 | tf_op jit(solution)/shard_map/ppermute | solution.py:21
  86.1 20.4 %copy-start.5 = (bf16[512,640]{1,0:T(8,128)(2,1)S(1)}, bf16[512,640]{1,0:T(8,128)(2,1)}, u32[]{:S(2)}) copy-start(bf16[512,640]{1,0:T(8,128)(2,1)} %shard_map.149) | copy-start | bytes 1966084
  86.1 20.4 %collective-permute-start.4 = (bf16[512,640]{1,0:T(8,128)(2,1)}, bf16[512,640]{1,0:T(8,128)(2,1)S(1)}, u32[]{:S(2)}, u32[]{:S(2)}) collective-permute-start(bf16[512,640]{1,0:T(8,128)(2,1)} %shard_map.149), channel_id=1, source_target_pairs={{128,0},{0,128},{129,1},{1,129},{130,2},{2,130},{131,3},{3,131},{1... | collective-permute-start | bytes 1966088 | tf_op jit(solution)/shard_map/ppermute | solution.py:21
  89.3 19.5 %copy-start.6 = (bf16[2,256,640]{2,1,0:T(8,128)(2,1)}, bf16[2,256,640]{2,1,0:T(8,128)(2,1)S(1)}, u32[]{:S(2)}) copy-start(bf16[2,256,640]{2,1,0:T(8,128)(2,1)S(1)} %get-tuple-element.33) | copy-start | bytes 1966084
  89.3 19.5 %copy-start.7 = (bf16[2,256,640]{2,1,0:T(8,128)(2,1)}, bf16[2,256,640]{2,1,0:T(8,128)(2,1)S(1)}, u32[]{:S(2)}) copy-start(bf16[2,256,640]{2,1,0:T(8,128)(2,1)S(1)} %get-tuple-element.34) | copy-start | bytes 1966084
  108.8 2.0 %copy-start.1 = (bf16[512,1280]{1,0:T(8,128)(2,1)S(1)}, bf16[512,1280]{1,0:T(8,128)(2,1)}, u32[]{:S(2)}) copy-start(bf16[512,1280]{1,0:T(8,128)(2,1)} %x_ref.1) | copy-start | bytes 3932164
  108.8 2.0 %copy-start.8 = (f32[1280]{0:T(1024)S(1)}, f32[1280]{0:T(1024)}, u32[]{:S(2)}) copy-start(f32[1280]{0:T(1024)} %param.19) | copy-start | bytes 15364

commit v7 on v6

--- a/solution.py
+++ b/solution.py
@@ -218,7 +218,6 @@
     fetched = [
         fetch_page(pool_keys, pool_values, prefix_pages, slot_index) for slot_index in range(PMAX)
     ]
-    key_rows, value_rows, fetched = lax.optimization_barrier((key_rows, value_rows, fetched))
     attended = attention(queries, key_rows, value_rows, fetched, req_len, prefix_len)
     other_attended = from_behind(attended, "kv", 1)
     branch = jnp.dot(

time: 114 us -> 109 us (0.956)
  the two profiles are of different devices: /device:TPU:6 before, /device:TPU:225 now
where the time goes in v7:
time: 109 us; the launch traced here: 108 us
  Pallas kernels  30.3 us (28%)
  waiting for transfers between devices  28.1 us (26%)
  between operations  14 us (13%)
  starting transfers between devices  13.3 us (12%)
  local copies, waits for them, and re-layouts  11.2 us (10%)
  other arithmetic  9.04 us (8%)
  matrix products  1.97 us (2%)
    ppermute x8, waiting for transfers between devices, from_behind(): return lax.ppermute(block, axis, route)  28.1 us
    pallas_call x1, Pallas kernels, attention(): pl.pallas_call(attention_kernel, out_shape=jax.ShapeDtypeStruct((tokens,...  21.2 us
    ppermute x8, starting transfers between devices, from_behind(): return lax.ppermute(block, axis, route)  13.3 us
    pallas_call x1, Pallas kernels, projections(): pl.pallas_call(projection_kernel, out_shape=(shape, shape, shape), grid=(...  9.09 us
    select_n x2, other arithmetic, in_kv_order(): low = jnp.where(first, mine, other)  2.27 us
    dynamic_update_slice x2, local copies, waits for them, and re-layouts, relay(): lax.dynamic_update_index_in_dim(value_out, received[1], target, 0)  2.19 us
  transfers between devices with their start and end apart: 8, of which 2 were waited for; matrix products, arithmetic and copies ran while one was open for 10% of the time, Pallas kernels for 28%

profile of v7, /device:TPU:225, one launch (start us, length us, event | category | flops | bytes accessed | tf_op | source)
XLA Modules:
  0.0 107.9 jit_solution(12261309434890973957)
XLA Ops:
  0.7 1.5 %constant_dynamic-slice_fusion.11 = (s32[1,1]{0,1:T(1,128)}, s32[1,1]{0,1:T(1,128)}, s32[1,1]{0,1:T(1,128)}, s32[1,1]{0,1:T(1,128)}) fusion(s32[128,4]{0,1:T(4,128)} %param.24, s32[]{:T(128)S(6)} %select_n.133, s32[]{:T(128)S(6)} %select_n.125, s32[]{:T(128)S(6)} %select_n.121, s32[]{:T(128)S(6)} %select_n.129), kind=kLoop, calls=%fused_computation.48 | loop fusion | bytes 48 | tf_op jit(solution)/shard_map/dynamic_slice | solution.py:166
  10.2 1.9 %constant_dynamic-slice_fusion = (bf16[1,256,640]{2,1,0:T(8,128)(2,1)S(1)}, bf16[1,256,640]{2,1,0:T(8,128)(2,1)S(1)}, bf16[1,256,640]{2,1,0:T(8,128)(2,1)S(1)}, ...) fusion(bf16[4,256,640]{2,1,0:T(8,128)(2,1)} %param.21, ...), kind=kLoop, calls=%fused_computation.34 | loop fusion | bytes 5242896 | tf_op jit(solution)/shard_map/jit(dynamic_index_in_dim)/dynamic_slice | solution.py:168
  12.1 0.0 copy-start
  12.1 0.9 pad_maximum_fusion.3
  13.0 1.8 %collective-permute-start.3 = (bf16[2,256,640]{2,1,0:T(8,128)(2,1)}, bf16[2,256,640]{2,1,0:T(8,128)(2,1)S(1)}, u32[]{:S(2)}, u32[]{:S(2)}) collective-permute-start(bf16[2,256,640]{2,1,0:T(8,128)(2,1)} %pad_maximum_fusion.3), channel_id=1, source_target_pairs={{97,0},{98,1},{99,2},{100,3},{101,4},{102,5},{103,6},{104,7},{105,... | collective-permute-start | bytes 1966088 | tf_op jit(solution)/shard_map/ppermute | solution.py:21
  14.8 0.0 copy-start.9
  14.8 0.9 pad_maximum_fusion.2
  15.8 2.6 %collective-permute-start.2 = (bf16[2,256,640]{2,1,0:T(8,128)(2,1)}, bf16[2,256,640]{2,1,0:T(8,128)(2,1)S(1)}, u32[]{:S(2)}, u32[]{:S(2)}) collective-permute-start(bf16[2,256,640]{2,1,0:T(8,128)(2,1)} %pad_maximum_fusion.2), channel_id=1, source_target_pairs={{65,0},{66,1},{67,2},{68,3},{69,4},{70,5},{71,6},{72,7},{73,8},{74... | collective-permute-start | bytes 1966088 | tf_op jit(solution)/shard_map/ppermute | solution.py:21
  18.3 0.1 pad_maximum_fusion.1
  18.4 1.8 %collective-permute-start.1 = (bf16[2,256,640]{2,1,0:T(8,128)(2,1)S(1)}, bf16[2,256,640]{2,1,0:T(8,128)(2,1)S(1)}, u32[]{:S(2)}, u32[]{:S(2)}) collective-permute-start(bf16[2,256,640]{2,1,0:T(8,128)(2,1)S(1)} %pad_maximum_fusion.1), channel_id=1, source_target_pairs={{33,0},{34,1},{35,2},{36,3},{37,4},{38,5},{39,6},{40,7},{41,8},{42... | collective-permute-start | bytes 1966088 | tf_op jit(solution)/shard_map/ppermute | solution.py:21
  20.2 0.1 pad_maximum_fusion
  20.3 0.4 collective-permute-start
  20.7 0.0 copy-done
  20.7 0.3 fusion.7
  21.0 0.9 copy.16.scale_ref
  21.9 0.0 copy-done.9
  21.9 0.6 reshape.53.gain_ref
  22.5 9.1 %shard_map.148 = (bf16[512,640]{1,0:T(8,128)(2,1)}, bf16[512,640]{1,0:T(8,128)(2,1)}, bf16[512,640]{1,0:T(8,128)(2,1)}) custom-call(bf16[512,1280]{1,0:T(8,128)(2,1)} %x_ref.1, f32[512,1]{1,0:T(8,128)} %copy.16.scale_ref, bf16[1280,640]{1,0:T(8,128)(2,1)} %wq_ref.1, bf16[1280,640]{1,0:T(8,128)(2,1)} %wk_ref.1, bf16[1280,640]{1,0:T(8,128)(2,1)} %wv_ref.1, ...), custom_call_target="tpu_custom_call" | custom-call | tf_op jit(solution)/shard_map/pallas_call | solution.py:84
  31.6 0.0 copy-start.10
  31.6 1.4 %slice_bitcast_fusion = (bf16[1,256,640]{2,1,0:T(8,128)(2,1)S(1)}, bf16[1,256,640]{2,1,0:T(8,128)(2,1)S(1)}, bf16[1,256,640]{2,1,0:T(8,128)(2,1)S(1)}, bf16[1,256,640]{2,1,0:T(8,128)(2,1)S(1)}) fusion(bf16[512,640]{1,0:T(8,128)(2,1)} %get-tuple-element.8.v_ref, bf16[512,640]{1,0:T(8,128)(2,1)} %get-tuple-element.7.k_ref), kind=kLoop, calls=%fused_computation.30 | loop fusion | bytes 2621440 | tf_op jit(solution)/shard_map/slice | solution.py:184
  33.0 0.9 pad_maximum_fusion.4
  33.9 0.4 collective-permute-start.6
  34.3 0.0 collective-permute-done.3.refs_3_.refs_7_
  34.3 0.0 copy-start.2
  34.3 2.9 %collective-permute-start.5 = (bf16[640,1280]{1,0:T(8,128)(2,1)}, bf16[640,1280]{1,0:T(8,128)(2,1)}, u32[]{:S(2)}, u32[]{:S(2)}) collective-permute-start(bf16[640,1280]{1,0:T(8,128)(2,1)} %param.17), channel_id=1, source_target_pairs={{128,0},{0,128},{129,1},{1,129},{130,2},{2,130},{131,3},{3,131},{1... | collective-permute-start | bytes 4915208 | tf_op jit(solution)/shard_map/ppermute | solution.py:21
  37.2 0.9 pad_maximum_fusion.5
  38.1 10.5 %collective-permute-done.2.refs_2_.refs_6_ = bf16[2,256,640]{2,1,0:T(8,128)(2,1)S(1)} collective-permute-done((bf16[2,256,640]{2,1,0:T(8,128)(2,1)}, bf16[2,256,640]{2,1,0:T(8,128)(2,1)S(1)}, u32[]{:S(2)}, u32[]{:S(2)}) %collective-permute-start.2) | collective-permute-done | bytes 655392 | tf_op jit(solution)/shard_map/ppermute | solution.py:21
  48.6 0.0 copy-start.3
  48.6 0.0 collective-permute-start.7
  48.6 0.0 copy-done.10
  48.6 0.7 fusion.12
  54.4 0.0 collective-permute-done.1.refs_1_.refs_5_
  54.4 0.0 copy-start.4
  54.4 0.0 collective-permute-done.refs_0_.refs_4_
  54.5 0.0 copy-done.2
  54.5 0.0 copy-done.3
  54.5 0.8 copy-done.4
  55.3 21.2 %shard_map.149 = bf16[512,640]{1,0:T(8,128)(2,1)} custom-call(s32[1]{0:T(128)S(6)} %copy.21.live_ref, s32[1]{0:T(128)S(6)} %copy.22.depth_ref, bf16[512,640]{1,0:T(8,128)(2,1)} %get-tuple-element.6.q_ref, bf16[512,640]{1,0:T(8,128)(2,1)} %get-tuple-element.7.k_ref, bf16[512,640]{1,0:T(8,128)(2,1)} %get-tuple-element.8.v_ref, ...), custom_call_target="tpu_custom_call" | custom-call | tf_op jit(solution)/shard_map/pallas_call | solution.py:154
  76.5 0.0 copy-start.5
  76.5 3.4 %collective-permute-start.4 = (bf16[512,640]{1,0:T(8,128)(2,1)}, bf16[512,640]{1,0:T(8,128)(2,1)S(1)}, u32[]{:S(2)}, u32[]{:S(2)}) collective-permute-start(bf16[512,640]{1,0:T(8,128)(2,1)} %shard_map.149), channel_id=1, source_target_pairs={{128,0},{0,128},{129,1},{1,129},{130,2},{2,130},{131,3},{3,131},{1... | collective-permute-start | bytes 1966088 | tf_op jit(solution)/shard_map/ppermute | solution.py:21
  79.9 0.0 collective-permute-done.6
  79.9 0.1 broadcast.69.clone.1
  80.0 1.0 slice_dynamic-update-slice_fusion.3
  81.0 0.1 broadcast.69.clone
  81.1 1.0 slice_dynamic-update-slice_fusion.1
  82.1 0.0 collective-permute-done.7
  82.1 1.2 %slice_dynamic-update-slice_fusion = (bf16[2,256,640]{2,1,0:T(8,128)(2,1)S(1)}, bf16[2,256,640]{2,1,0:T(8,128)(2,1)S(1)}) fusion(bf16[2,256,640]{2,1,0:T(8,128)(2,1)S(1)} %slice_dynamic-update-slice_fusion.1, s32[]{:T(128)S(6)} %select_n.148, bf16[2,256,640]{2,1,0:T(8,128)(2,1)} %collective-permute-done.7, ...), kind=kLoop, calls=%fused_computation.26 | loop fusion | bytes 1310724 | tf_op jit(solution)/shard_map/jit(dynamic_update_index_in_dim)/dynamic_update_slice | solution.py:189
  83.3 0.0 copy-start.6
  83.3 0.0 copy-start.7
  83.3 17.7 %collective-permute-done.4 = bf16[512,640]{1,0:T(8,128)(2,1)S(1)} collective-permute-done((bf16[512,640]{1,0:T(8,128)(2,1)}, bf16[512,640]{1,0:T(8,128)(2,1)S(1)}, u32[]{:S(2)}, u32[]{:S(2)}) %collective-permute-start.4) | collective-permute-done | bytes 655392 | tf_op jit(solution)/shard_map/ppermute | solution.py:21
  101.0 0.0 copy-done.5
  101.0 0.1 broadcast_select_fusion.3
  101.1 0.0 collective-permute-done.5
  101.1 2.1 %broadcast_select_fusion.1 = (bf16[640,1280]{1,0:T(8,128)(2,1)S(1)}, bf16[640,1280]{1,0:T(8,128)(2,1)S(1)}) fusion(bf16[640,1280]{1,0:T(8,128)(2,1)} %param.17, bf16[640,1280]{1,0:T(8,128)(2,1)} %collective-permute-done.5, pred[]{:T(512)S(6)} %eq.17), kind=kLoop, calls=%fused_computation.14 | loop fusion | flops 1638400 | bytes 6553601 | tf_op jit(solution)/shard_map/jit(_where)/select_n | solution.py:53
  103.3 0.0 copy-done.6
  103.3 0.0 copy-done.7
  103.3 0.0 copy-start.1
  103.3 0.0 copy-start.8
  103.3 2.0 %multiply_reduce_fusion.1 = (f32[512]{0:T(512)S(1)}, f32[512,1280]{1,0:T(8,128)S(1)}) fusion(bf16[640,1280]{1,0:T(8,128)(2,1)S(1)} %get-tuple-element.10, bf16[640,1280]{1,0:T(8,128)(2,1)S(1)} %get-tuple-element.9, bf16[512,640]{1,0:T(8,128)(2,1)S(1)} %get-tuple-element.12, bf16[512,640]{1,0:T(8,128)(2,1)S(1)} %get-tuple-element.11), kind=kOutput, calls=%fused_computation.12 | convolution fusion | flops 1688206848 | bytes 7211008 | tf_op jit(solution)/shard_map/dot_general | solution.py:223
  105.3 0.0 copy-done.1
  105.3 0.0 copy-done.8
  105.3 0.8 multiply_reduce_fusion
  106.1 1.8 %multiply_convert_fusion = bf16[512,1280]{1,0:T(8,128)(2,1)} fusion(f32[512]{0:T(512)S(1)} %add_rsqrt_fusion, f32[512,1280]{1,0:T(8,128)S(1)} %get-tuple-element.34, f32[512]{0:T(512)S(1)} %add_rsqrt_fusion.1, f32[1280]{0:T(1024)S(1)} %copy-done.8, f32[512]{0:T(512)S(1)} %add_rsqrt_fusion.2, bf16[512,1280]{1,0:T(8,128)(2,1)S(1)} %copy-done.1), kind=kLoop, calls=%fused_computation.10 | loop fusion | flops 5242880 | bytes 5254144 | tf_op jit(solution)/shard_map/convert_element_type | solution.py:229
  (3 shorter events, 0.0 us)
Async XLA Ops:
  12.1 8.6 %copy-start = (bf16[512,1280]{1,0:T(8,128)(2,1)S(1)}, bf16[512,1280]{1,0:T(8,128)(2,1)}, u32[]{:S(2)}) copy-start(bf16[512,1280]{1,0:T(8,128)(2,1)} %x_ref.1) | copy-start | bytes 3932164
  13.0 21.3 %collective-permute-start.3 = (bf16[2,256,640]{2,1,0:T(8,128)(2,1)}, bf16[2,256,640]{2,1,0:T(8,128)(2,1)S(1)}, u32[]{:S(2)}, u32[]{:S(2)}) collective-permute-start(bf16[2,256,640]{2,1,0:T(8,128)(2,1)} %pad_maximum_fusion.3), channel_id=1, source_target_pairs={{97,0},{98,1},{99,2},{100,3},{101,4},{102,5},{103,6},{104,7},{105,... | collective-permute-start | bytes 1966088 | tf_op jit(solution)/shard_map/ppermute | solution.py:21
  14.8 7.0 %copy-start.9 = (f32[640]{0:T(1024)S(1)}, f32[640]{0:T(1024)}, u32[]{:S(2)}) copy-start(f32[640]{0:T(1024)} %param.18) | copy-start | bytes 7684
  15.8 32.8 %collective-permute-start.2 = (bf16[2,256,640]{2,1,0:T(8,128)(2,1)}, bf16[2,256,640]{2,1,0:T(8,128)(2,1)S(1)}, u32[]{:S(2)}, u32[]{:S(2)}) collective-permute-start(bf16[2,256,640]{2,1,0:T(8,128)(2,1)} %pad_maximum_fusion.2), channel_id=1, source_target_pairs={{65,0},{66,1},{67,2},{68,3},{69,4},{70,5},{71,6},{72,7},{73,8},{74... | collective-permute-start | bytes 1966088 | tf_op jit(solution)/shard_map/ppermute | solution.py:21
  18.4 36.0 %collective-permute-start.1 = (bf16[2,256,640]{2,1,0:T(8,128)(2,1)S(1)}, bf16[2,256,640]{2,1,0:T(8,128)(2,1)S(1)}, u32[]{:S(2)}, u32[]{:S(2)}) collective-permute-start(bf16[2,256,640]{2,1,0:T(8,128)(2,1)S(1)} %pad_maximum_fusion.1), channel_id=1, source_target_pairs={{33,0},{34,1},{35,2},{36,3},{37,4},{38,5},{39,6},{40,7},{41,8},{42... | collective-permute-start | bytes 1966088 | tf_op jit(solution)/shard_map/ppermute | solution.py:21
  20.3 34.2 %collective-permute-start = (bf16[2,256,640]{2,1,0:T(8,128)(2,1)S(1)}, bf16[2,256,640]{2,1,0:T(8,128)(2,1)}, u32[]{:S(2)}, u32[]{:S(2)}) collective-permute-start(bf16[2,256,640]{2,1,0:T(8,128)(2,1)S(1)} %pad_maximum_fusion), channel_id=1, source_target_pairs={{1,0},{2,1},{3,2},{4,3},{5,4},{6,5},{7,6},{8,7},{9,8},{10,9},{11,1... | collective-permute-start | bytes 1966088 | tf_op jit(solution)/shard_map/ppermute | solution.py:21
  31.6 17.0 %copy-start.10 = (s32[256]{0:T(256)S(1)}, s32[256]{0:T(256)}, u32[]{:S(2)}) copy-start(s32[256]{0:T(256)} %param.25) | copy-start | bytes 3076
  33.9 46.1 %collective-permute-start.6 = (bf16[2,256,640]{2,1,0:T(8,128)(2,1)}, bf16[2,256,640]{2,1,0:T(8,128)(2,1)}, u32[]{:S(2)}, u32[]{:S(2)}) collective-permute-start(bf16[2,256,640]{2,1,0:T(8,128)(2,1)} %pad_maximum_fusion.4), channel_id=1, source_target_pairs={{96,0},{97,1},{98,2},{99,3},{100,4},{101,5},{102,6},{103,7},{104,8... | collective-permute-start | bytes 1966088 | tf_op jit(solution)/shard_map/ppermute | solution.py:21
  34.3 20.2 %copy-start.2 = (bf16[2,256,640]{2,1,0:T(8,128)(2,1)}, bf16[2,256,640]{2,1,0:T(8,128)(2,1)S(1)}, u32[]{:S(2)}) copy-start(bf16[2,256,640]{2,1,0:T(8,128)(2,1)S(1)} %collective-permute-done.3.refs_3_.refs_7_) | copy-start | bytes 1966084
  34.3 66.8 %collective-permute-start.5 = (bf16[640,1280]{1,0:T(8,128)(2,1)}, bf16[640,1280]{1,0:T(8,128)(2,1)}, u32[]{:S(2)}, u32[]{:S(2)}) collective-permute-start(bf16[640,1280]{1,0:T(8,128)(2,1)} %param.17), channel_id=1, source_target_pairs={{128,0},{0,128},{129,1},{1,129},{130,2},{2,130},{131,3},{3,131},{1... | collective-permute-start | bytes 4915208 | tf_op jit(solution)/shard_map/ppermute | solution.py:21
  48.6 5.9 %copy-start.3 = (bf16[2,256,640]{2,1,0:T(8,128)(2,1)}, bf16[2,256,640]{2,1,0:T(8,128)(2,1)S(1)}, u32[]{:S(2)}) copy-start(bf16[2,256,640]{2,1,0:T(8,128)(2,1)S(1)} %collective-permute-done.2.refs_2_.refs_6_) | copy-start | bytes 1966084
  48.6 33.5 %collective-permute-start.7 = (bf16[2,256,640]{2,1,0:T(8,128)(2,1)}, bf16[2,256,640]{2,1,0:T(8,128)(2,1)}, u32[]{:S(2)}, u32[]{:S(2)}) collective-permute-start(bf16[2,256,640]{2,1,0:T(8,128)(2,1)} %pad_maximum_fusion.5), channel_id=1, source_target_pairs={{32,0},{33,1},{34,2},{35,3},{36,4},{37,5},{38,6},{39,7},{40,8},{41... | collective-permute-start | bytes 1966088 | tf_op jit(solution)/shard_map/ppermute | solution.py:21
  54.4 0.8 copy-start.4
  76.5 24.5 %copy-start.5 = (bf16[512,640]{1,0:T(8,128)(2,1)S(1)}, bf16[512,640]{1,0:T(8,128)(2,1)}, u32[]{:S(2)}) copy-start(bf16[512,640]{1,0:T(8,128)(2,1)} %shard_map.149) | copy-start | bytes 1966084
  76.5 24.5 %collective-permute-start.4 = (bf16[512,640]{1,0:T(8,128)(2,1)}, bf16[512,640]{1,0:T(8,128)(2,1)S(1)}, u32[]{:S(2)}, u32[]{:S(2)}) collective-permute-start(bf16[512,640]{1,0:T(8,128)(2,1)} %shard_map.149), channel_id=1, source_target_pairs={{128,0},{0,128},{129,1},{1,129},{130,2},{2,130},{131,3},{3,131},{1... | collective-permute-start | bytes 1966088 | tf_op jit(solution)/shard_map/ppermute | solution.py:21
  83.3 20.0 %copy-start.6 = (bf16[2,256,640]{2,1,0:T(8,128)(2,1)}, bf16[2,256,640]{2,1,0:T(8,128)(2,1)S(1)}, u32[]{:S(2)}) copy-start(bf16[2,256,640]{2,1,0:T(8,128)(2,1)S(1)} %get-tuple-element.21) | copy-start | bytes 1966084
  83.3 20.0 %copy-start.7 = (bf16[2,256,640]{2,1,0:T(8,128)(2,1)}, bf16[2,256,640]{2,1,0:T(8,128)(2,1)S(1)}, u32[]{:S(2)}) copy-start(bf16[2,256,640]{2,1,0:T(8,128)(2,1)S(1)} %get-tuple-element.22) | copy-start | bytes 1966084
  103.3 2.0 %copy-start.1 = (bf16[512,1280]{1,0:T(8,128)(2,1)S(1)}, bf16[512,1280]{1,0:T(8,128)(2,1)}, u32[]{:S(2)}) copy-start(bf16[512,1280]{1,0:T(8,128)(2,1)} %x_ref.1) | copy-start | bytes 3932164
  103.3 2.0 %copy-start.8 = (f32[1280]{0:T(1024)S(1)}, f32[1280]{0:T(1024)}, u32[]{:S(2)}) copy-start(f32[1280]{0:T(1024)} %param.19) | copy-start | bytes 15364

commit v8 on v7

--- a/solution.py
+++ b/solution.py
@@ -1,3 +1,4 @@
+import functools
 import math
 
 import jax
@@ -158,15 +159,44 @@
     )(req_len, prefix_len, queries, key_rows, value_rows, *pages, *pages)
 
 
-def fetch_page(pool_keys, pool_values, prefix_pages, slot_index):
+def gather_kernel(devices, pages_ref, keys_hbm, values_hbm, *refs):
+    outs, sems = refs[:PMAX], refs[PMAX]
+    here = lax.axis_index("blk")
+    count = keys_hbm.shape[0]
+    copies = []
+    for slot_index in range(PMAX):
+        offset = slot_index * devices // PMAX + 1
+        asker = lax.rem(here + (devices - offset), devices)
+        local = lax.rem(pages_ref[asker, slot_index], count)
+        for part, source in enumerate((keys_hbm, values_hbm)):
+            copy = pltpu.make_async_copy(
+                source.at[local], outs[slot_index].at[part], sems.at[2 * slot_index + part]
+            )
+            copy.start()
+            copies.append(copy)
+    for copy in copies:
+        copy.wait()
+
+
+def fetch_pages(pool_keys, pool_values, prefix_pages):
     devices = lax.axis_size("blk")
-    here = lax.axis_index("blk")
-    offset = slot_index * devices // PMAX + 1
-    asker = (here - offset) % devices
-    local = prefix_pages[asker, slot_index] % pool_keys.shape[0]
-    send_keys = lax.dynamic_index_in_dim(pool_keys, local, 0, keepdims=False)
-    send_values = lax.dynamic_index_in_dim(pool_values, local, 0, keepdims=False)
-    return from_behind(jnp.stack([send_keys, send_values]), "blk", devices - offset)
+    page_shape = jax.ShapeDtypeStruct((2,) + pool_keys.shape[1:], pool_keys.dtype)
+    grid_spec = pltpu.PrefetchScalarGridSpec(
+        num_scalar_prefetch=1,
+        grid=(),
+        in_specs=[pl.BlockSpec(memory_space=pl.ANY)] * 2,
+        out_specs=[pl.BlockSpec(memory_space=pltpu.VMEM)] * PMAX,
+        scratch_shapes=[pltpu.SemaphoreType.DMA((2 * PMAX,))],
+    )
+    gathered = pl.pallas_call(
+        functools.partial(gather_kernel, devices),
+        out_shape=[page_shape] * PMAX,
+        grid_spec=grid_spec,
+    )(prefix_pages, pool_keys, pool_values)
+    return [
+        from_behind(gathered[slot_index], "blk", devices - (slot_index * devices // PMAX + 1))
+        for slot_index in range(PMAX)
+    ]
 
 
 def relay(key_rows, value_rows, placement):
@@ -215,9 +245,7 @@
     queries, key_rows, value_rows = projections(
         hidden_in, row_scale, w_query, w_key, w_value, head_gain
     )
-    fetched = [
-        fetch_page(pool_keys, pool_values, prefix_pages, slot_index) for slot_index in range(PMAX)
-    ]
+    fetched = fetch_pages(pool_keys, pool_values, prefix_pages)
     attended = attention(queries, key_rows, value_rows, fetched, req_len, prefix_len)
     other_attended = from_behind(attended, "kv", 1)
     branch = jnp.dot(

time: 109 us -> 103 us (0.945)
  between operations: 14 us -> 5.73 us
  Pallas kernels: 30.3 us -> 35.3 us
  waiting for transfers between devices: 28.1 us -> 31.8 us
  other arithmetic: 9.04 us -> 5.41 us
  local copies, waits for them, and re-layouts: 11.2 us -> 8.43 us
    pallas_call x0 -> x1, Pallas kernels: none -> 5.02 us  [fetch_pages(): pl.pallas_call(functools.partial(gather_kernel, devices), out_shape=[page...]
    ppermute x8, waiting for transfers between devices: 28.1 us -> 31.8 us  [from_behind(): return lax.ppermute(block, axis, route)]
    dynamic_slice x2 -> x0, local copies, waits for them, and re-layouts: 3.44 us -> none  [the longest x1 1.93 us: fetch_page(): lax.dynamic_index_in_dim(pool_values, local, 0, keepdims=False)]
    another operation x4 -> x0, other arithmetic: 1.98 us -> none  [fetch_page(): jnp.stack([send_keys, send_values])]
    another operation x2, other arithmetic: 1.82 us -> 0.15 us  [relay(): jnp.stack([key_pages[block_index], value_pages[block_index]])]
  transfers between devices with their start and end apart: 8 -> 8, of which waited for: 2 -> 3; matrix products, arithmetic and copies ran while one was open for 10% -> 7% of each run, Pallas kernels for 28% -> 30%
where the time goes in v8:
time: 103 us; the launch traced here: 102 us
  Pallas kernels  35.3 us (34%)
  waiting for transfers between devices  31.8 us (31%)
  starting transfers between devices  13.4 us (13%)
  local copies, waits for them, and re-layouts  8.43 us (8%)
  between operations  5.73 us (6%)
  other arithmetic  5.41 us (5%)
  matrix products  1.97 us (2%)
    ppermute x8, waiting for transfers between devices, from_behind(): return lax.ppermute(block, axis, route)  31.8 us
    pallas_call x1, Pallas kernels, attention(): pl.pallas_call(attention_kernel, out_shape=jax.ShapeDtypeStruct((tokens,...  21.2 us
    ppermute x8, starting transfers between devices, from_behind(): return lax.ppermute(block, axis, route)  13.4 us
    pallas_call x1, Pallas kernels, projections(): pl.pallas_call(projection_kernel, out_shape=(shape, shape, shape), grid=(...  9.09 us
    pallas_call x1, Pallas kernels, fetch_pages(): pl.pallas_call(functools.partial(gather_kernel, devices), out_shape=[page...  5.02 us
    select_n x2, other arithmetic, in_kv_order(): low = jnp.where(first, mine, other)  2.27 us
    dynamic_update_slice x2, local copies, waits for them, and re-layouts, relay(): lax.dynamic_update_index_in_dim(value_out, received[1], target, 0)  2.19 us
  transfers between devices with their start and end apart: 8, of which 3 were waited for; matrix products, arithmetic and copies ran while one was open for 7% of the time, Pallas kernels for 30%

profile of v8, /device:TPU:225, one launch (start us, length us, event | category | flops | bytes accessed | tf_op | source)
XLA Modules:
  0.0 102.1 jit_solution(4512544332645338856)
XLA Ops:
  0.6 0.0 copy-start
  0.6 0.0 copy-start.9
  0.7 1.5 %copy.18.pages_ref = s32[128,4]{1,0:T(8,128)} copy(s32[128,4]{0,1:T(4,128)} %param.24) | data formatting | bytes 4096 | tf_op args[11]
  2.2 5.0 %shard_map.149 = (bf16[2,256,640]{2,1,0:T(8,128)(2,1)}, bf16[2,256,640]{2,1,0:T(8,128)(2,1)}, bf16[2,256,640]{2,1,0:T(8,128)(2,1)}, bf16[2,256,640]{2,1,0:T(8,128)(2,1)}) custom-call(s32[128,4]{1,0:T(8,128)} %copy.18.pages_ref, bf16[4,256,640]{2,1,0:T(8,128)(2,1)} %keys_hbm.1, bf16[4,256,640]{2,1,0:T(8,128)(2,1)} %values_hbm.1), custom_call_target="tpu_custom_call" | custom-call | tf_op jit(solution)/shard_map/pallas_call | solution.py:191
  7.2 0.7 collective-permute-start
  7.9 2.8 %collective-permute-start.1 = (bf16[2,256,640]{2,1,0:T(8,128)(2,1)}, bf16[2,256,640]{2,1,0:T(8,128)(2,1)S(1)}, u32[]{:S(2)}, u32[]{:S(2)}) collective-permute-start(bf16[2,256,640]{2,1,0:T(8,128)(2,1)} %get-tuple-element.14), channel_id=1, source_target_pairs={{33,0},{34,1},{35,2},{36,3},{37,4},{38,5},{39,6},{40,7},{41,8},{42... | collective-permute-start | bytes 1966088 | tf_op jit(solution)/shard_map/ppermute | solution.py:22
  10.8 0.9 collective-permute-start.2
  11.7 0.9 collective-permute-start.3
  12.6 0.0 copy-done
  12.6 0.3 fusion.7
  12.9 0.9 copy.17.scale_ref
  13.8 0.0 copy-done.9
  13.8 0.6 reshape.53.gain_ref
  14.4 9.1 %shard_map.148 = (bf16[512,640]{1,0:T(8,128)(2,1)}, bf16[512,640]{1,0:T(8,128)(2,1)}, bf16[512,640]{1,0:T(8,128)(2,1)}) custom-call(bf16[512,1280]{1,0:T(8,128)(2,1)} %x_ref.1, f32[512,1]{1,0:T(8,128)} %copy.17.scale_ref, bf16[1280,640]{1,0:T(8,128)(2,1)} %wq_ref.1, bf16[1280,640]{1,0:T(8,128)(2,1)} %wk_ref.1, bf16[1280,640]{1,0:T(8,128)(2,1)} %wv_ref.1, ...), custom_call_target="tpu_custom_call" | custom-call | tf_op jit(solution)/shard_map/pallas_call | solution.py:85
  23.5 0.0 copy-start.10
  23.5 1.4 %slice_bitcast_fusion = (bf16[1,256,640]{2,1,0:T(8,128)(2,1)S(1)}, bf16[1,256,640]{2,1,0:T(8,128)(2,1)S(1)}, bf16[1,256,640]{2,1,0:T(8,128)(2,1)S(1)}, bf16[1,256,640]{2,1,0:T(8,128)(2,1)S(1)}) fusion(bf16[512,640]{1,0:T(8,128)(2,1)} %get-tuple-element.12.v_ref, bf16[512,640]{1,0:T(8,128)(2,1)} %get-tuple-element.11.k_ref), kind=kLoop, calls=%fused_computation.26 | loop fusion | bytes 2621440 | tf_op jit(solution)/shard_map/slice | solution.py:214
  24.9 0.1 pad_maximum_fusion
  25.0 1.6 %collective-permute-start.6 = (bf16[2,256,640]{2,1,0:T(8,128)(2,1)S(1)}, bf16[2,256,640]{2,1,0:T(8,128)(2,1)}, u32[]{:S(2)}, u32[]{:S(2)}) collective-permute-start(bf16[2,256,640]{2,1,0:T(8,128)(2,1)S(1)} %pad_maximum_fusion), channel_id=1, source_target_pairs={{96,0},{97,1},{98,2},{99,3},{100,4},{101,5},{102,6},{103,7},{104,8... | collective-permute-start | bytes 1966088 | tf_op jit(solution)/shard_map/ppermute | solution.py:22
  26.6 0.0 collective-permute-done.refs_0_.refs_4_
  26.6 0.0 copy-start.2
  26.6 2.9 %collective-permute-start.5 = (bf16[640,1280]{1,0:T(8,128)(2,1)}, bf16[640,1280]{1,0:T(8,128)(2,1)}, u32[]{:S(2)}, u32[]{:S(2)}) collective-permute-start(bf16[640,1280]{1,0:T(8,128)(2,1)} %param.17), channel_id=1, source_target_pairs={{128,0},{0,128},{129,1},{1,129},{130,2},{2,130},{131,3},{3,131},{1... | collective-permute-start | bytes 4915208 | tf_op jit(solution)/shard_map/ppermute | solution.py:22
  29.5 0.1 pad_maximum_fusion.1
  29.6 7.7 %collective-permute-done.1.refs_1_.refs_5_ = bf16[2,256,640]{2,1,0:T(8,128)(2,1)S(1)} collective-permute-done((bf16[2,256,640]{2,1,0:T(8,128)(2,1)}, bf16[2,256,640]{2,1,0:T(8,128)(2,1)S(1)}, u32[]{:S(2)}, u32[]{:S(2)}) %collective-permute-start.1) | collective-permute-done | bytes 655392 | tf_op jit(solution)/shard_map/ppermute | solution.py:22
  37.3 0.0 copy-start.3
  37.3 0.0 collective-permute-start.7
  37.3 0.0 copy-done.10
  37.3 0.7 fusion.12
  42.9 0.0 collective-permute-done.2.refs_2_.refs_6_
  42.9 0.0 copy-start.4
  42.9 2.8 %collective-permute-done.3.refs_3_.refs_7_ = bf16[2,256,640]{2,1,0:T(8,128)(2,1)} collective-permute-done((bf16[2,256,640]{2,1,0:T(8,128)(2,1)}, bf16[2,256,640]{2,1,0:T(8,128)(2,1)}, u32[]{:S(2)}, u32[]{:S(2)}) %collective-permute-start.3) | collective-permute-done | bytes 655392 | tf_op jit(solution)/shard_map/ppermute | solution.py:22
  45.7 0.0 copy-done.2
  45.7 0.0 copy-done.3
  45.7 0.0 copy-done.4
  45.7 21.2 %shard_map.150 = bf16[512,640]{1,0:T(8,128)(2,1)} custom-call(s32[1]{0:T(128)S(6)} %copy.23.live_ref, s32[1]{0:T(128)S(6)} %copy.24.depth_ref, bf16[512,640]{1,0:T(8,128)(2,1)} %get-tuple-element.10.q_ref, bf16[512,640]{1,0:T(8,128)(2,1)} %get-tuple-element.11.k_ref, bf16[512,640]{1,0:T(8,128)(2,1)} %get-tuple-element.12.v_ref, ...), custom_call_target="tpu_custom_call" | custom-call | tf_op jit(solution)/shard_map/pallas_call | solution.py:155
  66.9 0.0 copy-start.5
  66.9 3.4 %collective-permute-start.4 = (bf16[512,640]{1,0:T(8,128)(2,1)}, bf16[512,640]{1,0:T(8,128)(2,1)S(1)}, u32[]{:S(2)}, u32[]{:S(2)}) collective-permute-start(bf16[512,640]{1,0:T(8,128)(2,1)} %shard_map.150), channel_id=1, source_target_pairs={{128,0},{0,128},{129,1},{1,129},{130,2},{2,130},{131,3},{3,131},{1... | collective-permute-start | bytes 1966088 | tf_op jit(solution)/shard_map/ppermute | solution.py:22
  70.4 0.0 collective-permute-done.6
  70.4 0.1 broadcast.61.clone.1
  70.4 1.0 slice_dynamic-update-slice_fusion.3
  71.4 0.1 broadcast.61.clone
  71.5 1.0 slice_dynamic-update-slice_fusion.1
  72.5 0.0 collective-permute-done.7
  72.5 1.2 %slice_dynamic-update-slice_fusion = (bf16[2,256,640]{2,1,0:T(8,128)(2,1)S(1)}, bf16[2,256,640]{2,1,0:T(8,128)(2,1)S(1)}) fusion(bf16[2,256,640]{2,1,0:T(8,128)(2,1)S(1)} %slice_dynamic-update-slice_fusion.1, s32[]{:T(128)S(6)} %select_n.71, bf16[2,256,640]{2,1,0:T(8,128)(2,1)} %collective-permute-done.7, ...), kind=kLoop, calls=%fused_computation.22 | loop fusion | bytes 1310724 | tf_op jit(solution)/shard_map/jit(dynamic_update_index_in_dim)/dynamic_update_slice | solution.py:219
  73.7 0.0 copy-start.6
  73.7 0.0 copy-start.7
  73.7 21.3 %collective-permute-done.4 = bf16[512,640]{1,0:T(8,128)(2,1)S(1)} collective-permute-done((bf16[512,640]{1,0:T(8,128)(2,1)}, bf16[512,640]{1,0:T(8,128)(2,1)S(1)}, u32[]{:S(2)}, u32[]{:S(2)}) %collective-permute-start.4) | collective-permute-done | bytes 655392 | tf_op jit(solution)/shard_map/ppermute | solution.py:22
  95.1 0.0 copy-done.5
  95.1 0.1 broadcast_select_fusion.3
  95.2 0.0 collective-permute-done.5
  95.2 2.1 %broadcast_select_fusion.1 = (bf16[640,1280]{1,0:T(8,128)(2,1)S(1)}, bf16[640,1280]{1,0:T(8,128)(2,1)S(1)}) fusion(bf16[640,1280]{1,0:T(8,128)(2,1)} %param.17, bf16[640,1280]{1,0:T(8,128)(2,1)} %collective-permute-done.5, pred[]{:T(512)S(6)} %eq.9), kind=kLoop, calls=%fused_computation.14 | loop fusion | flops 1638400 | bytes 6553601 | tf_op jit(solution)/shard_map/jit(_where)/select_n | solution.py:54
  97.4 0.0 copy-done.6
  97.4 0.0 copy-done.7
  97.4 0.0 copy-start.1
  97.4 0.0 copy-start.8
  97.4 2.0 %multiply_reduce_fusion.1 = (f32[512]{0:T(512)S(1)}, f32[512,1280]{1,0:T(8,128)S(1)}) fusion(bf16[640,1280]{1,0:T(8,128)(2,1)S(1)} %get-tuple-element.18, bf16[640,1280]{1,0:T(8,128)(2,1)S(1)} %get-tuple-element.17, bf16[512,640]{1,0:T(8,128)(2,1)S(1)} %get-tuple-element.20, bf16[512,640]{1,0:T(8,128)(2,1)S(1)} %get-tuple-element.19), kind=kOutput, calls=%fused_computation.12 | convolution fusion | flops 1688206848 | bytes 7211008 | tf_op jit(solution)/shard_map/dot_general | solution.py:251
  99.4 0.0 copy-done.1
  99.4 0.0 copy-done.8
  99.4 0.8 multiply_reduce_fusion
  100.3 1.8 %multiply_convert_fusion = bf16[512,1280]{1,0:T(8,128)(2,1)} fusion(f32[512]{0:T(512)S(1)} %add_rsqrt_fusion, f32[512,1280]{1,0:T(8,128)S(1)} %get-tuple-element.30, f32[512]{0:T(512)S(1)} %add_rsqrt_fusion.1, f32[1280]{0:T(1024)S(1)} %copy-done.8, f32[512]{0:T(512)S(1)} %add_rsqrt_fusion.2, bf16[512,1280]{1,0:T(8,128)(2,1)S(1)} %copy-done.1), kind=kLoop, calls=%fused_computation.10 | loop fusion | flops 5242880 | bytes 5254144 | tf_op jit(solution)/shard_map/convert_element_type | solution.py:257
  (3 shorter events, 0.0 us)
Async XLA Ops:
  0.6 12.0 %copy-start = (bf16[512,1280]{1,0:T(8,128)(2,1)S(1)}, bf16[512,1280]{1,0:T(8,128)(2,1)}, u32[]{:S(2)}) copy-start(bf16[512,1280]{1,0:T(8,128)(2,1)} %x_ref.1) | copy-start | bytes 3932164
  0.6 13.2 %copy-start.9 = (f32[640]{0:T(1024)S(1)}, f32[640]{0:T(1024)}, u32[]{:S(2)}) copy-start(f32[640]{0:T(1024)} %param.18) | copy-start | bytes 7684
  7.2 19.4 %collective-permute-start = (bf16[2,256,640]{2,1,0:T(8,128)(2,1)}, bf16[2,256,640]{2,1,0:T(8,128)(2,1)S(1)}, u32[]{:S(2)}, u32[]{:S(2)}) collective-permute-start(bf16[2,256,640]{2,1,0:T(8,128)(2,1)} %get-tuple-element.13), channel_id=1, source_target_pairs={{1,0},{2,1},{3,2},{4,3},{5,4},{6,5},{7,6},{8,7},{9,8},{10,9},{11,1... | collective-permute-start | bytes 1966088 | tf_op jit(solution)/shard_map/ppermute | solution.py:22
  7.9 29.4 %collective-permute-start.1 = (bf16[2,256,640]{2,1,0:T(8,128)(2,1)}, bf16[2,256,640]{2,1,0:T(8,128)(2,1)S(1)}, u32[]{:S(2)}, u32[]{:S(2)}) collective-permute-start(bf16[2,256,640]{2,1,0:T(8,128)(2,1)} %get-tuple-element.14), channel_id=1, source_target_pairs={{33,0},{34,1},{35,2},{36,3},{37,4},{38,5},{39,6},{40,7},{41,8},{42... | collective-permute-start | bytes 1966088 | tf_op jit(solution)/shard_map/ppermute | solution.py:22
  10.8 32.2 %collective-permute-start.2 = (bf16[2,256,640]{2,1,0:T(8,128)(2,1)}, bf16[2,256,640]{2,1,0:T(8,128)(2,1)S(1)}, u32[]{:S(2)}, u32[]{:S(2)}) collective-permute-start(bf16[2,256,640]{2,1,0:T(8,128)(2,1)} %get-tuple-element.15), channel_id=1, source_target_pairs={{65,0},{66,1},{67,2},{68,3},{69,4},{70,5},{71,6},{72,7},{73,8},{74... | collective-permute-start | bytes 1966088 | tf_op jit(solution)/shard_map/ppermute | solution.py:22
  11.7 34.0 %collective-permute-start.3 = (bf16[2,256,640]{2,1,0:T(8,128)(2,1)}, bf16[2,256,640]{2,1,0:T(8,128)(2,1)}, u32[]{:S(2)}, u32[]{:S(2)}) collective-permute-start(bf16[2,256,640]{2,1,0:T(8,128)(2,1)} %get-tuple-element.16), channel_id=1, source_target_pairs={{97,0},{98,1},{99,2},{100,3},{101,4},{102,5},{103,6},{104,7},{105,... | collective-permute-start | bytes 1966088 | tf_op jit(solution)/shard_map/ppermute | solution.py:22
  23.5 13.8 %copy-start.10 = (s32[256]{0:T(256)S(1)}, s32[256]{0:T(256)}, u32[]{:S(2)}) copy-start(s32[256]{0:T(256)} %param.25) | copy-start | bytes 3076
  25.0 45.4 %collective-permute-start.6 = (bf16[2,256,640]{2,1,0:T(8,128)(2,1)S(1)}, bf16[2,256,640]{2,1,0:T(8,128)(2,1)}, u32[]{:S(2)}, u32[]{:S(2)}) collective-permute-start(bf16[2,256,640]{2,1,0:T(8,128)(2,1)S(1)} %pad_maximum_fusion), channel_id=1, source_target_pairs={{96,0},{97,1},{98,2},{99,3},{100,4},{101,5},{102,6},{103,7},{104,8... | collective-permute-start | bytes 1966088 | tf_op jit(solution)/shard_map/ppermute | solution.py:22
  26.6 19.1 %copy-start.2 = (bf16[2,256,640]{2,1,0:T(8,128)(2,1)}, bf16[2,256,640]{2,1,0:T(8,128)(2,1)S(1)}, u32[]{:S(2)}) copy-start(bf16[2,256,640]{2,1,0:T(8,128)(2,1)S(1)} %collective-permute-done.refs_0_.refs_4_) | copy-start | bytes 1966084
  26.6 68.6 %collective-permute-start.5 = (bf16[640,1280]{1,0:T(8,128)(2,1)}, bf16[640,1280]{1,0:T(8,128)(2,1)}, u32[]{:S(2)}, u32[]{:S(2)}) collective-permute-start(bf16[640,1280]{1,0:T(8,128)(2,1)} %param.17), channel_id=1, source_target_pairs={{128,0},{0,128},{129,1},{1,129},{130,2},{2,130},{131,3},{3,131},{1... | collective-permute-start | bytes 4915208 | tf_op jit(solution)/shard_map/ppermute | solution.py:22
  37.3 8.4 %copy-start.3 = (bf16[2,256,640]{2,1,0:T(8,128)(2,1)}, bf16[2,256,640]{2,1,0:T(8,128)(2,1)S(1)}, u32[]{:S(2)}) copy-start(bf16[2,256,640]{2,1,0:T(8,128)(2,1)S(1)} %collective-permute-done.1.refs_1_.refs_5_) | copy-start | bytes 1966084
  37.3 35.2 %collective-permute-start.7 = (bf16[2,256,640]{2,1,0:T(8,128)(2,1)S(1)}, bf16[2,256,640]{2,1,0:T(8,128)(2,1)}, u32[]{:S(2)}, u32[]{:S(2)}) collective-permute-start(bf16[2,256,640]{2,1,0:T(8,128)(2,1)S(1)} %pad_maximum_fusion.1), channel_id=1, source_target_pairs={{32,0},{33,1},{34,2},{35,3},{36,4},{37,5},{38,6},{39,7},{40,8},{41... | collective-permute-start | bytes 1966088 | tf_op jit(solution)/shard_map/ppermute | solution.py:22
  42.9 2.8 %copy-start.4 = (bf16[2,256,640]{2,1,0:T(8,128)(2,1)}, bf16[2,256,640]{2,1,0:T(8,128)(2,1)S(1)}, u32[]{:S(2)}) copy-start(bf16[2,256,640]{2,1,0:T(8,128)(2,1)S(1)} %collective-permute-done.2.refs_2_.refs_6_) | copy-start | bytes 1966084
  66.9 28.2 %copy-start.5 = (bf16[512,640]{1,0:T(8,128)(2,1)S(1)}, bf16[512,640]{1,0:T(8,128)(2,1)}, u32[]{:S(2)}) copy-start(bf16[512,640]{1,0:T(8,128)(2,1)} %shard_map.150) | copy-start | bytes 1966084
  66.9 28.2 %collective-permute-start.4 = (bf16[512,640]{1,0:T(8,128)(2,1)}, bf16[512,640]{1,0:T(8,128)(2,1)S(1)}, u32[]{:S(2)}, u32[]{:S(2)}) collective-permute-start(bf16[512,640]{1,0:T(8,128)(2,1)} %shard_map.150), channel_id=1, source_target_pairs={{128,0},{0,128},{129,1},{1,129},{130,2},{2,130},{131,3},{3,131},{1... | collective-permute-start | bytes 1966088 | tf_op jit(solution)/shard_map/ppermute | solution.py:22
  73.7 23.7 %copy-start.6 = (bf16[2,256,640]{2,1,0:T(8,128)(2,1)}, bf16[2,256,640]{2,1,0:T(8,128)(2,1)S(1)}, u32[]{:S(2)}) copy-start(bf16[2,256,640]{2,1,0:T(8,128)(2,1)S(1)} %get-tuple-element.21) | copy-start | bytes 1966084
  73.7 23.7 %copy-start.7 = (bf16[2,256,640]{2,1,0:T(8,128)(2,1)}, bf16[2,256,640]{2,1,0:T(8,128)(2,1)S(1)}, u32[]{:S(2)}) copy-start(bf16[2,256,640]{2,1,0:T(8,128)(2,1)S(1)} %get-tuple-element.22) | copy-start | bytes 1966084
  97.4 2.0 %copy-start.1 = (bf16[512,1280]{1,0:T(8,128)(2,1)S(1)}, bf16[512,1280]{1,0:T(8,128)(2,1)}, u32[]{:S(2)}) copy-start(bf16[512,1280]{1,0:T(8,128)(2,1)} %x_ref.1) | copy-start | bytes 3932164
  97.4 2.0 %copy-start.8 = (f32[1280]{0:T(1024)S(1)}, f32[1280]{0:T(1024)}, u32[]{:S(2)}) copy-start(f32[1280]{0:T(1024)} %param.19) | copy-start | bytes 15364

commit v9 on v8

--- a/solution.py
+++ b/solution.py
@@ -139,7 +139,7 @@
 
 def attention(queries, key_rows, value_rows, pages, req_len, prefix_len):
     tokens, width = queries.shape
-    tile = 128
+    tile = 256
     lanes = 2 * HD
     grid = (width // lanes, tokens // tile)
     own_spec = pl.BlockSpec((tokens, lanes), lambda h, t, *_: (0, h))

time: 103 us -> 103 us (level)
  Pallas kernels: 35.3 us -> 28.8 us
  waiting for transfers between devices: 31.8 us -> 38.3 us
    pallas_call x1, Pallas kernels: 21.2 us -> 14.7 us  [attention(): pl.pallas_call(attention_kernel, out_shape=jax.ShapeDtypeStruct((tokens,...]
    ppermute x8, waiting for transfers between devices: 31.8 us -> 38.3 us  [from_behind(): return lax.ppermute(block, axis, route)]
  transfers between devices with their start and end apart: 8 -> 8, of which waited for: 3 -> 3; matrix products, arithmetic and copies ran while one was open for 7% -> 7% of each run, Pallas kernels for 30% -> 23%
where the time goes in v9:
time: 103 us; the launch traced here: 102 us
  waiting for transfers between devices  38.3 us (37%)
  Pallas kernels  28.8 us (28%)
  starting transfers between devices  13.4 us (13%)
  local copies, waits for them, and re-layouts  8.43 us (8%)
  between operations  5.73 us (6%)
  other arithmetic  5.41 us (5%)
  matrix products  1.97 us (2%)
    ppermute x8, waiting for transfers between devices, from_behind(): return lax.ppermute(block, axis, route)  38.3 us
    pallas_call x1, Pallas kernels, attention(): pl.pallas_call(attention_kernel, out_shape=jax.ShapeDtypeStruct((tokens,...  14.7 us
    ppermute x8, starting transfers between devices, from_behind(): return lax.ppermute(block, axis, route)  13.4 us
    pallas_call x1, Pallas kernels, projections(): pl.pallas_call(projection_kernel, out_shape=(shape, shape, shape), grid=(...  9.09 us
    pallas_call x1, Pallas kernels, fetch_pages(): pl.pallas_call(functools.partial(gather_kernel, devices), out_shape=[page...  5.02 us
    select_n x2, other arithmetic, in_kv_order(): low = jnp.where(first, mine, other)  2.27 us
    dynamic_update_slice x2, local copies, waits for them, and re-layouts, relay(): lax.dynamic_update_index_in_dim(value_out, received[1], target, 0)  2.19 us
  transfers between devices with their start and end apart: 8, of which 3 were waited for; matrix products, arithmetic and copies ran while one was open for 7% of the time, Pallas kernels for 23%

profile of v9, /device:TPU:225, one launch (start us, length us, event | category | flops | bytes accessed | tf_op | source)
XLA Modules:
  0.0 102.1 jit_solution(4715486695755303560)
XLA Ops:
  0.6 0.0 copy-start
  0.6 0.0 copy-start.9
  0.7 1.5 %copy.18.pages_ref = s32[128,4]{1,0:T(8,128)} copy(s32[128,4]{0,1:T(4,128)} %param.24) | data formatting | bytes 4096 | tf_op args[11]
  2.2 5.0 %shard_map.149 = (bf16[2,256,640]{2,1,0:T(8,128)(2,1)}, bf16[2,256,640]{2,1,0:T(8,128)(2,1)}, bf16[2,256,640]{2,1,0:T(8,128)(2,1)}, bf16[2,256,640]{2,1,0:T(8,128)(2,1)}) custom-call(s32[128,4]{1,0:T(8,128)} %copy.18.pages_ref, bf16[4,256,640]{2,1,0:T(8,128)(2,1)} %keys_hbm.1, bf16[4,256,640]{2,1,0:T(8,128)(2,1)} %values_hbm.1), custom_call_target="tpu_custom_call" | custom-call | tf_op jit(solution)/shard_map/pallas_call | solution.py:191
  7.2 0.7 collective-permute-start
  7.9 3.0 %collective-permute-start.1 = (bf16[2,256,640]{2,1,0:T(8,128)(2,1)}, bf16[2,256,640]{2,1,0:T(8,128)(2,1)S(1)}, u32[]{:S(2)}, u32[]{:S(2)}) collective-permute-start(bf16[2,256,640]{2,1,0:T(8,128)(2,1)} %get-tuple-element.14), channel_id=1, source_target_pairs={{33,0},{34,1},{35,2},{36,3},{37,4},{38,5},{39,6},{40,7},{41,8},{42... | collective-permute-start | bytes 1966088 | tf_op jit(solution)/shard_map/ppermute | solution.py:22
  10.9 0.7 collective-permute-start.2
  11.7 1.0 collective-permute-start.3
  12.7 0.0 copy-done
  12.7 0.3 fusion.7
  13.0 0.9 copy.17.scale_ref
  13.9 0.0 copy-done.9
  13.9 0.6 reshape.53.gain_ref
  14.5 9.1 %shard_map.148 = (bf16[512,640]{1,0:T(8,128)(2,1)}, bf16[512,640]{1,0:T(8,128)(2,1)}, bf16[512,640]{1,0:T(8,128)(2,1)}) custom-call(bf16[512,1280]{1,0:T(8,128)(2,1)} %x_ref.1, f32[512,1]{1,0:T(8,128)} %copy.17.scale_ref, bf16[1280,640]{1,0:T(8,128)(2,1)} %wq_ref.1, bf16[1280,640]{1,0:T(8,128)(2,1)} %wk_ref.1, bf16[1280,640]{1,0:T(8,128)(2,1)} %wv_ref.1, ...), custom_call_target="tpu_custom_call" | custom-call | tf_op jit(solution)/shard_map/pallas_call | solution.py:85
  23.6 0.0 copy-start.10
  23.6 1.4 %slice_bitcast_fusion = (bf16[1,256,640]{2,1,0:T(8,128)(2,1)S(1)}, bf16[1,256,640]{2,1,0:T(8,128)(2,1)S(1)}, bf16[1,256,640]{2,1,0:T(8,128)(2,1)S(1)}, bf16[1,256,640]{2,1,0:T(8,128)(2,1)S(1)}) fusion(bf16[512,640]{1,0:T(8,128)(2,1)} %get-tuple-element.12.v_ref, bf16[512,640]{1,0:T(8,128)(2,1)} %get-tuple-element.11.k_ref), kind=kLoop, calls=%fused_computation.26 | loop fusion | bytes 2621440 | tf_op jit(solution)/shard_map/slice | solution.py:214
  25.0 0.1 pad_maximum_fusion
  25.0 1.6 %collective-permute-start.6 = (bf16[2,256,640]{2,1,0:T(8,128)(2,1)S(1)}, bf16[2,256,640]{2,1,0:T(8,128)(2,1)}, u32[]{:S(2)}, u32[]{:S(2)}) collective-permute-start(bf16[2,256,640]{2,1,0:T(8,128)(2,1)S(1)} %pad_maximum_fusion), channel_id=1, source_target_pairs={{96,0},{97,1},{98,2},{99,3},{100,4},{101,5},{102,6},{103,7},{104,8... | collective-permute-start | bytes 1966088 | tf_op jit(solution)/shard_map/ppermute | solution.py:22
  26.6 0.0 collective-permute-done.refs_0_.refs_4_
  26.6 0.0 copy-start.2
  26.6 2.9 %collective-permute-start.5 = (bf16[640,1280]{1,0:T(8,128)(2,1)}, bf16[640,1280]{1,0:T(8,128)(2,1)}, u32[]{:S(2)}, u32[]{:S(2)}) collective-permute-start(bf16[640,1280]{1,0:T(8,128)(2,1)} %param.17), channel_id=1, source_target_pairs={{128,0},{0,128},{129,1},{1,129},{130,2},{2,130},{131,3},{3,131},{1... | collective-permute-start | bytes 4915208 | tf_op jit(solution)/shard_map/ppermute | solution.py:22
  29.5 0.1 pad_maximum_fusion.1
  29.6 8.1 %collective-permute-done.1.refs_1_.refs_5_ = bf16[2,256,640]{2,1,0:T(8,128)(2,1)S(1)} collective-permute-done((bf16[2,256,640]{2,1,0:T(8,128)(2,1)}, bf16[2,256,640]{2,1,0:T(8,128)(2,1)S(1)}, u32[]{:S(2)}, u32[]{:S(2)}) %collective-permute-start.1) | collective-permute-done | bytes 655392 | tf_op jit(solution)/shard_map/ppermute | solution.py:22
  37.7 0.0 copy-start.3
  37.7 0.0 collective-permute-start.7
  37.7 0.0 copy-done.10
  37.7 0.7 fusion.12
  43.3 0.0 collective-permute-done.2.refs_2_.refs_6_
  43.3 0.0 copy-start.4
  43.4 2.4 %collective-permute-done.3.refs_3_.refs_7_ = bf16[2,256,640]{2,1,0:T(8,128)(2,1)} collective-permute-done((bf16[2,256,640]{2,1,0:T(8,128)(2,1)}, bf16[2,256,640]{2,1,0:T(8,128)(2,1)}, u32[]{:S(2)}, u32[]{:S(2)}) %collective-permute-start.3) | collective-permute-done | bytes 655392 | tf_op jit(solution)/shard_map/ppermute | solution.py:22
  45.7 0.0 copy-done.2
  45.7 0.0 copy-done.3
  45.7 0.0 copy-done.4
  45.7 14.7 %shard_map.150 = bf16[512,640]{1,0:T(8,128)(2,1)} custom-call(s32[1]{0:T(128)S(6)} %copy.23.live_ref, s32[1]{0:T(128)S(6)} %copy.24.depth_ref, bf16[512,640]{1,0:T(8,128)(2,1)} %get-tuple-element.10.q_ref, bf16[512,640]{1,0:T(8,128)(2,1)} %get-tuple-element.11.k_ref, bf16[512,640]{1,0:T(8,128)(2,1)} %get-tuple-element.12.v_ref, ...), custom_call_target="tpu_custom_call" | custom-call | tf_op jit(solution)/shard_map/pallas_call | solution.py:155
  60.4 0.0 copy-start.5
  60.4 3.4 %collective-permute-start.4 = (bf16[512,640]{1,0:T(8,128)(2,1)}, bf16[512,640]{1,0:T(8,128)(2,1)S(1)}, u32[]{:S(2)}, u32[]{:S(2)}) collective-permute-start(bf16[512,640]{1,0:T(8,128)(2,1)} %shard_map.150), channel_id=1, source_target_pairs={{128,0},{0,128},{129,1},{1,129},{130,2},{2,130},{131,3},{3,131},{1... | collective-permute-start | bytes 1966088 | tf_op jit(solution)/shard_map/ppermute | solution.py:22
  63.9 0.0 collective-permute-done.6
  63.9 0.1 broadcast.61.clone.1
  63.9 1.0 slice_dynamic-update-slice_fusion.3
  64.9 0.1 broadcast.61.clone
  65.0 1.0 slice_dynamic-update-slice_fusion.1
  66.0 0.0 collective-permute-done.7
  66.0 1.2 %slice_dynamic-update-slice_fusion = (bf16[2,256,640]{2,1,0:T(8,128)(2,1)S(1)}, bf16[2,256,640]{2,1,0:T(8,128)(2,1)S(1)}) fusion(bf16[2,256,640]{2,1,0:T(8,128)(2,1)S(1)} %slice_dynamic-update-slice_fusion.1, s32[]{:T(128)S(6)} %select_n.71, bf16[2,256,640]{2,1,0:T(8,128)(2,1)} %collective-permute-done.7, ...), kind=kLoop, calls=%fused_computation.22 | loop fusion | bytes 1310724 | tf_op jit(solution)/shard_map/jit(dynamic_update_index_in_dim)/dynamic_update_slice | solution.py:219
  67.2 0.0 copy-start.6
  67.2 0.0 copy-start.7
  67.2 27.8 %collective-permute-done.4 = bf16[512,640]{1,0:T(8,128)(2,1)S(1)} collective-permute-done((bf16[512,640]{1,0:T(8,128)(2,1)}, bf16[512,640]{1,0:T(8,128)(2,1)S(1)}, u32[]{:S(2)}, u32[]{:S(2)}) %collective-permute-start.4) | collective-permute-done | bytes 655392 | tf_op jit(solution)/shard_map/ppermute | solution.py:22
  95.1 0.0 copy-done.5
  95.1 0.1 broadcast_select_fusion.3
  95.2 0.0 collective-permute-done.5
  95.2 2.1 %broadcast_select_fusion.1 = (bf16[640,1280]{1,0:T(8,128)(2,1)S(1)}, bf16[640,1280]{1,0:T(8,128)(2,1)S(1)}) fusion(bf16[640,1280]{1,0:T(8,128)(2,1)} %param.17, bf16[640,1280]{1,0:T(8,128)(2,1)} %collective-permute-done.5, pred[]{:T(512)S(6)} %eq.9), kind=kLoop, calls=%fused_computation.14 | loop fusion | flops 1638400 | bytes 6553601 | tf_op jit(solution)/shard_map/jit(_where)/select_n | solution.py:54
  97.4 0.0 copy-done.6
  97.4 0.0 copy-done.7
  97.4 0.0 copy-start.1
  97.4 0.0 copy-start.8
  97.4 2.0 %multiply_reduce_fusion.1 = (f32[512]{0:T(512)S(1)}, f32[512,1280]{1,0:T(8,128)S(1)}) fusion(bf16[640,1280]{1,0:T(8,128)(2,1)S(1)} %get-tuple-element.18, bf16[640,1280]{1,0:T(8,128)(2,1)S(1)} %get-tuple-element.17, bf16[512,640]{1,0:T(8,128)(2,1)S(1)} %get-tuple-element.20, bf16[512,640]{1,0:T(8,128)(2,1)S(1)} %get-tuple-element.19), kind=kOutput, calls=%fused_computation.12 | convolution fusion | flops 1688206848 | bytes 7211008 | tf_op jit(solution)/shard_map/dot_general | solution.py:251
  99.4 0.0 copy-done.1
  99.4 0.0 copy-done.8
  99.4 0.8 multiply_reduce_fusion
  100.3 1.8 %multiply_convert_fusion = bf16[512,1280]{1,0:T(8,128)(2,1)} fusion(f32[512]{0:T(512)S(1)} %add_rsqrt_fusion, f32[512,1280]{1,0:T(8,128)S(1)} %get-tuple-element.30, f32[512]{0:T(512)S(1)} %add_rsqrt_fusion.1, f32[1280]{0:T(1024)S(1)} %copy-done.8, f32[512]{0:T(512)S(1)} %add_rsqrt_fusion.2, bf16[512,1280]{1,0:T(8,128)(2,1)S(1)} %copy-done.1), kind=kLoop, calls=%fused_computation.10 | loop fusion | flops 5242880 | bytes 5254144 | tf_op jit(solution)/shard_map/convert_element_type | solution.py:257
  (3 shorter events, 0.0 us)
Async XLA Ops:
  0.6 12.0 %copy-start = (bf16[512,1280]{1,0:T(8,128)(2,1)S(1)}, bf16[512,1280]{1,0:T(8,128)(2,1)}, u32[]{:S(2)}) copy-start(bf16[512,1280]{1,0:T(8,128)(2,1)} %x_ref.1) | copy-start | bytes 3932164
  0.6 13.2 %copy-start.9 = (f32[640]{0:T(1024)S(1)}, f32[640]{0:T(1024)}, u32[]{:S(2)}) copy-start(f32[640]{0:T(1024)} %param.18) | copy-start | bytes 7684
  7.2 19.4 %collective-permute-start = (bf16[2,256,640]{2,1,0:T(8,128)(2,1)}, bf16[2,256,640]{2,1,0:T(8,128)(2,1)S(1)}, u32[]{:S(2)}, u32[]{:S(2)}) collective-permute-start(bf16[2,256,640]{2,1,0:T(8,128)(2,1)} %get-tuple-element.13), channel_id=1, source_target_pairs={{1,0},{2,1},{3,2},{4,3},{5,4},{6,5},{7,6},{8,7},{9,8},{10,9},{11,1... | collective-permute-start | bytes 1966088 | tf_op jit(solution)/shard_map/ppermute | solution.py:22
  7.9 29.8 %collective-permute-start.1 = (bf16[2,256,640]{2,1,0:T(8,128)(2,1)}, bf16[2,256,640]{2,1,0:T(8,128)(2,1)S(1)}, u32[]{:S(2)}, u32[]{:S(2)}) collective-permute-start(bf16[2,256,640]{2,1,0:T(8,128)(2,1)} %get-tuple-element.14), channel_id=1, source_target_pairs={{33,0},{34,1},{35,2},{36,3},{37,4},{38,5},{39,6},{40,7},{41,8},{42... | collective-permute-start | bytes 1966088 | tf_op jit(solution)/shard_map/ppermute | solution.py:22
  10.9 32.4 %collective-permute-start.2 = (bf16[2,256,640]{2,1,0:T(8,128)(2,1)}, bf16[2,256,640]{2,1,0:T(8,128)(2,1)S(1)}, u32[]{:S(2)}, u32[]{:S(2)}) collective-permute-start(bf16[2,256,640]{2,1,0:T(8,128)(2,1)} %get-tuple-element.15), channel_id=1, source_target_pairs={{65,0},{66,1},{67,2},{68,3},{69,4},{70,5},{71,6},{72,7},{73,8},{74... | collective-permute-start | bytes 1966088 | tf_op jit(solution)/shard_map/ppermute | solution.py:22
  11.7 34.1 %collective-permute-start.3 = (bf16[2,256,640]{2,1,0:T(8,128)(2,1)}, bf16[2,256,640]{2,1,0:T(8,128)(2,1)}, u32[]{:S(2)}, u32[]{:S(2)}) collective-permute-start(bf16[2,256,640]{2,1,0:T(8,128)(2,1)} %get-tuple-element.16), channel_id=1, source_target_pairs={{97,0},{98,1},{99,2},{100,3},{101,4},{102,5},{103,6},{104,7},{105,... | collective-permute-start | bytes 1966088 | tf_op jit(solution)/shard_map/ppermute | solution.py:22
  23.6 14.2 %copy-start.10 = (s32[256]{0:T(256)S(1)}, s32[256]{0:T(256)}, u32[]{:S(2)}) copy-start(s32[256]{0:T(256)} %param.25) | copy-start | bytes 3076
  25.0 38.8 %collective-permute-start.6 = (bf16[2,256,640]{2,1,0:T(8,128)(2,1)S(1)}, bf16[2,256,640]{2,1,0:T(8,128)(2,1)}, u32[]{:S(2)}, u32[]{:S(2)}) collective-permute-start(bf16[2,256,640]{2,1,0:T(8,128)(2,1)S(1)} %pad_maximum_fusion), channel_id=1, source_target_pairs={{96,0},{97,1},{98,2},{99,3},{100,4},{101,5},{102,6},{103,7},{104,8... | collective-permute-start | bytes 1966088 | tf_op jit(solution)/shard_map/ppermute | solution.py:22
  26.6 19.1 %copy-start.2 = (bf16[2,256,640]{2,1,0:T(8,128)(2,1)}, bf16[2,256,640]{2,1,0:T(8,128)(2,1)S(1)}, u32[]{:S(2)}) copy-start(bf16[2,256,640]{2,1,0:T(8,128)(2,1)S(1)} %collective-permute-done.refs_0_.refs_4_) | copy-start | bytes 1966084
  26.6 68.6 %collective-permute-start.5 = (bf16[640,1280]{1,0:T(8,128)(2,1)}, bf16[640,1280]{1,0:T(8,128)(2,1)}, u32[]{:S(2)}, u32[]{:S(2)}) collective-permute-start(bf16[640,1280]{1,0:T(8,128)(2,1)} %param.17), channel_id=1, source_target_pairs={{128,0},{0,128},{129,1},{1,129},{130,2},{2,130},{131,3},{3,131},{1... | collective-permute-start | bytes 4915208 | tf_op jit(solution)/shard_map/ppermute | solution.py:22
  37.7 8.0 %copy-start.3 = (bf16[2,256,640]{2,1,0:T(8,128)(2,1)}, bf16[2,256,640]{2,1,0:T(8,128)(2,1)S(1)}, u32[]{:S(2)}) copy-start(bf16[2,256,640]{2,1,0:T(8,128)(2,1)S(1)} %collective-permute-done.1.refs_1_.refs_5_) | copy-start | bytes 1966084
  37.7 28.3 %collective-permute-start.7 = (bf16[2,256,640]{2,1,0:T(8,128)(2,1)S(1)}, bf16[2,256,640]{2,1,0:T(8,128)(2,1)}, u32[]{:S(2)}, u32[]{:S(2)}) collective-permute-start(bf16[2,256,640]{2,1,0:T(8,128)(2,1)S(1)} %pad_maximum_fusion.1), channel_id=1, source_target_pairs={{32,0},{33,1},{34,2},{35,3},{36,4},{37,5},{38,6},{39,7},{40,8},{41... | collective-permute-start | bytes 1966088 | tf_op jit(solution)/shard_map/ppermute | solution.py:22
  43.3 2.4 %copy-start.4 = (bf16[2,256,640]{2,1,0:T(8,128)(2,1)}, bf16[2,256,640]{2,1,0:T(8,128)(2,1)S(1)}, u32[]{:S(2)}) copy-start(bf16[2,256,640]{2,1,0:T(8,128)(2,1)S(1)} %collective-permute-done.2.refs_2_.refs_6_) | copy-start | bytes 1966084
  60.4 34.7 %copy-start.5 = (bf16[512,640]{1,0:T(8,128)(2,1)S(1)}, bf16[512,640]{1,0:T(8,128)(2,1)}, u32[]{:S(2)}) copy-start(bf16[512,640]{1,0:T(8,128)(2,1)} %shard_map.150) | copy-start | bytes 1966084
  60.4 34.6 %collective-permute-start.4 = (bf16[512,640]{1,0:T(8,128)(2,1)}, bf16[512,640]{1,0:T(8,128)(2,1)S(1)}, u32[]{:S(2)}, u32[]{:S(2)}) collective-permute-start(bf16[512,640]{1,0:T(8,128)(2,1)} %shard_map.150), channel_id=1, source_target_pairs={{128,0},{0,128},{129,1},{1,129},{130,2},{2,130},{131,3},{3,131},{1... | collective-permute-start | bytes 1966088 | tf_op jit(solution)/shard_map/ppermute | solution.py:22
  67.2 30.2 %copy-start.6 = (bf16[2,256,640]{2,1,0:T(8,128)(2,1)}, bf16[2,256,640]{2,1,0:T(8,128)(2,1)S(1)}, u32[]{:S(2)}) copy-start(bf16[2,256,640]{2,1,0:T(8,128)(2,1)S(1)} %get-tuple-element.21) | copy-start | bytes 1966084
  67.2 30.2 %copy-start.7 = (bf16[2,256,640]{2,1,0:T(8,128)(2,1)}, bf16[2,256,640]{2,1,0:T(8,128)(2,1)S(1)}, u32[]{:S(2)}) copy-start(bf16[2,256,640]{2,1,0:T(8,128)(2,1)S(1)} %get-tuple-element.22) | copy-start | bytes 1966084
  97.4 2.0 %copy-start.1 = (bf16[512,1280]{1,0:T(8,128)(2,1)S(1)}, bf16[512,1280]{1,0:T(8,128)(2,1)}, u32[]{:S(2)}) copy-start(bf16[512,1280]{1,0:T(8,128)(2,1)} %x_ref.1) | copy-start | bytes 3932164
  97.4 2.0 %copy-start.8 = (f32[1280]{0:T(1024)S(1)}, f32[1280]{0:T(1024)}, u32[]{:S(2)}) copy-start(f32[1280]{0:T(1024)} %param.19) | copy-start | bytes 15364

commit v10 on v9

--- a/solution.py
+++ b/solution.py
@@ -137,20 +137,22 @@
     out_ref[...] = jnp.where(first, results[0], results[1]).astype(out_ref.dtype)
 
 
-def attention(queries, key_rows, value_rows, pages, req_len, prefix_len):
-    tokens, width = queries.shape
+def attention(queries, key_rows, value_rows, pages, req_len, prefix_len, first_pair, pairs):
+    tokens = queries.shape[0]
     tile = 256
     lanes = 2 * HD
-    grid = (width // lanes, tokens // tile)
-    own_spec = pl.BlockSpec((tokens, lanes), lambda h, t, *_: (0, h))
-    key_spec = pl.BlockSpec((None, PAGE, lanes), lambda h, t, *_: (0, 0, h))
-    value_spec = pl.BlockSpec((None, PAGE, lanes), lambda h, t, *_: (1, 0, h))
-    tile_spec = pl.BlockSpec((tile, lanes), lambda h, t, *_: (t, h))
+    width = pairs * lanes
+    grid = (pairs, tokens // tile)
+    own_spec = pl.BlockSpec((tokens, lanes), lambda h, t, *_: (0, h + first_pair))
+    key_spec = pl.BlockSpec((None, PAGE, lanes), lambda h, t, *_: (0, 0, h + first_pair))
+    value_spec = pl.BlockSpec((None, PAGE, lanes), lambda h, t, *_: (1, 0, h + first_pair))
+    tile_spec = pl.BlockSpec((tile, lanes), lambda h, t, *_: (t, h + first_pair))
+    out_spec = pl.BlockSpec((tile, lanes), lambda h, t, *_: (t, h))
     grid_spec = pltpu.PrefetchScalarGridSpec(
         num_scalar_prefetch=2,
         grid=grid,
         in_specs=[tile_spec, own_spec, own_spec] + [key_spec] * PMAX + [value_spec] * PMAX,
-        out_specs=tile_spec,
+        out_specs=out_spec,
     )
     return pl.pallas_call(
         attention_kernel,
@@ -246,8 +248,15 @@
         hidden_in, row_scale, w_query, w_key, w_value, head_gain
     )
     fetched = fetch_pages(pool_keys, pool_values, prefix_pages)
-    attended = attention(queries, key_rows, value_rows, fetched, req_len, prefix_len)
-    other_attended = from_behind(attended, "kv", 1)
+    pairs_here = width_half // (2 * HD)
+    split = (pairs_here + 1) // 2
+    parts = [
+        attention(queries, key_rows, value_rows, fetched, req_len, prefix_len, first, count)
+        for first, count in ((0, split), (split, pairs_here - split))
+    ]
+    other_parts = [from_behind(part, "kv", 1) for part in parts]
+    attended = jnp.concatenate(parts, axis=1)
+    other_attended = jnp.concatenate(other_parts, axis=1)
     branch = jnp.dot(
         in_kv_order(attended, other_attended, 1),
         in_kv_order(w_out, other_w_out, 0),

time: 103 us -> 103 us (level)
  Pallas kernels: 28.8 us -> 30.7 us
  waiting for transfers between devices: 38.3 us -> 36.4 us
    ppermute x8 -> x9, waiting for transfers between devices: 38.3 us -> 36.4 us  [from_behind(): return lax.ppermute(block, axis, route)]
    pallas_call x1 -> x2, Pallas kernels: 14.7 us -> 16.5 us  [attention(): pl.pallas_call(attention_kernel, out_shape=jax.ShapeDtypeStruct((tokens,...]
    ppermute x8 -> x9, starting transfers between devices: 13.4 us -> 13.3 us  [from_behind(): return lax.ppermute(block, axis, route)]
  transfers between devices with their start and end apart: 8 -> 9, of which waited for: 3 -> 3; matrix products, arithmetic and copies ran while one was open for 7% -> 8% of each run, Pallas kernels for 23% -> 25%
where the time goes in v10:
time: 103 us; the launch traced here: 102 us
  waiting for transfers between devices  36.4 us (35%)
  Pallas kernels  30.7 us (30%)
  starting transfers between devices  13.3 us (13%)
  local copies, waits for them, and re-layouts  8.57 us (8%)
  between operations  5.78 us (6%)
  other arithmetic  5.52 us (5%)
  matrix products  1.97 us (2%)
    ppermute x9, waiting for transfers between devices, from_behind(): return lax.ppermute(block, axis, route)  36.4 us
    pallas_call x2, Pallas kernels, attention(): pl.pallas_call(attention_kernel, out_shape=jax.ShapeDtypeStruct((tokens,...  16.5 us
    ppermute x9, starting transfers between devices, from_behind(): return lax.ppermute(block, axis, route)  13.3 us
    pallas_call x1, Pallas kernels, projections(): pl.pallas_call(projection_kernel, out_shape=(shape, shape, shape), grid=(...  9.09 us
    pallas_call x1, Pallas kernels, fetch_pages(): pl.pallas_call(functools.partial(gather_kernel, devices), out_shape=[page...  5.08 us
    select_n x2, other arithmetic, in_kv_order(): low = jnp.where(first, mine, other)  2.38 us
    dynamic_update_slice x2, local copies, waits for them, and re-layouts, relay(): lax.dynamic_update_index_in_dim(value_out, received[1], target, 0)  2.19 us
  transfers between devices with their start and end apart: 9, of which 3 were waited for; matrix products, arithmetic and copies ran while one was open for 8% of the time, Pallas kernels for 25%

profile of v10, /device:TPU:225, one launch (start us, length us, event | category | flops | bytes accessed | tf_op | source)
XLA Modules:
  0.0 102.3 jit_solution(2551982198705424765)
XLA Ops:
  0.6 0.0 copy-start
  0.6 0.0 copy-start.10
  0.7 1.5 %copy.18.pages_ref = s32[128,4]{1,0:T(8,128)} copy(s32[128,4]{0,1:T(4,128)} %param.24) | data formatting | bytes 4096 | tf_op args[11]
  2.2 5.1 %shard_map.149 = (bf16[2,256,640]{2,1,0:T(8,128)(2,1)}, bf16[2,256,640]{2,1,0:T(8,128)(2,1)}, bf16[2,256,640]{2,1,0:T(8,128)(2,1)}, bf16[2,256,640]{2,1,0:T(8,128)(2,1)}) custom-call(s32[128,4]{1,0:T(8,128)} %copy.18.pages_ref, bf16[4,256,640]{2,1,0:T(8,128)(2,1)} %keys_hbm.1, bf16[4,256,640]{2,1,0:T(8,128)(2,1)} %values_hbm.1), custom_call_target="tpu_custom_call" | custom-call | tf_op jit(solution)/shard_map/pallas_call | solution.py:193
  7.3 0.7 collective-permute-start
  7.9 2.8 %collective-permute-start.1 = (bf16[2,256,640]{2,1,0:T(8,128)(2,1)}, bf16[2,256,640]{2,1,0:T(8,128)(2,1)S(1)}, u32[]{:S(2)}, u32[]{:S(2)}) collective-permute-start(bf16[2,256,640]{2,1,0:T(8,128)(2,1)} %get-tuple-element.14), channel_id=1, source_target_pairs={{33,0},{34,1},{35,2},{36,3},{37,4},{38,5},{39,6},{40,7},{41,8},{42... | collective-permute-start | bytes 1966088 | tf_op jit(solution)/shard_map/ppermute | solution.py:22
  10.8 0.9 collective-permute-start.2
  11.7 0.9 collective-permute-start.3
  12.6 0.0 copy-done
  12.6 0.3 fusion.7
  13.0 0.9 copy.17.scale_ref
  13.8 0.0 copy-done.10
  13.8 0.6 reshape.53.gain_ref
  14.4 9.1 %shard_map.148 = (bf16[512,640]{1,0:T(8,128)(2,1)}, bf16[512,640]{1,0:T(8,128)(2,1)}, bf16[512,640]{1,0:T(8,128)(2,1)}) custom-call(bf16[512,1280]{1,0:T(8,128)(2,1)} %x_ref.1, f32[512,1]{1,0:T(8,128)} %copy.17.scale_ref, bf16[1280,640]{1,0:T(8,128)(2,1)} %wq_ref.1, bf16[1280,640]{1,0:T(8,128)(2,1)} %wk_ref.1, bf16[1280,640]{1,0:T(8,128)(2,1)} %wv_ref.1, ...), custom_call_target="tpu_custom_call" | custom-call | tf_op jit(solution)/shard_map/pallas_call | solution.py:85
  23.5 0.0 copy-start.11
  23.5 1.4 %slice_bitcast_fusion = (bf16[1,256,640]{2,1,0:T(8,128)(2,1)S(1)}, bf16[1,256,640]{2,1,0:T(8,128)(2,1)S(1)}, bf16[1,256,640]{2,1,0:T(8,128)(2,1)S(1)}, bf16[1,256,640]{2,1,0:T(8,128)(2,1)S(1)}) fusion(bf16[512,640]{1,0:T(8,128)(2,1)} %get-tuple-element.12.v_ref, bf16[512,640]{1,0:T(8,128)(2,1)} %get-tuple-element.11.k_ref), kind=kLoop, calls=%fused_computation.27 | loop fusion | bytes 2621440 | tf_op jit(solution)/shard_map/slice | solution.py:216
  24.9 0.1 pad_maximum_fusion.1
  25.0 1.6 %collective-permute-start.7 = (bf16[2,256,640]{2,1,0:T(8,128)(2,1)S(1)}, bf16[2,256,640]{2,1,0:T(8,128)(2,1)}, u32[]{:S(2)}, u32[]{:S(2)}) collective-permute-start(bf16[2,256,640]{2,1,0:T(8,128)(2,1)S(1)} %pad_maximum_fusion.1), channel_id=1, source_target_pairs={{96,0},{97,1},{98,2},{99,3},{100,4},{101,5},{102,6},{103,7},{104,8... | collective-permute-start | bytes 1966088 | tf_op jit(solution)/shard_map/ppermute | solution.py:22
  26.6 0.0 collective-permute-done.refs_0_.refs_4_
  26.6 0.0 copy-start.2
  26.6 2.9 %collective-permute-start.6 = (bf16[640,1280]{1,0:T(8,128)(2,1)}, bf16[640,1280]{1,0:T(8,128)(2,1)}, u32[]{:S(2)}, u32[]{:S(2)}) collective-permute-start(bf16[640,1280]{1,0:T(8,128)(2,1)} %param.17), channel_id=1, source_target_pairs={{128,0},{0,128},{129,1},{1,129},{130,2},{2,130},{131,3},{3,131},{1... | collective-permute-start | bytes 4915208 | tf_op jit(solution)/shard_map/ppermute | solution.py:22
  29.5 0.1 pad_maximum_fusion.2
  29.6 7.7 %collective-permute-done.1.refs_1_.refs_5_ = bf16[2,256,640]{2,1,0:T(8,128)(2,1)S(1)} collective-permute-done((bf16[2,256,640]{2,1,0:T(8,128)(2,1)}, bf16[2,256,640]{2,1,0:T(8,128)(2,1)S(1)}, u32[]{:S(2)}, u32[]{:S(2)}) %collective-permute-start.1) | collective-permute-done | bytes 655392 | tf_op jit(solution)/shard_map/ppermute | solution.py:22
  37.3 0.0 copy-start.3
  37.3 0.0 collective-permute-start.8
  37.3 0.0 copy-done.11
  37.3 0.8 fusion.12
  42.9 0.0 collective-permute-done.2.refs_2_.refs_6_
  43.0 0.0 copy-start.4
  43.0 2.7 %collective-permute-done.3.refs_3_.refs_7_ = bf16[2,256,640]{2,1,0:T(8,128)(2,1)} collective-permute-done((bf16[2,256,640]{2,1,0:T(8,128)(2,1)}, bf16[2,256,640]{2,1,0:T(8,128)(2,1)}, u32[]{:S(2)}, u32[]{:S(2)}) %collective-permute-start.3) | collective-permute-done | bytes 655392 | tf_op jit(solution)/shard_map/ppermute | solution.py:22
  45.7 0.0 copy-done.2
  45.7 0.0 copy-done.3
  45.7 0.0 copy-done.4
  45.7 7.0 %shard_map.151 = bf16[512,256]{1,0:T(8,128)(2,1)} custom-call(s32[1]{0:T(128)S(6)} %copy.24.live_ref, s32[1]{0:T(128)S(6)} %copy.25.depth_ref, bf16[512,640]{1,0:T(8,128)(2,1)} %get-tuple-element.10.q_ref, bf16[512,640]{1,0:T(8,128)(2,1)} %get-tuple-element.11.k_ref, bf16[512,640]{1,0:T(8,128)(2,1)} %get-tuple-element.12.v_ref, ...), custom_call_target="tpu_custom_call" | custom-call | tf_op jit(solution)/shard_map/pallas_call | solution.py:157
  52.7 3.2 %collective-permute-start.5 = (bf16[512,256]{1,0:T(8,128)(2,1)}, bf16[512,256]{1,0:T(8,128)(2,1)S(1)}, u32[]{:S(2)}, u32[]{:S(2)}) collective-permute-start(bf16[512,256]{1,0:T(8,128)(2,1)} %shard_map.151), channel_id=1, source_target_pairs={{128,0},{0,128},{129,1},{1,129},{130,2},{2,130},{131,3},{3,131},{1... | collective-permute-start | bytes 786440 | tf_op jit(solution)/shard_map/ppermute | solution.py:22
  55.8 9.6 %shard_map.150 = bf16[512,384]{1,0:T(8,128)(2,1)} custom-call(s32[1]{0:T(128)S(6)} %copy.24.live_ref, s32[1]{0:T(128)S(6)} %copy.25.depth_ref, bf16[512,640]{1,0:T(8,128)(2,1)} %get-tuple-element.10.q_ref, bf16[512,640]{1,0:T(8,128)(2,1)} %get-tuple-element.11.k_ref, bf16[512,640]{1,0:T(8,128)(2,1)} %get-tuple-element.12.v_ref, ...), custom_call_target="tpu_custom_call" | custom-call | tf_op jit(solution)/shard_map/pallas_call | solution.py:157
  65.4 0.0 copy-start.5
  65.4 0.0 copy-start.6
  65.4 0.3 collective-permute-start.4
  65.7 0.0 collective-permute-done.7
  65.7 0.1 broadcast.61.clone.1
  65.8 1.0 slice_dynamic-update-slice_fusion.3
  66.8 0.1 broadcast.61.clone
  66.9 1.0 slice_dynamic-update-slice_fusion.1
  67.9 0.0 collective-permute-done.8
  67.9 1.2 %slice_dynamic-update-slice_fusion = (bf16[2,256,640]{2,1,0:T(8,128)(2,1)S(1)}, bf16[2,256,640]{2,1,0:T(8,128)(2,1)S(1)}) fusion(bf16[2,256,640]{2,1,0:T(8,128)(2,1)S(1)} %slice_dynamic-update-slice_fusion.1, s32[]{:T(128)S(6)} %select_n.71, bf16[2,256,640]{2,1,0:T(8,128)(2,1)} %collective-permute-done.8, ...), kind=kLoop, calls=%fused_computation.23 | loop fusion | bytes 1310724 | tf_op jit(solution)/shard_map/jit(dynamic_update_index_in_dim)/dynamic_update_slice | solution.py:221
  69.1 0.0 copy-start.7
  69.1 0.0 copy-start.8
  69.1 26.0 %collective-permute-done.4 = bf16[512,384]{1,0:T(8,128)(2,1)S(1)} collective-permute-done((bf16[512,384]{1,0:T(8,128)(2,1)}, bf16[512,384]{1,0:T(8,128)(2,1)S(1)}, u32[]{:S(2)}, u32[]{:S(2)}) %collective-permute-start.4) | collective-permute-done | bytes 393248 | tf_op jit(solution)/shard_map/ppermute | solution.py:22
  95.1 0.0 collective-permute-done.5
  95.2 0.0 copy-done.5
  95.2 0.0 copy-done.6
  95.2 0.2 broadcast_select_fusion.3
  95.4 0.0 collective-permute-done.6
  95.5 2.1 %broadcast_select_fusion.1 = (bf16[640,1280]{1,0:T(8,128)(2,1)S(1)}, bf16[640,1280]{1,0:T(8,128)(2,1)S(1)}) fusion(bf16[640,1280]{1,0:T(8,128)(2,1)} %param.17, bf16[640,1280]{1,0:T(8,128)(2,1)} %collective-permute-done.6, pred[]{:T(512)S(6)} %eq.9), kind=kLoop, calls=%fused_computation.14 | loop fusion | flops 1638400 | bytes 6553601 | tf_op jit(solution)/shard_map/jit(_where)/select_n | solution.py:54
  97.6 0.0 copy-done.7
  97.6 0.0 copy-done.8
  97.6 0.0 copy-start.1
  97.6 0.0 copy-start.9
  97.6 2.0 %multiply_reduce_fusion.1 = (f32[512]{0:T(512)S(1)}, f32[512,1280]{1,0:T(8,128)S(1)}) fusion(bf16[640,1280]{1,0:T(8,128)(2,1)S(1)} %get-tuple-element.18, bf16[640,1280]{1,0:T(8,128)(2,1)S(1)} %get-tuple-element.17, bf16[512,640]{1,0:T(8,128)(2,1)S(1)} %get-tuple-element.20, bf16[512,640]{1,0:T(8,128)(2,1)S(1)} %get-tuple-element.19), kind=kOutput, calls=%fused_computation.12 | convolution fusion | flops 1688206848 | bytes 7211008 | tf_op jit(solution)/shard_map/dot_general | solution.py:260
  99.6 0.0 copy-done.1
  99.6 0.0 copy-done.9
  99.6 0.8 multiply_reduce_fusion
  100.5 1.8 %multiply_convert_fusion = bf16[512,1280]{1,0:T(8,128)(2,1)} fusion(f32[512]{0:T(512)S(1)} %add_rsqrt_fusion, f32[512,1280]{1,0:T(8,128)S(1)} %get-tuple-element.30, f32[512]{0:T(512)S(1)} %add_rsqrt_fusion.1, f32[1280]{0:T(1024)S(1)} %copy-done.9, f32[512]{0:T(512)S(1)} %add_rsqrt_fusion.2, bf16[512,1280]{1,0:T(8,128)(2,1)S(1)} %copy-done.1), kind=kLoop, calls=%fused_computation.10 | loop fusion | flops 5242880 | bytes 5254144 | tf_op jit(solution)/shard_map/convert_element_type | solution.py:266
  (5 shorter events, 0.1 us)
Async XLA Ops:
  0.6 12.0 %copy-start = (bf16[512,1280]{1,0:T(8,128)(2,1)S(1)}, bf16[512,1280]{1,0:T(8,128)(2,1)}, u32[]{:S(2)}) copy-start(bf16[512,1280]{1,0:T(8,128)(2,1)} %x_ref.1) | copy-start | bytes 3932164
  0.6 13.2 %copy-start.10 = (f32[640]{0:T(1024)S(1)}, f32[640]{0:T(1024)}, u32[]{:S(2)}) copy-start(f32[640]{0:T(1024)} %param.18) | copy-start | bytes 7684
  7.3 19.3 %collective-permute-start = (bf16[2,256,640]{2,1,0:T(8,128)(2,1)}, bf16[2,256,640]{2,1,0:T(8,128)(2,1)S(1)}, u32[]{:S(2)}, u32[]{:S(2)}) collective-permute-start(bf16[2,256,640]{2,1,0:T(8,128)(2,1)} %get-tuple-element.13), channel_id=1, source_target_pairs={{1,0},{2,1},{3,2},{4,3},{5,4},{6,5},{7,6},{8,7},{9,8},{10,9},{11,1... | collective-permute-start | bytes 1966088 | tf_op jit(solution)/shard_map/ppermute | solution.py:22
  7.9 29.3 %collective-permute-start.1 = (bf16[2,256,640]{2,1,0:T(8,128)(2,1)}, bf16[2,256,640]{2,1,0:T(8,128)(2,1)S(1)}, u32[]{:S(2)}, u32[]{:S(2)}) collective-permute-start(bf16[2,256,640]{2,1,0:T(8,128)(2,1)} %get-tuple-element.14), channel_id=1, source_target_pairs={{33,0},{34,1},{35,2},{36,3},{37,4},{38,5},{39,6},{40,7},{41,8},{42... | collective-permute-start | bytes 1966088 | tf_op jit(solution)/shard_map/ppermute | solution.py:22
  10.8 32.2 %collective-permute-start.2 = (bf16[2,256,640]{2,1,0:T(8,128)(2,1)}, bf16[2,256,640]{2,1,0:T(8,128)(2,1)S(1)}, u32[]{:S(2)}, u32[]{:S(2)}) collective-permute-start(bf16[2,256,640]{2,1,0:T(8,128)(2,1)} %get-tuple-element.15), channel_id=1, source_target_pairs={{65,0},{66,1},{67,2},{68,3},{69,4},{70,5},{71,6},{72,7},{73,8},{74... | collective-permute-start | bytes 1966088 | tf_op jit(solution)/shard_map/ppermute | solution.py:22
  11.7 34.0 %collective-permute-start.3 = (bf16[2,256,640]{2,1,0:T(8,128)(2,1)}, bf16[2,256,640]{2,1,0:T(8,128)(2,1)}, u32[]{:S(2)}, u32[]{:S(2)}) collective-permute-start(bf16[2,256,640]{2,1,0:T(8,128)(2,1)} %get-tuple-element.16), channel_id=1, source_target_pairs={{97,0},{98,1},{99,2},{100,3},{101,4},{102,5},{103,6},{104,7},{105,... | collective-permute-start | bytes 1966088 | tf_op jit(solution)/shard_map/ppermute | solution.py:22
  23.5 13.8 %copy-start.11 = (s32[256]{0:T(256)S(1)}, s32[256]{0:T(256)}, u32[]{:S(2)}) copy-start(s32[256]{0:T(256)} %param.25) | copy-start | bytes 3076
  25.0 40.7 %collective-permute-start.7 = (bf16[2,256,640]{2,1,0:T(8,128)(2,1)S(1)}, bf16[2,256,640]{2,1,0:T(8,128)(2,1)}, u32[]{:S(2)}, u32[]{:S(2)}) collective-permute-start(bf16[2,256,640]{2,1,0:T(8,128)(2,1)S(1)} %pad_maximum_fusion.1), channel_id=1, source_target_pairs={{96,0},{97,1},{98,2},{99,3},{100,4},{101,5},{102,6},{103,7},{104,8... | collective-permute-start | bytes 1966088 | tf_op jit(solution)/shard_map/ppermute | solution.py:22
  26.6 19.1 %copy-start.2 = (bf16[2,256,640]{2,1,0:T(8,128)(2,1)}, bf16[2,256,640]{2,1,0:T(8,128)(2,1)S(1)}, u32[]{:S(2)}) copy-start(bf16[2,256,640]{2,1,0:T(8,128)(2,1)S(1)} %collective-permute-done.refs_0_.refs_4_) | copy-start | bytes 1966084
  26.6 68.8 %collective-permute-start.6 = (bf16[640,1280]{1,0:T(8,128)(2,1)}, bf16[640,1280]{1,0:T(8,128)(2,1)}, u32[]{:S(2)}, u32[]{:S(2)}) collective-permute-start(bf16[640,1280]{1,0:T(8,128)(2,1)} %param.17), channel_id=1, source_target_pairs={{128,0},{0,128},{129,1},{1,129},{130,2},{2,130},{131,3},{3,131},{1... | collective-permute-start | bytes 4915208 | tf_op jit(solution)/shard_map/ppermute | solution.py:22
  37.3 8.4 %copy-start.3 = (bf16[2,256,640]{2,1,0:T(8,128)(2,1)}, bf16[2,256,640]{2,1,0:T(8,128)(2,1)S(1)}, u32[]{:S(2)}) copy-start(bf16[2,256,640]{2,1,0:T(8,128)(2,1)S(1)} %collective-permute-done.1.refs_1_.refs_5_) | copy-start | bytes 1966084
  37.3 30.6 %collective-permute-start.8 = (bf16[2,256,640]{2,1,0:T(8,128)(2,1)S(1)}, bf16[2,256,640]{2,1,0:T(8,128)(2,1)}, u32[]{:S(2)}, u32[]{:S(2)}) collective-permute-start(bf16[2,256,640]{2,1,0:T(8,128)(2,1)S(1)} %pad_maximum_fusion.2), channel_id=1, source_target_pairs={{32,0},{33,1},{34,2},{35,3},{36,4},{37,5},{38,6},{39,7},{40,8},{41... | collective-permute-start | bytes 1966088 | tf_op jit(solution)/shard_map/ppermute | solution.py:22
  43.0 2.8 %copy-start.4 = (bf16[2,256,640]{2,1,0:T(8,128)(2,1)}, bf16[2,256,640]{2,1,0:T(8,128)(2,1)S(1)}, u32[]{:S(2)}) copy-start(bf16[2,256,640]{2,1,0:T(8,128)(2,1)S(1)} %collective-permute-done.2.refs_2_.refs_6_) | copy-start | bytes 1966084
  52.7 42.5 %collective-permute-start.5 = (bf16[512,256]{1,0:T(8,128)(2,1)}, bf16[512,256]{1,0:T(8,128)(2,1)S(1)}, u32[]{:S(2)}, u32[]{:S(2)}) collective-permute-start(bf16[512,256]{1,0:T(8,128)(2,1)} %shard_map.151), channel_id=1, source_target_pairs={{128,0},{0,128},{129,1},{1,129},{130,2},{2,130},{131,3},{3,131},{1... | collective-permute-start | bytes 786440 | tf_op jit(solution)/shard_map/ppermute | solution.py:22
  65.4 29.8 %copy-start.5 = (bf16[512,384]{1,0:T(8,128)(2,1)S(1)}, bf16[512,384]{1,0:T(8,128)(2,1)}, u32[]{:S(2)}) copy-start(bf16[512,384]{1,0:T(8,128)(2,1)} %shard_map.150) | copy-start | bytes 1179652
  65.4 29.8 %copy-start.6 = (bf16[512,256]{1,0:T(8,128)(2,1)S(1)}, bf16[512,256]{1,0:T(8,128)(2,1)}, u32[]{:S(2)}) copy-start(bf16[512,256]{1,0:T(8,128)(2,1)} %shard_map.151) | copy-start | bytes 786436
  65.4 29.7 %collective-permute-start.4 = (bf16[512,384]{1,0:T(8,128)(2,1)}, bf16[512,384]{1,0:T(8,128)(2,1)S(1)}, u32[]{:S(2)}, u32[]{:S(2)}) collective-permute-start(bf16[512,384]{1,0:T(8,128)(2,1)} %shard_map.150), channel_id=1, source_target_pairs={{128,0},{0,128},{129,1},{1,129},{130,2},{2,130},{131,3},{3,131},{1... | collective-permute-start | bytes 1179656 | tf_op jit(solution)/shard_map/ppermute | solution.py:22
  69.1 28.5 %copy-start.7 = (bf16[2,256,640]{2,1,0:T(8,128)(2,1)}, bf16[2,256,640]{2,1,0:T(8,128)(2,1)S(1)}, u32[]{:S(2)}) copy-start(bf16[2,256,640]{2,1,0:T(8,128)(2,1)S(1)} %get-tuple-element.21) | copy-start | bytes 1966084
  69.1 28.5 %copy-start.8 = (bf16[2,256,640]{2,1,0:T(8,128)(2,1)}, bf16[2,256,640]{2,1,0:T(8,128)(2,1)S(1)}, u32[]{:S(2)}) copy-start(bf16[2,256,640]{2,1,0:T(8,128)(2,1)S(1)} %get-tuple-element.22) | copy-start | bytes 1966084
  97.6 2.0 %copy-start.1 = (bf16[512,1280]{1,0:T(8,128)(2,1)S(1)}, bf16[512,1280]{1,0:T(8,128)(2,1)}, u32[]{:S(2)}) copy-start(bf16[512,1280]{1,0:T(8,128)(2,1)} %x_ref.1) | copy-start | bytes 3932164
  97.6 2.0 %copy-start.9 = (f32[1280]{0:T(1024)S(1)}, f32[1280]{0:T(1024)}, u32[]{:S(2)}) copy-start(f32[1280]{0:T(1024)} %param.19) | copy-start | bytes 15364

commit v11 on v10

--- a/solution.py
+++ b/solution.py
@@ -47,6 +47,19 @@
         preferred_element_type=jnp.float32,
     )
     return (totals, mixed)
+
+
+def other_half_once_per_chip(w_out):
+    rows = w_out.shape[0] // 2
+    core = lax.axis_index("blk") % 2
+    mine = lax.dynamic_slice_in_dim(w_out, core * rows, rows, 0)
+    pulled = from_behind(mine, "kv", 1)
+    devices = lax.axis_size("blk")
+    swapped = lax.ppermute(pulled, "blk", [(i, i ^ 1) for i in range(devices)])
+    first = core == 0
+    return jnp.concatenate(
+        [jnp.where(first, pulled, swapped), jnp.where(first, swapped, pulled)], axis=0
+    )
 
 
 def in_kv_order(mine, other, axis):
@@ -238,7 +251,7 @@
     placement,
 ):
     tokens_here = hidden_in.shape[0]
-    other_w_out = from_behind(w_out, "kv", 1)
+    other_w_out = other_half_once_per_chip(w_out)
     width_half = w_query.shape[1]
     heads_here = width_half // HD
     hidden_f = hidden_in.astype(jnp.float32)

time: 103 us -> 89.9 us (0.87)
  the two profiles are of different devices: /device:TPU:225 before, /device:TPU:6 now
where the time goes in v11:
time: 89.9 us; the launch traced here: 88.9 us
  Pallas kernels  30.7 us (34%)
  starting transfers between devices  18 us (20%)
  waiting for transfers between devices  16 us (18%)
  local copies, waits for them, and re-layouts  10.5 us (12%)
  between operations  5.84 us (6%)
  other arithmetic  5.78 us (6%)
  matrix products  1.98 us (2%)
    ppermute x9, starting transfers between devices, from_behind(): return lax.ppermute(block, axis, route)  17.8 us
    pallas_call x2, Pallas kernels, attention(): pl.pallas_call(attention_kernel, out_shape=jax.ShapeDtypeStruct((tokens,...  16.5 us
    ppermute x9, waiting for transfers between devices, from_behind(): return lax.ppermute(block, axis, route)  16 us
    pallas_call x1, Pallas kernels, projections(): pl.pallas_call(projection_kernel, out_shape=(shape, shape, shape), grid=(...  9.11 us
    pallas_call x1, Pallas kernels, fetch_pages(): pl.pallas_call(functools.partial(gather_kernel, devices), out_shape=[page...  5.08 us
    unnamed x28, local copies, waits for them, and re-layouts  2.65 us
    dynamic_slice x1, local copies, waits for them, and re-layouts, other_half_once_per_chip(): mine = lax.dynamic_slice_in_dim(w_out, core * rows, rows, 0)  2.09 us
    dot_general x1, matrix products, body(): jnp.dot(in_kv_order(attended, other_attended, 1), in_kv_order(w_out, othe...  1.98 us
  transfers between devices with their start and end apart: 10, of which 4 were waited for; matrix products, arithmetic and copies ran while one was open for 12% of the time, Pallas kernels for 29%

profile of v11, /device:TPU:6, one launch (start us, length us, event | category | flops | bytes accessed | tf_op | source)
XLA Modules:
  0.0 88.9 jit_solution(6856057410982691398)
XLA Ops:
  0.6 0.0 copy-start
  0.6 0.0 copy-start.11
  0.7 1.5 %copy.18.pages_ref = s32[128,4]{1,0:T(8,128)} copy(s32[128,4]{0,1:T(4,128)} %param.24) | data formatting | bytes 4096 | tf_op args[11]
  2.2 5.1 %shard_map.149 = (bf16[2,256,640]{2,1,0:T(8,128)(2,1)}, bf16[2,256,640]{2,1,0:T(8,128)(2,1)}, bf16[2,256,640]{2,1,0:T(8,128)(2,1)}, bf16[2,256,640]{2,1,0:T(8,128)(2,1)}) custom-call(s32[128,4]{1,0:T(8,128)} %copy.18.pages_ref, bf16[4,256,640]{2,1,0:T(8,128)(2,1)} %keys_hbm.1, bf16[4,256,640]{2,1,0:T(8,128)(2,1)} %values_hbm.1), custom_call_target="tpu_custom_call" | custom-call | tf_op jit(solution)/shard_map/pallas_call | solution.py:206
  7.3 6.6 %collective-permute-start = (bf16[2,256,640]{2,1,0:T(8,128)(2,1)}, bf16[2,256,640]{2,1,0:T(8,128)(2,1)S(1)}, u32[]{:S(2)}, u32[]{:S(2)}) collective-permute-start(bf16[2,256,640]{2,1,0:T(8,128)(2,1)} %get-tuple-element.13), channel_id=1, source_target_pairs={{1,0},{2,1},{3,2},{4,3},{5,4},{6,5},{7,6},{8,7},{9,8},{10,9},{11,1... | collective-permute-start | bytes 1966088 | tf_op jit(solution)/shard_map/ppermute | solution.py:22
  13.9 1.3 %collective-permute-start.1 = (bf16[2,256,640]{2,1,0:T(8,128)(2,1)}, bf16[2,256,640]{2,1,0:T(8,128)(2,1)S(1)}, u32[]{:S(2)}, u32[]{:S(2)}) collective-permute-start(bf16[2,256,640]{2,1,0:T(8,128)(2,1)} %get-tuple-element.14), channel_id=1, source_target_pairs={{33,0},{34,1},{35,2},{36,3},{37,4},{38,5},{39,6},{40,7},{41,8},{42... | collective-permute-start | bytes 1966088 | tf_op jit(solution)/shard_map/ppermute | solution.py:22
  15.2 1.8 %collective-permute-start.2 = (bf16[2,256,640]{2,1,0:T(8,128)(2,1)}, bf16[2,256,640]{2,1,0:T(8,128)(2,1)S(1)}, u32[]{:S(2)}, u32[]{:S(2)}) collective-permute-start(bf16[2,256,640]{2,1,0:T(8,128)(2,1)} %get-tuple-element.15), channel_id=1, source_target_pairs={{65,0},{66,1},{67,2},{68,3},{69,4},{70,5},{71,6},{72,7},{73,8},{74... | collective-permute-start | bytes 1966088 | tf_op jit(solution)/shard_map/ppermute | solution.py:22
  17.0 0.0 collective-permute-start.3
  17.0 0.0 copy-done
  17.0 0.3 fusion.7
  17.3 0.9 copy.17.scale_ref
  18.2 0.0 copy-done.11
  18.2 0.6 reshape.53.gain_ref
  18.8 9.1 %shard_map.148 = (bf16[512,640]{1,0:T(8,128)(2,1)}, bf16[512,640]{1,0:T(8,128)(2,1)}, bf16[512,640]{1,0:T(8,128)(2,1)}) custom-call(bf16[512,1280]{1,0:T(8,128)(2,1)} %x_ref.1, f32[512,1]{1,0:T(8,128)} %copy.17.scale_ref, bf16[1280,640]{1,0:T(8,128)(2,1)} %wq_ref.1, bf16[1280,640]{1,0:T(8,128)(2,1)} %wk_ref.1, bf16[1280,640]{1,0:T(8,128)(2,1)} %wv_ref.1, ...), custom_call_target="tpu_custom_call" | custom-call | tf_op jit(solution)/shard_map/pallas_call | solution.py:98
  27.9 1.4 %slice_bitcast_fusion = (bf16[1,256,640]{2,1,0:T(8,128)(2,1)S(1)}, bf16[1,256,640]{2,1,0:T(8,128)(2,1)S(1)}, bf16[1,256,640]{2,1,0:T(8,128)(2,1)S(1)}, bf16[1,256,640]{2,1,0:T(8,128)(2,1)S(1)}) fusion(bf16[512,640]{1,0:T(8,128)(2,1)} %get-tuple-element.12.v_ref, bf16[512,640]{1,0:T(8,128)(2,1)} %get-tuple-element.11.k_ref), kind=kLoop, calls=%fused_computation.30 | loop fusion | bytes 2621440 | tf_op jit(solution)/shard_map/slice | solution.py:229
  29.3 0.0 copy-start.12
  29.3 0.9 %pad_maximum_fusion.2 = bf16[2,256,640]{2,1,0:T(8,128)(2,1)} fusion(bf16[1,256,640]{2,1,0:T(8,128)(2,1)S(1)} %get-tuple-element.28, bf16[1,256,640]{2,1,0:T(8,128)(2,1)S(1)} %get-tuple-element.33), kind=kLoop, calls=%fused_computation.22 | loop fusion | flops 327680 | bytes 1310720 | tf_op jit(solution)/shard_map/stack | solution.py:229
  30.3 1.5 %collective-permute-start.8 = (bf16[2,256,640]{2,1,0:T(8,128)(2,1)}, bf16[2,256,640]{2,1,0:T(8,128)(2,1)}, u32[]{:S(2)}, u32[]{:S(2)}) collective-permute-start(bf16[2,256,640]{2,1,0:T(8,128)(2,1)} %pad_maximum_fusion.2), channel_id=1, source_target_pairs={{96,0},{97,1},{98,2},{99,3},{100,4},{101,5},{102,6},{103,7},{104,8... | collective-permute-start | bytes 1966088 | tf_op jit(solution)/shard_map/ppermute | solution.py:22
  31.8 2.1 %constant_dynamic-slice_fusion = bf16[320,1280]{1,0:T(8,128)(2,1)} fusion(bf16[640,1280]{1,0:T(8,128)(2,1)} %param.17, s32[]{:T(128)S(6)} %select_n.83), kind=kLoop, calls=%fused_computation.39 | loop fusion | bytes 1638404 | tf_op jit(solution)/shard_map/dynamic_slice | solution.py:55
  33.8 0.0 collective-permute-done.refs_0_.refs_4_
  33.9 2.9 %collective-permute-start.6 = (bf16[320,1280]{1,0:T(8,128)(2,1)}, bf16[320,1280]{1,0:T(8,128)(2,1)S(1)}, u32[]{:S(2)}, u32[]{:S(2)}) collective-permute-start(bf16[320,1280]{1,0:T(8,128)(2,1)} %constant_dynamic-slice_fusion), channel_id=1, source_target_pairs={{128,0},{0,128},{129,1},{1,129},{130,2},{2,130},{131,3},{3,131},{1... | collective-permute-start | bytes 2457608 | tf_op jit(solution)/shard_map/ppermute | solution.py:22
  36.8 0.9 %pad_maximum_fusion.3 = bf16[2,256,640]{2,1,0:T(8,128)(2,1)} fusion(bf16[1,256,640]{2,1,0:T(8,128)(2,1)S(1)} %get-tuple-element.27, bf16[1,256,640]{2,1,0:T(8,128)(2,1)S(1)} %get-tuple-element.34), kind=kLoop, calls=%fused_computation.23 | loop fusion | flops 327680 | bytes 1310720 | tf_op jit(solution)/shard_map/stack | solution.py:229
  37.7 1.3 %collective-permute-done.1.refs_1_.refs_5_ = bf16[2,256,640]{2,1,0:T(8,128)(2,1)S(1)} collective-permute-done((bf16[2,256,640]{2,1,0:T(8,128)(2,1)}, bf16[2,256,640]{2,1,0:T(8,128)(2,1)S(1)}, u32[]{:S(2)}, u32[]{:S(2)}) %collective-permute-start.1) | collective-permute-done | bytes 655392 | tf_op jit(solution)/shard_map/ppermute | solution.py:22
  39.0 0.0 collective-permute-start.9
  39.0 0.0 copy-done.12
  39.0 0.7 fusion.12
  44.6 5.6 %collective-permute-done.2.refs_2_.refs_6_ = bf16[2,256,640]{2,1,0:T(8,128)(2,1)S(1)} collective-permute-done((bf16[2,256,640]{2,1,0:T(8,128)(2,1)}, bf16[2,256,640]{2,1,0:T(8,128)(2,1)S(1)}, u32[]{:S(2)}, u32[]{:S(2)}) %collective-permute-start.2) | collective-permute-done | bytes 655392 | tf_op jit(solution)/shard_map/ppermute | solution.py:22
  50.3 4.3 %collective-permute-done.3.refs_3_.refs_7_ = bf16[2,256,640]{2,1,0:T(8,128)(2,1)} collective-permute-done((bf16[2,256,640]{2,1,0:T(8,128)(2,1)}, bf16[2,256,640]{2,1,0:T(8,128)(2,1)}, u32[]{:S(2)}, u32[]{:S(2)}) %collective-permute-start.3) | collective-permute-done | bytes 655392 | tf_op jit(solution)/shard_map/ppermute | solution.py:22
  54.6 0.0 copy-done.2
  54.6 0.0 copy-done.3
  54.6 0.0 copy-done.4
  54.6 9.5 %shard_map.150 = bf16[512,384]{1,0:T(8,128)(2,1)} custom-call(s32[1]{0:T(128)S(6)} %copy.24.live_ref, s32[1]{0:T(128)S(6)} %copy.25.depth_ref, bf16[512,640]{1,0:T(8,128)(2,1)} %get-tuple-element.10.q_ref, bf16[512,640]{1,0:T(8,128)(2,1)} %get-tuple-element.11.k_ref, bf16[512,640]{1,0:T(8,128)(2,1)} %get-tuple-element.12.v_ref, ...), custom_call_target="tpu_custom_call" | custom-call | tf_op jit(solution)/shard_map/pallas_call | solution.py:170
  64.1 2.9 %collective-permute-start.4 = (bf16[512,384]{1,0:T(8,128)(2,1)}, bf16[512,384]{1,0:T(8,128)(2,1)S(1)}, u32[]{:S(2)}, u32[]{:S(2)}) collective-permute-start(bf16[512,384]{1,0:T(8,128)(2,1)} %shard_map.150), channel_id=1, source_target_pairs={{128,0},{0,128},{129,1},{1,129},{130,2},{2,130},{131,3},{3,131},{1... | collective-permute-start | bytes 1179656 | tf_op jit(solution)/shard_map/ppermute | solution.py:22
  67.0 7.0 %shard_map.151 = bf16[512,256]{1,0:T(8,128)(2,1)} custom-call(s32[1]{0:T(128)S(6)} %copy.24.live_ref, s32[1]{0:T(128)S(6)} %copy.25.depth_ref, bf16[512,640]{1,0:T(8,128)(2,1)} %get-tuple-element.10.q_ref, bf16[512,640]{1,0:T(8,128)(2,1)} %get-tuple-element.11.k_ref, bf16[512,640]{1,0:T(8,128)(2,1)} %get-tuple-element.12.v_ref, ...), custom_call_target="tpu_custom_call" | custom-call | tf_op jit(solution)/shard_map/pallas_call | solution.py:170
  74.0 0.0 copy-start.7
  74.0 0.7 collective-permute-start.5
  74.7 0.0 collective-permute-done.8
  74.7 0.1 broadcast.62.clone
  74.8 1.0 %slice_dynamic-update-slice_fusion.1 = bf16[2,256,640]{2,1,0:T(8,128)(2,1)S(1)} fusion(bf16[2,256,640]{2,1,0:T(8,128)(2,1)S(1)} %broadcast.62.clone, s32[]{:T(128)S(6)} %select_n.91, bf16[2,256,640]{2,1,0:T(8,128)(2,1)} %collective-permute-done.8), kind=kLoop, calls=%fused_computation.27 | loop fusion | bytes 655364 | tf_op jit(solution)/shard_map/jit(dynamic_update_index_in_dim)/dynamic_update_slice | solution.py:234
  75.8 0.0 collective-permute-done.6
  75.8 0.3 collective-permute-start.7
  76.1 0.1 broadcast.62.clone.1
  76.2 1.0 %slice_dynamic-update-slice_fusion.3 = bf16[2,256,640]{2,1,0:T(8,128)(2,1)S(1)} fusion(bf16[2,256,640]{2,1,0:T(8,128)(2,1)S(1)} %broadcast.62.clone.1, s32[]{:T(128)S(6)} %select_n.91, bf16[2,256,640]{2,1,0:T(8,128)(2,1)} %collective-permute-done.8), kind=kLoop, calls=%fused_computation.29 | loop fusion | bytes 655364 | tf_op jit(solution)/shard_map/jit(dynamic_update_index_in_dim)/dynamic_update_slice | solution.py:233
  77.2 0.0 collective-permute-done.9
  77.2 0.1 slice_dynamic-update-slice_fusion
  77.3 0.0 copy-start.8
  77.3 0.0 copy-start.9
  77.3 0.0 collective-permute-done.4
  77.4 4.8 %collective-permute-done.5 = bf16[512,256]{1,0:T(8,128)(2,1)S(1)} collective-permute-done((bf16[512,256]{1,0:T(8,128)(2,1)}, bf16[512,256]{1,0:T(8,128)(2,1)S(1)}, u32[]{:S(2)}, u32[]{:S(2)}) %collective-permute-start.5) | collective-permute-done | bytes 262176 | tf_op jit(solution)/shard_map/ppermute | solution.py:22
  82.2 0.0 copy-done.6
  82.2 0.0 copy-done.7
  82.2 0.0 copy-start.5
  82.2 0.2 broadcast_select_fusion.5
  82.5 0.0 collective-permute-done.7
  82.5 0.1 broadcast_select_fusion.3
  82.6 0.0 copy-done.8
  82.6 0.0 copy-done.9
  82.6 1.0 %copy-done.5 = bf16[640,1280]{1,0:T(8,128)(2,1)S(1)} copy-done((bf16[640,1280]{1,0:T(8,128)(2,1)S(1)}, bf16[640,1280]{1,0:T(8,128)(2,1)}, u32[]{:S(2)}) %copy-start.5) | copy-done | bytes 1638424
  83.7 0.6 broadcast_select_fusion.1
  84.2 0.0 copy-start.1
  84.3 0.0 copy-start.10
  84.3 2.0 %multiply_reduce_fusion.1 = (f32[512]{0:T(512)S(1)}, f32[512,1280]{1,0:T(8,128)S(1)}) fusion(bf16[640,1280]{1,0:T(8,128)(2,1)S(1)} %get-tuple-element.18, bf16[640,1280]{1,0:T(8,128)(2,1)S(1)} %get-tuple-element.17, bf16[512,640]{1,0:T(8,128)(2,1)S(1)} %get-tuple-element.22, bf16[512,640]{1,0:T(8,128)(2,1)S(1)} %get-tuple-element.21), kind=kOutput, calls=%fused_computation.12 | convolution fusion | flops 1688206848 | bytes 7211008 | tf_op jit(solution)/shard_map/dot_general | solution.py:273
  86.3 0.8 multiply_reduce_fusion
  87.1 1.8 %multiply_convert_fusion = bf16[512,1280]{1,0:T(8,128)(2,1)} fusion(f32[512]{0:T(512)S(1)} %add_rsqrt_fusion, f32[512,1280]{1,0:T(8,128)S(1)} %get-tuple-element.32, f32[512]{0:T(512)S(1)} %add_rsqrt_fusion.1, f32[1280]{0:T(1024)S(1)} %copy-done.10, f32[512]{0:T(512)S(1)} %add_rsqrt_fusion.2, bf16[512,1280]{1,0:T(8,128)(2,1)S(1)} %copy-done.1), kind=kLoop, calls=%fused_computation.10 | loop fusion | flops 5242880 | bytes 5254144 | tf_op jit(solution)/shard_map/convert_element_type | solution.py:279
  (11 shorter events, 0.1 us)
Async XLA Ops:
  0.6 16.4 %copy-start = (bf16[512,1280]{1,0:T(8,128)(2,1)S(1)}, bf16[512,1280]{1,0:T(8,128)(2,1)}, u32[]{:S(2)}) copy-start(bf16[512,1280]{1,0:T(8,128)(2,1)} %x_ref.1) | copy-start | bytes 3932164
  0.6 17.6 %copy-start.11 = (f32[640]{0:T(1024)S(1)}, f32[640]{0:T(1024)}, u32[]{:S(2)}) copy-start(f32[640]{0:T(1024)} %param.18) | copy-start | bytes 7684
  7.3 26.6 %collective-permute-start = (bf16[2,256,640]{2,1,0:T(8,128)(2,1)}, bf16[2,256,640]{2,1,0:T(8,128)(2,1)S(1)}, u32[]{:S(2)}, u32[]{:S(2)}) collective-permute-start(bf16[2,256,640]{2,1,0:T(8,128)(2,1)} %get-tuple-element.13), channel_id=1, source_target_pairs={{1,0},{2,1},{3,2},{4,3},{5,4},{6,5},{7,6},{8,7},{9,8},{10,9},{11,1... | collective-permute-start | bytes 1966088 | tf_op jit(solution)/shard_map/ppermute | solution.py:22
  13.9 25.1 %collective-permute-start.1 = (bf16[2,256,640]{2,1,0:T(8,128)(2,1)}, bf16[2,256,640]{2,1,0:T(8,128)(2,1)S(1)}, u32[]{:S(2)}, u32[]{:S(2)}) collective-permute-start(bf16[2,256,640]{2,1,0:T(8,128)(2,1)} %get-tuple-element.14), channel_id=1, source_target_pairs={{33,0},{34,1},{35,2},{36,3},{37,4},{38,5},{39,6},{40,7},{41,8},{42... | collective-permute-start | bytes 1966088 | tf_op jit(solution)/shard_map/ppermute | solution.py:22
  15.2 35.1 %collective-permute-start.2 = (bf16[2,256,640]{2,1,0:T(8,128)(2,1)}, bf16[2,256,640]{2,1,0:T(8,128)(2,1)S(1)}, u32[]{:S(2)}, u32[]{:S(2)}) collective-permute-start(bf16[2,256,640]{2,1,0:T(8,128)(2,1)} %get-tuple-element.15), channel_id=1, source_target_pairs={{65,0},{66,1},{67,2},{68,3},{69,4},{70,5},{71,6},{72,7},{73,8},{74... | collective-permute-start | bytes 1966088 | tf_op jit(solution)/shard_map/ppermute | solution.py:22
  17.0 37.6 %collective-permute-start.3 = (bf16[2,256,640]{2,1,0:T(8,128)(2,1)}, bf16[2,256,640]{2,1,0:T(8,128)(2,1)}, u32[]{:S(2)}, u32[]{:S(2)}) collective-permute-start(bf16[2,256,640]{2,1,0:T(8,128)(2,1)} %get-tuple-element.16), channel_id=1, source_target_pairs={{97,0},{98,1},{99,2},{100,3},{101,4},{102,5},{103,6},{104,7},{105,... | collective-permute-start | bytes 1966088 | tf_op jit(solution)/shard_map/ppermute | solution.py:22
  29.3 9.7 %copy-start.12 = (s32[256]{0:T(256)S(1)}, s32[256]{0:T(256)}, u32[]{:S(2)}) copy-start(s32[256]{0:T(256)} %param.25) | copy-start | bytes 3076
  30.3 44.5 %collective-permute-start.8 = (bf16[2,256,640]{2,1,0:T(8,128)(2,1)}, bf16[2,256,640]{2,1,0:T(8,128)(2,1)}, u32[]{:S(2)}, u32[]{:S(2)}) collective-permute-start(bf16[2,256,640]{2,1,0:T(8,128)(2,1)} %pad_maximum_fusion.2), channel_id=1, source_target_pairs={{96,0},{97,1},{98,2},{99,3},{100,4},{101,5},{102,6},{103,7},{104,8... | collective-permute-start | bytes 1966088 | tf_op jit(solution)/shard_map/ppermute | solution.py:22
  33.9 20.7 %copy-start.2 = (bf16[2,256,640]{2,1,0:T(8,128)(2,1)}, bf16[2,256,640]{2,1,0:T(8,128)(2,1)S(1)}, u32[]{:S(2)}) copy-start(bf16[2,256,640]{2,1,0:T(8,128)(2,1)S(1)} %collective-permute-done.refs_0_.refs_4_) | copy-start | bytes 1966084
  33.9 41.9 %collective-permute-start.6 = (bf16[320,1280]{1,0:T(8,128)(2,1)}, bf16[320,1280]{1,0:T(8,128)(2,1)S(1)}, u32[]{:S(2)}, u32[]{:S(2)}) collective-permute-start(bf16[320,1280]{1,0:T(8,128)(2,1)} %constant_dynamic-slice_fusion), channel_id=1, source_target_pairs={{128,0},{0,128},{129,1},{1,129},{130,2},{2,130},{131,3},{3,131},{1... | collective-permute-start | bytes 2457608 | tf_op jit(solution)/shard_map/ppermute | solution.py:22
  39.0 15.6 %copy-start.3 = (bf16[2,256,640]{2,1,0:T(8,128)(2,1)}, bf16[2,256,640]{2,1,0:T(8,128)(2,1)S(1)}, u32[]{:S(2)}) copy-start(bf16[2,256,640]{2,1,0:T(8,128)(2,1)S(1)} %collective-permute-done.1.refs_1_.refs_5_) | copy-start | bytes 1966084
  39.0 38.2 %collective-permute-start.9 = (bf16[2,256,640]{2,1,0:T(8,128)(2,1)}, bf16[2,256,640]{2,1,0:T(8,128)(2,1)S(1)}, u32[]{:S(2)}, u32[]{:S(2)}) collective-permute-start(bf16[2,256,640]{2,1,0:T(8,128)(2,1)} %pad_maximum_fusion.3), channel_id=1, source_target_pairs={{32,0},{33,1},{34,2},{35,3},{36,4},{37,5},{38,6},{39,7},{40,8},{41... | collective-permute-start | bytes 1966088 | tf_op jit(solution)/shard_map/ppermute | solution.py:22
  50.2 4.3 %copy-start.4 = (bf16[2,256,640]{2,1,0:T(8,128)(2,1)}, bf16[2,256,640]{2,1,0:T(8,128)(2,1)S(1)}, u32[]{:S(2)}) copy-start(bf16[2,256,640]{2,1,0:T(8,128)(2,1)S(1)} %collective-permute-done.2.refs_2_.refs_6_) | copy-start | bytes 1966084
  64.1 13.2 %collective-permute-start.4 = (bf16[512,384]{1,0:T(8,128)(2,1)}, bf16[512,384]{1,0:T(8,128)(2,1)S(1)}, u32[]{:S(2)}, u32[]{:S(2)}) collective-permute-start(bf16[512,384]{1,0:T(8,128)(2,1)} %shard_map.150), channel_id=1, source_target_pairs={{128,0},{0,128},{129,1},{1,129},{130,2},{2,130},{131,3},{3,131},{1... | collective-permute-start | bytes 1179656 | tf_op jit(solution)/shard_map/ppermute | solution.py:22
  74.0 8.2 %copy-start.6 = (bf16[512,384]{1,0:T(8,128)(2,1)S(1)}, bf16[512,384]{1,0:T(8,128)(2,1)}, u32[]{:S(2)}) copy-start(bf16[512,384]{1,0:T(8,128)(2,1)} %shard_map.150) | copy-start | bytes 1179652
  74.0 8.2 %copy-start.7 = (bf16[512,256]{1,0:T(8,128)(2,1)S(1)}, bf16[512,256]{1,0:T(8,128)(2,1)}, u32[]{:S(2)}) copy-start(bf16[512,256]{1,0:T(8,128)(2,1)} %shard_map.151) | copy-start | bytes 786436
  74.0 8.2 %collective-permute-start.5 = (bf16[512,256]{1,0:T(8,128)(2,1)}, bf16[512,256]{1,0:T(8,128)(2,1)S(1)}, u32[]{:S(2)}, u32[]{:S(2)}) collective-permute-start(bf16[512,256]{1,0:T(8,128)(2,1)} %shard_map.151), channel_id=1, source_target_pairs={{128,0},{0,128},{129,1},{1,129},{130,2},{2,130},{131,3},{3,131},{1... | collective-permute-start | bytes 786440 | tf_op jit(solution)/shard_map/ppermute | solution.py:22
  75.8 6.7 %collective-permute-start.7 = (bf16[320,1280]{1,0:T(8,128)(2,1)S(1)}, bf16[320,1280]{1,0:T(8,128)(2,1)S(1)}, u32[]{:S(2)}, u32[]{:S(2)}) collective-permute-start(bf16[320,1280]{1,0:T(8,128)(2,1)S(1)} %collective-permute-done.6), channel_id=1, source_target_pairs={{0,1},{1,0},{2,3},{3,2},{4,5},{5,4},{6,7},{7,6},{8,9},{9,8},{10,11... | collective-permute-start | bytes 2457608 | tf_op jit(solution)/shard_map/ppermute | solution.py:58
  77.3 5.3 %copy-start.8 = (bf16[2,256,640]{2,1,0:T(8,128)(2,1)}, bf16[2,256,640]{2,1,0:T(8,128)(2,1)S(1)}, u32[]{:S(2)}) copy-start(bf16[2,256,640]{2,1,0:T(8,128)(2,1)S(1)} %get-tuple-element.24) | copy-start | bytes 1966084
  77.3 5.3 %copy-start.9 = (bf16[2,256,640]{2,1,0:T(8,128)(2,1)}, bf16[2,256,640]{2,1,0:T(8,128)(2,1)S(1)}, u32[]{:S(2)}) copy-start(bf16[2,256,640]{2,1,0:T(8,128)(2,1)S(1)} %get-tuple-element.23) | copy-start | bytes 1966084
  82.2 1.4 %copy-start.5 = (bf16[640,1280]{1,0:T(8,128)(2,1)S(1)}, bf16[640,1280]{1,0:T(8,128)(2,1)}, u32[]{:S(2)}) copy-start(bf16[640,1280]{1,0:T(8,128)(2,1)} %param.17) | copy-start | bytes 4915204
  84.2 2.0 %copy-start.1 = (bf16[512,1280]{1,0:T(8,128)(2,1)S(1)}, bf16[512,1280]{1,0:T(8,128)(2,1)}, u32[]{:S(2)}) copy-start(bf16[512,1280]{1,0:T(8,128)(2,1)} %x_ref.1) | copy-start | bytes 3932164
  84.3 2.0 %copy-start.10 = (f32[1280]{0:T(1024)S(1)}, f32[1280]{0:T(1024)}, u32[]{:S(2)}) copy-start(f32[1280]{0:T(1024)} %param.19) | copy-start | bytes 15364

commit v12 on v11

--- a/solution.py
+++ b/solution.py
@@ -214,7 +214,7 @@
     ]
 
 
-def relay(key_rows, value_rows, placement):
+def relay(key_rows, value_rows, placement, after):
     devices = lax.axis_size("blk")
     here = lax.axis_index("blk")
     blocks = key_rows.shape[0] // PAGE
@@ -223,11 +223,14 @@
     value_pages = value_rows.reshape(blocks, PAGE, width)
     key_out = jnp.zeros_like(key_pages)
     value_out = jnp.zeros_like(value_pages)
+    stacks = [
+        jnp.stack([key_pages[block_index], value_pages[block_index]])
+        for block_index in range(blocks)
+    ]
+    stacks, _ = lax.optimization_barrier((stacks, after))
     for block_index in range(blocks):
         offset = (2 * block_index + 1) * devices // (2 * blocks)
-        received = from_behind(
-            jnp.stack([key_pages[block_index], value_pages[block_index]]), "blk", offset
-        )
+        received = from_behind(stacks[block_index], "blk", offset)
         source = (here - offset) % devices
         target = placement[source * blocks + block_index] % blocks
         key_out = lax.dynamic_update_index_in_dim(key_out, received[0], target, 0)
@@ -277,7 +280,7 @@
     )
     updated = anchor + eigen_rate * (rms_scale(branch) - anchor)
     layer_out = rms_scale(updated).astype(jnp.bfloat16)
-    new_keys, new_values = relay(key_rows, value_rows, placement)
+    new_keys, new_values = relay(key_rows, value_rows, placement, fetched)
     return (layer_out, new_keys, new_values)
 
 

time: 89.9 us -> 96.6 us (1.075)
  waiting for transfers between devices: 16 us -> 22.7 us
  local copies, waits for them, and re-layouts: 10.5 us -> 8.71 us
  starting transfers between devices: 18 us -> 19 us
    ppermute x9, waiting for transfers between devices: 16 us -> 22.7 us  [from_behind(): return lax.ppermute(block, axis, route)]
    another operation x2, other arithmetic: 1.85 us -> 0.15 us  [relay(): jnp.stack([key_pages[block_index], value_pages[block_index]])]
    select_n x1, other arithmetic: 0.11 us -> 1.71 us  [other_half_once_per_chip(): jnp.where(first, pulled, swapped)]
    select_n x2, other arithmetic: 0.83 us -> 1.85 us  [in_kv_order(): low = jnp.where(first, mine, other)]
    dynamic_update_slice x2, local copies, waits for them, and re-layouts: 1.12 us -> 0.14 us  [relay(): lax.dynamic_update_index_in_dim(value_out, received[1], target, 0)]
    dynamic_update_slice x1, local copies, waits for them, and re-layouts: 1.02 us -> 0.05 us  [relay(): key_out = lax.dynamic_update_index_in_dim(key_out, received[0], target, 0)]
    unnamed x28 -> x26, local copies, waits for them, and re-layouts: 2.65 us -> 2.89 us
  transfers between devices with their start and end apart: 10 -> 10, of which waited for: 4 -> 5; matrix products, arithmetic and copies ran while one was open for 12% -> 9% of each run, Pallas kernels for 29% -> 27%
where the time goes in v12:
time: 96.6 us; the launch traced here: 96 us
  Pallas kernels  30.7 us (32%)
  waiting for transfers between devices  22.7 us (23%)
  starting transfers between devices  19 us (20%)
  local copies, waits for them, and re-layouts  8.71 us (9%)
  other arithmetic  6.71 us (7%)
  between operations  6.12 us (6%)
  matrix products  1.98 us (2%)
    ppermute x9, waiting for transfers between devices, from_behind(): return lax.ppermute(block, axis, route)  22.7 us
    ppermute x9, starting transfers between devices, from_behind(): return lax.ppermute(block, axis, route)  18.7 us
    pallas_call x2, Pallas kernels, attention(): pl.pallas_call(attention_kernel, out_shape=jax.ShapeDtypeStruct((tokens,...  16.5 us
    pallas_call x1, Pallas kernels, projections(): pl.pallas_call(projection_kernel, out_shape=(shape, shape, shape), grid=(...  9.13 us
    pallas_call x1, Pallas kernels, fetch_pages(): pl.pallas_call(functools.partial(gather_kernel, devices), out_shape=[page...  5.12 us
    unnamed x26, local copies, waits for them, and re-layouts  2.89 us
    dynamic_slice x1, local copies, waits for them, and re-layouts, other_half_once_per_chip(): mine = lax.dynamic_slice_in_dim(w_out, core * rows, rows, 0)  2.09 us
    dot_general x1, matrix products, body(): jnp.dot(in_kv_order(attended, other_attended, 1), in_kv_order(w_out, othe...  1.98 us
  transfers between devices with their start and end apart: 10, of which 5 were waited for; matrix products, arithmetic and copies ran while one was open for 9% of the time, Pallas kernels for 27%

profile of v12, /device:TPU:6, one launch (start us, length us, event | category | flops | bytes accessed | tf_op | source)
XLA Modules:
  0.0 96.0 jit_solution(454571375725075419)
XLA Ops:
  0.6 0.0 copy-start
  0.6 1.5 %copy.18.pages_ref = s32[128,4]{1,0:T(8,128)} copy(s32[128,4]{0,1:T(4,128)} %param.24) | data formatting | bytes 4096 | tf_op args[11]
  2.2 5.1 %shard_map.149 = (bf16[2,256,640]{2,1,0:T(8,128)(2,1)}, bf16[2,256,640]{2,1,0:T(8,128)(2,1)}, bf16[2,256,640]{2,1,0:T(8,128)(2,1)}, bf16[2,256,640]{2,1,0:T(8,128)(2,1)}) custom-call(s32[128,4]{1,0:T(8,128)} %copy.18.pages_ref, bf16[4,256,640]{2,1,0:T(8,128)(2,1)} %keys_hbm.1, bf16[4,256,640]{2,1,0:T(8,128)(2,1)} %values_hbm.1), custom_call_target="tpu_custom_call" | custom-call | tf_op jit(solution)/shard_map/pallas_call | solution.py:206
  7.3 6.7 %collective-permute-start = (bf16[2,256,640]{2,1,0:T(8,128)(2,1)}, bf16[2,256,640]{2,1,0:T(8,128)(2,1)S(1)}, u32[]{:S(2)}, u32[]{:S(2)}) collective-permute-start(bf16[2,256,640]{2,1,0:T(8,128)(2,1)} %get-tuple-element.15), channel_id=1, source_target_pairs={{1,0},{2,1},{3,2},{4,3},{5,4},{6,5},{7,6},{8,7},{9,8},{10,9},{11,1... | collective-permute-start | bytes 1966088 | tf_op jit(solution)/shard_map/ppermute | solution.py:22
  13.9 1.3 %collective-permute-start.1 = (bf16[2,256,640]{2,1,0:T(8,128)(2,1)}, bf16[2,256,640]{2,1,0:T(8,128)(2,1)S(1)}, u32[]{:S(2)}, u32[]{:S(2)}) collective-permute-start(bf16[2,256,640]{2,1,0:T(8,128)(2,1)} %get-tuple-element.16), channel_id=1, source_target_pairs={{33,0},{34,1},{35,2},{36,3},{37,4},{38,5},{39,6},{40,7},{41,8},{42... | collective-permute-start | bytes 1966088 | tf_op jit(solution)/shard_map/ppermute | solution.py:22
  15.2 2.0 %collective-permute-start.2 = (bf16[2,256,640]{2,1,0:T(8,128)(2,1)}, bf16[2,256,640]{2,1,0:T(8,128)(2,1)S(1)}, u32[]{:S(2)}, u32[]{:S(2)}) collective-permute-start(bf16[2,256,640]{2,1,0:T(8,128)(2,1)} %get-tuple-element.17), channel_id=1, source_target_pairs={{65,0},{66,1},{67,2},{68,3},{69,4},{70,5},{71,6},{72,7},{73,8},{74... | collective-permute-start | bytes 1966088 | tf_op jit(solution)/shard_map/ppermute | solution.py:22
  17.2 0.0 collective-permute-start.3
  17.2 2.1 %constant_dynamic-slice_fusion = bf16[320,1280]{1,0:T(8,128)(2,1)} fusion(bf16[640,1280]{1,0:T(8,128)(2,1)} %param.17, s32[]{:T(128)S(6)} %select_n.83), kind=kLoop, calls=%fused_computation.39 | loop fusion | bytes 1638404 | tf_op jit(solution)/shard_map/dynamic_slice | solution.py:55
  19.3 2.9 %collective-permute-start.6 = (bf16[320,1280]{1,0:T(8,128)(2,1)}, bf16[320,1280]{1,0:T(8,128)(2,1)}, u32[]{:S(2)}, u32[]{:S(2)}) collective-permute-start(bf16[320,1280]{1,0:T(8,128)(2,1)} %constant_dynamic-slice_fusion), channel_id=1, source_target_pairs={{128,0},{0,128},{129,1},{1,129},{130,2},{2,130},{131,3},{3,131},{1... | collective-permute-start | bytes 2457608 | tf_op jit(solution)/shard_map/ppermute | solution.py:22
  22.2 0.0 copy-done
  22.2 0.3 fusion.7
  22.5 0.9 copy.17.scale_ref
  23.4 0.0 copy-done.10
  23.4 0.6 reshape.53.gain_ref
  25.3 9.1 %shard_map.148 = (bf16[512,640]{1,0:T(8,128)(2,1)}, bf16[512,640]{1,0:T(8,128)(2,1)}, bf16[512,640]{1,0:T(8,128)(2,1)}) custom-call(bf16[512,1280]{1,0:T(8,128)(2,1)} %x_ref.1, f32[512,1]{1,0:T(8,128)} %copy.17.scale_ref, bf16[1280,640]{1,0:T(8,128)(2,1)} %wq_ref.1, bf16[1280,640]{1,0:T(8,128)(2,1)} %wk_ref.1, bf16[1280,640]{1,0:T(8,128)(2,1)} %wv_ref.1, ...), custom_call_target="tpu_custom_call" | custom-call | tf_op jit(solution)/shard_map/pallas_call | solution.py:98
  34.4 1.4 %slice_bitcast_fusion = (bf16[1,256,640]{2,1,0:T(8,128)(2,1)S(1)}, bf16[1,256,640]{2,1,0:T(8,128)(2,1)S(1)}, bf16[1,256,640]{2,1,0:T(8,128)(2,1)S(1)}, bf16[1,256,640]{2,1,0:T(8,128)(2,1)S(1)}) fusion(bf16[512,640]{1,0:T(8,128)(2,1)} %get-tuple-element.14.v_ref, bf16[512,640]{1,0:T(8,128)(2,1)} %get-tuple-element.13.k_ref), kind=kLoop, calls=%fused_computation.30 | loop fusion | bytes 2621440 | tf_op jit(solution)/shard_map/slice | solution.py:227
  35.8 0.0 collective-permute-done.refs_0_.refs_4_
  35.8 0.0 copy-start.2
  35.8 3.2 %collective-permute-done.1.refs_1_.refs_5_ = bf16[2,256,640]{2,1,0:T(8,128)(2,1)S(1)} collective-permute-done((bf16[2,256,640]{2,1,0:T(8,128)(2,1)}, bf16[2,256,640]{2,1,0:T(8,128)(2,1)S(1)}, u32[]{:S(2)}, u32[]{:S(2)}) %collective-permute-start.1) | collective-permute-done | bytes 655392 | tf_op jit(solution)/shard_map/ppermute | solution.py:22
  39.0 7.9 %collective-permute-done.2.refs_2_.refs_6_ = bf16[2,256,640]{2,1,0:T(8,128)(2,1)S(1)} collective-permute-done((bf16[2,256,640]{2,1,0:T(8,128)(2,1)}, bf16[2,256,640]{2,1,0:T(8,128)(2,1)S(1)}, u32[]{:S(2)}, u32[]{:S(2)}) %collective-permute-start.2) | collective-permute-done | bytes 655392 | tf_op jit(solution)/shard_map/ppermute | solution.py:22
  47.0 0.6 collective-permute-done.3.refs_3_.refs_7_
  47.6 0.0 copy-done.2
  47.6 0.0 copy-done.3
  47.6 0.3 copy-done.4
  47.8 9.5 %shard_map.150 = bf16[512,384]{1,0:T(8,128)(2,1)} custom-call(s32[1]{0:T(128)S(6)} %copy.24.live_ref, s32[1]{0:T(128)S(6)} %copy.25.depth_ref, bf16[512,640]{1,0:T(8,128)(2,1)} %get-tuple-element.12.q_ref, bf16[512,640]{1,0:T(8,128)(2,1)} %get-tuple-element.13.k_ref, bf16[512,640]{1,0:T(8,128)(2,1)} %get-tuple-element.14.v_ref, ...), custom_call_target="tpu_custom_call" | custom-call | tf_op jit(solution)/shard_map/pallas_call | solution.py:170
  57.4 3.0 %collective-permute-start.4 = (bf16[512,384]{1,0:T(8,128)(2,1)}, bf16[512,384]{1,0:T(8,128)(2,1)}, u32[]{:S(2)}, u32[]{:S(2)}) collective-permute-start(bf16[512,384]{1,0:T(8,128)(2,1)} %shard_map.150), channel_id=1, source_target_pairs={{128,0},{0,128},{129,1},{1,129},{130,2},{2,130},{131,3},{3,131},{1... | collective-permute-start | bytes 1179656 | tf_op jit(solution)/shard_map/ppermute | solution.py:22
  60.4 0.1 pad_maximum_fusion.2
  60.4 0.1 pad_maximum_fusion.3
  60.5 0.0 copy-start.11
  60.5 0.0 copy-start.6
  60.5 2.2 %collective-permute-start.8 = (bf16[2,256,640]{2,1,0:T(8,128)(2,1)S(1)}, bf16[2,256,640]{2,1,0:T(8,128)(2,1)S(1)}, u32[]{:S(2)}, u32[]{:S(2)}) collective-permute-start(bf16[2,256,640]{2,1,0:T(8,128)(2,1)S(1)} %pad_maximum_fusion.2), channel_id=1, source_target_pairs={{96,0},{97,1},{98,2},{99,3},{100,4},{101,5},{102,6},{103,7},{104,8... | collective-permute-start | bytes 1966088 | tf_op jit(solution)/shard_map/ppermute | solution.py:22
  62.7 7.0 %shard_map.151 = bf16[512,256]{1,0:T(8,128)(2,1)} custom-call(s32[1]{0:T(128)S(6)} %copy.24.live_ref, s32[1]{0:T(128)S(6)} %copy.25.depth_ref, bf16[512,640]{1,0:T(8,128)(2,1)} %get-tuple-element.12.q_ref, bf16[512,640]{1,0:T(8,128)(2,1)} %get-tuple-element.13.k_ref, bf16[512,640]{1,0:T(8,128)(2,1)} %get-tuple-element.14.v_ref, ...), custom_call_target="tpu_custom_call" | custom-call | tf_op jit(solution)/shard_map/pallas_call | solution.py:170
  69.7 0.6 collective-permute-start.5
  70.3 0.0 copy-done.11
  70.3 0.6 fusion.12
  74.9 0.1 collective-permute-start.9
  74.9 0.0 collective-permute-done.6
  75.0 0.3 collective-permute-start.7
  75.2 0.0 collective-permute-done.4
  75.2 1.0 %constant_dynamic-update-slice_fusion.1 = bf16[512,640]{1,0:T(8,128)(2,1)S(1)} fusion(bf16[512,384]{1,0:T(8,128)(2,1)} %collective-permute-done.4), kind=kLoop, calls=%fused_computation.35 | loop fusion | bytes 786432
  76.3 1.5 %collective-permute-done.5 = bf16[512,256]{1,0:T(8,128)(2,1)S(1)} collective-permute-done((bf16[512,256]{1,0:T(8,128)(2,1)}, bf16[512,256]{1,0:T(8,128)(2,1)S(1)}, u32[]{:S(2)}, u32[]{:S(2)}) %collective-permute-start.5) | collective-permute-done | bytes 262176 | tf_op jit(solution)/shard_map/ppermute | solution.py:22
  77.8 0.0 copy-done.6
  77.8 1.2 %broadcast_select_fusion.5 = (bf16[512,640]{1,0:T(8,128)(2,1)S(1)}, bf16[512,640]{1,0:T(8,128)(2,1)S(1)}) fusion(bf16[512,640]{1,0:T(8,128)(2,1)S(1)} %constant_dynamic-update-slice_fusion, pred[]{:T(512)S(6)} %eq.13, bf16[512,256]{1,0:T(8,128)(2,1)} %shard_map.151, bf16[512,384]{1,0:T(8,128)(2,1)S(1)} %copy-done.6), kind=kLoop, calls=%fused_computation.25 | loop fusion | flops 1966080 | bytes 2621441 | tf_op jit(solution)/shard_map/jit(_where)/select_n | solution.py:67
  79.0 0.0 collective-permute-done.8
  79.0 0.1 broadcast.62.clone.1
  79.2 0.1 broadcast.62.clone
  79.2 0.0 copy-start.5
  79.3 9.5 %collective-permute-done.9 = bf16[2,256,640]{2,1,0:T(8,128)(2,1)S(1)} collective-permute-done((bf16[2,256,640]{2,1,0:T(8,128)(2,1)S(1)}, bf16[2,256,640]{2,1,0:T(8,128)(2,1)S(1)}, u32[]{:S(2)}, u32[]{:S(2)}) %collective-permute-start.9) | collective-permute-done | bytes 655392 | tf_op jit(solution)/shard_map/ppermute | solution.py:22
  88.8 0.1 slice_dynamic-update-slice_fusion
  88.9 0.0 copy-start.7
  88.9 0.0 copy-start.8
  88.9 0.0 collective-permute-done.7
  88.9 1.7 %broadcast_select_fusion.3 = (bf16[320,1280]{1,0:T(8,128)(2,1)S(1)}, bf16[320,1280]{1,0:T(8,128)(2,1)S(1)}) fusion(bf16[320,1280]{1,0:T(8,128)(2,1)} %collective-permute-done.6, bf16[320,1280]{1,0:T(8,128)(2,1)S(1)} %collective-permute-done.7, pred[]{:T(512)S(6)} %eq.14), kind=kLoop, calls=%fused_computation.20 | loop fusion | flops 819200 | bytes 3276801 | tf_op jit(solution)/shard_map/jit(_where)/select_n | solution.py:61
  90.6 0.0 copy-done.5
  90.6 0.6 broadcast_select_fusion.1
  91.3 0.0 copy-done.7
  91.3 0.0 copy-done.8
  91.3 0.0 copy-start.1
  91.3 0.0 copy-start.9
  91.3 2.0 %multiply_reduce_fusion.1 = (f32[512]{0:T(512)S(1)}, f32[512,1280]{1,0:T(8,128)S(1)}) fusion(bf16[640,1280]{1,0:T(8,128)(2,1)S(1)} %get-tuple-element.22, bf16[640,1280]{1,0:T(8,128)(2,1)S(1)} %get-tuple-element.21, bf16[512,640]{1,0:T(8,128)(2,1)S(1)} %get-tuple-element.26, bf16[512,640]{1,0:T(8,128)(2,1)S(1)} %get-tuple-element.25), kind=kOutput, calls=%fused_computation.12 | convolution fusion | flops 1688206848 | bytes 7211008 | tf_op jit(solution)/shard_map/dot_general | solution.py:276
  93.3 0.0 copy-done.1
  93.3 0.0 copy-done.9
  93.3 0.8 multiply_reduce_fusion
  94.2 1.8 %multiply_convert_fusion = bf16[512,1280]{1,0:T(8,128)(2,1)} fusion(f32[512]{0:T(512)S(1)} %add_rsqrt_fusion, f32[512,1280]{1,0:T(8,128)S(1)} %get-tuple-element.36, f32[512]{0:T(512)S(1)} %add_rsqrt_fusion.1, f32[1280]{0:T(1024)S(1)} %copy-done.9, f32[512]{0:T(512)S(1)} %add_rsqrt_fusion.2, bf16[512,1280]{1,0:T(8,128)(2,1)S(1)} %copy-done.1), kind=kLoop, calls=%fused_computation.10 | loop fusion | flops 5242880 | bytes 5254144 | tf_op jit(solution)/shard_map/convert_element_type | solution.py:282
  (9 shorter events, 0.1 us)
Async XLA Ops:
  0.6 21.5 %copy-start = (bf16[512,1280]{1,0:T(8,128)(2,1)S(1)}, bf16[512,1280]{1,0:T(8,128)(2,1)}, u32[]{:S(2)}) copy-start(bf16[512,1280]{1,0:T(8,128)(2,1)} %x_ref.1) | copy-start | bytes 3932164
  2.2 21.2 %copy-start.10 = (f32[640]{0:T(1024)S(1)}, f32[640]{0:T(1024)}, u32[]{:S(2)}) copy-start(f32[640]{0:T(1024)} %param.18) | copy-start | bytes 7684
  7.3 28.5 %collective-permute-start = (bf16[2,256,640]{2,1,0:T(8,128)(2,1)}, bf16[2,256,640]{2,1,0:T(8,128)(2,1)S(1)}, u32[]{:S(2)}, u32[]{:S(2)}) collective-permute-start(bf16[2,256,640]{2,1,0:T(8,128)(2,1)} %get-tuple-element.15), channel_id=1, source_target_pairs={{1,0},{2,1},{3,2},{4,3},{5,4},{6,5},{7,6},{8,7},{9,8},{10,9},{11,1... | collective-permute-start | bytes 1966088 | tf_op jit(solution)/shard_map/ppermute | solution.py:22
  13.9 25.1 %collective-permute-start.1 = (bf16[2,256,640]{2,1,0:T(8,128)(2,1)}, bf16[2,256,640]{2,1,0:T(8,128)(2,1)S(1)}, u32[]{:S(2)}, u32[]{:S(2)}) collective-permute-start(bf16[2,256,640]{2,1,0:T(8,128)(2,1)} %get-tuple-element.16), channel_id=1, source_target_pairs={{33,0},{34,1},{35,2},{36,3},{37,4},{38,5},{39,6},{40,7},{41,8},{42... | collective-permute-start | bytes 1966088 | tf_op jit(solution)/shard_map/ppermute | solution.py:22
  15.2 31.8 %collective-permute-start.2 = (bf16[2,256,640]{2,1,0:T(8,128)(2,1)}, bf16[2,256,640]{2,1,0:T(8,128)(2,1)S(1)}, u32[]{:S(2)}, u32[]{:S(2)}) collective-permute-start(bf16[2,256,640]{2,1,0:T(8,128)(2,1)} %get-tuple-element.17), channel_id=1, source_target_pairs={{65,0},{66,1},{67,2},{68,3},{69,4},{70,5},{71,6},{72,7},{73,8},{74... | collective-permute-start | bytes 1966088 | tf_op jit(solution)/shard_map/ppermute | solution.py:22
  17.2 30.4 %collective-permute-start.3 = (bf16[2,256,640]{2,1,0:T(8,128)(2,1)}, bf16[2,256,640]{2,1,0:T(8,128)(2,1)}, u32[]{:S(2)}, u32[]{:S(2)}) collective-permute-start(bf16[2,256,640]{2,1,0:T(8,128)(2,1)} %get-tuple-element.18), channel_id=1, source_target_pairs={{97,0},{98,1},{99,2},{100,3},{101,4},{102,5},{103,6},{104,7},{105,... | collective-permute-start | bytes 1966088 | tf_op jit(solution)/shard_map/ppermute | solution.py:22
  19.3 55.7 %collective-permute-start.6 = (bf16[320,1280]{1,0:T(8,128)(2,1)}, bf16[320,1280]{1,0:T(8,128)(2,1)}, u32[]{:S(2)}, u32[]{:S(2)}) collective-permute-start(bf16[320,1280]{1,0:T(8,128)(2,1)} %constant_dynamic-slice_fusion), channel_id=1, source_target_pairs={{128,0},{0,128},{129,1},{1,129},{130,2},{2,130},{131,3},{3,131},{1... | collective-permute-start | bytes 2457608 | tf_op jit(solution)/shard_map/ppermute | solution.py:22
  35.8 11.8 %copy-start.2 = (bf16[2,256,640]{2,1,0:T(8,128)(2,1)}, bf16[2,256,640]{2,1,0:T(8,128)(2,1)S(1)}, u32[]{:S(2)}) copy-start(bf16[2,256,640]{2,1,0:T(8,128)(2,1)S(1)} %collective-permute-done.refs_0_.refs_4_) | copy-start | bytes 1966084
  39.0 8.5 %copy-start.3 = (bf16[2,256,640]{2,1,0:T(8,128)(2,1)}, bf16[2,256,640]{2,1,0:T(8,128)(2,1)S(1)}, u32[]{:S(2)}) copy-start(bf16[2,256,640]{2,1,0:T(8,128)(2,1)S(1)} %collective-permute-done.1.refs_1_.refs_5_) | copy-start | bytes 1966084
  47.0 0.8 copy-start.4
  57.4 17.9 %collective-permute-start.4 = (bf16[512,384]{1,0:T(8,128)(2,1)}, bf16[512,384]{1,0:T(8,128)(2,1)}, u32[]{:S(2)}, u32[]{:S(2)}) collective-permute-start(bf16[512,384]{1,0:T(8,128)(2,1)} %shard_map.150), channel_id=1, source_target_pairs={{128,0},{0,128},{129,1},{1,129},{130,2},{2,130},{131,3},{3,131},{1... | collective-permute-start | bytes 1179656 | tf_op jit(solution)/shard_map/ppermute | solution.py:22
  60.5 9.8 %copy-start.11 = (s32[256]{0:T(256)S(1)}, s32[256]{0:T(256)}, u32[]{:S(2)}) copy-start(s32[256]{0:T(256)} %param.25) | copy-start | bytes 3076
  60.5 17.3 %copy-start.6 = (bf16[512,384]{1,0:T(8,128)(2,1)S(1)}, bf16[512,384]{1,0:T(8,128)(2,1)}, u32[]{:S(2)}) copy-start(bf16[512,384]{1,0:T(8,128)(2,1)} %shard_map.150) | copy-start | bytes 1179652
  60.5 18.5 %collective-permute-start.8 = (bf16[2,256,640]{2,1,0:T(8,128)(2,1)S(1)}, bf16[2,256,640]{2,1,0:T(8,128)(2,1)S(1)}, u32[]{:S(2)}, u32[]{:S(2)}) collective-permute-start(bf16[2,256,640]{2,1,0:T(8,128)(2,1)S(1)} %pad_maximum_fusion.2), channel_id=1, source_target_pairs={{96,0},{97,1},{98,2},{99,3},{100,4},{101,5},{102,6},{103,7},{104,8... | collective-permute-start | bytes 1966088 | tf_op jit(solution)/shard_map/ppermute | solution.py:22
  69.7 8.1 %collective-permute-start.5 = (bf16[512,256]{1,0:T(8,128)(2,1)}, bf16[512,256]{1,0:T(8,128)(2,1)S(1)}, u32[]{:S(2)}, u32[]{:S(2)}) collective-permute-start(bf16[512,256]{1,0:T(8,128)(2,1)} %shard_map.151), channel_id=1, source_target_pairs={{128,0},{0,128},{129,1},{1,129},{130,2},{2,130},{131,3},{3,131},{1... | collective-permute-start | bytes 786440 | tf_op jit(solution)/shard_map/ppermute | solution.py:22
  74.9 13.9 %collective-permute-start.9 = (bf16[2,256,640]{2,1,0:T(8,128)(2,1)S(1)}, bf16[2,256,640]{2,1,0:T(8,128)(2,1)S(1)}, u32[]{:S(2)}, u32[]{:S(2)}) collective-permute-start(bf16[2,256,640]{2,1,0:T(8,128)(2,1)S(1)} %pad_maximum_fusion.3), channel_id=1, source_target_pairs={{32,0},{33,1},{34,2},{35,3},{36,4},{37,5},{38,6},{39,7},{40,8},{41... | collective-permute-start | bytes 1966088 | tf_op jit(solution)/shard_map/ppermute | solution.py:22
  75.0 13.9 %collective-permute-start.7 = (bf16[320,1280]{1,0:T(8,128)(2,1)}, bf16[320,1280]{1,0:T(8,128)(2,1)S(1)}, u32[]{:S(2)}, u32[]{:S(2)}) collective-permute-start(bf16[320,1280]{1,0:T(8,128)(2,1)} %collective-permute-done.6), channel_id=1, source_target_pairs={{0,1},{1,0},{2,3},{3,2},{4,5},{5,4},{6,7},{7,6},{8,9},{9,8},{10,11... | collective-permute-start | bytes 2457608 | tf_op jit(solution)/shard_map/ppermute | solution.py:58
  79.2 11.4 %copy-start.5 = (bf16[640,1280]{1,0:T(8,128)(2,1)S(1)}, bf16[640,1280]{1,0:T(8,128)(2,1)}, u32[]{:S(2)}) copy-start(bf16[640,1280]{1,0:T(8,128)(2,1)} %param.17) | copy-start | bytes 4915204
  88.9 2.4 %copy-start.7 = (bf16[2,256,640]{2,1,0:T(8,128)(2,1)}, bf16[2,256,640]{2,1,0:T(8,128)(2,1)S(1)}, u32[]{:S(2)}) copy-start(bf16[2,256,640]{2,1,0:T(8,128)(2,1)S(1)} %get-tuple-element.27) | copy-start | bytes 1966084
  88.9 2.4 %copy-start.8 = (bf16[2,256,640]{2,1,0:T(8,128)(2,1)}, bf16[2,256,640]{2,1,0:T(8,128)(2,1)S(1)}, u32[]{:S(2)}) copy-start(bf16[2,256,640]{2,1,0:T(8,128)(2,1)S(1)} %get-tuple-element.28) | copy-start | bytes 1966084
  91.3 2.0 %copy-start.1 = (bf16[512,1280]{1,0:T(8,128)(2,1)S(1)}, bf16[512,1280]{1,0:T(8,128)(2,1)}, u32[]{:S(2)}) copy-start(bf16[512,1280]{1,0:T(8,128)(2,1)} %x_ref.1) | copy-start | bytes 3932164
  91.3 2.0 %copy-start.9 = (f32[1280]{0:T(1024)S(1)}, f32[1280]{0:T(1024)}, u32[]{:S(2)}) copy-start(f32[1280]{0:T(1024)} %param.19) | copy-start | bytes 15364

commit v13 on v10

--- a/solution.py
+++ b/solution.py
@@ -47,6 +47,24 @@
         preferred_element_type=jnp.float32,
     )
     return (totals, mixed)
+
+
+def other_half_once_per_group(w_out, group=4):
+    rows = w_out.shape[0] // group
+    devices = lax.axis_size("blk")
+    member = lax.axis_index("blk") % group
+    mine = lax.dynamic_slice_in_dim(w_out, member * rows, rows, 0)
+    pulled = from_behind(mine, "kv", 1)
+    received = [pulled] + [
+        lax.ppermute(pulled, "blk", [(i, i ^ step) for i in range(devices)])
+        for step in range(1, group)
+    ]
+    stacked = jnp.stack(received)
+    chunks = [
+        lax.dynamic_index_in_dim(stacked, lax.bitwise_xor(member, chunk), 0, keepdims=False)
+        for chunk in range(group)
+    ]
+    return jnp.concatenate(chunks, axis=0)
 
 
 def in_kv_order(mine, other, axis):
@@ -238,7 +256,7 @@
     placement,
 ):
     tokens_here = hidden_in.shape[0]
-    other_w_out = from_behind(w_out, "kv", 1)
+    other_w_out = other_half_once_per_group(w_out)
     width_half = w_query.shape[1]
     heads_here = width_half // HD
     hidden_f = hidden_in.astype(jnp.float32)

time: 103 us -> 102 us (level)
  the two profiles are of different devices: /device:TPU:225 before, /device:TPU:1 now
where the time goes in v13:
time: 102 us; the launch traced here: 101 us
  Pallas kernels  30.7 us (30%)
  starting transfers between devices  27.2 us (27%)
  waiting for transfers between devices  18 us (18%)
  local copies, waits for them, and re-layouts  9.46 us (9%)
  other arithmetic  7.72 us (8%)
  between operations  6.18 us (6%)
  matrix products  2 us (2%)
    ppermute x9, starting transfers between devices, from_behind(): return lax.ppermute(block, axis, route)  19.5 us
    ppermute x9, waiting for transfers between devices, from_behind(): return lax.ppermute(block, axis, route)  18 us
    pallas_call x2, Pallas kernels, attention(): pl.pallas_call(attention_kernel, out_shape=jax.ShapeDtypeStruct((tokens,...  16.6 us
    pallas_call x1, Pallas kernels, projections(): pl.pallas_call(projection_kernel, out_shape=(shape, shape, shape), grid=(...  9.1 us
    ppermute x3, starting transfers between devices, other_half_once_per_group(): lax.ppermute(pulled, 'blk', [(i, i ^ step) for i in range(devices)])  7.69 us
    pallas_call x1, Pallas kernels, fetch_pages(): pl.pallas_call(functools.partial(gather_kernel, devices), out_shape=[page...  5.04 us
    another operation x1, other arithmetic, other_half_once_per_group(): stacked = jnp.stack(received)  2.04 us
  transfers between devices with their start and end apart: 12, of which 3 were waited for; matrix products, arithmetic and copies ran while one was open for 12% of the time, Pallas kernels for 30%

profile of v13, /device:TPU:1, one launch (start us, length us, event | category | flops | bytes accessed | tf_op | source)
XLA Modules:
  0.0 101.3 jit_solution(3650475160623741785)
XLA Ops:
  0.6 0.0 copy-start
  0.6 0.0 copy-start.11
  0.7 1.9 %constant_dynamic-slice_fusion = bf16[160,1280]{1,0:T(8,128)(2,1)} fusion(bf16[640,1280]{1,0:T(8,128)(2,1)} %param.17, s32[]{:T(128)S(6)} %select_n.83), kind=kLoop, calls=%fused_computation.39 | loop fusion | bytes 819204 | tf_op jit(solution)/shard_map/dynamic_slice | solution.py:56
  2.5 3.7 %collective-permute-start.6 = (bf16[160,1280]{1,0:T(8,128)(2,1)}, bf16[160,1280]{1,0:T(8,128)(2,1)}, u32[]{:S(2)}, u32[]{:S(2)}) collective-permute-start(bf16[160,1280]{1,0:T(8,128)(2,1)} %constant_dynamic-slice_fusion), channel_id=1, source_target_pairs={{128,0},{0,128},{129,1},{1,129},{130,2},{2,130},{131,3},{3,131},{1... | collective-permute-start | bytes 1228808 | tf_op jit(solution)/shard_map/ppermute | solution.py:22
  6.3 1.4 %copy.18.pages_ref = s32[128,4]{1,0:T(8,128)} copy(s32[128,4]{0,1:T(4,128)} %param.24) | data formatting | bytes 4096 | tf_op args[11]
  7.7 5.0 %shard_map.149 = (bf16[2,256,640]{2,1,0:T(8,128)(2,1)}, bf16[2,256,640]{2,1,0:T(8,128)(2,1)}, bf16[2,256,640]{2,1,0:T(8,128)(2,1)}, bf16[2,256,640]{2,1,0:T(8,128)(2,1)}) custom-call(s32[128,4]{1,0:T(8,128)} %copy.18.pages_ref, bf16[4,256,640]{2,1,0:T(8,128)(2,1)} %keys_hbm.1, bf16[4,256,640]{2,1,0:T(8,128)(2,1)} %values_hbm.1), custom_call_target="tpu_custom_call" | custom-call | tf_op jit(solution)/shard_map/pallas_call | solution.py:211
  12.8 1.0 %collective-permute-start = (bf16[2,256,640]{2,1,0:T(8,128)(2,1)}, bf16[2,256,640]{2,1,0:T(8,128)(2,1)S(1)}, u32[]{:S(2)}, u32[]{:S(2)}) collective-permute-start(bf16[2,256,640]{2,1,0:T(8,128)(2,1)} %get-tuple-element.13), channel_id=1, source_target_pairs={{1,0},{2,1},{3,2},{4,3},{5,4},{6,5},{7,6},{8,7},{9,8},{10,9},{11,1... | collective-permute-start | bytes 1966088 | tf_op jit(solution)/shard_map/ppermute | solution.py:22
  13.8 7.9 %collective-permute-start.1 = (bf16[2,256,640]{2,1,0:T(8,128)(2,1)}, bf16[2,256,640]{2,1,0:T(8,128)(2,1)S(1)}, u32[]{:S(2)}, u32[]{:S(2)}) collective-permute-start(bf16[2,256,640]{2,1,0:T(8,128)(2,1)} %get-tuple-element.14), channel_id=1, source_target_pairs={{33,0},{34,1},{35,2},{36,3},{37,4},{38,5},{39,6},{40,7},{41,8},{42... | collective-permute-start | bytes 1966088 | tf_op jit(solution)/shard_map/ppermute | solution.py:22
  21.7 0.8 collective-permute-start.2
  22.5 0.0 collective-permute-start.3
  22.5 0.0 copy-done
  22.5 0.3 fusion.7
  22.9 0.9 copy.17.scale_ref
  23.8 0.0 copy-done.11
  23.8 0.6 reshape.53.gain_ref
  24.4 9.1 %shard_map.148 = (bf16[512,640]{1,0:T(8,128)(2,1)}, bf16[512,640]{1,0:T(8,128)(2,1)}, bf16[512,640]{1,0:T(8,128)(2,1)}) custom-call(bf16[512,1280]{1,0:T(8,128)(2,1)} %x_ref.1, f32[512,1]{1,0:T(8,128)} %copy.17.scale_ref, bf16[1280,640]{1,0:T(8,128)(2,1)} %wq_ref.1, bf16[1280,640]{1,0:T(8,128)(2,1)} %wk_ref.1, bf16[1280,640]{1,0:T(8,128)(2,1)} %wv_ref.1, ...), custom_call_target="tpu_custom_call" | custom-call | tf_op jit(solution)/shard_map/pallas_call | solution.py:103
  33.5 1.4 %slice_bitcast_fusion = (bf16[1,256,640]{2,1,0:T(8,128)(2,1)S(1)}, bf16[1,256,640]{2,1,0:T(8,128)(2,1)S(1)}, bf16[1,256,640]{2,1,0:T(8,128)(2,1)S(1)}, bf16[1,256,640]{2,1,0:T(8,128)(2,1)S(1)}) fusion(bf16[512,640]{1,0:T(8,128)(2,1)} %get-tuple-element.12.v_ref, bf16[512,640]{1,0:T(8,128)(2,1)} %get-tuple-element.11.k_ref), kind=kLoop, calls=%fused_computation.33 | loop fusion | bytes 2621440 | tf_op jit(solution)/shard_map/slice | solution.py:234
  34.9 0.9 pad_maximum_fusion.3
  35.8 0.0 collective-permute-done.6
  35.8 1.1 %collective-permute-start.10 = (bf16[2,256,640]{2,1,0:T(8,128)(2,1)}, bf16[2,256,640]{2,1,0:T(8,128)(2,1)}, u32[]{:S(2)}, u32[]{:S(2)}) collective-permute-start(bf16[2,256,640]{2,1,0:T(8,128)(2,1)} %pad_maximum_fusion.3), channel_id=1, source_target_pairs={{96,0},{97,1},{98,2},{99,3},{100,4},{101,5},{102,6},{103,7},{104,8... | collective-permute-start | bytes 1966088 | tf_op jit(solution)/shard_map/ppermute | solution.py:22
  36.9 0.9 pad_maximum_fusion.4
  37.8 0.0 collective-permute-done.refs_0_.refs_4_
  37.8 1.6 %collective-permute-start.11 = (bf16[2,256,640]{2,1,0:T(8,128)(2,1)}, bf16[2,256,640]{2,1,0:T(8,128)(2,1)S(1)}, u32[]{:S(2)}, u32[]{:S(2)}) collective-permute-start(bf16[2,256,640]{2,1,0:T(8,128)(2,1)} %pad_maximum_fusion.4), channel_id=1, source_target_pairs={{32,0},{33,1},{34,2},{35,3},{36,4},{37,5},{38,6},{39,7},{40,8},{41... | collective-permute-start | bytes 1966088 | tf_op jit(solution)/shard_map/ppermute | solution.py:22
  39.4 0.0 copy-done.12
  39.4 0.7 fusion.12
  45.3 0.0 collective-permute-done.1.refs_1_.refs_5_
  45.3 0.0 copy-start.3
  45.4 3.2 %collective-permute-start.9 = (bf16[160,1280]{1,0:T(8,128)(2,1)}, bf16[160,1280]{1,0:T(8,128)(2,1)}, u32[]{:S(2)}, u32[]{:S(2)}) collective-permute-start(bf16[160,1280]{1,0:T(8,128)(2,1)} %collective-permute-done.6), channel_id=1, source_target_pairs={{0,3},{1,2},{2,1},{3,0},{4,7},{5,6},{6,5},{7,4},{8,11},{9,10},{10,... | collective-permute-start | bytes 1228808 | tf_op jit(solution)/shard_map/ppermute | solution.py:59
  48.6 0.0 collective-permute-done.2.refs_2_.refs_6_
  48.6 1.1 %collective-permute-start.8 = (bf16[160,1280]{1,0:T(8,128)(2,1)}, bf16[160,1280]{1,0:T(8,128)(2,1)}, u32[]{:S(2)}, u32[]{:S(2)}) collective-permute-start(bf16[160,1280]{1,0:T(8,128)(2,1)} %collective-permute-done.6), channel_id=1, source_target_pairs={{0,2},{1,3},{2,0},{3,1},{4,6},{5,7},{6,4},{7,5},{8,10},{9,11},{10,... | collective-permute-start | bytes 1228808 | tf_op jit(solution)/shard_map/ppermute | solution.py:59
  49.7 8.5 %collective-permute-done.3.refs_3_.refs_7_ = bf16[2,256,640]{2,1,0:T(8,128)(2,1)} collective-permute-done((bf16[2,256,640]{2,1,0:T(8,128)(2,1)}, bf16[2,256,640]{2,1,0:T(8,128)(2,1)}, u32[]{:S(2)}, u32[]{:S(2)}) %collective-permute-start.3) | collective-permute-done | bytes 655392 | tf_op jit(solution)/shard_map/ppermute | solution.py:22
  58.2 3.4 %collective-permute-start.7 = (bf16[160,1280]{1,0:T(8,128)(2,1)}, bf16[160,1280]{1,0:T(8,128)(2,1)}, u32[]{:S(2)}, u32[]{:S(2)}) collective-permute-start(bf16[160,1280]{1,0:T(8,128)(2,1)} %collective-permute-done.6), channel_id=1, source_target_pairs={{0,1},{1,0},{2,3},{3,2},{4,5},{5,4},{6,7},{7,6},{8,9},{9,8},{10,11... | collective-permute-start | bytes 1228808 | tf_op jit(solution)/shard_map/ppermute | solution.py:59
  61.6 0.0 copy-done.2
  61.6 0.0 copy-done.3
  61.6 9.6 %shard_map.150 = bf16[512,384]{1,0:T(8,128)(2,1)} custom-call(s32[1]{0:T(128)S(6)} %copy.24.live_ref, s32[1]{0:T(128)S(6)} %copy.25.depth_ref, bf16[512,640]{1,0:T(8,128)(2,1)} %get-tuple-element.10.q_ref, bf16[512,640]{1,0:T(8,128)(2,1)} %get-tuple-element.11.k_ref, bf16[512,640]{1,0:T(8,128)(2,1)} %get-tuple-element.12.v_ref, ...), custom_call_target="tpu_custom_call" | custom-call | tf_op jit(solution)/shard_map/pallas_call | solution.py:175
  71.1 7.0 %shard_map.151 = bf16[512,256]{1,0:T(8,128)(2,1)} custom-call(s32[1]{0:T(128)S(6)} %copy.24.live_ref, s32[1]{0:T(128)S(6)} %copy.25.depth_ref, bf16[512,640]{1,0:T(8,128)(2,1)} %get-tuple-element.10.q_ref, bf16[512,640]{1,0:T(8,128)(2,1)} %get-tuple-element.11.k_ref, bf16[512,640]{1,0:T(8,128)(2,1)} %get-tuple-element.12.v_ref, ...), custom_call_target="tpu_custom_call" | custom-call | tf_op jit(solution)/shard_map/pallas_call | solution.py:175
  78.2 0.0 collective-permute-done.10
  78.2 1.8 %collective-permute-start.4 = (bf16[512,384]{1,0:T(8,128)(2,1)S(1)}, bf16[512,384]{1,0:T(8,128)(2,1)S(1)}, u32[]{:S(2)}, u32[]{:S(2)}) collective-permute-start(bf16[512,384]{1,0:T(8,128)(2,1)S(1)} %copy-done.6), channel_id=1, source_target_pairs={{128,0},{0,128},{129,1},{1,129},{130,2},{2,130},{131,3},{3,131},{1... | collective-permute-start | bytes 1179656 | tf_op jit(solution)/shard_map/ppermute | solution.py:22
  80.0 0.1 broadcast.62.clone
  80.1 1.0 %slice_dynamic-update-slice_fusion.1 = bf16[2,256,640]{2,1,0:T(8,128)(2,1)S(1)} fusion(bf16[2,256,640]{2,1,0:T(8,128)(2,1)S(1)} %broadcast.62.clone, s32[]{:T(128)S(6)} %select_n.93, bf16[2,256,640]{2,1,0:T(8,128)(2,1)} %collective-permute-done.10), kind=kLoop, calls=%fused_computation.30 | loop fusion | bytes 655364 | tf_op jit(solution)/shard_map/jit(dynamic_update_index_in_dim)/dynamic_update_slice | solution.py:239
  81.1 0.1 broadcast.62.clone.1
  81.2 1.0 %slice_dynamic-update-slice_fusion.3 = bf16[2,256,640]{2,1,0:T(8,128)(2,1)S(1)} fusion(bf16[2,256,640]{2,1,0:T(8,128)(2,1)S(1)} %broadcast.62.clone.1, s32[]{:T(128)S(6)} %select_n.93, bf16[2,256,640]{2,1,0:T(8,128)(2,1)} %collective-permute-done.10), kind=kLoop, calls=%fused_computation.32 | loop fusion | bytes 655364 | tf_op jit(solution)/shard_map/jit(dynamic_update_index_in_dim)/dynamic_update_slice | solution.py:238
  82.2 0.0 collective-permute-done.11
  82.2 1.5 %collective-permute-start.5 = (bf16[512,256]{1,0:T(8,128)(2,1)S(1)}, bf16[512,256]{1,0:T(8,128)(2,1)S(1)}, u32[]{:S(2)}, u32[]{:S(2)}) collective-permute-start(bf16[512,256]{1,0:T(8,128)(2,1)S(1)} %copy-done.7), channel_id=1, source_target_pairs={{128,0},{0,128},{129,1},{1,129},{130,2},{2,130},{131,3},{3,131},{1... | collective-permute-start | bytes 786440 | tf_op jit(solution)/shard_map/ppermute | solution.py:22
  83.7 0.1 slice_dynamic-update-slice_fusion
  83.8 0.0 copy-start.8
  83.8 0.0 copy-start.9
  83.8 0.0 collective-permute-done.9
  83.8 0.0 collective-permute-done.8
  83.9 0.0 collective-permute-done.7
  83.9 0.0 copy-start.5
  83.9 2.0 %pad_maximum_fusion = bf16[4,160,1280]{2,1,0:T(8,128)(2,1)S(1)} fusion(bf16[1,160,1280]{2,1,0:T(8,128)(2,1)} %bitcast.4, bf16[1,160,1280]{2,1,0:T(8,128)(2,1)} %bitcast.3, bf16[1,160,1280]{2,1,0:T(8,128)(2,1)} %bitcast.2, bf16[1,160,1280]{2,1,0:T(8,128)(2,1)} %bitcast.1), kind=kLoop, calls=%fused_computation.13 | loop fusion | flops 2457600 | bytes 3276800 | tf_op jit(solution)/shard_map/stack | solution.py:62
  85.9 0.1 dynamic-slice_bitcast_fusion.3
  86.1 0.2 copy-done.5
  86.2 0.6 broadcast_select_fusion.1
  86.8 3.9 %collective-permute-done.4 = bf16[512,384]{1,0:T(8,128)(2,1)S(1)} collective-permute-done((bf16[512,384]{1,0:T(8,128)(2,1)S(1)}, bf16[512,384]{1,0:T(8,128)(2,1)S(1)}, u32[]{:S(2)}, u32[]{:S(2)}) %collective-permute-start.4) | collective-permute-done | bytes 393248 | tf_op jit(solution)/shard_map/ppermute | solution.py:22
  90.8 5.6 %collective-permute-done.5 = bf16[512,256]{1,0:T(8,128)(2,1)S(1)} collective-permute-done((bf16[512,256]{1,0:T(8,128)(2,1)S(1)}, bf16[512,256]{1,0:T(8,128)(2,1)S(1)}, u32[]{:S(2)}, u32[]{:S(2)}) %collective-permute-start.5) | collective-permute-done | bytes 262176 | tf_op jit(solution)/shard_map/ppermute | solution.py:22
  96.3 0.3 broadcast_select_fusion.3
  96.6 0.0 copy-start.1
  96.6 0.0 copy-start.10
  96.6 2.0 %multiply_reduce_fusion.1 = (f32[512]{0:T(512)S(1)}, f32[512,1280]{1,0:T(8,128)S(1)}) fusion(bf16[640,1280]{1,0:T(8,128)(2,1)S(1)} %get-tuple-element.18, bf16[640,1280]{1,0:T(8,128)(2,1)S(1)} %get-tuple-element.17, bf16[512,640]{1,0:T(8,128)(2,1)S(1)} %get-tuple-element.24, bf16[512,640]{1,0:T(8,128)(2,1)S(1)} %get-tuple-element.23), kind=kOutput, calls=%fused_computation.12 | convolution fusion | flops 1688206848 | bytes 7211008 | tf_op jit(solution)/shard_map/dot_general | solution.py:278
  98.7 0.0 copy-done.10
  98.7 0.8 multiply_reduce_fusion
  99.5 1.8 %multiply_convert_fusion = bf16[512,1280]{1,0:T(8,128)(2,1)} fusion(f32[512]{0:T(512)S(1)} %add_rsqrt_fusion, f32[512,1280]{1,0:T(8,128)S(1)} %get-tuple-element.34, f32[512]{0:T(512)S(1)} %add_rsqrt_fusion.1, f32[1280]{0:T(1024)S(1)} %copy-done.10, f32[512]{0:T(512)S(1)} %add_rsqrt_fusion.2, bf16[512,1280]{1,0:T(8,128)(2,1)S(1)} %copy-done.1), kind=kLoop, calls=%fused_computation.10 | loop fusion | flops 5242880 | bytes 5254144 | tf_op jit(solution)/shard_map/convert_element_type | solution.py:284
  (16 shorter events, 0.1 us)
Async XLA Ops:
  0.6 21.9 %copy-start = (bf16[512,1280]{1,0:T(8,128)(2,1)S(1)}, bf16[512,1280]{1,0:T(8,128)(2,1)}, u32[]{:S(2)}) copy-start(bf16[512,1280]{1,0:T(8,128)(2,1)} %x_ref.1) | copy-start | bytes 3932164
  0.6 23.1 %copy-start.11 = (f32[640]{0:T(1024)S(1)}, f32[640]{0:T(1024)}, u32[]{:S(2)}) copy-start(f32[640]{0:T(1024)} %param.18) | copy-start | bytes 7684
  2.5 33.2 %collective-permute-start.6 = (bf16[160,1280]{1,0:T(8,128)(2,1)}, bf16[160,1280]{1,0:T(8,128)(2,1)}, u32[]{:S(2)}, u32[]{:S(2)}) collective-permute-start(bf16[160,1280]{1,0:T(8,128)(2,1)} %constant_dynamic-slice_fusion), channel_id=1, source_target_pairs={{128,0},{0,128},{129,1},{1,129},{130,2},{2,130},{131,3},{3,131},{1... | collective-permute-start | bytes 1228808 | tf_op jit(solution)/shard_map/ppermute | solution.py:22
  12.8 25.1 %collective-permute-start = (bf16[2,256,640]{2,1,0:T(8,128)(2,1)}, bf16[2,256,640]{2,1,0:T(8,128)(2,1)S(1)}, u32[]{:S(2)}, u32[]{:S(2)}) collective-permute-start(bf16[2,256,640]{2,1,0:T(8,128)(2,1)} %get-tuple-element.13), channel_id=1, source_target_pairs={{1,0},{2,1},{3,2},{4,3},{5,4},{6,5},{7,6},{8,7},{9,8},{10,9},{11,1... | collective-permute-start | bytes 1966088 | tf_op jit(solution)/shard_map/ppermute | solution.py:22
  13.8 31.5 %collective-permute-start.1 = (bf16[2,256,640]{2,1,0:T(8,128)(2,1)}, bf16[2,256,640]{2,1,0:T(8,128)(2,1)S(1)}, u32[]{:S(2)}, u32[]{:S(2)}) collective-permute-start(bf16[2,256,640]{2,1,0:T(8,128)(2,1)} %get-tuple-element.14), channel_id=1, source_target_pairs={{33,0},{34,1},{35,2},{36,3},{37,4},{38,5},{39,6},{40,7},{41,8},{42... | collective-permute-start | bytes 1966088 | tf_op jit(solution)/shard_map/ppermute | solution.py:22
  21.7 26.9 %collective-permute-start.2 = (bf16[2,256,640]{2,1,0:T(8,128)(2,1)}, bf16[2,256,640]{2,1,0:T(8,128)(2,1)S(1)}, u32[]{:S(2)}, u32[]{:S(2)}) collective-permute-start(bf16[2,256,640]{2,1,0:T(8,128)(2,1)} %get-tuple-element.15), channel_id=1, source_target_pairs={{65,0},{66,1},{67,2},{68,3},{69,4},{70,5},{71,6},{72,7},{73,8},{74... | collective-permute-start | bytes 1966088 | tf_op jit(solution)/shard_map/ppermute | solution.py:22
  22.5 35.7 %collective-permute-start.3 = (bf16[2,256,640]{2,1,0:T(8,128)(2,1)}, bf16[2,256,640]{2,1,0:T(8,128)(2,1)}, u32[]{:S(2)}, u32[]{:S(2)}) collective-permute-start(bf16[2,256,640]{2,1,0:T(8,128)(2,1)} %get-tuple-element.16), channel_id=1, source_target_pairs={{97,0},{98,1},{99,2},{100,3},{101,4},{102,5},{103,6},{104,7},{105,... | collective-permute-start | bytes 1966088 | tf_op jit(solution)/shard_map/ppermute | solution.py:22
  33.4 5.9 %copy-start.12 = (s32[256]{0:T(256)S(1)}, s32[256]{0:T(256)}, u32[]{:S(2)}) copy-start(s32[256]{0:T(256)} %param.25) | copy-start | bytes 3076
  35.8 42.4 %collective-permute-start.10 = (bf16[2,256,640]{2,1,0:T(8,128)(2,1)}, bf16[2,256,640]{2,1,0:T(8,128)(2,1)}, u32[]{:S(2)}, u32[]{:S(2)}) collective-permute-start(bf16[2,256,640]{2,1,0:T(8,128)(2,1)} %pad_maximum_fusion.3), channel_id=1, source_target_pairs={{96,0},{97,1},{98,2},{99,3},{100,4},{101,5},{102,6},{103,7},{104,8... | collective-permute-start | bytes 1966088 | tf_op jit(solution)/shard_map/ppermute | solution.py:22
  37.8 23.8 %copy-start.2 = (bf16[2,256,640]{2,1,0:T(8,128)(2,1)}, bf16[2,256,640]{2,1,0:T(8,128)(2,1)S(1)}, u32[]{:S(2)}) copy-start(bf16[2,256,640]{2,1,0:T(8,128)(2,1)S(1)} %collective-permute-done.refs_0_.refs_4_) | copy-start | bytes 1966084
  37.8 44.4 %collective-permute-start.11 = (bf16[2,256,640]{2,1,0:T(8,128)(2,1)}, bf16[2,256,640]{2,1,0:T(8,128)(2,1)S(1)}, u32[]{:S(2)}, u32[]{:S(2)}) collective-permute-start(bf16[2,256,640]{2,1,0:T(8,128)(2,1)} %pad_maximum_fusion.4), channel_id=1, source_target_pairs={{32,0},{33,1},{34,2},{35,3},{36,4},{37,5},{38,6},{39,7},{40,8},{41... | collective-permute-start | bytes 1966088 | tf_op jit(solution)/shard_map/ppermute | solution.py:22
  45.3 16.2 %copy-start.3 = (bf16[2,256,640]{2,1,0:T(8,128)(2,1)}, bf16[2,256,640]{2,1,0:T(8,128)(2,1)S(1)}, u32[]{:S(2)}) copy-start(bf16[2,256,640]{2,1,0:T(8,128)(2,1)S(1)} %collective-permute-done.1.refs_1_.refs_5_) | copy-start | bytes 1966084
  45.4 38.5 %collective-permute-start.9 = (bf16[160,1280]{1,0:T(8,128)(2,1)}, bf16[160,1280]{1,0:T(8,128)(2,1)}, u32[]{:S(2)}, u32[]{:S(2)}) collective-permute-start(bf16[160,1280]{1,0:T(8,128)(2,1)} %collective-permute-done.6), channel_id=1, source_target_pairs={{0,3},{1,2},{2,1},{3,0},{4,7},{5,6},{6,5},{7,4},{8,11},{9,10},{10,... | collective-permute-start | bytes 1228808 | tf_op jit(solution)/shard_map/ppermute | solution.py:59
  48.6 13.0 %copy-start.4 = (bf16[2,256,640]{2,1,0:T(8,128)(2,1)}, bf16[2,256,640]{2,1,0:T(8,128)(2,1)S(1)}, u32[]{:S(2)}) copy-start(bf16[2,256,640]{2,1,0:T(8,128)(2,1)S(1)} %collective-permute-done.2.refs_2_.refs_6_) | copy-start | bytes 1966084
  48.6 35.3 %collective-permute-start.8 = (bf16[160,1280]{1,0:T(8,128)(2,1)}, bf16[160,1280]{1,0:T(8,128)(2,1)}, u32[]{:S(2)}, u32[]{:S(2)}) collective-permute-start(bf16[160,1280]{1,0:T(8,128)(2,1)} %collective-permute-done.6), channel_id=1, source_target_pairs={{0,2},{1,3},{2,0},{3,1},{4,6},{5,7},{6,4},{7,5},{8,10},{9,11},{10,... | collective-permute-start | bytes 1228808 | tf_op jit(solution)/shard_map/ppermute | solution.py:59
  58.2 25.6 %collective-permute-start.7 = (bf16[160,1280]{1,0:T(8,128)(2,1)}, bf16[160,1280]{1,0:T(8,128)(2,1)}, u32[]{:S(2)}, u32[]{:S(2)}) collective-permute-start(bf16[160,1280]{1,0:T(8,128)(2,1)} %collective-permute-done.6), channel_id=1, source_target_pairs={{0,1},{1,0},{2,3},{3,2},{4,5},{5,4},{6,7},{7,6},{8,9},{9,8},{10,11... | collective-permute-start | bytes 1228808 | tf_op jit(solution)/shard_map/ppermute | solution.py:59
  71.1 7.1 %copy-start.6 = (bf16[512,384]{1,0:T(8,128)(2,1)S(1)}, bf16[512,384]{1,0:T(8,128)(2,1)}, u32[]{:S(2)}) copy-start(bf16[512,384]{1,0:T(8,128)(2,1)} %shard_map.150) | copy-start | bytes 1179652
  78.2 4.0 %copy-start.7 = (bf16[512,256]{1,0:T(8,128)(2,1)S(1)}, bf16[512,256]{1,0:T(8,128)(2,1)}, u32[]{:S(2)}) copy-start(bf16[512,256]{1,0:T(8,128)(2,1)} %shard_map.151) | copy-start | bytes 786436
  78.2 12.5 %collective-permute-start.4 = (bf16[512,384]{1,0:T(8,128)(2,1)S(1)}, bf16[512,384]{1,0:T(8,128)(2,1)S(1)}, u32[]{:S(2)}, u32[]{:S(2)}) collective-permute-start(bf16[512,384]{1,0:T(8,128)(2,1)S(1)} %copy-done.6), channel_id=1, source_target_pairs={{128,0},{0,128},{129,1},{1,129},{130,2},{2,130},{131,3},{3,131},{1... | collective-permute-start | bytes 1179656 | tf_op jit(solution)/shard_map/ppermute | solution.py:22
  82.2 14.1 %collective-permute-start.5 = (bf16[512,256]{1,0:T(8,128)(2,1)S(1)}, bf16[512,256]{1,0:T(8,128)(2,1)S(1)}, u32[]{:S(2)}, u32[]{:S(2)}) collective-permute-start(bf16[512,256]{1,0:T(8,128)(2,1)S(1)} %copy-done.7), channel_id=1, source_target_pairs={{128,0},{0,128},{129,1},{1,129},{130,2},{2,130},{131,3},{3,131},{1... | collective-permute-start | bytes 786440 | tf_op jit(solution)/shard_map/ppermute | solution.py:22
  83.8 2.2 %copy-start.8 = (bf16[2,256,640]{2,1,0:T(8,128)(2,1)}, bf16[2,256,640]{2,1,0:T(8,128)(2,1)S(1)}, u32[]{:S(2)}) copy-start(bf16[2,256,640]{2,1,0:T(8,128)(2,1)S(1)} %get-tuple-element.26) | copy-start | bytes 1966084
  83.8 2.2 %copy-start.9 = (bf16[2,256,640]{2,1,0:T(8,128)(2,1)}, bf16[2,256,640]{2,1,0:T(8,128)(2,1)S(1)}, u32[]{:S(2)}) copy-start(bf16[2,256,640]{2,1,0:T(8,128)(2,1)S(1)} %get-tuple-element.25) | copy-start | bytes 1966084
  83.9 2.4 %copy-start.5 = (bf16[640,1280]{1,0:T(8,128)(2,1)S(1)}, bf16[640,1280]{1,0:T(8,128)(2,1)}, u32[]{:S(2)}) copy-start(bf16[640,1280]{1,0:T(8,128)(2,1)} %param.17) | copy-start | bytes 4915204
  96.6 2.0 %copy-start.1 = (bf16[512,1280]{1,0:T(8,128)(2,1)S(1)}, bf16[512,1280]{1,0:T(8,128)(2,1)}, u32[]{:S(2)}) copy-start(bf16[512,1280]{1,0:T(8,128)(2,1)} %x_ref.1) | copy-start | bytes 3932164
  96.6 2.0 %copy-start.10 = (f32[1280]{0:T(1024)S(1)}, f32[1280]{0:T(1024)}, u32[]{:S(2)}) copy-start(f32[1280]{0:T(1024)} %param.19) | copy-start | bytes 15364

commit v14 on v11

--- a/solution.py
+++ b/solution.py
@@ -262,10 +262,8 @@
     )
     fetched = fetch_pages(pool_keys, pool_values, prefix_pages)
     pairs_here = width_half // (2 * HD)
-    split = (pairs_here + 1) // 2
     parts = [
-        attention(queries, key_rows, value_rows, fetched, req_len, prefix_len, first, count)
-        for first, count in ((0, split), (split, pairs_here - split))
+        attention(queries, key_rows, value_rows, fetched, req_len, prefix_len, 0, pairs_here)
     ]
     other_parts = [from_behind(part, "kv", 1) for part in parts]
     attended = jnp.concatenate(parts, axis=1)

time: 89.9 us -> 98.4 us (1.095)
  waiting for transfers between devices: 16 us -> 29.5 us
  starting transfers between devices: 18 us -> 15.5 us
  Pallas kernels: 30.7 us -> 28.8 us
    ppermute x9 -> x8, waiting for transfers between devices: 16 us -> 29.5 us  [from_behind(): return lax.ppermute(block, axis, route)]
    ppermute x9 -> x8, starting transfers between devices: 17.8 us -> 15.5 us  [from_behind(): return lax.ppermute(block, axis, route)]
    pallas_call x2 -> x1, Pallas kernels: 16.5 us -> 14.7 us  [attention(): pl.pallas_call(attention_kernel, out_shape=jax.ShapeDtypeStruct((tokens,...]
    another operation x2, other arithmetic: 1.85 us -> 0.15 us  [relay(): jnp.stack([key_pages[block_index], value_pages[block_index]])]
    unnamed x28 -> x25, local copies, waits for them, and re-layouts: 2.65 us -> 1.48 us
    select_n x1, other arithmetic: 0.11 us -> 1.26 us  [other_half_once_per_chip(): jnp.where(first, pulled, swapped)]
    dynamic_update_slice x2, local copies, waits for them, and re-layouts: 1.12 us -> 2.19 us  [relay(): lax.dynamic_update_index_in_dim(value_out, received[1], target, 0)]
  transfers between devices with their start and end apart: 10 -> 9, of which waited for: 4 -> 4; matrix products, arithmetic and copies ran while one was open for 12% -> 9% of each run, Pallas kernels for 29% -> 30%
where the time goes in v14:
time: 98.4 us; the launch traced here: 97.3 us
  waiting for transfers between devices  29.5 us (30%)
  Pallas kernels  28.8 us (29%)
  starting transfers between devices  15.5 us (16%)
  local copies, waits for them, and re-layouts  10.5 us (11%)
  between operations  5.7 us (6%)
  other arithmetic  5.19 us (5%)
  matrix products  1.98 us (2%)
    ppermute x8, waiting for transfers between devices, from_behind(): return lax.ppermute(block, axis, route)  29.5 us
    ppermute x8, starting transfers between devices, from_behind(): return lax.ppermute(block, axis, route)  15.5 us
    pallas_call x1, Pallas kernels, attention(): pl.pallas_call(attention_kernel, out_shape=jax.ShapeDtypeStruct((tokens,...  14.7 us
    pallas_call x1, Pallas kernels, projections(): pl.pallas_call(projection_kernel, out_shape=(shape, shape, shape), grid=(...  9.11 us
    pallas_call x1, Pallas kernels, fetch_pages(): pl.pallas_call(functools.partial(gather_kernel, devices), out_shape=[page...  5.03 us
    dynamic_update_slice x2, local copies, waits for them, and re-layouts, relay(): lax.dynamic_update_index_in_dim(value_out, received[1], target, 0)  2.19 us
    dynamic_slice x1, local copies, waits for them, and re-layouts, other_half_once_per_chip(): mine = lax.dynamic_slice_in_dim(w_out, core * rows, rows, 0)  2.19 us
    dot_general x1, matrix products, body(): jnp.dot(in_kv_order(attended, other_attended, 1), in_kv_order(w_out, othe...  1.98 us
  transfers between devices with their start and end apart: 9, of which 4 were waited for; matrix products, arithmetic and copies ran while one was open for 9% of the time, Pallas kernels for 30%

profile of v14, /device:TPU:6, one launch (start us, length us, event | category | flops | bytes accessed | tf_op | source)
XLA Modules:
  0.0 97.3 jit_solution(15521686247933699555)
XLA Ops:
  0.6 0.0 copy-start
  0.7 0.0 copy-start.10
  0.7 2.2 %constant_dynamic-slice_fusion = bf16[320,1280]{1,0:T(8,128)(2,1)} fusion(bf16[640,1280]{1,0:T(8,128)(2,1)} %param.17, s32[]{:T(128)S(6)} %select_n.83), kind=kLoop, calls=%fused_computation.36 | loop fusion | bytes 1638404 | tf_op jit(solution)/shard_map/dynamic_slice | solution.py:55
  2.9 3.2 %collective-permute-start.5 = (bf16[320,1280]{1,0:T(8,128)(2,1)}, bf16[320,1280]{1,0:T(8,128)(2,1)}, u32[]{:S(2)}, u32[]{:S(2)}) collective-permute-start(bf16[320,1280]{1,0:T(8,128)(2,1)} %constant_dynamic-slice_fusion), channel_id=1, source_target_pairs={{128,0},{0,128},{129,1},{1,129},{130,2},{2,130},{131,3},{3,131},{1... | collective-permute-start | bytes 2457608 | tf_op jit(solution)/shard_map/ppermute | solution.py:22
  6.1 1.4 %copy.18.pages_ref = s32[128,4]{1,0:T(8,128)} copy(s32[128,4]{0,1:T(4,128)} %param.24) | data formatting | bytes 4096 | tf_op args[11]
  7.5 5.0 %shard_map.149 = (bf16[2,256,640]{2,1,0:T(8,128)(2,1)}, bf16[2,256,640]{2,1,0:T(8,128)(2,1)}, bf16[2,256,640]{2,1,0:T(8,128)(2,1)}, bf16[2,256,640]{2,1,0:T(8,128)(2,1)}) custom-call(s32[128,4]{1,0:T(8,128)} %copy.18.pages_ref, bf16[4,256,640]{2,1,0:T(8,128)(2,1)} %keys_hbm.1, bf16[4,256,640]{2,1,0:T(8,128)(2,1)} %values_hbm.1), custom_call_target="tpu_custom_call" | custom-call | tf_op jit(solution)/shard_map/pallas_call | solution.py:206
  12.5 5.4 %collective-permute-start = (bf16[2,256,640]{2,1,0:T(8,128)(2,1)}, bf16[2,256,640]{2,1,0:T(8,128)(2,1)S(1)}, u32[]{:S(2)}, u32[]{:S(2)}) collective-permute-start(bf16[2,256,640]{2,1,0:T(8,128)(2,1)} %get-tuple-element.13), channel_id=1, source_target_pairs={{1,0},{2,1},{3,2},{4,3},{5,4},{6,5},{7,6},{8,7},{9,8},{10,9},{11,1... | collective-permute-start | bytes 1966088 | tf_op jit(solution)/shard_map/ppermute | solution.py:22
  17.9 1.6 %collective-permute-start.1 = (bf16[2,256,640]{2,1,0:T(8,128)(2,1)}, bf16[2,256,640]{2,1,0:T(8,128)(2,1)S(1)}, u32[]{:S(2)}, u32[]{:S(2)}) collective-permute-start(bf16[2,256,640]{2,1,0:T(8,128)(2,1)} %get-tuple-element.14), channel_id=1, source_target_pairs={{33,0},{34,1},{35,2},{36,3},{37,4},{38,5},{39,6},{40,7},{41,8},{42... | collective-permute-start | bytes 1966088 | tf_op jit(solution)/shard_map/ppermute | solution.py:22
  19.5 1.8 %collective-permute-start.2 = (bf16[2,256,640]{2,1,0:T(8,128)(2,1)}, bf16[2,256,640]{2,1,0:T(8,128)(2,1)S(1)}, u32[]{:S(2)}, u32[]{:S(2)}) collective-permute-start(bf16[2,256,640]{2,1,0:T(8,128)(2,1)} %get-tuple-element.15), channel_id=1, source_target_pairs={{65,0},{66,1},{67,2},{68,3},{69,4},{70,5},{71,6},{72,7},{73,8},{74... | collective-permute-start | bytes 1966088 | tf_op jit(solution)/shard_map/ppermute | solution.py:22
  21.3 0.0 collective-permute-start.3
  21.3 0.0 copy-done
  21.4 0.3 fusion.7
  21.7 0.9 copy.17.scale_ref
  22.6 0.0 copy-done.10
  22.6 0.6 reshape.53.gain_ref
  23.1 9.1 %shard_map.148 = (bf16[512,640]{1,0:T(8,128)(2,1)}, bf16[512,640]{1,0:T(8,128)(2,1)}, bf16[512,640]{1,0:T(8,128)(2,1)}) custom-call(bf16[512,1280]{1,0:T(8,128)(2,1)} %x_ref.1, f32[512,1]{1,0:T(8,128)} %copy.17.scale_ref, bf16[1280,640]{1,0:T(8,128)(2,1)} %wq_ref.1, bf16[1280,640]{1,0:T(8,128)(2,1)} %wk_ref.1, bf16[1280,640]{1,0:T(8,128)(2,1)} %wv_ref.1, ...), custom_call_target="tpu_custom_call" | custom-call | tf_op jit(solution)/shard_map/pallas_call | solution.py:98
  32.2 0.0 copy-start.11
  32.2 1.4 %slice_bitcast_fusion = (bf16[1,256,640]{2,1,0:T(8,128)(2,1)S(1)}, bf16[1,256,640]{2,1,0:T(8,128)(2,1)S(1)}, bf16[1,256,640]{2,1,0:T(8,128)(2,1)S(1)}, bf16[1,256,640]{2,1,0:T(8,128)(2,1)S(1)}) fusion(bf16[512,640]{1,0:T(8,128)(2,1)} %get-tuple-element.12.v_ref, bf16[512,640]{1,0:T(8,128)(2,1)} %get-tuple-element.11.k_ref), kind=kLoop, calls=%fused_computation.29 | loop fusion | bytes 2621440 | tf_op jit(solution)/shard_map/slice | solution.py:229
  33.6 0.1 pad_maximum_fusion.1
  33.7 0.0 collective-permute-done.refs_0_.refs_4_
  33.7 0.0 copy-start.3
  33.7 1.5 %collective-permute-start.7 = (bf16[2,256,640]{2,1,0:T(8,128)(2,1)S(1)}, bf16[2,256,640]{2,1,0:T(8,128)(2,1)}, u32[]{:S(2)}, u32[]{:S(2)}) collective-permute-start(bf16[2,256,640]{2,1,0:T(8,128)(2,1)S(1)} %pad_maximum_fusion.1), channel_id=1, source_target_pairs={{96,0},{97,1},{98,2},{99,3},{100,4},{101,5},{102,6},{103,7},{104,8... | collective-permute-start | bytes 1966088 | tf_op jit(solution)/shard_map/ppermute | solution.py:22
  35.3 0.1 pad_maximum_fusion.2
  35.4 8.0 %collective-permute-done.1.refs_1_.refs_5_ = bf16[2,256,640]{2,1,0:T(8,128)(2,1)S(1)} collective-permute-done((bf16[2,256,640]{2,1,0:T(8,128)(2,1)}, bf16[2,256,640]{2,1,0:T(8,128)(2,1)S(1)}, u32[]{:S(2)}, u32[]{:S(2)}) %collective-permute-start.1) | collective-permute-done | bytes 655392 | tf_op jit(solution)/shard_map/ppermute | solution.py:22
  43.4 0.0 copy-start.4
  43.4 0.0 collective-permute-start.8
  43.4 0.0 copy-done.11
  43.4 0.7 fusion.12
  49.0 5.7 %collective-permute-done.2.refs_2_.refs_6_ = bf16[2,256,640]{2,1,0:T(8,128)(2,1)S(1)} collective-permute-done((bf16[2,256,640]{2,1,0:T(8,128)(2,1)}, bf16[2,256,640]{2,1,0:T(8,128)(2,1)S(1)}, u32[]{:S(2)}, u32[]{:S(2)}) %collective-permute-start.2) | collective-permute-done | bytes 655392 | tf_op jit(solution)/shard_map/ppermute | solution.py:22
  54.6 0.0 copy-start.5
  54.6 4.4 %collective-permute-done.3.refs_3_.refs_7_ = bf16[2,256,640]{2,1,0:T(8,128)(2,1)} collective-permute-done((bf16[2,256,640]{2,1,0:T(8,128)(2,1)}, bf16[2,256,640]{2,1,0:T(8,128)(2,1)}, u32[]{:S(2)}, u32[]{:S(2)}) %collective-permute-start.3) | collective-permute-done | bytes 655392 | tf_op jit(solution)/shard_map/ppermute | solution.py:22
  59.1 0.0 copy-done.3
  59.1 0.0 copy-done.4
  59.1 0.0 copy-done.5
  59.1 14.7 %shard_map.150 = bf16[512,640]{1,0:T(8,128)(2,1)} custom-call(s32[1]{0:T(128)S(6)} %copy.23.live_ref, s32[1]{0:T(128)S(6)} %copy.24.depth_ref, bf16[512,640]{1,0:T(8,128)(2,1)} %get-tuple-element.10.q_ref, bf16[512,640]{1,0:T(8,128)(2,1)} %get-tuple-element.11.k_ref, bf16[512,640]{1,0:T(8,128)(2,1)} %get-tuple-element.12.v_ref, ...), custom_call_target="tpu_custom_call" | custom-call | tf_op jit(solution)/shard_map/pallas_call | solution.py:170
  73.8 1.9 %collective-permute-start.4 = (bf16[512,640]{1,0:T(8,128)(2,1)}, bf16[512,640]{1,0:T(8,128)(2,1)S(1)}, u32[]{:S(2)}, u32[]{:S(2)}) collective-permute-start(bf16[512,640]{1,0:T(8,128)(2,1)} %shard_map.150), channel_id=1, source_target_pairs={{128,0},{0,128},{129,1},{1,129},{130,2},{2,130},{131,3},{3,131},{1... | collective-permute-start | bytes 1966088 | tf_op jit(solution)/shard_map/ppermute | solution.py:22
  75.7 0.0 collective-permute-done.5
  75.7 0.0 collective-permute-start.6
  75.7 0.0 collective-permute-done.7
  75.7 0.1 broadcast.62.clone
  75.8 1.0 %slice_dynamic-update-slice_fusion.1 = bf16[2,256,640]{2,1,0:T(8,128)(2,1)S(1)} fusion(bf16[2,256,640]{2,1,0:T(8,128)(2,1)S(1)} %broadcast.62.clone, s32[]{:T(128)S(6)} %select_n.91, bf16[2,256,640]{2,1,0:T(8,128)(2,1)} %collective-permute-done.7), kind=kLoop, calls=%fused_computation.26 | loop fusion | bytes 655364 | tf_op jit(solution)/shard_map/jit(dynamic_update_index_in_dim)/dynamic_update_slice | solution.py:234
  76.8 0.1 broadcast.62.clone.1
  76.9 1.0 %slice_dynamic-update-slice_fusion.3 = bf16[2,256,640]{2,1,0:T(8,128)(2,1)S(1)} fusion(bf16[2,256,640]{2,1,0:T(8,128)(2,1)S(1)} %broadcast.62.clone.1, s32[]{:T(128)S(6)} %select_n.91, bf16[2,256,640]{2,1,0:T(8,128)(2,1)} %collective-permute-done.7), kind=kLoop, calls=%fused_computation.28 | loop fusion | bytes 655364 | tf_op jit(solution)/shard_map/jit(dynamic_update_index_in_dim)/dynamic_update_slice | solution.py:233
  77.9 0.0 collective-permute-done.8
  77.9 1.2 %slice_dynamic-update-slice_fusion = (bf16[2,256,640]{2,1,0:T(8,128)(2,1)S(1)}, bf16[2,256,640]{2,1,0:T(8,128)(2,1)S(1)}) fusion(bf16[2,256,640]{2,1,0:T(8,128)(2,1)S(1)} %slice_dynamic-update-slice_fusion.1, s32[]{:T(128)S(6)} %select_n.95, bf16[2,256,640]{2,1,0:T(8,128)(2,1)} %collective-permute-done.8, ...), kind=kLoop, calls=%fused_computation.25 | loop fusion | bytes 1310724 | tf_op jit(solution)/shard_map/jit(dynamic_update_index_in_dim)/dynamic_update_slice | solution.py:234
  79.1 0.0 copy-start.7
  79.1 0.0 copy-start.8
  79.1 0.0 copy-start.2
  79.1 11.4 %collective-permute-done.4 = bf16[512,640]{1,0:T(8,128)(2,1)S(1)} collective-permute-done((bf16[512,640]{1,0:T(8,128)(2,1)}, bf16[512,640]{1,0:T(8,128)(2,1)S(1)}, u32[]{:S(2)}, u32[]{:S(2)}) %collective-permute-start.4) | collective-permute-done | bytes 655392 | tf_op jit(solution)/shard_map/ppermute | solution.py:22
  90.5 0.0 copy-done.6
  90.5 0.1 broadcast_select_fusion.5
  90.7 0.0 collective-permute-done.6
  90.7 1.3 %broadcast_select_fusion.3 = (bf16[320,1280]{1,0:T(8,128)(2,1)S(1)}, bf16[320,1280]{1,0:T(8,128)(2,1)S(1)}) fusion(bf16[320,1280]{1,0:T(8,128)(2,1)} %collective-permute-done.5, bf16[320,1280]{1,0:T(8,128)(2,1)S(1)} %collective-permute-done.6, pred[]{:T(512)S(6)} %eq.14), kind=kLoop, calls=%fused_computation.20 | loop fusion | flops 819200 | bytes 3276801 | tf_op jit(solution)/shard_map/jit(_where)/select_n | solution.py:61
  91.9 0.0 copy-done.7
  91.9 0.0 copy-done.8
  91.9 0.0 copy-done.2
  92.0 0.6 broadcast_select_fusion.1
  92.6 0.0 copy-start.1
  92.6 0.0 copy-start.9
  92.6 2.0 %multiply_reduce_fusion.1 = (f32[512]{0:T(512)S(1)}, f32[512,1280]{1,0:T(8,128)S(1)}) fusion(bf16[640,1280]{1,0:T(8,128)(2,1)S(1)} %get-tuple-element.18, bf16[640,1280]{1,0:T(8,128)(2,1)S(1)} %get-tuple-element.17, bf16[512,640]{1,0:T(8,128)(2,1)S(1)} %get-tuple-element.22, bf16[512,640]{1,0:T(8,128)(2,1)S(1)} %get-tuple-element.21), kind=kOutput, calls=%fused_computation.12 | convolution fusion | flops 1688206848 | bytes 7211008 | tf_op jit(solution)/shard_map/dot_general | solution.py:271
  94.6 0.0 copy-done.1
  94.6 0.0 copy-done.9
  94.6 0.8 multiply_reduce_fusion
  95.5 1.8 %multiply_convert_fusion = bf16[512,1280]{1,0:T(8,128)(2,1)} fusion(f32[512]{0:T(512)S(1)} %add_rsqrt_fusion, f32[512,1280]{1,0:T(8,128)S(1)} %get-tuple-element.32, f32[512]{0:T(512)S(1)} %add_rsqrt_fusion.1, f32[1280]{0:T(1024)S(1)} %copy-done.9, f32[512]{0:T(512)S(1)} %add_rsqrt_fusion.2, bf16[512,1280]{1,0:T(8,128)(2,1)S(1)} %copy-done.1), kind=kLoop, calls=%fused_computation.10 | loop fusion | flops 5242880 | bytes 5254144 | tf_op jit(solution)/shard_map/convert_element_type | solution.py:277
  (4 shorter events, 0.0 us)
Async XLA Ops:
  0.6 20.7 %copy-start = (bf16[512,1280]{1,0:T(8,128)(2,1)S(1)}, bf16[512,1280]{1,0:T(8,128)(2,1)}, u32[]{:S(2)}) copy-start(bf16[512,1280]{1,0:T(8,128)(2,1)} %x_ref.1) | copy-start | bytes 3932164
  0.7 21.9 %copy-start.10 = (f32[640]{0:T(1024)S(1)}, f32[640]{0:T(1024)}, u32[]{:S(2)}) copy-start(f32[640]{0:T(1024)} %param.18) | copy-start | bytes 7684
  2.9 72.8 %collective-permute-start.5 = (bf16[320,1280]{1,0:T(8,128)(2,1)}, bf16[320,1280]{1,0:T(8,128)(2,1)}, u32[]{:S(2)}, u32[]{:S(2)}) collective-permute-start(bf16[320,1280]{1,0:T(8,128)(2,1)} %constant_dynamic-slice_fusion), channel_id=1, source_target_pairs={{128,0},{0,128},{129,1},{1,129},{130,2},{2,130},{131,3},{3,131},{1... | collective-permute-start | bytes 2457608 | tf_op jit(solution)/shard_map/ppermute | solution.py:22
  12.5 21.2 %collective-permute-start = (bf16[2,256,640]{2,1,0:T(8,128)(2,1)}, bf16[2,256,640]{2,1,0:T(8,128)(2,1)S(1)}, u32[]{:S(2)}, u32[]{:S(2)}) collective-permute-start(bf16[2,256,640]{2,1,0:T(8,128)(2,1)} %get-tuple-element.13), channel_id=1, source_target_pairs={{1,0},{2,1},{3,2},{4,3},{5,4},{6,5},{7,6},{8,7},{9,8},{10,9},{11,1... | collective-permute-start | bytes 1966088 | tf_op jit(solution)/shard_map/ppermute | solution.py:22
  17.9 25.5 %collective-permute-start.1 = (bf16[2,256,640]{2,1,0:T(8,128)(2,1)}, bf16[2,256,640]{2,1,0:T(8,128)(2,1)S(1)}, u32[]{:S(2)}, u32[]{:S(2)}) collective-permute-start(bf16[2,256,640]{2,1,0:T(8,128)(2,1)} %get-tuple-element.14), channel_id=1, source_target_pairs={{33,0},{34,1},{35,2},{36,3},{37,4},{38,5},{39,6},{40,7},{41,8},{42... | collective-permute-start | bytes 1966088 | tf_op jit(solution)/shard_map/ppermute | solution.py:22
  19.5 35.1 %collective-permute-start.2 = (bf16[2,256,640]{2,1,0:T(8,128)(2,1)}, bf16[2,256,640]{2,1,0:T(8,128)(2,1)S(1)}, u32[]{:S(2)}, u32[]{:S(2)}) collective-permute-start(bf16[2,256,640]{2,1,0:T(8,128)(2,1)} %get-tuple-element.15), channel_id=1, source_target_pairs={{65,0},{66,1},{67,2},{68,3},{69,4},{70,5},{71,6},{72,7},{73,8},{74... | collective-permute-start | bytes 1966088 | tf_op jit(solution)/shard_map/ppermute | solution.py:22
  21.3 37.7 %collective-permute-start.3 = (bf16[2,256,640]{2,1,0:T(8,128)(2,1)}, bf16[2,256,640]{2,1,0:T(8,128)(2,1)}, u32[]{:S(2)}, u32[]{:S(2)}) collective-permute-start(bf16[2,256,640]{2,1,0:T(8,128)(2,1)} %get-tuple-element.16), channel_id=1, source_target_pairs={{97,0},{98,1},{99,2},{100,3},{101,4},{102,5},{103,6},{104,7},{105,... | collective-permute-start | bytes 1966088 | tf_op jit(solution)/shard_map/ppermute | solution.py:22
  32.2 11.2 %copy-start.11 = (s32[256]{0:T(256)S(1)}, s32[256]{0:T(256)}, u32[]{:S(2)}) copy-start(s32[256]{0:T(256)} %param.25) | copy-start | bytes 3076
  33.7 25.3 %copy-start.3 = (bf16[2,256,640]{2,1,0:T(8,128)(2,1)}, bf16[2,256,640]{2,1,0:T(8,128)(2,1)S(1)}, u32[]{:S(2)}) copy-start(bf16[2,256,640]{2,1,0:T(8,128)(2,1)S(1)} %collective-permute-done.refs_0_.refs_4_) | copy-start | bytes 1966084
  33.7 42.0 %collective-permute-start.7 = (bf16[2,256,640]{2,1,0:T(8,128)(2,1)S(1)}, bf16[2,256,640]{2,1,0:T(8,128)(2,1)}, u32[]{:S(2)}, u32[]{:S(2)}) collective-permute-start(bf16[2,256,640]{2,1,0:T(8,128)(2,1)S(1)} %pad_maximum_fusion.1), channel_id=1, source_target_pairs={{96,0},{97,1},{98,2},{99,3},{100,4},{101,5},{102,6},{103,7},{104,8... | collective-permute-start | bytes 1966088 | tf_op jit(solution)/shard_map/ppermute | solution.py:22
  43.4 15.7 %copy-start.4 = (bf16[2,256,640]{2,1,0:T(8,128)(2,1)}, bf16[2,256,640]{2,1,0:T(8,128)(2,1)S(1)}, u32[]{:S(2)}) copy-start(bf16[2,256,640]{2,1,0:T(8,128)(2,1)S(1)} %collective-permute-done.1.refs_1_.refs_5_) | copy-start | bytes 1966084
  43.4 34.5 %collective-permute-start.8 = (bf16[2,256,640]{2,1,0:T(8,128)(2,1)S(1)}, bf16[2,256,640]{2,1,0:T(8,128)(2,1)}, u32[]{:S(2)}, u32[]{:S(2)}) collective-permute-start(bf16[2,256,640]{2,1,0:T(8,128)(2,1)S(1)} %pad_maximum_fusion.2), channel_id=1, source_target_pairs={{32,0},{33,1},{34,2},{35,3},{36,4},{37,5},{38,6},{39,7},{40,8},{41... | collective-permute-start | bytes 1966088 | tf_op jit(solution)/shard_map/ppermute | solution.py:22
  54.6 4.5 %copy-start.5 = (bf16[2,256,640]{2,1,0:T(8,128)(2,1)}, bf16[2,256,640]{2,1,0:T(8,128)(2,1)S(1)}, u32[]{:S(2)}) copy-start(bf16[2,256,640]{2,1,0:T(8,128)(2,1)S(1)} %collective-permute-done.2.refs_2_.refs_6_) | copy-start | bytes 1966084
  73.8 16.7 %copy-start.6 = (bf16[512,640]{1,0:T(8,128)(2,1)S(1)}, bf16[512,640]{1,0:T(8,128)(2,1)}, u32[]{:S(2)}) copy-start(bf16[512,640]{1,0:T(8,128)(2,1)} %shard_map.150) | copy-start | bytes 1966084
  73.8 16.7 %collective-permute-start.4 = (bf16[512,640]{1,0:T(8,128)(2,1)}, bf16[512,640]{1,0:T(8,128)(2,1)S(1)}, u32[]{:S(2)}, u32[]{:S(2)}) collective-permute-start(bf16[512,640]{1,0:T(8,128)(2,1)} %shard_map.150), channel_id=1, source_target_pairs={{128,0},{0,128},{129,1},{1,129},{130,2},{2,130},{131,3},{3,131},{1... | collective-permute-start | bytes 1966088 | tf_op jit(solution)/shard_map/ppermute | solution.py:22
  75.7 15.0 %collective-permute-start.6 = (bf16[320,1280]{1,0:T(8,128)(2,1)}, bf16[320,1280]{1,0:T(8,128)(2,1)S(1)}, u32[]{:S(2)}, u32[]{:S(2)}) collective-permute-start(bf16[320,1280]{1,0:T(8,128)(2,1)} %collective-permute-done.5), channel_id=1, source_target_pairs={{0,1},{1,0},{2,3},{3,2},{4,5},{5,4},{6,7},{7,6},{8,9},{9,8},{10,11... | collective-permute-start | bytes 2457608 | tf_op jit(solution)/shard_map/ppermute | solution.py:58
  79.1 12.9 %copy-start.7 = (bf16[2,256,640]{2,1,0:T(8,128)(2,1)}, bf16[2,256,640]{2,1,0:T(8,128)(2,1)S(1)}, u32[]{:S(2)}) copy-start(bf16[2,256,640]{2,1,0:T(8,128)(2,1)S(1)} %get-tuple-element.24) | copy-start | bytes 1966084
  79.1 12.9 %copy-start.8 = (bf16[2,256,640]{2,1,0:T(8,128)(2,1)}, bf16[2,256,640]{2,1,0:T(8,128)(2,1)S(1)}, u32[]{:S(2)}) copy-start(bf16[2,256,640]{2,1,0:T(8,128)(2,1)S(1)} %get-tuple-element.23) | copy-start | bytes 1966084
  79.1 12.9 %copy-start.2 = (bf16[640,1280]{1,0:T(8,128)(2,1)S(1)}, bf16[640,1280]{1,0:T(8,128)(2,1)}, u32[]{:S(2)}) copy-start(bf16[640,1280]{1,0:T(8,128)(2,1)} %param.17) | copy-start | bytes 4915204
  92.6 2.0 %copy-start.1 = (bf16[512,1280]{1,0:T(8,128)(2,1)S(1)}, bf16[512,1280]{1,0:T(8,128)(2,1)}, u32[]{:S(2)}) copy-start(bf16[512,1280]{1,0:T(8,128)(2,1)} %x_ref.1) | copy-start | bytes 3932164
  92.6 2.0 %copy-start.9 = (f32[1280]{0:T(1024)S(1)}, f32[1280]{0:T(1024)}, u32[]{:S(2)}) copy-start(f32[1280]{0:T(1024)} %param.19) | copy-start | bytes 15364

commit v15 on v11

--- a/solution.py
+++ b/solution.py
@@ -262,7 +262,7 @@
     )
     fetched = fetch_pages(pool_keys, pool_values, prefix_pages)
     pairs_here = width_half // (2 * HD)
-    split = (pairs_here + 1) // 2
+    split = pairs_here - 1
     parts = [
         attention(queries, key_rows, value_rows, fetched, req_len, prefix_len, first, count)
         for first, count in ((0, split), (split, pairs_here - split))

time: 89.9 us -> 91.2 us (1.014)
  waiting for transfers between devices: 16 us -> 17.3 us
    ppermute x9, waiting for transfers between devices: 16 us -> 17.3 us  [from_behind(): return lax.ppermute(block, axis, route)]
  transfers between devices with their start and end apart: 10 -> 10, of which waited for: 4 -> 5; matrix products, arithmetic and copies ran while one was open for 12% -> 12% of each run, Pallas kernels for 29% -> 28%
where the time goes in v15:
time: 91.2 us; the launch traced here: 90.1 us
  Pallas kernels  30.6 us (34%)
  starting transfers between devices  18 us (20%)
  waiting for transfers between devices  17.3 us (19%)
  local copies, waits for them, and re-layouts  10.5 us (12%)
  between operations  5.83 us (6%)
  other arithmetic  5.82 us (6%)
  matrix products  1.98 us (2%)
    ppermute x9, starting transfers between devices, from_behind(): return lax.ppermute(block, axis, route)  17.8 us
    ppermute x9, waiting for transfers between devices, from_behind(): return lax.ppermute(block, axis, route)  17.3 us
    pallas_call x2, Pallas kernels, attention(): pl.pallas_call(attention_kernel, out_shape=jax.ShapeDtypeStruct((tokens,...  16.4 us
    pallas_call x1, Pallas kernels, projections(): pl.pallas_call(projection_kernel, out_shape=(shape, shape, shape), grid=(...  9.11 us
    pallas_call x1, Pallas kernels, fetch_pages(): pl.pallas_call(functools.partial(gather_kernel, devices), out_shape=[page...  5.05 us
    unnamed x28, local copies, waits for them, and re-layouts  2.61 us
    dynamic_slice x1, local copies, waits for them, and re-layouts, other_half_once_per_chip(): mine = lax.dynamic_slice_in_dim(w_out, core * rows, rows, 0)  2.09 us
    dot_general x1, matrix products, body(): jnp.dot(in_kv_order(attended, other_attended, 1), in_kv_order(w_out, othe...  1.98 us
  transfers between devices with their start and end apart: 10, of which 5 were waited for; matrix products, arithmetic and copies ran while one was open for 12% of the time, Pallas kernels for 28%

profile of v15, /device:TPU:6, one launch (start us, length us, event | category | flops | bytes accessed | tf_op | source)
XLA Modules:
  0.0 90.1 jit_solution(2257739891086960722)
XLA Ops:
  0.6 0.0 copy-start
  0.6 0.0 copy-start.11
  0.7 1.5 %copy.18.pages_ref = s32[128,4]{1,0:T(8,128)} copy(s32[128,4]{0,1:T(4,128)} %param.24) | data formatting | bytes 4096 | tf_op args[11]
  2.2 5.1 %shard_map.149 = (bf16[2,256,640]{2,1,0:T(8,128)(2,1)}, bf16[2,256,640]{2,1,0:T(8,128)(2,1)}, bf16[2,256,640]{2,1,0:T(8,128)(2,1)}, bf16[2,256,640]{2,1,0:T(8,128)(2,1)}) custom-call(s32[128,4]{1,0:T(8,128)} %copy.18.pages_ref, bf16[4,256,640]{2,1,0:T(8,128)(2,1)} %keys_hbm.1, bf16[4,256,640]{2,1,0:T(8,128)(2,1)} %values_hbm.1), custom_call_target="tpu_custom_call" | custom-call | tf_op jit(solution)/shard_map/pallas_call | solution.py:206
  7.2 6.7 %collective-permute-start = (bf16[2,256,640]{2,1,0:T(8,128)(2,1)}, bf16[2,256,640]{2,1,0:T(8,128)(2,1)S(1)}, u32[]{:S(2)}, u32[]{:S(2)}) collective-permute-start(bf16[2,256,640]{2,1,0:T(8,128)(2,1)} %get-tuple-element.13), channel_id=1, source_target_pairs={{1,0},{2,1},{3,2},{4,3},{5,4},{6,5},{7,6},{8,7},{9,8},{10,9},{11,1... | collective-permute-start | bytes 1966088 | tf_op jit(solution)/shard_map/ppermute | solution.py:22
  13.9 1.3 %collective-permute-start.1 = (bf16[2,256,640]{2,1,0:T(8,128)(2,1)}, bf16[2,256,640]{2,1,0:T(8,128)(2,1)S(1)}, u32[]{:S(2)}, u32[]{:S(2)}) collective-permute-start(bf16[2,256,640]{2,1,0:T(8,128)(2,1)} %get-tuple-element.14), channel_id=1, source_target_pairs={{33,0},{34,1},{35,2},{36,3},{37,4},{38,5},{39,6},{40,7},{41,8},{42... | collective-permute-start | bytes 1966088 | tf_op jit(solution)/shard_map/ppermute | solution.py:22
  15.2 1.8 %collective-permute-start.2 = (bf16[2,256,640]{2,1,0:T(8,128)(2,1)}, bf16[2,256,640]{2,1,0:T(8,128)(2,1)S(1)}, u32[]{:S(2)}, u32[]{:S(2)}) collective-permute-start(bf16[2,256,640]{2,1,0:T(8,128)(2,1)} %get-tuple-element.15), channel_id=1, source_target_pairs={{65,0},{66,1},{67,2},{68,3},{69,4},{70,5},{71,6},{72,7},{73,8},{74... | collective-permute-start | bytes 1966088 | tf_op jit(solution)/shard_map/ppermute | solution.py:22
  17.0 0.0 collective-permute-start.3
  17.0 0.0 copy-done
  17.0 0.3 fusion.7
  17.3 0.9 copy.17.scale_ref
  18.2 0.0 copy-done.11
  18.2 0.6 reshape.53.gain_ref
  18.8 9.1 %shard_map.148 = (bf16[512,640]{1,0:T(8,128)(2,1)}, bf16[512,640]{1,0:T(8,128)(2,1)}, bf16[512,640]{1,0:T(8,128)(2,1)}) custom-call(bf16[512,1280]{1,0:T(8,128)(2,1)} %x_ref.1, f32[512,1]{1,0:T(8,128)} %copy.17.scale_ref, bf16[1280,640]{1,0:T(8,128)(2,1)} %wq_ref.1, bf16[1280,640]{1,0:T(8,128)(2,1)} %wk_ref.1, bf16[1280,640]{1,0:T(8,128)(2,1)} %wv_ref.1, ...), custom_call_target="tpu_custom_call" | custom-call | tf_op jit(solution)/shard_map/pallas_call | solution.py:98
  27.9 1.4 %slice_bitcast_fusion = (bf16[1,256,640]{2,1,0:T(8,128)(2,1)S(1)}, bf16[1,256,640]{2,1,0:T(8,128)(2,1)S(1)}, bf16[1,256,640]{2,1,0:T(8,128)(2,1)S(1)}, bf16[1,256,640]{2,1,0:T(8,128)(2,1)S(1)}) fusion(bf16[512,640]{1,0:T(8,128)(2,1)} %get-tuple-element.12.v_ref, bf16[512,640]{1,0:T(8,128)(2,1)} %get-tuple-element.11.k_ref), kind=kLoop, calls=%fused_computation.30 | loop fusion | bytes 2621440 | tf_op jit(solution)/shard_map/slice | solution.py:229
  29.3 0.0 copy-start.12
  29.3 0.9 %pad_maximum_fusion.2 = bf16[2,256,640]{2,1,0:T(8,128)(2,1)} fusion(bf16[1,256,640]{2,1,0:T(8,128)(2,1)S(1)} %get-tuple-element.28, bf16[1,256,640]{2,1,0:T(8,128)(2,1)S(1)} %get-tuple-element.33), kind=kLoop, calls=%fused_computation.22 | loop fusion | flops 327680 | bytes 1310720 | tf_op jit(solution)/shard_map/stack | solution.py:229
  30.3 1.5 %collective-permute-start.8 = (bf16[2,256,640]{2,1,0:T(8,128)(2,1)}, bf16[2,256,640]{2,1,0:T(8,128)(2,1)}, u32[]{:S(2)}, u32[]{:S(2)}) collective-permute-start(bf16[2,256,640]{2,1,0:T(8,128)(2,1)} %pad_maximum_fusion.2), channel_id=1, source_target_pairs={{96,0},{97,1},{98,2},{99,3},{100,4},{101,5},{102,6},{103,7},{104,8... | collective-permute-start | bytes 1966088 | tf_op jit(solution)/shard_map/ppermute | solution.py:22
  31.7 2.1 %constant_dynamic-slice_fusion = bf16[320,1280]{1,0:T(8,128)(2,1)} fusion(bf16[640,1280]{1,0:T(8,128)(2,1)} %param.17, s32[]{:T(128)S(6)} %select_n.83), kind=kLoop, calls=%fused_computation.39 | loop fusion | bytes 1638404 | tf_op jit(solution)/shard_map/dynamic_slice | solution.py:55
  33.8 0.0 collective-permute-done.refs_0_.refs_4_
  33.8 2.9 %collective-permute-start.6 = (bf16[320,1280]{1,0:T(8,128)(2,1)}, bf16[320,1280]{1,0:T(8,128)(2,1)S(1)}, u32[]{:S(2)}, u32[]{:S(2)}) collective-permute-start(bf16[320,1280]{1,0:T(8,128)(2,1)} %constant_dynamic-slice_fusion), channel_id=1, source_target_pairs={{128,0},{0,128},{129,1},{1,129},{130,2},{2,130},{131,3},{3,131},{1... | collective-permute-start | bytes 2457608 | tf_op jit(solution)/shard_map/ppermute | solution.py:22
  36.7 0.9 %pad_maximum_fusion.3 = bf16[2,256,640]{2,1,0:T(8,128)(2,1)} fusion(bf16[1,256,640]{2,1,0:T(8,128)(2,1)S(1)} %get-tuple-element.27, bf16[1,256,640]{2,1,0:T(8,128)(2,1)S(1)} %get-tuple-element.34), kind=kLoop, calls=%fused_computation.23 | loop fusion | flops 327680 | bytes 1310720 | tf_op jit(solution)/shard_map/stack | solution.py:229
  37.6 1.4 %collective-permute-done.1.refs_1_.refs_5_ = bf16[2,256,640]{2,1,0:T(8,128)(2,1)S(1)} collective-permute-done((bf16[2,256,640]{2,1,0:T(8,128)(2,1)}, bf16[2,256,640]{2,1,0:T(8,128)(2,1)S(1)}, u32[]{:S(2)}, u32[]{:S(2)}) %collective-permute-start.1) | collective-permute-done | bytes 655392 | tf_op jit(solution)/shard_map/ppermute | solution.py:22
  39.0 0.0 collective-permute-start.9
  39.0 0.0 copy-done.12
  39.0 0.7 fusion.12
  44.7 5.5 %collective-permute-done.2.refs_2_.refs_6_ = bf16[2,256,640]{2,1,0:T(8,128)(2,1)S(1)} collective-permute-done((bf16[2,256,640]{2,1,0:T(8,128)(2,1)}, bf16[2,256,640]{2,1,0:T(8,128)(2,1)S(1)}, u32[]{:S(2)}, u32[]{:S(2)}) %collective-permute-start.2) | collective-permute-done | bytes 655392 | tf_op jit(solution)/shard_map/ppermute | solution.py:22
  50.2 4.4 %collective-permute-done.3.refs_3_.refs_7_ = bf16[2,256,640]{2,1,0:T(8,128)(2,1)} collective-permute-done((bf16[2,256,640]{2,1,0:T(8,128)(2,1)}, bf16[2,256,640]{2,1,0:T(8,128)(2,1)}, u32[]{:S(2)}, u32[]{:S(2)}) %collective-permute-start.3) | collective-permute-done | bytes 655392 | tf_op jit(solution)/shard_map/ppermute | solution.py:22
  54.5 0.0 copy-done.2
  54.6 0.0 copy-done.3
  54.6 0.0 copy-done.4
  54.6 12.1 %shard_map.150 = bf16[512,512]{1,0:T(8,128)(2,1)} custom-call(s32[1]{0:T(128)S(6)} %copy.24.live_ref, s32[1]{0:T(128)S(6)} %copy.25.depth_ref, bf16[512,640]{1,0:T(8,128)(2,1)} %get-tuple-element.10.q_ref, bf16[512,640]{1,0:T(8,128)(2,1)} %get-tuple-element.11.k_ref, bf16[512,640]{1,0:T(8,128)(2,1)} %get-tuple-element.12.v_ref, ...), custom_call_target="tpu_custom_call" | custom-call | tf_op jit(solution)/shard_map/pallas_call | solution.py:170
  66.7 2.9 %collective-permute-start.4 = (bf16[512,512]{1,0:T(8,128)(2,1)}, bf16[512,512]{1,0:T(8,128)(2,1)S(1)}, u32[]{:S(2)}, u32[]{:S(2)}) collective-permute-start(bf16[512,512]{1,0:T(8,128)(2,1)} %shard_map.150), channel_id=1, source_target_pairs={{128,0},{0,128},{129,1},{1,129},{130,2},{2,130},{131,3},{3,131},{1... | collective-permute-start | bytes 1572872 | tf_op jit(solution)/shard_map/ppermute | solution.py:22
  69.6 4.3 %shard_map.151 = bf16[512,128]{1,0:T(8,128)(2,1)} custom-call(s32[1]{0:T(128)S(6)} %copy.24.live_ref, s32[1]{0:T(128)S(6)} %copy.25.depth_ref, bf16[512,640]{1,0:T(8,128)(2,1)} %get-tuple-element.10.q_ref, bf16[512,640]{1,0:T(8,128)(2,1)} %get-tuple-element.11.k_ref, bf16[512,640]{1,0:T(8,128)(2,1)} %get-tuple-element.12.v_ref, ...), custom_call_target="tpu_custom_call" | custom-call | tf_op jit(solution)/shard_map/pallas_call | solution.py:170
  73.9 0.7 collective-permute-start.5
  74.6 0.0 collective-permute-done.8
  74.6 0.1 broadcast.62.clone
  74.7 1.0 %slice_dynamic-update-slice_fusion.1 = bf16[2,256,640]{2,1,0:T(8,128)(2,1)S(1)} fusion(bf16[2,256,640]{2,1,0:T(8,128)(2,1)S(1)} %broadcast.62.clone, s32[]{:T(128)S(6)} %select_n.91, bf16[2,256,640]{2,1,0:T(8,128)(2,1)} %collective-permute-done.8), kind=kLoop, calls=%fused_computation.27 | loop fusion | bytes 655364 | tf_op jit(solution)/shard_map/jit(dynamic_update_index_in_dim)/dynamic_update_slice | solution.py:234
  75.7 0.0 collective-permute-done.6
  75.7 0.3 collective-permute-start.7
  76.0 0.1 broadcast.62.clone.1
  76.1 1.0 %slice_dynamic-update-slice_fusion.3 = bf16[2,256,640]{2,1,0:T(8,128)(2,1)S(1)} fusion(bf16[2,256,640]{2,1,0:T(8,128)(2,1)S(1)} %broadcast.62.clone.1, s32[]{:T(128)S(6)} %select_n.91, bf16[2,256,640]{2,1,0:T(8,128)(2,1)} %collective-permute-done.8), kind=kLoop, calls=%fused_computation.29 | loop fusion | bytes 655364 | tf_op jit(solution)/shard_map/jit(dynamic_update_index_in_dim)/dynamic_update_slice | solution.py:233
  77.1 0.0 collective-permute-done.9
  77.1 0.1 slice_dynamic-update-slice_fusion
  77.2 0.0 copy-start.7
  77.2 0.0 copy-start.8
  77.2 4.7 %collective-permute-done.4 = bf16[512,512]{1,0:T(8,128)(2,1)S(1)} collective-permute-done((bf16[512,512]{1,0:T(8,128)(2,1)}, bf16[512,512]{1,0:T(8,128)(2,1)S(1)}, u32[]{:S(2)}, u32[]{:S(2)}) %collective-permute-start.4) | collective-permute-done | bytes 524320 | tf_op jit(solution)/shard_map/ppermute | solution.py:22
  82.0 1.4 %collective-permute-done.5 = bf16[512,128]{1,0:T(8,128)(2,1)S(1)} collective-permute-done((bf16[512,128]{1,0:T(8,128)(2,1)}, bf16[512,128]{1,0:T(8,128)(2,1)S(1)}, u32[]{:S(2)}, u32[]{:S(2)}) %collective-permute-start.5) | collective-permute-done | bytes 131104 | tf_op jit(solution)/shard_map/ppermute | solution.py:22
  83.4 0.0 copy-done.6
  83.4 0.0 copy-done.9
  83.4 0.0 copy-start.5
  83.4 0.3 broadcast_select_fusion.5
  83.7 0.0 collective-permute-done.7
  83.7 0.1 broadcast_select_fusion.3
  83.8 0.0 copy-done.7
  83.8 0.0 copy-done.8
  83.8 1.0 %copy-done.5 = bf16[640,1280]{1,0:T(8,128)(2,1)S(1)} copy-done((bf16[640,1280]{1,0:T(8,128)(2,1)S(1)}, bf16[640,1280]{1,0:T(8,128)(2,1)}, u32[]{:S(2)}) %copy-start.5) | copy-done | bytes 1638424
  84.8 0.6 broadcast_select_fusion.1
  85.4 0.0 copy-start.1
  85.4 0.0 copy-start.10
  85.4 2.0 %multiply_reduce_fusion.1 = (f32[512]{0:T(512)S(1)}, f32[512,1280]{1,0:T(8,128)S(1)}) fusion(bf16[640,1280]{1,0:T(8,128)(2,1)S(1)} %get-tuple-element.18, bf16[640,1280]{1,0:T(8,128)(2,1)S(1)} %get-tuple-element.17, bf16[512,640]{1,0:T(8,128)(2,1)S(1)} %get-tuple-element.22, bf16[512,640]{1,0:T(8,128)(2,1)S(1)} %get-tuple-element.21), kind=kOutput, calls=%fused_computation.12 | convolution fusion | flops 1688206848 | bytes 7211008 | tf_op jit(solution)/shard_map/dot_general | solution.py:273
  87.4 0.0 copy-done.1
  87.5 0.8 multiply_reduce_fusion
  88.3 1.8 %multiply_convert_fusion = bf16[512,1280]{1,0:T(8,128)(2,1)} fusion(f32[512]{0:T(512)S(1)} %add_rsqrt_fusion, f32[512,1280]{1,0:T(8,128)S(1)} %get-tuple-element.32, f32[512]{0:T(512)S(1)} %add_rsqrt_fusion.1, f32[1280]{0:T(1024)S(1)} %copy-done.10, f32[512]{0:T(512)S(1)} %add_rsqrt_fusion.2, bf16[512,1280]{1,0:T(8,128)(2,1)S(1)} %copy-done.1), kind=kLoop, calls=%fused_computation.10 | loop fusion | flops 5242880 | bytes 5254144 | tf_op jit(solution)/shard_map/convert_element_type | solution.py:279
  (11 shorter events, 0.1 us)
Async XLA Ops:
  0.6 16.4 %copy-start = (bf16[512,1280]{1,0:T(8,128)(2,1)S(1)}, bf16[512,1280]{1,0:T(8,128)(2,1)}, u32[]{:S(2)}) copy-start(bf16[512,1280]{1,0:T(8,128)(2,1)} %x_ref.1) | copy-start | bytes 3932164
  0.6 17.6 %copy-start.11 = (f32[640]{0:T(1024)S(1)}, f32[640]{0:T(1024)}, u32[]{:S(2)}) copy-start(f32[640]{0:T(1024)} %param.18) | copy-start | bytes 7684
  7.2 26.6 %collective-permute-start = (bf16[2,256,640]{2,1,0:T(8,128)(2,1)}, bf16[2,256,640]{2,1,0:T(8,128)(2,1)S(1)}, u32[]{:S(2)}, u32[]{:S(2)}) collective-permute-start(bf16[2,256,640]{2,1,0:T(8,128)(2,1)} %get-tuple-element.13), channel_id=1, source_target_pairs={{1,0},{2,1},{3,2},{4,3},{5,4},{6,5},{7,6},{8,7},{9,8},{10,9},{11,1... | collective-permute-start | bytes 1966088 | tf_op jit(solution)/shard_map/ppermute | solution.py:22
  13.9 25.1 %collective-permute-start.1 = (bf16[2,256,640]{2,1,0:T(8,128)(2,1)}, bf16[2,256,640]{2,1,0:T(8,128)(2,1)S(1)}, u32[]{:S(2)}, u32[]{:S(2)}) collective-permute-start(bf16[2,256,640]{2,1,0:T(8,128)(2,1)} %get-tuple-element.14), channel_id=1, source_target_pairs={{33,0},{34,1},{35,2},{36,3},{37,4},{38,5},{39,6},{40,7},{41,8},{42... | collective-permute-start | bytes 1966088 | tf_op jit(solution)/shard_map/ppermute | solution.py:22
  15.2 35.0 %collective-permute-start.2 = (bf16[2,256,640]{2,1,0:T(8,128)(2,1)}, bf16[2,256,640]{2,1,0:T(8,128)(2,1)S(1)}, u32[]{:S(2)}, u32[]{:S(2)}) collective-permute-start(bf16[2,256,640]{2,1,0:T(8,128)(2,1)} %get-tuple-element.15), channel_id=1, source_target_pairs={{65,0},{66,1},{67,2},{68,3},{69,4},{70,5},{71,6},{72,7},{73,8},{74... | collective-permute-start | bytes 1966088 | tf_op jit(solution)/shard_map/ppermute | solution.py:22
  17.0 37.6 %collective-permute-start.3 = (bf16[2,256,640]{2,1,0:T(8,128)(2,1)}, bf16[2,256,640]{2,1,0:T(8,128)(2,1)}, u32[]{:S(2)}, u32[]{:S(2)}) collective-permute-start(bf16[2,256,640]{2,1,0:T(8,128)(2,1)} %get-tuple-element.16), channel_id=1, source_target_pairs={{97,0},{98,1},{99,2},{100,3},{101,4},{102,5},{103,6},{104,7},{105,... | collective-permute-start | bytes 1966088 | tf_op jit(solution)/shard_map/ppermute | solution.py:22
  29.3 9.7 %copy-start.12 = (s32[256]{0:T(256)S(1)}, s32[256]{0:T(256)}, u32[]{:S(2)}) copy-start(s32[256]{0:T(256)} %param.25) | copy-start | bytes 3076
  30.3 44.4 %collective-permute-start.8 = (bf16[2,256,640]{2,1,0:T(8,128)(2,1)}, bf16[2,256,640]{2,1,0:T(8,128)(2,1)}, u32[]{:S(2)}, u32[]{:S(2)}) collective-permute-start(bf16[2,256,640]{2,1,0:T(8,128)(2,1)} %pad_maximum_fusion.2), channel_id=1, source_target_pairs={{96,0},{97,1},{98,2},{99,3},{100,4},{101,5},{102,6},{103,7},{104,8... | collective-permute-start | bytes 1966088 | tf_op jit(solution)/shard_map/ppermute | solution.py:22
  33.8 20.7 %copy-start.2 = (bf16[2,256,640]{2,1,0:T(8,128)(2,1)}, bf16[2,256,640]{2,1,0:T(8,128)(2,1)S(1)}, u32[]{:S(2)}) copy-start(bf16[2,256,640]{2,1,0:T(8,128)(2,1)S(1)} %collective-permute-done.refs_0_.refs_4_) | copy-start | bytes 1966084
  33.8 41.9 %collective-permute-start.6 = (bf16[320,1280]{1,0:T(8,128)(2,1)}, bf16[320,1280]{1,0:T(8,128)(2,1)S(1)}, u32[]{:S(2)}, u32[]{:S(2)}) collective-permute-start(bf16[320,1280]{1,0:T(8,128)(2,1)} %constant_dynamic-slice_fusion), channel_id=1, source_target_pairs={{128,0},{0,128},{129,1},{1,129},{130,2},{2,130},{131,3},{3,131},{1... | collective-permute-start | bytes 2457608 | tf_op jit(solution)/shard_map/ppermute | solution.py:22
  39.0 15.6 %copy-start.3 = (bf16[2,256,640]{2,1,0:T(8,128)(2,1)}, bf16[2,256,640]{2,1,0:T(8,128)(2,1)S(1)}, u32[]{:S(2)}) copy-start(bf16[2,256,640]{2,1,0:T(8,128)(2,1)S(1)} %collective-permute-done.1.refs_1_.refs_5_) | copy-start | bytes 1966084
  39.0 38.1 %collective-permute-start.9 = (bf16[2,256,640]{2,1,0:T(8,128)(2,1)}, bf16[2,256,640]{2,1,0:T(8,128)(2,1)S(1)}, u32[]{:S(2)}, u32[]{:S(2)}) collective-permute-start(bf16[2,256,640]{2,1,0:T(8,128)(2,1)} %pad_maximum_fusion.3), channel_id=1, source_target_pairs={{32,0},{33,1},{34,2},{35,3},{36,4},{37,5},{38,6},{39,7},{40,8},{41... | collective-permute-start | bytes 1966088 | tf_op jit(solution)/shard_map/ppermute | solution.py:22
  50.2 4.4 %copy-start.4 = (bf16[2,256,640]{2,1,0:T(8,128)(2,1)}, bf16[2,256,640]{2,1,0:T(8,128)(2,1)S(1)}, u32[]{:S(2)}) copy-start(bf16[2,256,640]{2,1,0:T(8,128)(2,1)S(1)} %collective-permute-done.2.refs_2_.refs_6_) | copy-start | bytes 1966084
  66.7 15.2 %collective-permute-start.4 = (bf16[512,512]{1,0:T(8,128)(2,1)}, bf16[512,512]{1,0:T(8,128)(2,1)S(1)}, u32[]{:S(2)}, u32[]{:S(2)}) collective-permute-start(bf16[512,512]{1,0:T(8,128)(2,1)} %shard_map.150), channel_id=1, source_target_pairs={{128,0},{0,128},{129,1},{1,129},{130,2},{2,130},{131,3},{3,131},{1... | collective-permute-start | bytes 1572872 | tf_op jit(solution)/shard_map/ppermute | solution.py:22
  73.9 9.5 %copy-start.6 = (bf16[512,512]{1,0:T(8,128)(2,1)S(1)}, bf16[512,512]{1,0:T(8,128)(2,1)}, u32[]{:S(2)}) copy-start(bf16[512,512]{1,0:T(8,128)(2,1)} %shard_map.150) | copy-start | bytes 1572868
  73.9 9.5 %copy-start.9 = (bf16[512,128]{1,0:T(8,128)(2,1)S(1)}, bf16[512,128]{1,0:T(8,128)(2,1)}, u32[]{:S(2)}) copy-start(bf16[512,128]{1,0:T(8,128)(2,1)} %shard_map.151) | copy-start | bytes 393220
  73.9 9.4 %collective-permute-start.5 = (bf16[512,128]{1,0:T(8,128)(2,1)}, bf16[512,128]{1,0:T(8,128)(2,1)S(1)}, u32[]{:S(2)}, u32[]{:S(2)}) collective-permute-start(bf16[512,128]{1,0:T(8,128)(2,1)} %shard_map.151), channel_id=1, source_target_pairs={{128,0},{0,128},{129,1},{1,129},{130,2},{2,130},{131,3},{3,131},{1... | collective-permute-start | bytes 393224 | tf_op jit(solution)/shard_map/ppermute | solution.py:22
  75.7 8.0 %collective-permute-start.7 = (bf16[320,1280]{1,0:T(8,128)(2,1)S(1)}, bf16[320,1280]{1,0:T(8,128)(2,1)S(1)}, u32[]{:S(2)}, u32[]{:S(2)}) collective-permute-start(bf16[320,1280]{1,0:T(8,128)(2,1)S(1)} %collective-permute-done.6), channel_id=1, source_target_pairs={{0,1},{1,0},{2,3},{3,2},{4,5},{5,4},{6,7},{7,6},{8,9},{9,8},{10,11... | collective-permute-start | bytes 2457608 | tf_op jit(solution)/shard_map/ppermute | solution.py:58
  77.2 6.6 %copy-start.7 = (bf16[2,256,640]{2,1,0:T(8,128)(2,1)}, bf16[2,256,640]{2,1,0:T(8,128)(2,1)S(1)}, u32[]{:S(2)}) copy-start(bf16[2,256,640]{2,1,0:T(8,128)(2,1)S(1)} %get-tuple-element.24) | copy-start | bytes 1966084
  77.2 6.6 %copy-start.8 = (bf16[2,256,640]{2,1,0:T(8,128)(2,1)}, bf16[2,256,640]{2,1,0:T(8,128)(2,1)S(1)}, u32[]{:S(2)}) copy-start(bf16[2,256,640]{2,1,0:T(8,128)(2,1)S(1)} %get-tuple-element.23) | copy-start | bytes 1966084
  83.4 1.4 %copy-start.5 = (bf16[640,1280]{1,0:T(8,128)(2,1)S(1)}, bf16[640,1280]{1,0:T(8,128)(2,1)}, u32[]{:S(2)}) copy-start(bf16[640,1280]{1,0:T(8,128)(2,1)} %param.17) | copy-start | bytes 4915204
  85.4 2.0 %copy-start.1 = (bf16[512,1280]{1,0:T(8,128)(2,1)S(1)}, bf16[512,1280]{1,0:T(8,128)(2,1)}, u32[]{:S(2)}) copy-start(bf16[512,1280]{1,0:T(8,128)(2,1)} %x_ref.1) | copy-start | bytes 3932164
  85.4 2.0 %copy-start.10 = (f32[1280]{0:T(1024)S(1)}, f32[1280]{0:T(1024)}, u32[]{:S(2)}) copy-start(f32[1280]{0:T(1024)} %param.19) | copy-start | bytes 15364

commit v16 on v15

--- a/solution.py
+++ b/solution.py
@@ -262,7 +262,7 @@
     )
     fetched = fetch_pages(pool_keys, pool_values, prefix_pages)
     pairs_here = width_half // (2 * HD)
-    split = pairs_here - 1
+    split = pairs_here // 2
     parts = [
         attention(queries, key_rows, value_rows, fetched, req_len, prefix_len, first, count)
         for first, count in ((0, split), (split, pairs_here - split))

time: 91.2 us -> 92.8 us (1.018)
  waiting for transfers between devices: 17.3 us -> 19.2 us
    ppermute x9, waiting for transfers between devices: 17.3 us -> 19.2 us  [from_behind(): return lax.ppermute(block, axis, route)]
  transfers between devices with their start and end apart: 10 -> 10, of which waited for: 5 -> 4; matrix products, arithmetic and copies ran while one was open for 12% -> 11% of each run, Pallas kernels for 28% -> 28%
where the time goes in v16:
time: 92.8 us; the launch traced here: 92.2 us
  Pallas kernels  30.7 us (33%)
  waiting for transfers between devices  19.2 us (21%)
  starting transfers between devices  18.2 us (20%)
  local copies, waits for them, and re-layouts  10.6 us (11%)
  between operations  5.84 us (6%)
  other arithmetic  5.78 us (6%)
  matrix products  1.98 us (2%)
    ppermute x9, waiting for transfers between devices, from_behind(): return lax.ppermute(block, axis, route)  19.2 us
    ppermute x9, starting transfers between devices, from_behind(): return lax.ppermute(block, axis, route)  17.9 us
    pallas_call x2, Pallas kernels, attention(): pl.pallas_call(attention_kernel, out_shape=jax.ShapeDtypeStruct((tokens,...  16.5 us
    pallas_call x1, Pallas kernels, projections(): pl.pallas_call(projection_kernel, out_shape=(shape, shape, shape), grid=(...  9.11 us
    pallas_call x1, Pallas kernels, fetch_pages(): pl.pallas_call(functools.partial(gather_kernel, devices), out_shape=[page...  5.03 us
    unnamed x28, local copies, waits for them, and re-layouts  2.63 us
    dynamic_slice x1, local copies, waits for them, and re-layouts, other_half_once_per_chip(): mine = lax.dynamic_slice_in_dim(w_out, core * rows, rows, 0)  2.09 us
    dot_general x1, matrix products, body(): jnp.dot(in_kv_order(attended, other_attended, 1), in_kv_order(w_out, othe...  1.98 us
  transfers between devices with their start and end apart: 10, of which 4 were waited for; matrix products, arithmetic and copies ran while one was open for 11% of the time, Pallas kernels for 28%

profile of v16, /device:TPU:6, one launch (start us, length us, event | category | flops | bytes accessed | tf_op | source)
XLA Modules:
  0.0 92.2 jit_solution(13953608803943114750)
XLA Ops:
  0.6 0.0 copy-start
  0.6 0.0 copy-start.11
  0.7 1.5 %copy.18.pages_ref = s32[128,4]{1,0:T(8,128)} copy(s32[128,4]{0,1:T(4,128)} %param.24) | data formatting | bytes 4096 | tf_op args[11]
  2.2 5.0 %shard_map.149 = (bf16[2,256,640]{2,1,0:T(8,128)(2,1)}, bf16[2,256,640]{2,1,0:T(8,128)(2,1)}, bf16[2,256,640]{2,1,0:T(8,128)(2,1)}, bf16[2,256,640]{2,1,0:T(8,128)(2,1)}) custom-call(s32[128,4]{1,0:T(8,128)} %copy.18.pages_ref, bf16[4,256,640]{2,1,0:T(8,128)(2,1)} %keys_hbm.1, bf16[4,256,640]{2,1,0:T(8,128)(2,1)} %values_hbm.1), custom_call_target="tpu_custom_call" | custom-call | tf_op jit(solution)/shard_map/pallas_call | solution.py:206
  7.2 6.6 %collective-permute-start = (bf16[2,256,640]{2,1,0:T(8,128)(2,1)}, bf16[2,256,640]{2,1,0:T(8,128)(2,1)S(1)}, u32[]{:S(2)}, u32[]{:S(2)}) collective-permute-start(bf16[2,256,640]{2,1,0:T(8,128)(2,1)} %get-tuple-element.13), channel_id=1, source_target_pairs={{1,0},{2,1},{3,2},{4,3},{5,4},{6,5},{7,6},{8,7},{9,8},{10,9},{11,1... | collective-permute-start | bytes 1966088 | tf_op jit(solution)/shard_map/ppermute | solution.py:22
  13.9 1.3 %collective-permute-start.1 = (bf16[2,256,640]{2,1,0:T(8,128)(2,1)}, bf16[2,256,640]{2,1,0:T(8,128)(2,1)S(1)}, u32[]{:S(2)}, u32[]{:S(2)}) collective-permute-start(bf16[2,256,640]{2,1,0:T(8,128)(2,1)} %get-tuple-element.14), channel_id=1, source_target_pairs={{33,0},{34,1},{35,2},{36,3},{37,4},{38,5},{39,6},{40,7},{41,8},{42... | collective-permute-start | bytes 1966088 | tf_op jit(solution)/shard_map/ppermute | solution.py:22
  15.1 1.9 %collective-permute-start.2 = (bf16[2,256,640]{2,1,0:T(8,128)(2,1)}, bf16[2,256,640]{2,1,0:T(8,128)(2,1)S(1)}, u32[]{:S(2)}, u32[]{:S(2)}) collective-permute-start(bf16[2,256,640]{2,1,0:T(8,128)(2,1)} %get-tuple-element.15), channel_id=1, source_target_pairs={{65,0},{66,1},{67,2},{68,3},{69,4},{70,5},{71,6},{72,7},{73,8},{74... | collective-permute-start | bytes 1966088 | tf_op jit(solution)/shard_map/ppermute | solution.py:22
  17.0 0.0 collective-permute-start.3
  17.0 0.0 copy-done
  17.0 0.3 fusion.7
  17.3 0.9 copy.17.scale_ref
  18.2 0.0 copy-done.11
  18.2 0.6 reshape.53.gain_ref
  18.8 9.1 %shard_map.148 = (bf16[512,640]{1,0:T(8,128)(2,1)}, bf16[512,640]{1,0:T(8,128)(2,1)}, bf16[512,640]{1,0:T(8,128)(2,1)}) custom-call(bf16[512,1280]{1,0:T(8,128)(2,1)} %x_ref.1, f32[512,1]{1,0:T(8,128)} %copy.17.scale_ref, bf16[1280,640]{1,0:T(8,128)(2,1)} %wq_ref.1, bf16[1280,640]{1,0:T(8,128)(2,1)} %wk_ref.1, bf16[1280,640]{1,0:T(8,128)(2,1)} %wv_ref.1, ...), custom_call_target="tpu_custom_call" | custom-call | tf_op jit(solution)/shard_map/pallas_call | solution.py:98
  27.9 1.4 %slice_bitcast_fusion = (bf16[1,256,640]{2,1,0:T(8,128)(2,1)S(1)}, bf16[1,256,640]{2,1,0:T(8,128)(2,1)S(1)}, bf16[1,256,640]{2,1,0:T(8,128)(2,1)S(1)}, bf16[1,256,640]{2,1,0:T(8,128)(2,1)S(1)}) fusion(bf16[512,640]{1,0:T(8,128)(2,1)} %get-tuple-element.12.v_ref, bf16[512,640]{1,0:T(8,128)(2,1)} %get-tuple-element.11.k_ref), kind=kLoop, calls=%fused_computation.30 | loop fusion | bytes 2621440 | tf_op jit(solution)/shard_map/slice | solution.py:229
  29.3 0.0 copy-start.12
  29.3 0.9 %pad_maximum_fusion.2 = bf16[2,256,640]{2,1,0:T(8,128)(2,1)} fusion(bf16[1,256,640]{2,1,0:T(8,128)(2,1)S(1)} %get-tuple-element.28, bf16[1,256,640]{2,1,0:T(8,128)(2,1)S(1)} %get-tuple-element.33), kind=kLoop, calls=%fused_computation.22 | loop fusion | flops 327680 | bytes 1310720 | tf_op jit(solution)/shard_map/stack | solution.py:229
  30.3 1.6 %collective-permute-start.8 = (bf16[2,256,640]{2,1,0:T(8,128)(2,1)}, bf16[2,256,640]{2,1,0:T(8,128)(2,1)}, u32[]{:S(2)}, u32[]{:S(2)}) collective-permute-start(bf16[2,256,640]{2,1,0:T(8,128)(2,1)} %pad_maximum_fusion.2), channel_id=1, source_target_pairs={{96,0},{97,1},{98,2},{99,3},{100,4},{101,5},{102,6},{103,7},{104,8... | collective-permute-start | bytes 1966088 | tf_op jit(solution)/shard_map/ppermute | solution.py:22
  31.8 2.1 %constant_dynamic-slice_fusion = bf16[320,1280]{1,0:T(8,128)(2,1)} fusion(bf16[640,1280]{1,0:T(8,128)(2,1)} %param.17, s32[]{:T(128)S(6)} %select_n.83), kind=kLoop, calls=%fused_computation.39 | loop fusion | bytes 1638404 | tf_op jit(solution)/shard_map/dynamic_slice | solution.py:55
  33.9 0.0 collective-permute-done.refs_0_.refs_4_
  33.9 2.9 %collective-permute-start.6 = (bf16[320,1280]{1,0:T(8,128)(2,1)}, bf16[320,1280]{1,0:T(8,128)(2,1)S(1)}, u32[]{:S(2)}, u32[]{:S(2)}) collective-permute-start(bf16[320,1280]{1,0:T(8,128)(2,1)} %constant_dynamic-slice_fusion), channel_id=1, source_target_pairs={{128,0},{0,128},{129,1},{1,129},{130,2},{2,130},{131,3},{3,131},{1... | collective-permute-start | bytes 2457608 | tf_op jit(solution)/shard_map/ppermute | solution.py:22
  36.8 0.9 pad_maximum_fusion.3
  37.7 1.2 %collective-permute-done.1.refs_1_.refs_5_ = bf16[2,256,640]{2,1,0:T(8,128)(2,1)S(1)} collective-permute-done((bf16[2,256,640]{2,1,0:T(8,128)(2,1)}, bf16[2,256,640]{2,1,0:T(8,128)(2,1)S(1)}, u32[]{:S(2)}, u32[]{:S(2)}) %collective-permute-start.1) | collective-permute-done | bytes 655392 | tf_op jit(solution)/shard_map/ppermute | solution.py:22
  39.0 0.0 collective-permute-start.9
  39.0 0.0 copy-done.12
  39.0 0.7 fusion.12
  44.6 5.5 %collective-permute-done.2.refs_2_.refs_6_ = bf16[2,256,640]{2,1,0:T(8,128)(2,1)S(1)} collective-permute-done((bf16[2,256,640]{2,1,0:T(8,128)(2,1)}, bf16[2,256,640]{2,1,0:T(8,128)(2,1)S(1)}, u32[]{:S(2)}, u32[]{:S(2)}) %collective-permute-start.2) | collective-permute-done | bytes 655392 | tf_op jit(solution)/shard_map/ppermute | solution.py:22
  50.2 4.3 %collective-permute-done.3.refs_3_.refs_7_ = bf16[2,256,640]{2,1,0:T(8,128)(2,1)} collective-permute-done((bf16[2,256,640]{2,1,0:T(8,128)(2,1)}, bf16[2,256,640]{2,1,0:T(8,128)(2,1)}, u32[]{:S(2)}, u32[]{:S(2)}) %collective-permute-start.3) | collective-permute-done | bytes 655392 | tf_op jit(solution)/shard_map/ppermute | solution.py:22
  54.5 0.0 copy-done.2
  54.5 0.0 copy-done.3
  54.5 0.0 copy-done.4
  54.5 7.0 %shard_map.150 = bf16[512,256]{1,0:T(8,128)(2,1)} custom-call(s32[1]{0:T(128)S(6)} %copy.24.live_ref, s32[1]{0:T(128)S(6)} %copy.25.depth_ref, bf16[512,640]{1,0:T(8,128)(2,1)} %get-tuple-element.10.q_ref, bf16[512,640]{1,0:T(8,128)(2,1)} %get-tuple-element.11.k_ref, bf16[512,640]{1,0:T(8,128)(2,1)} %get-tuple-element.12.v_ref, ...), custom_call_target="tpu_custom_call" | custom-call | tf_op jit(solution)/shard_map/pallas_call | solution.py:170
  61.5 2.9 %collective-permute-start.4 = (bf16[512,256]{1,0:T(8,128)(2,1)}, bf16[512,256]{1,0:T(8,128)(2,1)S(1)}, u32[]{:S(2)}, u32[]{:S(2)}) collective-permute-start(bf16[512,256]{1,0:T(8,128)(2,1)} %shard_map.150), channel_id=1, source_target_pairs={{128,0},{0,128},{129,1},{1,129},{130,2},{2,130},{131,3},{3,131},{1... | collective-permute-start | bytes 786440 | tf_op jit(solution)/shard_map/ppermute | solution.py:22
  64.4 9.6 %shard_map.151 = bf16[512,384]{1,0:T(8,128)(2,1)} custom-call(s32[1]{0:T(128)S(6)} %copy.24.live_ref, s32[1]{0:T(128)S(6)} %copy.25.depth_ref, bf16[512,640]{1,0:T(8,128)(2,1)} %get-tuple-element.10.q_ref, bf16[512,640]{1,0:T(8,128)(2,1)} %get-tuple-element.11.k_ref, bf16[512,640]{1,0:T(8,128)(2,1)} %get-tuple-element.12.v_ref, ...), custom_call_target="tpu_custom_call" | custom-call | tf_op jit(solution)/shard_map/pallas_call | solution.py:170
  73.9 0.0 copy-start.7
  73.9 0.7 collective-permute-start.5
  74.7 0.0 collective-permute-done.8
  74.7 0.1 broadcast.62.clone
  74.7 1.0 %slice_dynamic-update-slice_fusion.1 = bf16[2,256,640]{2,1,0:T(8,128)(2,1)S(1)} fusion(bf16[2,256,640]{2,1,0:T(8,128)(2,1)S(1)} %broadcast.62.clone, s32[]{:T(128)S(6)} %select_n.91, bf16[2,256,640]{2,1,0:T(8,128)(2,1)} %collective-permute-done.8), kind=kLoop, calls=%fused_computation.27 | loop fusion | bytes 655364 | tf_op jit(solution)/shard_map/jit(dynamic_update_index_in_dim)/dynamic_update_slice | solution.py:234
  75.7 0.0 collective-permute-done.6
  75.8 0.3 collective-permute-start.7
  76.0 0.1 broadcast.62.clone.1
  76.1 1.0 %slice_dynamic-update-slice_fusion.3 = bf16[2,256,640]{2,1,0:T(8,128)(2,1)S(1)} fusion(bf16[2,256,640]{2,1,0:T(8,128)(2,1)S(1)} %broadcast.62.clone.1, s32[]{:T(128)S(6)} %select_n.91, bf16[2,256,640]{2,1,0:T(8,128)(2,1)} %collective-permute-done.8), kind=kLoop, calls=%fused_computation.29 | loop fusion | bytes 655364 | tf_op jit(solution)/shard_map/jit(dynamic_update_index_in_dim)/dynamic_update_slice | solution.py:233
  77.1 0.0 collective-permute-done.9
  77.1 0.1 slice_dynamic-update-slice_fusion
  77.2 0.0 copy-start.8
  77.3 0.0 copy-start.9
  77.3 0.0 collective-permute-done.4
  77.3 8.1 %collective-permute-done.5 = bf16[512,384]{1,0:T(8,128)(2,1)S(1)} collective-permute-done((bf16[512,384]{1,0:T(8,128)(2,1)}, bf16[512,384]{1,0:T(8,128)(2,1)S(1)}, u32[]{:S(2)}, u32[]{:S(2)}) %collective-permute-start.5) | collective-permute-done | bytes 393248 | tf_op jit(solution)/shard_map/ppermute | solution.py:22
  85.4 0.1 constant_dynamic-update-slice_fusion
  85.5 0.0 copy-done.6
  85.5 0.0 copy-done.7
  85.5 0.0 copy-start.5
  85.5 0.2 broadcast_select_fusion.5
  85.7 0.0 collective-permute-done.7
  85.7 0.1 broadcast_select_fusion.3
  85.9 0.0 copy-done.8
  85.9 1.0 %copy-done.5 = bf16[640,1280]{1,0:T(8,128)(2,1)S(1)} copy-done((bf16[640,1280]{1,0:T(8,128)(2,1)S(1)}, bf16[640,1280]{1,0:T(8,128)(2,1)}, u32[]{:S(2)}) %copy-start.5) | copy-done | bytes 1638424
  86.9 0.6 broadcast_select_fusion.1
  87.5 0.0 copy-start.1
  87.5 0.0 copy-start.10
  87.5 2.0 %multiply_reduce_fusion.1 = (f32[512]{0:T(512)S(1)}, f32[512,1280]{1,0:T(8,128)S(1)}) fusion(bf16[640,1280]{1,0:T(8,128)(2,1)S(1)} %get-tuple-element.18, bf16[640,1280]{1,0:T(8,128)(2,1)S(1)} %get-tuple-element.17, bf16[512,640]{1,0:T(8,128)(2,1)S(1)} %get-tuple-element.22, bf16[512,640]{1,0:T(8,128)(2,1)S(1)} %get-tuple-element.21), kind=kOutput, calls=%fused_computation.12 | convolution fusion | flops 1688206848 | bytes 7211008 | tf_op jit(solution)/shard_map/dot_general | solution.py:273
  89.5 0.8 multiply_reduce_fusion
  90.4 1.8 %multiply_convert_fusion = bf16[512,1280]{1,0:T(8,128)(2,1)} fusion(f32[512]{0:T(512)S(1)} %add_rsqrt_fusion, f32[512,1280]{1,0:T(8,128)S(1)} %get-tuple-element.32, f32[512]{0:T(512)S(1)} %add_rsqrt_fusion.1, f32[1280]{0:T(1024)S(1)} %copy-done.10, f32[512]{0:T(512)S(1)} %add_rsqrt_fusion.2, bf16[512,1280]{1,0:T(8,128)(2,1)S(1)} %copy-done.1), kind=kLoop, calls=%fused_computation.10 | loop fusion | flops 5242880 | bytes 5254144 | tf_op jit(solution)/shard_map/convert_element_type | solution.py:279
  (11 shorter events, 0.1 us)
Async XLA Ops:
  0.6 16.4 %copy-start = (bf16[512,1280]{1,0:T(8,128)(2,1)S(1)}, bf16[512,1280]{1,0:T(8,128)(2,1)}, u32[]{:S(2)}) copy-start(bf16[512,1280]{1,0:T(8,128)(2,1)} %x_ref.1) | copy-start | bytes 3932164
  0.6 17.6 %copy-start.11 = (f32[640]{0:T(1024)S(1)}, f32[640]{0:T(1024)}, u32[]{:S(2)}) copy-start(f32[640]{0:T(1024)} %param.18) | copy-start | bytes 7684
  7.2 26.7 %collective-permute-start = (bf16[2,256,640]{2,1,0:T(8,128)(2,1)}, bf16[2,256,640]{2,1,0:T(8,128)(2,1)S(1)}, u32[]{:S(2)}, u32[]{:S(2)}) collective-permute-start(bf16[2,256,640]{2,1,0:T(8,128)(2,1)} %get-tuple-element.13), channel_id=1, source_target_pairs={{1,0},{2,1},{3,2},{4,3},{5,4},{6,5},{7,6},{8,7},{9,8},{10,9},{11,1... | collective-permute-start | bytes 1966088 | tf_op jit(solution)/shard_map/ppermute | solution.py:22
  13.9 25.1 %collective-permute-start.1 = (bf16[2,256,640]{2,1,0:T(8,128)(2,1)}, bf16[2,256,640]{2,1,0:T(8,128)(2,1)S(1)}, u32[]{:S(2)}, u32[]{:S(2)}) collective-permute-start(bf16[2,256,640]{2,1,0:T(8,128)(2,1)} %get-tuple-element.14), channel_id=1, source_target_pairs={{33,0},{34,1},{35,2},{36,3},{37,4},{38,5},{39,6},{40,7},{41,8},{42... | collective-permute-start | bytes 1966088 | tf_op jit(solution)/shard_map/ppermute | solution.py:22
  15.1 35.1 %collective-permute-start.2 = (bf16[2,256,640]{2,1,0:T(8,128)(2,1)}, bf16[2,256,640]{2,1,0:T(8,128)(2,1)S(1)}, u32[]{:S(2)}, u32[]{:S(2)}) collective-permute-start(bf16[2,256,640]{2,1,0:T(8,128)(2,1)} %get-tuple-element.15), channel_id=1, source_target_pairs={{65,0},{66,1},{67,2},{68,3},{69,4},{70,5},{71,6},{72,7},{73,8},{74... | collective-permute-start | bytes 1966088 | tf_op jit(solution)/shard_map/ppermute | solution.py:22
  17.0 37.5 %collective-permute-start.3 = (bf16[2,256,640]{2,1,0:T(8,128)(2,1)}, bf16[2,256,640]{2,1,0:T(8,128)(2,1)}, u32[]{:S(2)}, u32[]{:S(2)}) collective-permute-start(bf16[2,256,640]{2,1,0:T(8,128)(2,1)} %get-tuple-element.16), channel_id=1, source_target_pairs={{97,0},{98,1},{99,2},{100,3},{101,4},{102,5},{103,6},{104,7},{105,... | collective-permute-start | bytes 1966088 | tf_op jit(solution)/shard_map/ppermute | solution.py:22
  29.3 9.7 %copy-start.12 = (s32[256]{0:T(256)S(1)}, s32[256]{0:T(256)}, u32[]{:S(2)}) copy-start(s32[256]{0:T(256)} %param.25) | copy-start | bytes 3076
  30.3 44.4 %collective-permute-start.8 = (bf16[2,256,640]{2,1,0:T(8,128)(2,1)}, bf16[2,256,640]{2,1,0:T(8,128)(2,1)}, u32[]{:S(2)}, u32[]{:S(2)}) collective-permute-start(bf16[2,256,640]{2,1,0:T(8,128)(2,1)} %pad_maximum_fusion.2), channel_id=1, source_target_pairs={{96,0},{97,1},{98,2},{99,3},{100,4},{101,5},{102,6},{103,7},{104,8... | collective-permute-start | bytes 1966088 | tf_op jit(solution)/shard_map/ppermute | solution.py:22
  33.9 20.6 %copy-start.2 = (bf16[2,256,640]{2,1,0:T(8,128)(2,1)}, bf16[2,256,640]{2,1,0:T(8,128)(2,1)S(1)}, u32[]{:S(2)}) copy-start(bf16[2,256,640]{2,1,0:T(8,128)(2,1)S(1)} %collective-permute-done.refs_0_.refs_4_) | copy-start | bytes 1966084
  33.9 41.8 %collective-permute-start.6 = (bf16[320,1280]{1,0:T(8,128)(2,1)}, bf16[320,1280]{1,0:T(8,128)(2,1)S(1)}, u32[]{:S(2)}, u32[]{:S(2)}) collective-permute-start(bf16[320,1280]{1,0:T(8,128)(2,1)} %constant_dynamic-slice_fusion), channel_id=1, source_target_pairs={{128,0},{0,128},{129,1},{1,129},{130,2},{2,130},{131,3},{3,131},{1... | collective-permute-start | bytes 2457608 | tf_op jit(solution)/shard_map/ppermute | solution.py:22
  39.0 15.5 %copy-start.3 = (bf16[2,256,640]{2,1,0:T(8,128)(2,1)}, bf16[2,256,640]{2,1,0:T(8,128)(2,1)S(1)}, u32[]{:S(2)}) copy-start(bf16[2,256,640]{2,1,0:T(8,128)(2,1)S(1)} %collective-permute-done.1.refs_1_.refs_5_) | copy-start | bytes 1966084
  39.0 38.2 %collective-permute-start.9 = (bf16[2,256,640]{2,1,0:T(8,128)(2,1)}, bf16[2,256,640]{2,1,0:T(8,128)(2,1)S(1)}, u32[]{:S(2)}, u32[]{:S(2)}) collective-permute-start(bf16[2,256,640]{2,1,0:T(8,128)(2,1)} %pad_maximum_fusion.3), channel_id=1, source_target_pairs={{32,0},{33,1},{34,2},{35,3},{36,4},{37,5},{38,6},{39,7},{40,8},{41... | collective-permute-start | bytes 1966088 | tf_op jit(solution)/shard_map/ppermute | solution.py:22
  50.2 4.3 %copy-start.4 = (bf16[2,256,640]{2,1,0:T(8,128)(2,1)}, bf16[2,256,640]{2,1,0:T(8,128)(2,1)S(1)}, u32[]{:S(2)}) copy-start(bf16[2,256,640]{2,1,0:T(8,128)(2,1)S(1)} %collective-permute-done.2.refs_2_.refs_6_) | copy-start | bytes 1966084
  61.5 15.8 %collective-permute-start.4 = (bf16[512,256]{1,0:T(8,128)(2,1)}, bf16[512,256]{1,0:T(8,128)(2,1)S(1)}, u32[]{:S(2)}, u32[]{:S(2)}) collective-permute-start(bf16[512,256]{1,0:T(8,128)(2,1)} %shard_map.150), channel_id=1, source_target_pairs={{128,0},{0,128},{129,1},{1,129},{130,2},{2,130},{131,3},{3,131},{1... | collective-permute-start | bytes 786440 | tf_op jit(solution)/shard_map/ppermute | solution.py:22
  73.9 11.5 %copy-start.6 = (bf16[512,384]{1,0:T(8,128)(2,1)S(1)}, bf16[512,384]{1,0:T(8,128)(2,1)}, u32[]{:S(2)}) copy-start(bf16[512,384]{1,0:T(8,128)(2,1)} %shard_map.151) | copy-start | bytes 1179652
  73.9 11.5 %copy-start.7 = (bf16[512,256]{1,0:T(8,128)(2,1)S(1)}, bf16[512,256]{1,0:T(8,128)(2,1)}, u32[]{:S(2)}) copy-start(bf16[512,256]{1,0:T(8,128)(2,1)} %shard_map.150) | copy-start | bytes 786436
  73.9 11.4 %collective-permute-start.5 = (bf16[512,384]{1,0:T(8,128)(2,1)}, bf16[512,384]{1,0:T(8,128)(2,1)S(1)}, u32[]{:S(2)}, u32[]{:S(2)}) collective-permute-start(bf16[512,384]{1,0:T(8,128)(2,1)} %shard_map.151), channel_id=1, source_target_pairs={{128,0},{0,128},{129,1},{1,129},{130,2},{2,130},{131,3},{3,131},{1... | collective-permute-start | bytes 1179656 | tf_op jit(solution)/shard_map/ppermute | solution.py:22
  75.8 10.0 %collective-permute-start.7 = (bf16[320,1280]{1,0:T(8,128)(2,1)S(1)}, bf16[320,1280]{1,0:T(8,128)(2,1)S(1)}, u32[]{:S(2)}, u32[]{:S(2)}) collective-permute-start(bf16[320,1280]{1,0:T(8,128)(2,1)S(1)} %collective-permute-done.6), channel_id=1, source_target_pairs={{0,1},{1,0},{2,3},{3,2},{4,5},{5,4},{6,7},{7,6},{8,9},{9,8},{10,11... | collective-permute-start | bytes 2457608 | tf_op jit(solution)/shard_map/ppermute | solution.py:58
  77.2 8.6 %copy-start.8 = (bf16[2,256,640]{2,1,0:T(8,128)(2,1)}, bf16[2,256,640]{2,1,0:T(8,128)(2,1)S(1)}, u32[]{:S(2)}) copy-start(bf16[2,256,640]{2,1,0:T(8,128)(2,1)S(1)} %get-tuple-element.24) | copy-start | bytes 1966084
  77.3 8.6 %copy-start.9 = (bf16[2,256,640]{2,1,0:T(8,128)(2,1)}, bf16[2,256,640]{2,1,0:T(8,128)(2,1)S(1)}, u32[]{:S(2)}) copy-start(bf16[2,256,640]{2,1,0:T(8,128)(2,1)S(1)} %get-tuple-element.23) | copy-start | bytes 1966084
  85.5 1.4 %copy-start.5 = (bf16[640,1280]{1,0:T(8,128)(2,1)S(1)}, bf16[640,1280]{1,0:T(8,128)(2,1)}, u32[]{:S(2)}) copy-start(bf16[640,1280]{1,0:T(8,128)(2,1)} %param.17) | copy-start | bytes 4915204
  87.5 2.0 %copy-start.1 = (bf16[512,1280]{1,0:T(8,128)(2,1)S(1)}, bf16[512,1280]{1,0:T(8,128)(2,1)}, u32[]{:S(2)}) copy-start(bf16[512,1280]{1,0:T(8,128)(2,1)} %x_ref.1) | copy-start | bytes 3932164
  87.5 2.0 %copy-start.10 = (f32[1280]{0:T(1024)S(1)}, f32[1280]{0:T(1024)}, u32[]{:S(2)}) copy-start(f32[1280]{0:T(1024)} %param.19) | copy-start | bytes 15364

commit v17 on v11

--- a/solution.py
+++ b/solution.py
@@ -152,7 +152,7 @@
 
 def attention(queries, key_rows, value_rows, pages, req_len, prefix_len, first_pair, pairs):
     tokens = queries.shape[0]
-    tile = 256
+    tile = 512
     lanes = 2 * HD
     width = pairs * lanes
     grid = (pairs, tokens // tile)

time: 89.9 us -> 88.4 us (0.983)
  Pallas kernels: 30.7 us -> 29.1 us
    pallas_call x2, Pallas kernels: 16.5 us -> 14.9 us  [attention(): pl.pallas_call(attention_kernel, out_shape=jax.ShapeDtypeStruct((tokens,...]
  transfers between devices with their start and end apart: 10 -> 10, of which waited for: 4 -> 4; matrix products, arithmetic and copies ran while one was open for 12% -> 12% of each run, Pallas kernels for 29% -> 27%
where the time goes in v17:
time: 88.4 us; the launch traced here: 87.4 us
  Pallas kernels  29.1 us (33%)
  starting transfers between devices  18 us (20%)
  waiting for transfers between devices  16.2 us (18%)
  local copies, waits for them, and re-layouts  10.5 us (12%)
  between operations  5.84 us (7%)
  other arithmetic  5.78 us (7%)
  matrix products  1.98 us (2%)
    ppermute x9, starting transfers between devices, from_behind(): return lax.ppermute(block, axis, route)  17.9 us
    ppermute x9, waiting for transfers between devices, from_behind(): return lax.ppermute(block, axis, route)  16.2 us
    pallas_call x2, Pallas kernels, attention(): pl.pallas_call(attention_kernel, out_shape=jax.ShapeDtypeStruct((tokens,...  14.9 us
    pallas_call x1, Pallas kernels, projections(): pl.pallas_call(projection_kernel, out_shape=(shape, shape, shape), grid=(...  9.11 us
    pallas_call x1, Pallas kernels, fetch_pages(): pl.pallas_call(functools.partial(gather_kernel, devices), out_shape=[page...  5.07 us
    unnamed x28, local copies, waits for them, and re-layouts  2.65 us
    dynamic_slice x1, local copies, waits for them, and re-layouts, other_half_once_per_chip(): mine = lax.dynamic_slice_in_dim(w_out, core * rows, rows, 0)  2.09 us
    dot_general x1, matrix products, body(): jnp.dot(in_kv_order(attended, other_attended, 1), in_kv_order(w_out, othe...  1.98 us
  transfers between devices with their start and end apart: 10, of which 4 were waited for; matrix products, arithmetic and copies ran while one was open for 12% of the time, Pallas kernels for 27%

profile of v17, /device:TPU:6, one launch (start us, length us, event | category | flops | bytes accessed | tf_op | source)
XLA Modules:
  0.0 87.4 jit_solution(6412290039091163238)
XLA Ops:
  0.6 0.0 copy-start
  0.6 0.0 copy-start.11
  0.7 1.5 %copy.18.pages_ref = s32[128,4]{1,0:T(8,128)} copy(s32[128,4]{0,1:T(4,128)} %param.24) | data formatting | bytes 4096 | tf_op args[11]
  2.2 5.1 %shard_map.149 = (bf16[2,256,640]{2,1,0:T(8,128)(2,1)}, bf16[2,256,640]{2,1,0:T(8,128)(2,1)}, bf16[2,256,640]{2,1,0:T(8,128)(2,1)}, bf16[2,256,640]{2,1,0:T(8,128)(2,1)}) custom-call(s32[128,4]{1,0:T(8,128)} %copy.18.pages_ref, bf16[4,256,640]{2,1,0:T(8,128)(2,1)} %keys_hbm.1, bf16[4,256,640]{2,1,0:T(8,128)(2,1)} %values_hbm.1), custom_call_target="tpu_custom_call" | custom-call | tf_op jit(solution)/shard_map/pallas_call | solution.py:206
  7.2 6.6 %collective-permute-start = (bf16[2,256,640]{2,1,0:T(8,128)(2,1)}, bf16[2,256,640]{2,1,0:T(8,128)(2,1)S(1)}, u32[]{:S(2)}, u32[]{:S(2)}) collective-permute-start(bf16[2,256,640]{2,1,0:T(8,128)(2,1)} %get-tuple-element.13), channel_id=1, source_target_pairs={{1,0},{2,1},{3,2},{4,3},{5,4},{6,5},{7,6},{8,7},{9,8},{10,9},{11,1... | collective-permute-start | bytes 1966088 | tf_op jit(solution)/shard_map/ppermute | solution.py:22
  13.9 1.4 %collective-permute-start.1 = (bf16[2,256,640]{2,1,0:T(8,128)(2,1)}, bf16[2,256,640]{2,1,0:T(8,128)(2,1)S(1)}, u32[]{:S(2)}, u32[]{:S(2)}) collective-permute-start(bf16[2,256,640]{2,1,0:T(8,128)(2,1)} %get-tuple-element.14), channel_id=1, source_target_pairs={{33,0},{34,1},{35,2},{36,3},{37,4},{38,5},{39,6},{40,7},{41,8},{42... | collective-permute-start | bytes 1966088 | tf_op jit(solution)/shard_map/ppermute | solution.py:22
  15.3 1.9 %collective-permute-start.2 = (bf16[2,256,640]{2,1,0:T(8,128)(2,1)}, bf16[2,256,640]{2,1,0:T(8,128)(2,1)S(1)}, u32[]{:S(2)}, u32[]{:S(2)}) collective-permute-start(bf16[2,256,640]{2,1,0:T(8,128)(2,1)} %get-tuple-element.15), channel_id=1, source_target_pairs={{65,0},{66,1},{67,2},{68,3},{69,4},{70,5},{71,6},{72,7},{73,8},{74... | collective-permute-start | bytes 1966088 | tf_op jit(solution)/shard_map/ppermute | solution.py:22
  17.2 0.0 collective-permute-start.3
  17.2 0.0 copy-done
  17.2 0.3 fusion.7
  17.5 0.9 copy.17.scale_ref
  18.4 0.0 copy-done.11
  18.4 0.6 reshape.53.gain_ref
  19.0 9.1 %shard_map.148 = (bf16[512,640]{1,0:T(8,128)(2,1)}, bf16[512,640]{1,0:T(8,128)(2,1)}, bf16[512,640]{1,0:T(8,128)(2,1)}) custom-call(bf16[512,1280]{1,0:T(8,128)(2,1)} %x_ref.1, f32[512,1]{1,0:T(8,128)} %copy.17.scale_ref, bf16[1280,640]{1,0:T(8,128)(2,1)} %wq_ref.1, bf16[1280,640]{1,0:T(8,128)(2,1)} %wk_ref.1, bf16[1280,640]{1,0:T(8,128)(2,1)} %wv_ref.1, ...), custom_call_target="tpu_custom_call" | custom-call | tf_op jit(solution)/shard_map/pallas_call | solution.py:98
  28.1 1.4 %slice_bitcast_fusion = (bf16[1,256,640]{2,1,0:T(8,128)(2,1)S(1)}, bf16[1,256,640]{2,1,0:T(8,128)(2,1)S(1)}, bf16[1,256,640]{2,1,0:T(8,128)(2,1)S(1)}, bf16[1,256,640]{2,1,0:T(8,128)(2,1)S(1)}) fusion(bf16[512,640]{1,0:T(8,128)(2,1)} %get-tuple-element.12.v_ref, bf16[512,640]{1,0:T(8,128)(2,1)} %get-tuple-element.11.k_ref), kind=kLoop, calls=%fused_computation.30 | loop fusion | bytes 2621440 | tf_op jit(solution)/shard_map/slice | solution.py:229
  29.5 0.0 copy-start.12
  29.5 0.9 %pad_maximum_fusion.2 = bf16[2,256,640]{2,1,0:T(8,128)(2,1)} fusion(bf16[1,256,640]{2,1,0:T(8,128)(2,1)S(1)} %get-tuple-element.28, bf16[1,256,640]{2,1,0:T(8,128)(2,1)S(1)} %get-tuple-element.33), kind=kLoop, calls=%fused_computation.22 | loop fusion | flops 327680 | bytes 1310720 | tf_op jit(solution)/shard_map/stack | solution.py:229
  30.4 1.3 %collective-permute-start.8 = (bf16[2,256,640]{2,1,0:T(8,128)(2,1)}, bf16[2,256,640]{2,1,0:T(8,128)(2,1)}, u32[]{:S(2)}, u32[]{:S(2)}) collective-permute-start(bf16[2,256,640]{2,1,0:T(8,128)(2,1)} %pad_maximum_fusion.2), channel_id=1, source_target_pairs={{96,0},{97,1},{98,2},{99,3},{100,4},{101,5},{102,6},{103,7},{104,8... | collective-permute-start | bytes 1966088 | tf_op jit(solution)/shard_map/ppermute | solution.py:22
  31.7 2.1 %constant_dynamic-slice_fusion = bf16[320,1280]{1,0:T(8,128)(2,1)} fusion(bf16[640,1280]{1,0:T(8,128)(2,1)} %param.17, s32[]{:T(128)S(6)} %select_n.83), kind=kLoop, calls=%fused_computation.39 | loop fusion | bytes 1638404 | tf_op jit(solution)/shard_map/dynamic_slice | solution.py:55
  33.8 0.0 collective-permute-done.refs_0_.refs_4_
  33.8 2.9 %collective-permute-start.6 = (bf16[320,1280]{1,0:T(8,128)(2,1)}, bf16[320,1280]{1,0:T(8,128)(2,1)S(1)}, u32[]{:S(2)}, u32[]{:S(2)}) collective-permute-start(bf16[320,1280]{1,0:T(8,128)(2,1)} %constant_dynamic-slice_fusion), channel_id=1, source_target_pairs={{128,0},{0,128},{129,1},{1,129},{130,2},{2,130},{131,3},{3,131},{1... | collective-permute-start | bytes 2457608 | tf_op jit(solution)/shard_map/ppermute | solution.py:22
  36.7 0.9 %pad_maximum_fusion.3 = bf16[2,256,640]{2,1,0:T(8,128)(2,1)} fusion(bf16[1,256,640]{2,1,0:T(8,128)(2,1)S(1)} %get-tuple-element.27, bf16[1,256,640]{2,1,0:T(8,128)(2,1)S(1)} %get-tuple-element.34), kind=kLoop, calls=%fused_computation.23 | loop fusion | flops 327680 | bytes 1310720 | tf_op jit(solution)/shard_map/stack | solution.py:229
  37.6 1.5 %collective-permute-done.1.refs_1_.refs_5_ = bf16[2,256,640]{2,1,0:T(8,128)(2,1)S(1)} collective-permute-done((bf16[2,256,640]{2,1,0:T(8,128)(2,1)}, bf16[2,256,640]{2,1,0:T(8,128)(2,1)S(1)}, u32[]{:S(2)}, u32[]{:S(2)}) %collective-permute-start.1) | collective-permute-done | bytes 655392 | tf_op jit(solution)/shard_map/ppermute | solution.py:22
  39.1 0.0 collective-permute-start.9
  39.2 0.0 copy-done.12
  39.2 0.7 fusion.12
  44.8 5.4 %collective-permute-done.2.refs_2_.refs_6_ = bf16[2,256,640]{2,1,0:T(8,128)(2,1)S(1)} collective-permute-done((bf16[2,256,640]{2,1,0:T(8,128)(2,1)}, bf16[2,256,640]{2,1,0:T(8,128)(2,1)S(1)}, u32[]{:S(2)}, u32[]{:S(2)}) %collective-permute-start.2) | collective-permute-done | bytes 655392 | tf_op jit(solution)/shard_map/ppermute | solution.py:22
  50.2 4.3 %collective-permute-done.3.refs_3_.refs_7_ = bf16[2,256,640]{2,1,0:T(8,128)(2,1)} collective-permute-done((bf16[2,256,640]{2,1,0:T(8,128)(2,1)}, bf16[2,256,640]{2,1,0:T(8,128)(2,1)}, u32[]{:S(2)}, u32[]{:S(2)}) %collective-permute-start.3) | collective-permute-done | bytes 655392 | tf_op jit(solution)/shard_map/ppermute | solution.py:22
  54.5 0.0 copy-done.2
  54.5 0.0 copy-done.3
  54.5 0.0 copy-done.4
  54.5 8.6 %shard_map.150 = bf16[512,384]{1,0:T(8,128)(2,1)} custom-call(s32[1]{0:T(128)S(6)} %copy.24.live_ref, s32[1]{0:T(128)S(6)} %copy.25.depth_ref, bf16[512,640]{1,0:T(8,128)(2,1)} %get-tuple-element.10.q_ref, bf16[512,640]{1,0:T(8,128)(2,1)} %get-tuple-element.11.k_ref, bf16[512,640]{1,0:T(8,128)(2,1)} %get-tuple-element.12.v_ref, ...), custom_call_target="tpu_custom_call" | custom-call | tf_op jit(solution)/shard_map/pallas_call | solution.py:170
  63.1 2.9 %collective-permute-start.4 = (bf16[512,384]{1,0:T(8,128)(2,1)}, bf16[512,384]{1,0:T(8,128)(2,1)S(1)}, u32[]{:S(2)}, u32[]{:S(2)}) collective-permute-start(bf16[512,384]{1,0:T(8,128)(2,1)} %shard_map.150), channel_id=1, source_target_pairs={{128,0},{0,128},{129,1},{1,129},{130,2},{2,130},{131,3},{3,131},{1... | collective-permute-start | bytes 1179656 | tf_op jit(solution)/shard_map/ppermute | solution.py:22
  66.0 6.3 %shard_map.151 = bf16[512,256]{1,0:T(8,128)(2,1)} custom-call(s32[1]{0:T(128)S(6)} %copy.24.live_ref, s32[1]{0:T(128)S(6)} %copy.25.depth_ref, bf16[512,640]{1,0:T(8,128)(2,1)} %get-tuple-element.10.q_ref, bf16[512,640]{1,0:T(8,128)(2,1)} %get-tuple-element.11.k_ref, bf16[512,640]{1,0:T(8,128)(2,1)} %get-tuple-element.12.v_ref, ...), custom_call_target="tpu_custom_call" | custom-call | tf_op jit(solution)/shard_map/pallas_call | solution.py:170
  72.3 0.0 copy-start.7
  72.3 0.9 %collective-permute-start.5 = (bf16[512,256]{1,0:T(8,128)(2,1)}, bf16[512,256]{1,0:T(8,128)(2,1)S(1)}, u32[]{:S(2)}, u32[]{:S(2)}) collective-permute-start(bf16[512,256]{1,0:T(8,128)(2,1)} %shard_map.151), channel_id=1, source_target_pairs={{128,0},{0,128},{129,1},{1,129},{130,2},{2,130},{131,3},{3,131},{1... | collective-permute-start | bytes 786440 | tf_op jit(solution)/shard_map/ppermute | solution.py:22
  73.2 0.0 collective-permute-done.8
  73.2 0.1 broadcast.62.clone
  73.3 1.0 %slice_dynamic-update-slice_fusion.1 = bf16[2,256,640]{2,1,0:T(8,128)(2,1)S(1)} fusion(bf16[2,256,640]{2,1,0:T(8,128)(2,1)S(1)} %broadcast.62.clone, s32[]{:T(128)S(6)} %select_n.91, bf16[2,256,640]{2,1,0:T(8,128)(2,1)} %collective-permute-done.8), kind=kLoop, calls=%fused_computation.27 | loop fusion | bytes 655364 | tf_op jit(solution)/shard_map/jit(dynamic_update_index_in_dim)/dynamic_update_slice | solution.py:234
  74.3 0.0 collective-permute-done.6
  74.3 0.1 collective-permute-start.7
  74.4 0.1 broadcast.62.clone.1
  74.5 1.0 %slice_dynamic-update-slice_fusion.3 = bf16[2,256,640]{2,1,0:T(8,128)(2,1)S(1)} fusion(bf16[2,256,640]{2,1,0:T(8,128)(2,1)S(1)} %broadcast.62.clone.1, s32[]{:T(128)S(6)} %select_n.91, bf16[2,256,640]{2,1,0:T(8,128)(2,1)} %collective-permute-done.8), kind=kLoop, calls=%fused_computation.29 | loop fusion | bytes 655364 | tf_op jit(solution)/shard_map/jit(dynamic_update_index_in_dim)/dynamic_update_slice | solution.py:233
  75.5 0.0 collective-permute-done.9
  75.5 0.1 slice_dynamic-update-slice_fusion
  75.6 0.0 copy-start.8
  75.6 0.0 copy-start.9
  75.7 0.0 collective-permute-done.4
  75.7 5.0 %collective-permute-done.5 = bf16[512,256]{1,0:T(8,128)(2,1)S(1)} collective-permute-done((bf16[512,256]{1,0:T(8,128)(2,1)}, bf16[512,256]{1,0:T(8,128)(2,1)S(1)}, u32[]{:S(2)}, u32[]{:S(2)}) %collective-permute-start.5) | collective-permute-done | bytes 262176 | tf_op jit(solution)/shard_map/ppermute | solution.py:22
  80.7 0.0 copy-done.6
  80.7 0.0 copy-done.7
  80.7 0.0 copy-start.5
  80.7 0.2 broadcast_select_fusion.5
  81.0 0.0 collective-permute-done.7
  81.0 0.1 broadcast_select_fusion.3
  81.1 0.0 copy-done.8
  81.1 1.0 %copy-done.5 = bf16[640,1280]{1,0:T(8,128)(2,1)S(1)} copy-done((bf16[640,1280]{1,0:T(8,128)(2,1)S(1)}, bf16[640,1280]{1,0:T(8,128)(2,1)}, u32[]{:S(2)}) %copy-start.5) | copy-done | bytes 1638424
  82.2 0.6 broadcast_select_fusion.1
  82.8 0.0 copy-start.1
  82.8 0.0 copy-start.10
  82.8 2.0 %multiply_reduce_fusion.1 = (f32[512]{0:T(512)S(1)}, f32[512,1280]{1,0:T(8,128)S(1)}) fusion(bf16[640,1280]{1,0:T(8,128)(2,1)S(1)} %get-tuple-element.18, bf16[640,1280]{1,0:T(8,128)(2,1)S(1)} %get-tuple-element.17, bf16[512,640]{1,0:T(8,128)(2,1)S(1)} %get-tuple-element.22, bf16[512,640]{1,0:T(8,128)(2,1)S(1)} %get-tuple-element.21), kind=kOutput, calls=%fused_computation.12 | convolution fusion | flops 1688206848 | bytes 7211008 | tf_op jit(solution)/shard_map/dot_general | solution.py:273
  84.8 0.0 copy-done.1
  84.8 0.8 multiply_reduce_fusion
  85.6 1.8 %multiply_convert_fusion = bf16[512,1280]{1,0:T(8,128)(2,1)} fusion(f32[512]{0:T(512)S(1)} %add_rsqrt_fusion, f32[512,1280]{1,0:T(8,128)S(1)} %get-tuple-element.32, f32[512]{0:T(512)S(1)} %add_rsqrt_fusion.1, f32[1280]{0:T(1024)S(1)} %copy-done.10, f32[512]{0:T(512)S(1)} %add_rsqrt_fusion.2, bf16[512,1280]{1,0:T(8,128)(2,1)S(1)} %copy-done.1), kind=kLoop, calls=%fused_computation.10 | loop fusion | flops 5242880 | bytes 5254144 | tf_op jit(solution)/shard_map/convert_element_type | solution.py:279
  (11 shorter events, 0.1 us)
Async XLA Ops:
  0.6 16.5 %copy-start = (bf16[512,1280]{1,0:T(8,128)(2,1)S(1)}, bf16[512,1280]{1,0:T(8,128)(2,1)}, u32[]{:S(2)}) copy-start(bf16[512,1280]{1,0:T(8,128)(2,1)} %x_ref.1) | copy-start | bytes 3932164
  0.6 17.7 %copy-start.11 = (f32[640]{0:T(1024)S(1)}, f32[640]{0:T(1024)}, u32[]{:S(2)}) copy-start(f32[640]{0:T(1024)} %param.18) | copy-start | bytes 7684
  7.2 26.6 %collective-permute-start = (bf16[2,256,640]{2,1,0:T(8,128)(2,1)}, bf16[2,256,640]{2,1,0:T(8,128)(2,1)S(1)}, u32[]{:S(2)}, u32[]{:S(2)}) collective-permute-start(bf16[2,256,640]{2,1,0:T(8,128)(2,1)} %get-tuple-element.13), channel_id=1, source_target_pairs={{1,0},{2,1},{3,2},{4,3},{5,4},{6,5},{7,6},{8,7},{9,8},{10,9},{11,1... | collective-permute-start | bytes 1966088 | tf_op jit(solution)/shard_map/ppermute | solution.py:22
  13.9 25.3 %collective-permute-start.1 = (bf16[2,256,640]{2,1,0:T(8,128)(2,1)}, bf16[2,256,640]{2,1,0:T(8,128)(2,1)S(1)}, u32[]{:S(2)}, u32[]{:S(2)}) collective-permute-start(bf16[2,256,640]{2,1,0:T(8,128)(2,1)} %get-tuple-element.14), channel_id=1, source_target_pairs={{33,0},{34,1},{35,2},{36,3},{37,4},{38,5},{39,6},{40,7},{41,8},{42... | collective-permute-start | bytes 1966088 | tf_op jit(solution)/shard_map/ppermute | solution.py:22
  15.3 34.9 %collective-permute-start.2 = (bf16[2,256,640]{2,1,0:T(8,128)(2,1)}, bf16[2,256,640]{2,1,0:T(8,128)(2,1)S(1)}, u32[]{:S(2)}, u32[]{:S(2)}) collective-permute-start(bf16[2,256,640]{2,1,0:T(8,128)(2,1)} %get-tuple-element.15), channel_id=1, source_target_pairs={{65,0},{66,1},{67,2},{68,3},{69,4},{70,5},{71,6},{72,7},{73,8},{74... | collective-permute-start | bytes 1966088 | tf_op jit(solution)/shard_map/ppermute | solution.py:22
  17.2 37.3 %collective-permute-start.3 = (bf16[2,256,640]{2,1,0:T(8,128)(2,1)}, bf16[2,256,640]{2,1,0:T(8,128)(2,1)}, u32[]{:S(2)}, u32[]{:S(2)}) collective-permute-start(bf16[2,256,640]{2,1,0:T(8,128)(2,1)} %get-tuple-element.16), channel_id=1, source_target_pairs={{97,0},{98,1},{99,2},{100,3},{101,4},{102,5},{103,6},{104,7},{105,... | collective-permute-start | bytes 1966088 | tf_op jit(solution)/shard_map/ppermute | solution.py:22
  29.5 9.7 %copy-start.12 = (s32[256]{0:T(256)S(1)}, s32[256]{0:T(256)}, u32[]{:S(2)}) copy-start(s32[256]{0:T(256)} %param.25) | copy-start | bytes 3076
  30.4 42.8 %collective-permute-start.8 = (bf16[2,256,640]{2,1,0:T(8,128)(2,1)}, bf16[2,256,640]{2,1,0:T(8,128)(2,1)}, u32[]{:S(2)}, u32[]{:S(2)}) collective-permute-start(bf16[2,256,640]{2,1,0:T(8,128)(2,1)} %pad_maximum_fusion.2), channel_id=1, source_target_pairs={{96,0},{97,1},{98,2},{99,3},{100,4},{101,5},{102,6},{103,7},{104,8... | collective-permute-start | bytes 1966088 | tf_op jit(solution)/shard_map/ppermute | solution.py:22
  33.8 20.7 %copy-start.2 = (bf16[2,256,640]{2,1,0:T(8,128)(2,1)}, bf16[2,256,640]{2,1,0:T(8,128)(2,1)S(1)}, u32[]{:S(2)}) copy-start(bf16[2,256,640]{2,1,0:T(8,128)(2,1)S(1)} %collective-permute-done.refs_0_.refs_4_) | copy-start | bytes 1966084
  33.8 40.5 %collective-permute-start.6 = (bf16[320,1280]{1,0:T(8,128)(2,1)}, bf16[320,1280]{1,0:T(8,128)(2,1)S(1)}, u32[]{:S(2)}, u32[]{:S(2)}) collective-permute-start(bf16[320,1280]{1,0:T(8,128)(2,1)} %constant_dynamic-slice_fusion), channel_id=1, source_target_pairs={{128,0},{0,128},{129,1},{1,129},{130,2},{2,130},{131,3},{3,131},{1... | collective-permute-start | bytes 2457608 | tf_op jit(solution)/shard_map/ppermute | solution.py:22
  39.1 15.3 %copy-start.3 = (bf16[2,256,640]{2,1,0:T(8,128)(2,1)}, bf16[2,256,640]{2,1,0:T(8,128)(2,1)S(1)}, u32[]{:S(2)}) copy-start(bf16[2,256,640]{2,1,0:T(8,128)(2,1)S(1)} %collective-permute-done.1.refs_1_.refs_5_) | copy-start | bytes 1966084
  39.1 36.4 %collective-permute-start.9 = (bf16[2,256,640]{2,1,0:T(8,128)(2,1)}, bf16[2,256,640]{2,1,0:T(8,128)(2,1)S(1)}, u32[]{:S(2)}, u32[]{:S(2)}) collective-permute-start(bf16[2,256,640]{2,1,0:T(8,128)(2,1)} %pad_maximum_fusion.3), channel_id=1, source_target_pairs={{32,0},{33,1},{34,2},{35,3},{36,4},{37,5},{38,6},{39,7},{40,8},{41... | collective-permute-start | bytes 1966088 | tf_op jit(solution)/shard_map/ppermute | solution.py:22
  50.2 4.3 %copy-start.4 = (bf16[2,256,640]{2,1,0:T(8,128)(2,1)}, bf16[2,256,640]{2,1,0:T(8,128)(2,1)S(1)}, u32[]{:S(2)}) copy-start(bf16[2,256,640]{2,1,0:T(8,128)(2,1)S(1)} %collective-permute-done.2.refs_2_.refs_6_) | copy-start | bytes 1966084
  63.1 12.6 %collective-permute-start.4 = (bf16[512,384]{1,0:T(8,128)(2,1)}, bf16[512,384]{1,0:T(8,128)(2,1)S(1)}, u32[]{:S(2)}, u32[]{:S(2)}) collective-permute-start(bf16[512,384]{1,0:T(8,128)(2,1)} %shard_map.150), channel_id=1, source_target_pairs={{128,0},{0,128},{129,1},{1,129},{130,2},{2,130},{131,3},{3,131},{1... | collective-permute-start | bytes 1179656 | tf_op jit(solution)/shard_map/ppermute | solution.py:22
  72.3 8.4 %copy-start.6 = (bf16[512,384]{1,0:T(8,128)(2,1)S(1)}, bf16[512,384]{1,0:T(8,128)(2,1)}, u32[]{:S(2)}) copy-start(bf16[512,384]{1,0:T(8,128)(2,1)} %shard_map.150) | copy-start | bytes 1179652
  72.3 8.4 %copy-start.7 = (bf16[512,256]{1,0:T(8,128)(2,1)S(1)}, bf16[512,256]{1,0:T(8,128)(2,1)}, u32[]{:S(2)}) copy-start(bf16[512,256]{1,0:T(8,128)(2,1)} %shard_map.151) | copy-start | bytes 786436
  72.3 8.4 %collective-permute-start.5 = (bf16[512,256]{1,0:T(8,128)(2,1)}, bf16[512,256]{1,0:T(8,128)(2,1)S(1)}, u32[]{:S(2)}, u32[]{:S(2)}) collective-permute-start(bf16[512,256]{1,0:T(8,128)(2,1)} %shard_map.151), channel_id=1, source_target_pairs={{128,0},{0,128},{129,1},{1,129},{130,2},{2,130},{131,3},{3,131},{1... | collective-permute-start | bytes 786440 | tf_op jit(solution)/shard_map/ppermute | solution.py:22
  74.3 6.7 %collective-permute-start.7 = (bf16[320,1280]{1,0:T(8,128)(2,1)S(1)}, bf16[320,1280]{1,0:T(8,128)(2,1)S(1)}, u32[]{:S(2)}, u32[]{:S(2)}) collective-permute-start(bf16[320,1280]{1,0:T(8,128)(2,1)S(1)} %collective-permute-done.6), channel_id=1, source_target_pairs={{0,1},{1,0},{2,3},{3,2},{4,5},{5,4},{6,7},{7,6},{8,9},{9,8},{10,11... | collective-permute-start | bytes 2457608 | tf_op jit(solution)/shard_map/ppermute | solution.py:58
  75.6 5.5 %copy-start.8 = (bf16[2,256,640]{2,1,0:T(8,128)(2,1)}, bf16[2,256,640]{2,1,0:T(8,128)(2,1)S(1)}, u32[]{:S(2)}) copy-start(bf16[2,256,640]{2,1,0:T(8,128)(2,1)S(1)} %get-tuple-element.24) | copy-start | bytes 1966084
  75.6 5.5 %copy-start.9 = (bf16[2,256,640]{2,1,0:T(8,128)(2,1)}, bf16[2,256,640]{2,1,0:T(8,128)(2,1)S(1)}, u32[]{:S(2)}) copy-start(bf16[2,256,640]{2,1,0:T(8,128)(2,1)S(1)} %get-tuple-element.23) | copy-start | bytes 1966084
  80.7 1.4 %copy-start.5 = (bf16[640,1280]{1,0:T(8,128)(2,1)S(1)}, bf16[640,1280]{1,0:T(8,128)(2,1)}, u32[]{:S(2)}) copy-start(bf16[640,1280]{1,0:T(8,128)(2,1)} %param.17) | copy-start | bytes 4915204
  82.8 2.0 %copy-start.1 = (bf16[512,1280]{1,0:T(8,128)(2,1)S(1)}, bf16[512,1280]{1,0:T(8,128)(2,1)}, u32[]{:S(2)}) copy-start(bf16[512,1280]{1,0:T(8,128)(2,1)} %x_ref.1) | copy-start | bytes 3932164
  82.8 2.0 %copy-start.10 = (f32[1280]{0:T(1024)S(1)}, f32[1280]{0:T(1024)}, u32[]{:S(2)}) copy-start(f32[1280]{0:T(1024)} %param.19) | copy-start | bytes 15364
